TPU v7x, 32 devices: a whole 2x2x4 slice. The times are simulated.
32 devices in a mesh: dp: 8 (over y, x, core), tensor: 4 (over z).
Axes of the slice: x: 2, y: 2, z: 4, core: 2. Of those that a mesh axis runs over, the one named last changes fastest.
Arguments:
- tokens: bfloat16 [16, 1024, 1024], P('dp', 'tensor'), may hold values from -6 to 6
- segments: int32 [16, 1024], P('dp'), may hold values from 0 to 3, as said below
- qkv_weight: bfloat16 [3, 1024, 1024], P(None, None, 'tensor'), may hold values from -0.1875 to 0.1875
- qkv_bias: float32 [3, 1024], P(None, 'tensor'), may hold values from -1.5 to 1.5
- out_weight: bfloat16 [1024, 1024], P('tensor'), may hold values from -0.75 to 0.75
- out_bias: float32 [1024], replicated, may hold values from -1.5 to 1.5
- gain_one: float32 [1024], replicated, may hold values from 0.5 to 1.5
- shift_one: float32 [1024], replicated, may hold values from -1.5 to 1.5
- up_weight: bfloat16 [1024, 4096], P(None, 'tensor'), may hold values from -0.1875 to 0.1875
- up_bias: float32 [4096], P('tensor'), may hold values from -1.5 to 1.5
- down_weight: bfloat16 [4096, 1024], P('tensor'), may hold values from -0.1875 to 0.1875
- down_bias: float32 [1024], replicated, may hold values from -1.5 to 1.5
- gain_two: float32 [1024], replicated, may hold values from 0.5 to 1.5
- shift_two: float32 [1024], replicated, may hold values from -1.5 to 1.5
- proj_weight: bfloat16 [1024, 288], replicated, may hold values from -0.1875 to 0.1875
- out_grad: bfloat16 [16, 1024, 1024], P('dp', 'tensor'), may hold values from -6 to 6
- embed_grad: bfloat16 [16, 1024, 288], P('dp', 'tensor'), may hold values from -6 to 6
Outputs:
- layer_out: bfloat16 [16, 1024, 1024], P('dp', 'tensor')
- embeddings: bfloat16 [16, 1024, 288], P('dp', 'tensor')
- tokens_grad: float32 [16, 1024, 1024], P('dp', 'tensor')
- qkv_weight_grad: float32 [3, 1024, 1024], P(None, None, 'tensor')
- qkv_bias_grad: float32 [3, 1024], P(None, 'tensor')
- out_weight_grad: float32 [1024, 1024], P('tensor')
- out_bias_grad: float32 [1024], replicated
- gain_one_grad: float32 [1024], replicated
- shift_one_grad: float32 [1024], replicated
- up_weight_grad: float32 [1024, 4096], P(None, 'tensor')
- up_bias_grad: float32 [4096], P('tensor')
- down_weight_grad: float32 [4096, 1024], P('tensor')
- down_bias_grad: float32 [1024], replicated
- gain_two_grad: float32 [1024], replicated
- shift_two_grad: float32 [1024], replicated
- proj_weight_grad: float32 [1024, 288], replicated
Inputs may be any that keep to these rules, and one draw needn't show every extreme that they name: `segments`: segment numbers never fall along a sequence; every sequence holds 4 documents, each of at least 200 tokens, and in every sequence some document has exactly 200.
All inputs are finite; a program needn't handle non-finite values.
Results may differ from a plain program's by a relative error of at most 0.018.
Values may be sent and summed in bfloat16 or wider, within the bound.
A program may use at most 192 MiB of HBM per device.

v0:
```python
import math

import jax
import jax.numpy as jnp
from jax import lax
from jax.sharding import PartitionSpec as P

HEAD_DIM = 64


eps = 1e-05


def as_sent(array):

    def short(part):
        return part.astype(jnp.bfloat16) if part.dtype == jnp.float32 else part

    return jax.tree.map(short, array)


def doc_positions(segment_rows):
    length = segment_rows.shape[-1]
    row_index = jnp.broadcast_to(jnp.arange(length, dtype=jnp.int32), segment_rows.shape)
    change = jnp.concatenate(
        [
            jnp.ones(segment_rows.shape[:-1] + (1,), jnp.bool_),
            segment_rows[..., 1:] != segment_rows[..., :-1],
        ],
        axis=-1,
    )
    doc_start = lax.cummax(
        jnp.where(change, row_index, jnp.zeros_like(row_index)), axis=segment_rows.ndim - 1
    )
    return row_index - doc_start


def rotary_tables(positions, head_dim):
    half_dim = head_dim // 2
    exponent = jnp.arange(half_dim, dtype=jnp.float32) * (2.0 / head_dim)
    frequency = jnp.exp(-exponent * math.log(10000.0))
    angles = positions.astype(jnp.float32)[..., None] * frequency
    angles = jnp.concatenate([angles, angles], axis=-1)
    return (jnp.cos(angles), jnp.sin(angles))


def rotate(field, cosine, sine):
    half_dim = field.shape[-1] // 2
    rotated = jnp.concatenate([-field[..., half_dim:], field[..., :half_dim]], axis=-1)
    return field * cosine + rotated * sine


def rotate_back(field, cosine, sine):
    half_dim = field.shape[-1] // 2
    rotated = jnp.concatenate([-field[..., half_dim:], field[..., :half_dim]], axis=-1)
    return field * cosine - rotated * sine


def norm_forward(field, gain, shift):
    row_mean = jnp.mean(field, axis=-1, keepdims=True)
    centred = field - row_mean
    variance = jnp.mean(centred * centred, axis=-1, keepdims=True)
    inv_std = lax.rsqrt(variance + eps)
    scaled = centred * inv_std
    return (scaled * gain + shift, scaled, inv_std)


def norm_backward(upstream, scaled, inv_std, gain):
    grad_scaled = upstream * gain
    grad_input = inv_std * (
        grad_scaled
        - jnp.mean(grad_scaled, axis=-1, keepdims=True)
        - scaled * jnp.mean(grad_scaled * scaled, axis=-1, keepdims=True)
    )
    return (grad_input, jnp.sum(upstream * scaled, axis=(0, 1)), jnp.sum(upstream, axis=(0, 1)))


def device_rows(full_rows, row_count):
    groups, length, model_width = full_rows.shape
    local_rows = length // lax.axis_size("tensor")
    blocks = row_count // (groups * local_rows)
    picked = full_rows
    picked = picked.reshape(groups, blocks, local_rows, model_width).transpose(1, 0, 2, 3)
    return picked.reshape(row_count, model_width)


def masked_scores(queries, keys, seg_row):
    scores = jnp.einsum("hqd,hkd->hqk", queries, keys, preferred_element_type=jnp.float32)
    same_doc = seg_row[:, None] == seg_row[None, :]
    return jnp.where(same_doc[None], scores, -1000000000.0)


def attend(inputs):
    queries, keys, values_low, seg_row = inputs
    scores = masked_scores(queries, keys, seg_row)
    row_peak = jnp.max(scores, axis=-1, keepdims=True)
    shifted = jnp.exp(scores - row_peak)
    row_total = jnp.sum(shifted, axis=-1, keepdims=True)
    probs = (shifted / row_total).astype(jnp.bfloat16)
    mixed_heads = jnp.einsum("hqk,hkd->hqd", probs, values_low, preferred_element_type=jnp.float32)
    return (mixed_heads, row_peak + jnp.log(row_total))


def attend_back(inputs):
    queries, keys, values_low, seg_row, log_total, grad_mixed = inputs
    scores = masked_scores(queries, keys, seg_row)
    probs = jnp.exp(scores - log_total)
    grad_values = jnp.einsum(
        "hqk,hqd->hkd", probs.astype(jnp.bfloat16), grad_mixed, preferred_element_type=jnp.float32
    )
    grad_probs = jnp.einsum(
        "hqd,hkd->hqk", grad_mixed, values_low, preferred_element_type=jnp.float32
    )
    row_inner = jnp.sum(probs * grad_probs, axis=-1, keepdims=True)
    grad_scores = (probs * (grad_probs - row_inner)).astype(jnp.bfloat16)
    grad_queries = jnp.einsum("hqk,hkd->hqd", grad_scores, keys, preferred_element_type=jnp.float32)
    grad_keys = jnp.einsum("hqk,hqd->hkd", grad_scores, queries, preferred_element_type=jnp.float32)
    return (grad_queries, grad_keys, grad_values)


def process(tokens, segments, out_grad, embed_grad, weights):
    (
        qkv_weight,
        qkv_bias,
        out_weight,
        out_bias,
        gain_one,
        shift_one,
        up_weight,
        up_bias,
        down_weight,
        down_bias,
        gain_two,
        shift_two,
        proj_weight,
    ) = weights
    groups, local_rows, model_width = tokens.shape
    length = segments.shape[1]
    heads_here = qkv_weight.shape[2] // HEAD_DIM
    q_scale = HEAD_DIM ** (-0.5)
    cosine, sine = rotary_tables(doc_positions(segments), HEAD_DIM)
    cosine = cosine[:, None]
    sine = sine[:, None]

    def split_heads(field):
        return field.reshape(groups, length, heads_here, HEAD_DIM).transpose(0, 2, 1, 3)

    def join_heads(field):
        return field.transpose(0, 2, 1, 3).reshape(groups, length, heads_here * HEAD_DIM)

    whole_tokens = lax.all_gather(tokens, "tensor", axis=1, tiled=True)
    projected = jnp.einsum(
        "gld,cde->cgle", whole_tokens, qkv_weight, preferred_element_type=jnp.float32
    )
    projected = projected + qkv_bias[:, None, None, :]
    queries = (rotate(split_heads(projected[0]), cosine, sine) * q_scale).astype(jnp.bfloat16)
    keys = rotate(split_heads(projected[1]), cosine, sine).astype(jnp.bfloat16)
    values_low = split_heads(projected[2]).astype(jnp.bfloat16)
    mixed_heads, log_total = lax.map(attend, (queries, keys, values_low, segments))
    mixed = join_heads(mixed_heads).astype(jnp.bfloat16)
    attn_part = lax.psum_scatter(
        jnp.dot(
            device_rows(mixed, lax.axis_size("tensor") * (groups * local_rows)),
            out_weight,
            preferred_element_type=jnp.float32,
        ),
        "tensor",
        scatter_dimension=0,
        tiled=True,
    )
    attn_part = attn_part.reshape(groups, local_rows, model_width)
    first_sum = tokens.astype(jnp.float32) + (attn_part + out_bias)
    normed, scaled_one, inv_one = norm_forward(first_sum, gain_one, shift_one)
    whole_normed = lax.all_gather(normed.astype(jnp.bfloat16), "tensor", axis=1, tiled=True)
    hidden = (
        jnp.einsum("gld,df->glf", whole_normed, up_weight, preferred_element_type=jnp.float32)
        + up_bias
    )
    active = jax.nn.gelu(hidden, approximate=False).astype(jnp.bfloat16)
    ffn_part = lax.psum_scatter(
        jnp.dot(
            device_rows(active, lax.axis_size("tensor") * (groups * local_rows)),
            down_weight,
            preferred_element_type=jnp.float32,
        ),
        "tensor",
        scatter_dimension=0,
        tiled=True,
    )
    second_sum = normed + (ffn_part.reshape(groups, local_rows, model_width) + down_bias)
    result, scaled_two, inv_two = norm_forward(second_sum, gain_two, shift_two)
    result_low = result.astype(jnp.bfloat16)
    embedded = jnp.einsum(
        "gld,dp->glp", result_low, proj_weight, preferred_element_type=jnp.float32
    )
    grad_result = out_grad.astype(jnp.float32) + jnp.einsum(
        "glp,dp->gld", embed_grad, proj_weight, preferred_element_type=jnp.float32
    )
    proj_grad = jnp.einsum(
        "gld,glp->dp", result_low, embed_grad, preferred_element_type=jnp.float32
    )
    grad_second, gain_two_grad, shift_two_grad = norm_backward(
        grad_result, scaled_two, inv_two, gain_two
    )
    second_low = grad_second.astype(jnp.bfloat16)
    down_bias_grad = jnp.sum(second_low.astype(jnp.float32), axis=(0, 1))
    whole_second = lax.all_gather(second_low, "tensor", axis=1, tiled=True)
    down_weight_grad = jnp.einsum(
        "glf,gld->fd", active, whole_second, preferred_element_type=jnp.float32
    )
    grad_active = jnp.einsum(
        "gld,fd->glf", whole_second, down_weight, preferred_element_type=jnp.float32
    )
    gelu_pull = jax.vjp(lambda field: jax.nn.gelu(field, approximate=False), hidden)[1]
    grad_hidden = gelu_pull(grad_active)[0].astype(jnp.bfloat16)
    up_bias_grad = jnp.sum(grad_hidden.astype(jnp.float32), axis=(0, 1))
    up_weight_grad = jnp.einsum(
        "gld,glf->df", whole_normed, grad_hidden, preferred_element_type=jnp.float32
    )
    ffn_back = lax.psum_scatter(
        jnp.einsum(
            "nf,df->nd",
            device_rows(grad_hidden, lax.axis_size("tensor") * (groups * local_rows)),
            up_weight,
            preferred_element_type=jnp.float32,
        ),
        "tensor",
        scatter_dimension=0,
        tiled=True,
    )
    grad_normed = grad_second + ffn_back.reshape(groups, local_rows, model_width)
    grad_first, gain_one_grad, shift_one_grad = norm_backward(
        grad_normed, scaled_one, inv_one, gain_one
    )
    first_low = grad_first.astype(jnp.bfloat16)
    out_bias_grad = jnp.sum(first_low.astype(jnp.float32), axis=(0, 1))
    whole_first = lax.all_gather(first_low, "tensor", axis=1, tiled=True)
    out_weight_grad = jnp.einsum(
        "glh,gld->hd", mixed, whole_first, preferred_element_type=jnp.float32
    )
    grad_mixed = jnp.einsum(
        "gld,hd->glh", whole_first, out_weight, preferred_element_type=jnp.float32
    )
    grad_mixed = split_heads(grad_mixed.astype(jnp.bfloat16))
    grad_queries, grad_keys, grad_values = lax.map(
        attend_back, (queries, keys, values_low, segments, log_total, grad_mixed)
    )
    grad_queries = rotate_back(grad_queries * q_scale, cosine, sine)
    grad_keys = rotate_back(grad_keys, cosine, sine)
    grad_qkv = jnp.stack(
        [join_heads(grad_queries), join_heads(grad_keys), join_heads(grad_values)]
    ).astype(jnp.bfloat16)
    qkv_bias_grad = jnp.sum(grad_qkv.astype(jnp.float32), axis=(1, 2))
    qkv_weight_grad = jnp.einsum(
        "gld,cgle->cde", whole_tokens, grad_qkv, preferred_element_type=jnp.float32
    )
    joined_grad = grad_qkv.transpose(1, 2, 0, 3).reshape(groups, length, 3 * heads_here * HEAD_DIM)
    joined_weight = qkv_weight.transpose(1, 0, 2).reshape(model_width, 3 * heads_here * HEAD_DIM)
    input_back = lax.psum_scatter(
        jnp.einsum(
            "ne,de->nd",
            device_rows(joined_grad, groups * local_rows * lax.axis_size("tensor")),
            joined_weight,
            preferred_element_type=jnp.float32,
        ).astype(jnp.bfloat16),
        "tensor",
        scatter_dimension=0,
        tiled=True,
    ).astype(jnp.float32)
    tokens_grad = grad_first + input_back.reshape(groups, local_rows, model_width)
    sharded_grads = (
        qkv_weight_grad,
        qkv_bias_grad,
        out_weight_grad,
        up_weight_grad,
        up_bias_grad,
        down_weight_grad,
    )
    shared_grads = (
        out_bias_grad,
        gain_one_grad,
        shift_one_grad,
        down_bias_grad,
        gain_two_grad,
        shift_two_grad,
        proj_grad,
    )
    return (result_low, embedded.astype(jnp.bfloat16), tokens_grad, sharded_grads, shared_grads)


def per_device(
    tokens,
    segments,
    qkv_weight,
    qkv_bias,
    out_weight,
    out_bias,
    gain_one,
    shift_one,
    up_weight,
    up_bias,
    down_weight,
    down_bias,
    gain_two,
    shift_two,
    proj_weight,
    out_grad,
    embed_grad,
):
    weights = (
        qkv_weight,
        qkv_bias,
        out_weight,
        out_bias,
        gain_one,
        shift_one,
        up_weight,
        up_bias,
        down_weight,
        down_bias,
        gain_two,
        shift_two,
        proj_weight,
    )

    def one_seq(running, per_seq):
        tok_row, seg_row, dy_row, de_row = per_seq
        results = process(tok_row[None], seg_row[None], dy_row[None], de_row[None], weights)
        running = jax.tree.map(jnp.add, running, (results[3], results[4]))
        return (running, (results[0][0], results[1][0], results[2][0]))

    empty_grads = (
        tuple(
            (
                jnp.zeros(w.shape, jnp.float32)
                for w in (qkv_weight, qkv_bias, out_weight, up_weight, up_bias, down_weight)
            )
        ),
        tuple(
            (
                jnp.zeros(w.shape, jnp.float32)
                for w in (
                    out_bias,
                    gain_one,
                    shift_one,
                    down_bias,
                    gain_two,
                    shift_two,
                    proj_weight,
                )
            )
        ),
    )
    (sharded_grads, shared_grads), (layer_out, embeddings, tokens_grad) = lax.scan(
        one_seq, empty_grads, (tokens, segments, out_grad, embed_grad)
    )
    sharded_grads = jax.tree.map(
        lambda part: part.astype(jnp.float32), lax.psum(as_sent(sharded_grads), "dp")
    )
    shared_grads = lax.psum(shared_grads, ("dp", "tensor"))
    return (
        layer_out,
        embeddings,
        tokens_grad,
        sharded_grads[0],
        sharded_grads[1],
        sharded_grads[2],
        shared_grads[0],
        shared_grads[1],
        shared_grads[2],
        sharded_grads[3],
        sharded_grads[4],
        sharded_grads[5],
        shared_grads[3],
        shared_grads[4],
        shared_grads[5],
        shared_grads[6],
    )


def solution(mesh):
    in_specs = (
        P("dp", "tensor", None),
        P("dp", None),
        P(None, None, "tensor"),
        P(None, "tensor"),
        P("tensor", None),
        P(),
        P(),
        P(),
        P(None, "tensor"),
        P("tensor"),
        P("tensor", None),
        P(),
        P(),
        P(),
        P(),
        P("dp", "tensor", None),
        P("dp", "tensor", None),
    )
    out_specs = (
        P("dp", "tensor", None),
        P("dp", "tensor", None),
        P("dp", "tensor", None),
        P(None, None, "tensor"),
        P(None, "tensor"),
        P("tensor", None),
        P(),
        P(),
        P(),
        P(None, "tensor"),
        P("tensor"),
        P("tensor", None),
        P(),
        P(),
        P(),
        P(),
    )
    return jax.shard_map(
        per_device, mesh=mesh, in_specs=in_specs, out_specs=out_specs, check_vma=False
    )
```

profile of v0, /device:TPU:1, one launch (start us, length us, event | category | flops | bytes accessed | tf_op | source)
XLA Modules:
  0.0 1447.1 jit_solution(7580111649799563815)
XLA Ops:
  10.8 1174.1 %while.6 = (s32[]{:T(128)}, f32[3,1024,256]{1,2,0:T(8,128)}, f32[3,256]{1,0:T(4,128)}, f32[256,1024]{1,0:T(8,128)}, f32[1024,1024]{1,0:T(8,128)}, /*index=5*/f32...) while((s32[]{:T(128)}, f32[3,1024,256]{1,2,0:T(8,128)}, ...), condition=%wide.region_26.27_spmd.clone, body=%wide.region_0.26_spmd.clone.sunk | while | flops 23216961536 | bytes 635246848 | solution.py:354
  17.6 43.7 %all-gather.5.cloned.1.call-done = bf16[1,1024,1024]{2,1,0:T(8,128)(2,1)} async-done(((bf16[1,256,1024]{2,1,0:T(8,128)(2,1)}), bf16[1,1024,1024]{2,1,0:T(8,128)(2,1)}) %all-gather.5.cloned.1.call-update) | async-done | bytes 2097168 | tf_op jit(solution)/shard_map/while/body/eval_jaxpr/all_gather | solution.py:151
  94.4 75.3 %reduce-scatter.5.cloned.1.call-done = f32[256,1024]{1,0:T(8,128)} async-done(((f32[1024,1024]{1,0:T(8,128)}), f32[256,1024]{1,0:T(8,128)}) %reduce-scatter.5.cloned.1.call-update) | async-done | bytes 1048592 | tf_op jit(solution)/shard_map/while/body/eval_jaxpr/reduce_scatter | solution.py:161
  172.6 46.5 %all-gather.7.cloned.1.call-done = bf16[1,1024,1024]{2,1,0:T(8,128)(2,1)} async-done(((bf16[1,256,1024]{2,1,0:T(8,128)(2,1)}), bf16[1,1024,1024]{2,1,0:T(8,128)(2,1)}) %all-gather.7.cloned.1.call-update) | async-done | bytes 2097168 | tf_op jit(solution)/shard_map/while/body/eval_jaxpr/all_gather | solution.py:174
  219.1 14.9 %multiply_convert_fusion.4 = (bf16[1024,1024]{1,0:T(8,128)(2,1)S(1)}, f32[1024,1024]{1,0:T(8,128)}, f32[1024,1024]{1,0:T(8,128)}) fusion(f32[1024]{0:T(1024)S(1)} %copy-done.58, bf16[1024,1024]{1,0:T(8,128)(2,1)} %get-tuple-element.999, bf16[1,1024,1024]{2,1,0:T(8,128)(2,1)} %all-gather.7.cloned.1.call-done), kind=kOutput, calls=%fused_computation.17.clone.1 | convolution fusion | flops 2216689664 | bytes 14684160 | tf_op jit(solution)/shard_map/while/body/eval_jaxpr/gld,df->glf/dot_general | solution.py:176
  239.7 75.6 %reduce-scatter.7.cloned.1.call-done = f32[256,1024]{1,0:T(8,128)} async-done(((f32[1024,1024]{1,0:T(8,128)}), f32[256,1024]{1,0:T(8,128)}) %reduce-scatter.7.cloned.1.call-update) | async-done | bytes 1048592 | tf_op jit(solution)/shard_map/while/body/eval_jaxpr/reduce_scatter | solution.py:180
  321.5 45.9 %all-gather.9.cloned.1.call-done = bf16[1,1024,1024]{2,1,0:T(8,128)(2,1)} async-done(((bf16[1,256,1024]{2,1,0:T(8,128)(2,1)}), bf16[1,1024,1024]{2,1,0:T(8,128)(2,1)}) %all-gather.9.cloned.1.call-update) | async-done | bytes 2097168 | tf_op jit(solution)/shard_map/while/body/eval_jaxpr/all_gather | solution.py:207
  381.7 75.6 %reduce-scatter.9.cloned.1.call-done = f32[256,1024]{1,0:T(8,128)} async-done(((f32[1024,1024]{1,0:T(8,128)}), f32[256,1024]{1,0:T(8,128)}) %reduce-scatter.9.cloned.1.call-update) | async-done | bytes 1048592 | tf_op jit(solution)/shard_map/while/body/eval_jaxpr/reduce_scatter | solution.py:220
  461.1 46.5 %all-gather.11.cloned.1.call-done = bf16[1,1024,1024]{2,1,0:T(8,128)(2,1)} async-done(((bf16[1,256,1024]{2,1,0:T(8,128)(2,1)}), bf16[1,1024,1024]{2,1,0:T(8,128)(2,1)}) %all-gather.11.cloned.1.call-update) | async-done | bytes 2097168 | tf_op jit(solution)/shard_map/while/body/eval_jaxpr/all_gather | solution.py:237
  530.6 12.2 multiply_convert_fusion.5
  575.8 19.6 %reduce-scatter.11.cloned.1.call-done = bf16[256,1024]{1,0:T(8,128)(2,1)} async-done(((bf16[1024,1024]{1,0:T(8,128)(2,1)}), bf16[256,1024]{1,0:T(8,128)(2,1)}) %reduce-scatter.11.cloned.1.call-update) | async-done | bytes 524304 | tf_op jit(solution)/shard_map/while/body/eval_jaxpr/reduce_scatter | solution.py:259
  604.5 41.1 %all-gather.5.cloned.1.call-done = bf16[1,1024,1024]{2,1,0:T(8,128)(2,1)} async-done(((bf16[1,256,1024]{2,1,0:T(8,128)(2,1)}), bf16[1,1024,1024]{2,1,0:T(8,128)(2,1)}) %all-gather.5.cloned.1.call-update) | async-done | bytes 2097168 | tf_op jit(solution)/shard_map/while/body/eval_jaxpr/all_gather | solution.py:151
  678.9 75.1 %reduce-scatter.5.cloned.1.call-done = f32[256,1024]{1,0:T(8,128)} async-done(((f32[1024,1024]{1,0:T(8,128)}), f32[256,1024]{1,0:T(8,128)}) %reduce-scatter.5.cloned.1.call-update) | async-done | bytes 1048592 | tf_op jit(solution)/shard_map/while/body/eval_jaxpr/reduce_scatter | solution.py:161
  756.9 46.5 %all-gather.7.cloned.1.call-done = bf16[1,1024,1024]{2,1,0:T(8,128)(2,1)} async-done(((bf16[1,256,1024]{2,1,0:T(8,128)(2,1)}), bf16[1,1024,1024]{2,1,0:T(8,128)(2,1)}) %all-gather.7.cloned.1.call-update) | async-done | bytes 2097168 | tf_op jit(solution)/shard_map/while/body/eval_jaxpr/all_gather | solution.py:174
  803.5 14.9 %multiply_convert_fusion.4 = (bf16[1024,1024]{1,0:T(8,128)(2,1)S(1)}, f32[1024,1024]{1,0:T(8,128)}, f32[1024,1024]{1,0:T(8,128)}) fusion(f32[1024]{0:T(1024)S(1)} %copy-done.58, bf16[1024,1024]{1,0:T(8,128)(2,1)} %get-tuple-element.999, bf16[1,1024,1024]{2,1,0:T(8,128)(2,1)} %all-gather.7.cloned.1.call-done), kind=kOutput, calls=%fused_computation.17.clone.1 | convolution fusion | flops 2216689664 | bytes 14684160 | tf_op jit(solution)/shard_map/while/body/eval_jaxpr/gld,df->glf/dot_general | solution.py:176
  824.0 75.6 %reduce-scatter.7.cloned.1.call-done = f32[256,1024]{1,0:T(8,128)} async-done(((f32[1024,1024]{1,0:T(8,128)}), f32[256,1024]{1,0:T(8,128)}) %reduce-scatter.7.cloned.1.call-update) | async-done | bytes 1048592 | tf_op jit(solution)/shard_map/while/body/eval_jaxpr/reduce_scatter | solution.py:180
  905.4 46.3 %all-gather.9.cloned.1.call-done = bf16[1,1024,1024]{2,1,0:T(8,128)(2,1)} async-done(((bf16[1,256,1024]{2,1,0:T(8,128)(2,1)}), bf16[1,1024,1024]{2,1,0:T(8,128)(2,1)}) %all-gather.9.cloned.1.call-update) | async-done | bytes 2097168 | tf_op jit(solution)/shard_map/while/body/eval_jaxpr/all_gather | solution.py:207
  966.0 75.6 %reduce-scatter.9.cloned.1.call-done = f32[256,1024]{1,0:T(8,128)} async-done(((f32[1024,1024]{1,0:T(8,128)}), f32[256,1024]{1,0:T(8,128)}) %reduce-scatter.9.cloned.1.call-update) | async-done | bytes 1048592 | tf_op jit(solution)/shard_map/while/body/eval_jaxpr/reduce_scatter | solution.py:220
  1045.5 46.5 %all-gather.11.cloned.1.call-done = bf16[1,1024,1024]{2,1,0:T(8,128)(2,1)} async-done(((bf16[1,256,1024]{2,1,0:T(8,128)(2,1)}), bf16[1,1024,1024]{2,1,0:T(8,128)(2,1)}) %all-gather.11.cloned.1.call-update) | async-done | bytes 2097168 | tf_op jit(solution)/shard_map/while/body/eval_jaxpr/all_gather | solution.py:237
  1114.9 12.3 multiply_convert_fusion.5
  1162.3 17.4 %reduce-scatter.11.cloned.1.call-done = bf16[256,1024]{1,0:T(8,128)(2,1)} async-done(((bf16[1024,1024]{1,0:T(8,128)(2,1)}), bf16[256,1024]{1,0:T(8,128)(2,1)}) %reduce-scatter.11.cloned.1.call-update) | async-done | bytes 524304 | tf_op jit(solution)/shard_map/while/body/eval_jaxpr/reduce_scatter | solution.py:259
  1209.9 41.8 %all-reduce = (f32[1024]{0:T(1024)}, f32[1024]{0:T(1024)}, f32[1024]{0:T(1024)}, f32[1024]{0:T(1024)}, f32[1024]{0:T(1024)}, /*index=5*/f32[1024]{0:T(1024)}) all-reduce(f32[1024]{0:T(1024)S(1)} %copy-done.49, f32[1024]{0:T(1024)S(1)} %copy-done.46, f32[1024]{0:T(1024)S(1)} %copy-done.43, ...), channel_id=1, replica_groups=mesh['dp'=8,'tensor'=4] {'dp','tensor'}, use_global_device_ids=true, to_apply=%region_30.31 | all-reduce | flops 6144 | bytes 49152 | tf_op jit(solution)/shard_map/psum | solution.py:360
  1251.7 48.9 %all-reduce.8.cloned.1.call-done = (bf16[3,1024,256]{2,1,0:T(8,128)(2,1)}, bf16[256,1024]{1,0:T(8,128)(2,1)}, bf16[1024,1024]{1,0:T(8,128)(2,1)}, bf16[1024,1024]{1,0:T(8,128)(2,1)}) async-done(((bf16[3,1024,256]{2,1,0:T(8,128)(2,1)}, bf16[256,1024]{1,0:T(8,128)(2,1)}, bf16[1024,1024]{1,0:T(8,128)(2,1)}, bf16[1024,1024]{1,0:T(8,128)(2,1)}), (bf16[3,1024,256]{2,1,0:T(8,128)(2,1)}, ...) | async-done | bytes 6291472 | tf_op jit(solution)/shard_map/psum | solution.py:358
  1311.1 126.2 %all-reduce.6.cloned.1.call-done = f32[1024,288]{0,1:T(8,128)} async-done(((f32[1024,288]{0,1:T(8,128)}), f32[1024,288]{0,1:T(8,128)}) %all-reduce.6.cloned.1.call-update) | async-done | bytes 1179664 | tf_op jit(solution)/shard_map/psum | solution.py:360
  (437 shorter events, 302.5 us)
Async XLA Ops:
  10.8 50.4 %all-gather.5.cloned.1.call-start = ((), (), s32[]{:S(2)}) async-start(), calls=%async_computation.6 | async-start | bytes 2621440 | tf_op jit(solution)/shard_map/while/body/eval_jaxpr/all_gather | solution.py:151
  12.7 157.0 %reduce-scatter.5.cloned.1.call-start = ((), (), s32[]{:S(2)}) async-start(), calls=%async_computation.7 | async-start | bytes 5242880 | tf_op jit(solution)/shard_map/while/body/eval_jaxpr/reduce_scatter | solution.py:161
  94.0 77.4 %copy-start.30 = (f32[1024]{0:T(1024)S(1)}, f32[1024]{0:T(1024)}, u32[]{:S(2)}) copy-start(f32[1024]{0:T(1024)} %get-tuple-element.998) | copy-start | bytes 12292 | tf_op jit(solution)/shard_map/while
  94.0 125.1 %copy-start.58 = (f32[1024]{0:T(1024)S(1)}, f32[1024]{0:T(1024)}, u32[]{:S(2)}) copy-start(f32[1024]{0:T(1024)} %get-tuple-element.1000) | copy-start | bytes 12292 | tf_op jit(solution)/shard_map/while
  94.1 125.1 %all-gather.7.cloned.1.call-start = ((), (), s32[]{:S(2)}) async-start(), calls=%async_computation.8 | async-start | bytes 2621440 | tf_op jit(solution)/shard_map/while/body/eval_jaxpr/all_gather | solution.py:174
  172.6 142.7 %reduce-scatter.7.cloned.1.call-start = ((), (), s32[]{:S(2)}) async-start(), calls=%async_computation.9 | async-start | bytes 5242880 | tf_op jit(solution)/shard_map/while/body/eval_jaxpr/reduce_scatter | solution.py:180
  239.6 77.6 %copy-start.31 = (f32[1024]{0:T(1024)S(1)}, f32[1024]{0:T(1024)}, u32[]{:S(2)}) copy-start(f32[1024]{0:T(1024)} %get-tuple-element.1006) | copy-start | bytes 12292 | tf_op jit(solution)/shard_map/while
  239.6 127.8 %all-gather.9.cloned.1.call-start = ((), (), s32[]{:S(2)}) async-start(), calls=%async_computation.10 | async-start | bytes 2621440 | tf_op jit(solution)/shard_map/while/body/eval_jaxpr/all_gather | solution.py:207
  320.9 136.4 %reduce-scatter.9.cloned.1.call-start = ((), (), s32[]{:S(2)}) async-start(), calls=%async_computation.11 | async-start | bytes 5242880 | tf_op jit(solution)/shard_map/while/body/eval_jaxpr/reduce_scatter | solution.py:220
  381.6 125.9 %all-gather.11.cloned.1.call-start = ((), (), s32[]{:S(2)}) async-start(), calls=%async_computation.12 | async-start | bytes 2621440 | tf_op jit(solution)/shard_map/while/body/eval_jaxpr/all_gather | solution.py:237
  461.0 134.3 %reduce-scatter.11.cloned.1.call-start = ((), (), s32[]{:S(2)}) async-start(), calls=%async_computation.13 | async-start | bytes 2621440 | tf_op jit(solution)/shard_map/while/body/eval_jaxpr/reduce_scatter | solution.py:259
  597.7 47.9 %all-gather.5.cloned.1.call-start = ((), (), s32[]{:S(2)}) async-start(), calls=%async_computation.6 | async-start | bytes 2621440 | tf_op jit(solution)/shard_map/while/body/eval_jaxpr/all_gather | solution.py:151
  599.7 154.4 %reduce-scatter.5.cloned.1.call-start = ((), (), s32[]{:S(2)}) async-start(), calls=%async_computation.7 | async-start | bytes 5242880 | tf_op jit(solution)/shard_map/while/body/eval_jaxpr/reduce_scatter | solution.py:161
  678.4 77.4 %copy-start.30 = (f32[1024]{0:T(1024)S(1)}, f32[1024]{0:T(1024)}, u32[]{:S(2)}) copy-start(f32[1024]{0:T(1024)} %get-tuple-element.998) | copy-start | bytes 12292 | tf_op jit(solution)/shard_map/while
  678.4 125.1 %copy-start.58 = (f32[1024]{0:T(1024)S(1)}, f32[1024]{0:T(1024)}, u32[]{:S(2)}) copy-start(f32[1024]{0:T(1024)} %get-tuple-element.1000) | copy-start | bytes 12292 | tf_op jit(solution)/shard_map/while
  678.4 125.1 %all-gather.7.cloned.1.call-start = ((), (), s32[]{:S(2)}) async-start(), calls=%async_computation.8 | async-start | bytes 2621440 | tf_op jit(solution)/shard_map/while/body/eval_jaxpr/all_gather | solution.py:174
  756.9 142.8 %reduce-scatter.7.cloned.1.call-start = ((), (), s32[]{:S(2)}) async-start(), calls=%async_computation.9 | async-start | bytes 5242880 | tf_op jit(solution)/shard_map/while/body/eval_jaxpr/reduce_scatter | solution.py:180
  824.0 77.6 %copy-start.31 = (f32[1024]{0:T(1024)S(1)}, f32[1024]{0:T(1024)}, u32[]{:S(2)}) copy-start(f32[1024]{0:T(1024)} %get-tuple-element.1006) | copy-start | bytes 12292 | tf_op jit(solution)/shard_map/while
  824.0 127.8 %all-gather.9.cloned.1.call-start = ((), (), s32[]{:S(2)}) async-start(), calls=%async_computation.10 | async-start | bytes 2621440 | tf_op jit(solution)/shard_map/while/body/eval_jaxpr/all_gather | solution.py:207
  905.2 136.4 %reduce-scatter.9.cloned.1.call-start = ((), (), s32[]{:S(2)}) async-start(), calls=%async_computation.11 | async-start | bytes 5242880 | tf_op jit(solution)/shard_map/while/body/eval_jaxpr/reduce_scatter | solution.py:220
  966.0 125.9 %all-gather.11.cloned.1.call-start = ((), (), s32[]{:S(2)}) async-start(), calls=%async_computation.12 | async-start | bytes 2621440 | tf_op jit(solution)/shard_map/while/body/eval_jaxpr/all_gather | solution.py:237
  1045.4 134.3 %reduce-scatter.11.cloned.1.call-start = ((), (), s32[]{:S(2)}) async-start(), calls=%async_computation.13 | async-start | bytes 2621440 | tf_op jit(solution)/shard_map/while/body/eval_jaxpr/reduce_scatter | solution.py:259
  1184.9 115.6 %all-reduce.8.cloned.1.call-start = ((), (), s32[]{:S(2)}) async-start(), calls=%async_computation.5 | async-start | bytes 12582912 | tf_op jit(solution)/shard_map/psum | solution.py:358
  1195.8 241.5 %all-reduce.6.cloned.1.call-start = ((), (), s32[]{:S(2)}) async-start(), calls=%async_computation.4 | async-start | bytes 2359296 | tf_op jit(solution)/shard_map/psum | solution.py:360
  (109 other events, 1301.8 us)
Sparse Core Ops, SparseCore 0:
  13.2 48.0 all-gather.4
  94.2 75.4 reduce-scatter.4
  172.7 46.4 all-gather.6
  239.8 75.4 reduce-scatter.6
  321.0 46.3 all-gather.8
  381.7 75.5 reduce-scatter.8
  461.1 46.3 all-gather.10
  552.9 42.4 reduce-scatter.10
  600.1 45.4 all-gather.4
  678.5 75.4 reduce-scatter.4
  757.0 46.4 all-gather.6
  824.1 75.4 reduce-scatter.6
  905.3 46.3 all-gather.8
  966.1 75.5 reduce-scatter.8
  1045.5 46.3 all-gather.10
  1137.3 42.4 reduce-scatter.10
Sparse Core Ops, SparseCore 1:
  1195.9 104.6 all-reduce.7
  1307.3 130.0 all-reduce.5
where the time goes:
time: 1450 us
  waiting for transfers between devices  1030 us (71%)
  matrix products  209 us (14%)
  other arithmetic  99.4 us (7%)
  blocking collectives  54 us (4%)
  local copies, waits for them, and re-layouts  33.1 us (2%)
  between operations  15.6 us (1%)
    reduce_scatter x2, waiting for transfers between devices, process(): lax.psum_scatter(jnp.einsum('nf,df->nd', device_rows(grad_hidden, lax.axi...  151 us
    reduce_scatter x2, waiting for transfers between devices, process(): lax.psum_scatter(jnp.dot(device_rows(active, lax.axis_size('tensor') * (g...  151 us
    reduce_scatter x2, waiting for transfers between devices, process(): lax.psum_scatter(jnp.dot(device_rows(mixed, lax.axis_size('tensor') * (gr...  150 us
    psum x1, waiting for transfers between devices, per_device(): shared_grads = lax.psum(shared_grads, ('dp', 'tensor'))  126 us
    all_gather x2, waiting for transfers between devices, process(): lax.all_gather(normed.astype(jnp.bfloat16), 'tensor', axis=1, tiled=True)  93.1 us
    all_gather x2, waiting for transfers between devices, process(): whole_first = lax.all_gather(first_low, 'tensor', axis=1, tiled=True)  92.9 us
    all_gather x2, waiting for transfers between devices, process(): whole_second = lax.all_gather(second_low, 'tensor', axis=1, tiled=True)  92.3 us
    all_gather x2, waiting for transfers between devices, process(): whole_tokens = lax.all_gather(tokens, 'tensor', axis=1, tiled=True)  84.7 us
  transfers between devices with their start and end apart: 18, of which 18 were waited for; matrix products, arithmetic and copies ran while one was open for 4% of the time, Pallas kernels for 0%

commit v1 on v0

v1 whole, which is shorter than its diff:
```python
import math

import jax
import jax.numpy as jnp
from jax import lax
from jax.sharding import Mesh
from jax.sharding import PartitionSpec as P

HEAD_DIM = 64
eps = 1e-05
DP = ("xb", "x", "yb", "y", "core")
CELL = ("x", "y", "core")
ALL = DP + ("z",)
f32 = jnp.float32
bf16 = jnp.bfloat16


def doc_positions(segment_rows):
    length = segment_rows.shape[-1]
    row_index = jnp.broadcast_to(jnp.arange(length, dtype=jnp.int32), segment_rows.shape)
    change = jnp.concatenate(
        [
            jnp.ones(segment_rows.shape[:-1] + (1,), jnp.bool_),
            segment_rows[..., 1:] != segment_rows[..., :-1],
        ],
        axis=-1,
    )
    doc_start = lax.cummax(
        jnp.where(change, row_index, jnp.zeros_like(row_index)), axis=segment_rows.ndim - 1
    )
    return row_index - doc_start


def rotary_tables(positions, head_dim):
    half_dim = head_dim // 2
    exponent = jnp.arange(half_dim, dtype=f32) * (2.0 / head_dim)
    frequency = jnp.exp(-exponent * math.log(10000.0))
    angles = positions.astype(f32)[..., None] * frequency
    angles = jnp.concatenate([angles, angles], axis=-1)
    return (jnp.cos(angles), jnp.sin(angles))


def rotate(field, cosine, sine):
    half_dim = field.shape[-1] // 2
    rotated = jnp.concatenate([-field[..., half_dim:], field[..., :half_dim]], axis=-1)
    return field * cosine + rotated * sine


def rotate_back(field, cosine, sine):
    half_dim = field.shape[-1] // 2
    rotated = jnp.concatenate([-field[..., half_dim:], field[..., :half_dim]], axis=-1)
    return field * cosine - rotated * sine


def norm_forward(field, gain, shift):
    row_mean = jnp.mean(field, axis=-1, keepdims=True)
    centred = field - row_mean
    variance = jnp.mean(centred * centred, axis=-1, keepdims=True)
    inv_std = lax.rsqrt(variance + eps)
    scaled = centred * inv_std
    return (scaled * gain + shift, scaled, inv_std)


def norm_backward(upstream, scaled, inv_std, gain):
    grad_scaled = upstream * gain
    grad_input = inv_std * (
        grad_scaled
        - jnp.mean(grad_scaled, axis=-1, keepdims=True)
        - scaled * jnp.mean(grad_scaled * scaled, axis=-1, keepdims=True)
    )
    return (grad_input, jnp.sum(upstream * scaled, axis=0), jnp.sum(upstream, axis=0))


def masked_scores(queries, keys, seg_row):
    scores = jnp.einsum("hqd,hkd->hqk", queries, keys, preferred_element_type=f32)
    same_doc = seg_row[:, None] == seg_row[None, :]
    return jnp.where(same_doc[None], scores, -1000000000.0)


def attend(inputs):
    queries, keys, values_low, seg_row = inputs
    scores = masked_scores(queries, keys, seg_row)
    row_peak = jnp.max(scores, axis=-1, keepdims=True)
    shifted = jnp.exp(scores - row_peak)
    row_total = jnp.sum(shifted, axis=-1, keepdims=True)
    probs = (shifted / row_total).astype(bf16)
    mixed_heads = jnp.einsum("hqk,hkd->hqd", probs, values_low, preferred_element_type=f32)
    return (mixed_heads, row_peak + jnp.log(row_total))


def attend_back(inputs):
    queries, keys, values_low, seg_row, log_total, grad_mixed = inputs
    scores = masked_scores(queries, keys, seg_row)
    probs = jnp.exp(scores - log_total)
    grad_values = jnp.einsum("hqk,hqd->hkd", probs.astype(bf16), grad_mixed, preferred_element_type=f32)
    grad_probs = jnp.einsum("hqd,hkd->hqk", grad_mixed, values_low, preferred_element_type=f32)
    row_inner = jnp.sum(probs * grad_probs, axis=-1, keepdims=True)
    grad_scores = (probs * (grad_probs - row_inner)).astype(bf16)
    grad_queries = jnp.einsum("hqk,hkd->hqd", grad_scores, keys, preferred_element_type=f32)
    grad_keys = jnp.einsum("hqk,hqd->hkd", grad_scores, queries, preferred_element_type=f32)
    return (grad_queries, grad_keys, grad_values)


def piece_of(shard):
    rows = shard.shape[0] // 8
    return lax.dynamic_slice_in_dim(shard, lax.axis_index(CELL) * rows, rows, 0)


def gather_all(shard, zsize):
    whole = lax.all_gather(piece_of(shard), ("z",) + CELL, axis=0, tiled=True)
    return whole.reshape((zsize,) + shard.shape)


def reduce_all(partial):
    rows = partial.shape[0] * partial.shape[1]
    piece = lax.psum_scatter(
        partial.reshape(rows, partial.shape[2]), ("z",) + CELL, scatter_dimension=0, tiled=True
    )
    return lax.all_gather(piece, CELL, axis=0, tiled=True)


def per_device(blocks, tokens, segments, qkv_weight, qkv_bias, out_weight, out_bias, gain_one, shift_one,
               up_weight, up_bias, down_weight, down_bias, gain_two, shift_two, proj_weight, out_grad, embed_grad):
    groups, local_rows, model_width = tokens.shape
    length = segments.shape[1]
    zsize = length // local_rows
    heads_here = qkv_weight.shape[2] // HEAD_DIM
    head_cols = qkv_weight.shape[2]
    units_here = up_weight.shape[1]
    rows = groups * local_rows
    zi = lax.axis_index("z")
    q_scale = HEAD_DIM ** (-0.5)
    cosine, sine = rotary_tables(doc_positions(segments), HEAD_DIM)
    cosine = cosine[:, None]
    sine = sine[:, None]

    def split_heads(field):
        return field.reshape(groups, length, heads_here, HEAD_DIM).transpose(0, 2, 1, 3)

    def join_heads(field):
        return field.transpose(0, 2, 1, 3).reshape(groups, length, head_cols)

    whole_tokens = lax.all_gather(tokens, "z", axis=1, tiled=True)
    out_all = gather_all(out_weight, zsize).reshape(model_width, model_width)
    up_all = gather_all(up_weight, zsize)
    down_all = gather_all(down_weight, zsize)
    full_up_bias = lax.all_gather(up_bias, "z", axis=0, tiled=False)

    projected = jnp.einsum("gld,cde->cgle", whole_tokens, qkv_weight, preferred_element_type=f32)
    projected = projected + qkv_bias[:, None, None, :]
    queries = (rotate(split_heads(projected[0]), cosine, sine) * q_scale).astype(bf16)
    keys = rotate(split_heads(projected[1]), cosine, sine).astype(bf16)
    values_low = split_heads(projected[2]).astype(bf16)
    got = [attend((queries[g], keys[g], values_low[g], segments[g])) for g in range(groups)]
    log_total = [g[1] for g in got]
    mixed = join_heads(jnp.stack([g[0] for g in got])).astype(bf16)
    mixed = lax.all_to_all(mixed, "z", split_axis=1, concat_axis=2, tiled=True).reshape(rows, model_width)

    first_sum = tokens.reshape(rows, model_width).astype(f32) + (
        jnp.dot(mixed, out_all, preferred_element_type=f32) + out_bias
    )
    normed, scaled_one, inv_one = norm_forward(first_sum, gain_one, shift_one)
    normed_low = normed.astype(bf16)
    hidden = jnp.einsum("nd,zdf->znf", normed_low, up_all, preferred_element_type=f32)
    hidden = hidden + full_up_bias[:, None, :]
    active, gelu_pull = jax.vjp(lambda field: jax.nn.gelu(field, approximate=False), hidden)
    active = active.astype(bf16)
    ffn = jnp.einsum("znf,zfd->nd", active, down_all, preferred_element_type=f32)
    second_sum = normed + (ffn + down_bias)
    result, scaled_two, inv_two = norm_forward(second_sum, gain_two, shift_two)
    result_low = result.astype(bf16)
    embedded = jnp.dot(result_low, proj_weight, preferred_element_type=f32).astype(bf16)
    embed_rows = embed_grad.reshape(rows, -1)
    grad_result = out_grad.reshape(rows, model_width).astype(f32) + jnp.einsum(
        "np,dp->nd", embed_rows, proj_weight, preferred_element_type=f32
    )
    proj_grad = jnp.einsum("nd,np->dp", result_low, embed_rows, preferred_element_type=f32)
    grad_second, gain_two_grad, shift_two_grad = norm_backward(grad_result, scaled_two, inv_two, gain_two)
    second_low = grad_second.astype(bf16)
    down_bias_grad = jnp.sum(second_low.astype(f32), axis=0)
    down_grad = jnp.einsum("znf,nd->zfd", active, second_low, preferred_element_type=f32).astype(bf16)
    grad_active = jnp.einsum("nd,zfd->znf", second_low, down_all, preferred_element_type=f32)
    grad_hidden = gelu_pull(grad_active)[0].astype(bf16)
    up_bias_grad = jnp.sum(grad_hidden.astype(f32), axis=1)
    up_grad = jnp.einsum("nd,znf->zdf", normed_low, grad_hidden, preferred_element_type=f32).astype(bf16)
    grad_normed = grad_second + jnp.einsum("znf,zdf->nd", grad_hidden, up_all, preferred_element_type=f32)
    grad_first, gain_one_grad, shift_one_grad = norm_backward(grad_normed, scaled_one, inv_one, gain_one)
    first_low = grad_first.astype(bf16)
    out_bias_grad = jnp.sum(first_low.astype(f32), axis=0)
    out_grad_w = jnp.einsum("nh,nd->hd", mixed, first_low, preferred_element_type=f32).astype(bf16)
    grad_mixed = jnp.einsum("nd,hd->nh", first_low, out_all, preferred_element_type=f32).astype(bf16)
    grad_mixed = grad_mixed.reshape(groups, local_rows, model_width)
    grad_mixed = lax.all_to_all(grad_mixed, "z", split_axis=2, concat_axis=1, tiled=True)
    grad_mixed = split_heads(grad_mixed)
    back = [
        attend_back((queries[g], keys[g], values_low[g], segments[g], log_total[g], grad_mixed[g]))
        for g in range(groups)
    ]
    grad_queries = rotate_back(jnp.stack([b[0] for b in back]) * q_scale, cosine, sine)
    grad_keys = rotate_back(jnp.stack([b[1] for b in back]), cosine, sine)
    grad_values = jnp.stack([b[2] for b in back])
    grad_qkv = jnp.stack(
        [join_heads(grad_queries), join_heads(grad_keys), join_heads(grad_values)]
    ).astype(bf16)
    qkv_bias_grad = jnp.sum(grad_qkv.astype(f32), axis=(1, 2))
    qkv_weight_grad = jnp.einsum("gld,cgle->cde", whole_tokens, grad_qkv, preferred_element_type=f32)
    input_back = jnp.einsum("cgle,cde->gld", grad_qkv, qkv_weight, preferred_element_type=f32).astype(bf16)
    input_back = lax.psum_scatter(input_back, "z", scatter_dimension=1, tiled=True)
    tokens_grad = grad_first.reshape(groups, local_rows, model_width) + input_back.astype(f32)

    qkv_weight_grad = lax.psum(qkv_weight_grad.astype(bf16), DP).astype(f32)
    down_grad = reduce_all(down_grad)
    up_grad = reduce_all(up_grad)
    out_grad_w = reduce_all(out_grad_w.reshape(zsize, head_cols, model_width))
    if blocks > 1:
        down_grad, up_grad, out_grad_w = lax.psum((down_grad, up_grad, out_grad_w), ("xb", "yb"))
    small = jnp.concatenate(
        [
            out_bias_grad, gain_one_grad, shift_one_grad, down_bias_grad, gain_two_grad, shift_two_grad,
            up_bias_grad.reshape(-1),
            lax.dynamic_update_slice(
                jnp.zeros((zsize, 3 * head_cols), f32), qkv_bias_grad.reshape(1, -1), (zi, 0)
            ).reshape(-1),
        ]
    )
    small = lax.psum(small, ALL)
    proj_grad = lax.psum(proj_grad, ALL)
    base = 6 * model_width
    vec = [small[i * model_width:(i + 1) * model_width] for i in range(6)]
    up_bias_grad = lax.dynamic_slice(small, (base + zi * units_here,), (units_here,))
    qkv_bias_grad = lax.dynamic_slice(
        small, (base + zsize * units_here + zi * 3 * head_cols,), (3 * head_cols,)
    ).reshape(3, head_cols)
    shape3 = (groups, local_rows, model_width)
    return (
        result_low.reshape(shape3),
        embedded.reshape(groups, local_rows, -1),
        tokens_grad,
        qkv_weight_grad,
        qkv_bias_grad,
        out_grad_w.astype(f32),
        vec[0], vec[1], vec[2],
        up_grad.astype(f32),
        up_bias_grad,
        down_grad.astype(f32),
        vec[3], vec[4], vec[5],
        proj_grad,
    )


def solution(mesh):
    dp_size, zsize = mesh.shape["dp"], mesh.shape["tensor"]
    side = math.isqrt(dp_size // 2) // 2
    cut = Mesh(mesh.devices.reshape(side, 2, side, 2, 2, zsize), DP + ("z",))
    rows3 = P(DP, "z", None)
    in_specs = (
        rows3, P(DP, None), P(None, None, "z"), P(None, "z"), P("z", None), P(), P(), P(),
        P(None, "z"), P("z"), P("z", None), P(), P(), P(), P(), rows3, rows3,
    )
    out_specs = (
        rows3, rows3, rows3, P(None, None, "z"), P(None, "z"), P("z", None), P(), P(), P(),
        P(None, "z"), P("z"), P("z", None), P(), P(), P(), P(),
    )

    def run(*args):
        return per_device(side * side, *args)

    return jax.shard_map(run, mesh=cut, in_specs=in_specs, out_specs=out_specs, check_vma=False)
```

time: 1450 us -> 1150 us (0.79)
  waiting for transfers between devices: 1030 us -> 701 us
  blocking collectives: 54 us -> 91.7 us
  other arithmetic: 99.4 us -> 73.6 us
    reduce_scatter x8 -> x4, waiting for transfers between devices: 490 us -> 304 us  [the longest x3 239 us: reduce_all(): lax.psum_scatter(partial.reshape(rows, partial.shape[2]), ('z',) + CELL,...]
    all_gather x8 -> x6, waiting for transfers between devices: 363 us -> 221 us  [the longest x3 94 us: gather_all(): whole = lax.all_gather(piece_of(shard), ('z',) + CELL, axis=0, tiled=True)]
    all_gather x0 -> x2, blocking collectives: none -> 49.2 us  [the longest x1 34.1 us: per_device(): full_up_bias = lax.all_gather(up_bias, 'z', axis=0, tiled=False)]
    psum x2, waiting for transfers between devices: 175 us -> 146 us  [the longest x1 132 us: per_device(): proj_grad = lax.psum(proj_grad, ALL)]
    all_to_all x0 -> x2, waiting for transfers between devices: none -> 29.2 us  [the longest x1 29.2 us: per_device(): lax.all_to_all(grad_mixed, 'z', split_axis=2, concat_axis=1, tiled=True)]
    while x213 -> x0, local copies, waits for them, and re-layouts: 21.9 us -> none
    psum x2 -> x1, blocking collectives: 54 us -> 42.5 us  [per_device(): small = lax.psum(small, ALL)]
    convert_element_type x17 -> x7, other arithmetic: 46.1 us -> 35.3 us  [the longest x2 24.7 us: attend_back(): grad_scores = (probs * (grad_probs - row_inner)).astype(bf16)]
  transfers between devices with their start and end apart: 18 -> 14, of which waited for: 18 -> 11; matrix products, arithmetic and copies ran while one was open for 4% -> 24% of each run, Pallas kernels for 0% -> 0%
where the time goes in v1:
time: 1150 us; the launch traced here: 1140 us
  waiting for transfers between devices  701 us (61%)
  matrix products  208 us (18%)
  blocking collectives  91.7 us (8%)
  other arithmetic  73.6 us (6%)
  local copies, waits for them, and re-layouts  40.8 us (4%)
  between operations  15.2 us (1%)
    reduce_scatter x3, waiting for transfers between devices, reduce_all(): lax.psum_scatter(partial.reshape(rows, partial.shape[2]), ('z',) + CELL,...  239 us
    psum x1, waiting for transfers between devices, per_device(): proj_grad = lax.psum(proj_grad, ALL)  132 us
    all_gather x3, waiting for transfers between devices, gather_all(): whole = lax.all_gather(piece_of(shard), ('z',) + CELL, axis=0, tiled=True)  94 us
    all_gather x1, waiting for transfers between devices, per_device(): whole_tokens = lax.all_gather(tokens, 'z', axis=1, tiled=True)  73.4 us
    reduce_scatter x1, waiting for transfers between devices, per_device(): lax.psum_scatter(input_back, 'z', scatter_dimension=1, tiled=True)  64.8 us
    all_gather x2, waiting for transfers between devices, reduce_all(): return lax.all_gather(piece, CELL, axis=0, tiled=True)  53.5 us
    psum x1, blocking collectives, per_device(): small = lax.psum(small, ALL)  42.5 us
    all_gather x1, blocking collectives, per_device(): full_up_bias = lax.all_gather(up_bias, 'z', axis=0, tiled=False)  34.1 us
  transfers between devices with their start and end apart: 14, of which 11 were waited for; matrix products, arithmetic and copies ran while one was open for 24% of the time, Pallas kernels for 0%

profile of v1, /device:TPU:1, one launch (start us, length us, event | category | flops | bytes accessed | tf_op | source)
XLA Modules:
  0.0 1138.3 jit_solution(14915674222163912071)
XLA Ops:
  19.1 73.4 %all-gather.8.cloned.1.call-done = bf16[2,1024,1024]{2,1,0:T(8,128)(2,1)} async-done(((bf16[2,256,1024]{2,1,0:T(8,128)(2,1)}), bf16[2,1024,1024]{2,1,0:T(8,128)(2,1)}) %all-gather.8.cloned.1.call-update) | async-done | bytes 4194320 | tf_op jit(solution)/shard_map/all_gather | solution.py:143
  157.3 34.1 %all-gather = f32[4096]{0:T(1024)S(1)} all-gather(f32[1024]{0:T(1024)S(1)} %copy-done.31), channel_id=2, replica_groups=mesh['xb'=1,'x'=2,'yb'=1,'y'=2,'core'=2,'z'=4] {'z'}, dimensions={0}, use_global_device_ids=true | all-gather | bytes 20480 | tf_op jit(solution)/shard_map/all_gather | solution.py:147
  199.8 42.4 %all-gather.12.cloned.1.call-done = bf16[4096,1024]{1,0:T(8,128)(2,1)} async-done(((bf16[128,1024]{1,0:T(8,128)(2,1)}), bf16[4096,1024]{1,0:T(8,128)(2,1)}) %all-gather.12.cloned.1.call-update) | async-done | bytes 8388624 | tf_op jit(solution)/shard_map/all_gather | solution.py:110
  242.2 27.7 %fusion.13 = (bf16[4,512,1024]{2,1,0:T(8,128)(2,1)}, f32[4,512,1024]{2,1,0:T(8,128)}, f32[4,1024,512]{1,2,0:T(8,128)}) fusion(f32[4,1024]{1,0:T(4,128)S(1)} %reshape.290, bf16[4,1024,1024]{2,1,0:T(8,128)(2,1)} %bitcast.330, f32[512,1024]{1,0:T(8,128)} %copy-done.11, f32[1024]{0:T(1024)S(1)} %copy-done.40, f32[1024]{0:T(1024)S(1)} %copy-done.30, ...), kind=kOutput, calls=%fused_computation.34 | convolution fusion | flops 4436000768 | bytes 31485952 | tf_op jit(solution)/shard_map/nd,zdf->znf/dot_general | solution.py:164
  269.9 51.6 %all-gather.14.cloned.1.call-done = bf16[4096,1024]{1,0:T(8,128)(2,1)} async-done(((bf16[128,1024]{1,0:T(8,128)(2,1)}), bf16[4096,1024]{1,0:T(8,128)(2,1)}) %all-gather.14.cloned.1.call-update) | async-done | bytes 8388624 | tf_op jit(solution)/shard_map/all_gather | solution.py:110
  335.3 13.3 %convert_reduce_fusion = (f32[4,1024]{1,0:T(4,128)S(1)}, bf16[4,512,1024]{2,1,0:T(8,128)(2,1)}) fusion(f32[4,512,1024]{2,1,0:T(8,128)} %get-tuple-element.93, bf16[4,1024,1024]{2,1,0:T(8,128)(2,1)S(1)} %bitcast.335, f32[512,1024]{1,0:T(8,128)S(1)} %get-tuple-element.89, f32[4,1024,512]{1,2,0:T(8,128)} %get-tuple-element.127, f32[4,1024]{1,0:T(4,128)S(1)} %reshape.290), kind=kOutput, calls=%fused_computation.35 | convolution fusion | flops 4331139072 | bytes 31490048 | tf_op jit(solution)/shard_map/nd,zfd->znf/dot_general | solution.py:182
  358.7 10.7 convolution_convert_fusion
  369.4 11.8 %multiply_reduce_fusion.3 = (f32[1024]{0:T(1024)}, f32[512]{0:T(512)S(1)}, f32[512]{0:T(512)S(1)}, f32[1024]{0:T(1024)}, f32[512,1024]{1,0:T(8,128)S(1)}) fusion(f32[512,1024]{1,0:T(8,128)} %copy-done.11, f32[512]{0:T(512)S(1)} %add_rsqrt_fusion.1, f32[512]{0:T(512)S(1)} %broadcast_multiply_fusion.7, f32[1024]{0:T(1024)S(1)} %copy-done.30, ...), kind=kOutput, calls=%fused_computation.93 | convolution fusion | flops 4300207104 | bytes 18894848 | tf_op jit(solution)/shard_map/znf,zdf->nd/dot_general | solution.py:186
  393.2 29.2 %all-to-all-done.1 = bf16[2,256,1024]{1,0,2:T(2,128)(2,1)} async-done(((bf16[2,256,1024]{1,0,2:T(2,128)(2,1)}), bf16[2,256,1024]{1,0,2:T(2,128)(2,1)}, u32[]{:S(2)}, u32[]{:S(2)}) %all-to-all-start.1) | async-done | bytes 1048608 | tf_op jit(solution)/shard_map/all_to_all | solution.py:193
  428.3 10.6 fusion.70
  439.0 10.6 fusion.73
  454.1 11.8 %multiply_reduce_fusion = (f32[4,1024]{1,0:T(4,128)S(1)}, f32[4,1024,1024]{1,2,0:T(8,128)}) fusion(f32[4,1024,1024]{1,2,0:T(8,128)} %get-tuple-element.122, f32[4,1024]{1,0:T(4,128)S(1)} %log_add_fusion, pred[1024,1024]{0,1:T(8,128)(4,1)S(1)} %copy-done.4, bf16[2,4,1024,64]{2,3,1,0:T(8,128)(2,1)S(1)} %bitcast.300, bf16[2,4,1024,64]{2,3,1,0:T(8,128)(2,1)} %bitcast.304), kind=kOutput, calls=%fused_computation.1 | convolution fusion | flops 553644032 | bytes 35684352 | tf_op jit(solution)/shard_map/hqd,hkd->hqk/dot_general | solution.py:96
  466.0 12.5 %multiply_convert_fusion = bf16[4,1024,1024]{1,2,0:T(8,128)(2,1)S(1)} fusion(f32[4,1024,1024]{1,2,0:T(8,128)} %get-tuple-element.135, f32[4,1024,1024]{1,2,0:T(8,128)} %get-tuple-element.122, f32[4,1024]{1,0:T(4,128)S(1)} %get-tuple-element.134, f32[4,1024]{1,0:T(4,128)S(1)} %log_add_fusion, pred[1024,1024]{0,1:T(8,128)(4,1)S(1)} %copy-done.4), kind=kLoop, calls=%fused_computation | loop fusion | flops 20971520 | bytes 43024384 | tf_op jit(solution)/shard_map/convert_element_type | solution.py:98
  480.1 11.9 %multiply_reduce_fusion.1 = (f32[4,1024]{1,0:T(4,128)S(1)}, f32[4,1024,1024]{1,2,0:T(8,128)}) fusion(f32[4,1024,1024]{1,2,0:T(8,128)} %get-tuple-element.124, f32[4,1024]{1,0:T(4,128)S(1)} %log_add_fusion.1, pred[1024,1024]{0,1:T(8,128)(4,1)S(1)} %broadcast_compare_fusion.1, bf16[2,4,1024,64]{2,3,1,0:T(8,128)(2,1)S(1)} %bitcast.301, ...), kind=kOutput, calls=%fused_computation.4 | convolution fusion | flops 553644032 | bytes 35684352 | tf_op jit(solution)/shard_map/hqd,hkd->hqk/dot_general | solution.py:96
  492.0 12.2 %multiply_convert_fusion.1 = bf16[4,1024,1024]{1,2,0:T(8,128)(2,1)S(1)} fusion(f32[4,1024,1024]{1,2,0:T(8,128)} %get-tuple-element.137, f32[4,1024,1024]{1,2,0:T(8,128)} %get-tuple-element.124, f32[4,1024]{1,0:T(4,128)S(1)} %get-tuple-element.136, f32[4,1024]{1,0:T(4,128)S(1)} %log_add_fusion.1, pred[1024,1024]{0,1:T(8,128)(4,1)S(1)} %broadcast_compare_fusion.1), kind=kLoop, calls=%fused_computation.3 | loop fusion | flops 20971520 | bytes 43024384 | tf_op jit(solution)/shard_map/convert_element_type | solution.py:98
  545.1 107.4 %reduce-scatter.11.cloned.1.call-done = bf16[128,1024]{1,0:T(8,128)(2,1)} async-done(((bf16[4096,1024]{1,0:T(8,128)(2,1)}), bf16[128,1024]{1,0:T(8,128)(2,1)}) %reduce-scatter.11.cloned.1.call-update) | async-done | bytes 262160 | tf_op jit(solution)/shard_map/reduce_scatter | solution.py:116
  658.9 42.5 %psum.22 = f32[13312]{0:T(1024)S(1)} all-reduce(f32[13312]{0:T(1024)S(1)} %constant_dynamic-update-slice_fusion), channel_id=1, replica_groups=mesh['xb'=1,'x'=2,'yb'=1,'y'=2,'core'=2,'z'=4] {'xb','x','yb','y','core'..., use_global_device_ids=true, to_apply=%region_26.27 | all-reduce | flops 13312 | bytes 106496 | tf_op jit(solution)/shard_map/psum | solution.py:226
  702.7 13.2 %all-reduce.4.cloned.1.call-done = bf16[3,1024,256]{1,2,0:T(8,128)(2,1)} async-done(((bf16[3,1024,256]{1,2,0:T(8,128)(2,1)}), bf16[3,1024,256]{1,2,0:T(8,128)(2,1)}) %all-reduce.4.cloned.1.call-update) | async-done | bytes 1572880 | tf_op jit(solution)/shard_map/psum | solution.py:211
  719.0 131.6 %reduce-scatter.7.cloned.1.call-done = bf16[32,1024]{1,0:T(8,128)(2,1)} async-done(((bf16[1024,1024]{1,0:T(8,128)(2,1)}), bf16[32,1024]{1,0:T(8,128)(2,1)}) %reduce-scatter.7.cloned.1.call-update) | async-done | bytes 65552 | tf_op jit(solution)/shard_map/reduce_scatter | solution.py:116
  850.6 15.1 %all_gather.33 = bf16[256,1024]{1,0:T(8,128)(2,1)S(1)} all-gather(bf16[32,1024]{1,0:T(8,128)(2,1)} %reduce-scatter.7.cloned.1.call-done), channel_id=1, replica_groups=mesh['xb'=1,'x'=2,'yb'=1,'y'=2,'core'=2,'z'=4] {'x','y','core'}, dimensions={0}, use_global_device_ids=true | all-gather | bytes 589824 | tf_op jit(solution)/shard_map/all_gather | solution.py:119
  866.8 64.8 %reduce-scatter.5.cloned.1.call-done = bf16[2,256,1024]{2,1,0:T(8,128)(2,1)} async-done(((bf16[2,1024,1024]{2,1,0:T(8,128)(2,1)}), bf16[2,256,1024]{2,1,0:T(8,128)(2,1)}) %reduce-scatter.5.cloned.1.call-update) | async-done | bytes 1048592 | tf_op jit(solution)/shard_map/reduce_scatter | solution.py:208
  934.6 27.7 %all-gather.16.cloned.1.call-done = bf16[1024,1024]{1,0:T(8,128)(2,1)} async-done(((bf16[128,1024]{1,0:T(8,128)(2,1)}), bf16[1024,1024]{1,0:T(8,128)(2,1)}) %all-gather.16.cloned.1.call-update) | async-done | bytes 2097168 | tf_op jit(solution)/shard_map/all_gather | solution.py:119
  966.6 25.8 %all-gather.18.cloned.1.call-done = bf16[1024,1024]{1,0:T(8,128)(2,1)} async-done(((bf16[128,1024]{1,0:T(8,128)(2,1)}), bf16[1024,1024]{1,0:T(8,128)(2,1)}) %all-gather.18.cloned.1.call-update) | async-done | bytes 2097168 | tf_op jit(solution)/shard_map/all_gather | solution.py:119
  996.4 132.4 %all-reduce.6.cloned.1.call-done = f32[1024,288]{0,1:T(8,128)} async-done(((f32[1024,288]{0,1:T(8,128)}), f32[1024,288]{0,1:T(8,128)}) %all-reduce.6.cloned.1.call-update) | async-done | bytes 1179664 | tf_op jit(solution)/shard_map/psum | solution.py:227
  (213 shorter events, 198.7 us)
Async XLA Ops:
  7.2 85.3 %copy-start.37 = (f32[3,256]{1,0:T(4,128)S(1)}, f32[3,256]{1,0:T(4,128)}, u32[]{:S(2)}) copy-start(f32[3,256]{1,0:T(4,128)} %param.20) | copy-start | bytes 9220
  7.2 85.3 %all-gather.8.cloned.1.call-start = ((), (), s32[]{:S(2)}) async-start(), calls=%async_computation.6 | async-start | bytes 5242880 | tf_op jit(solution)/shard_map/all_gather | solution.py:143
  7.9 186.6 %all-gather.10.cloned.1.call-start = ((), (), s32[]{:S(2)}) async-start(), calls=%async_computation.7 | async-start | bytes 2162688 | tf_op jit(solution)/shard_map/all_gather | solution.py:110
  9.5 232.7 %all-gather.12.cloned.1.call-start = ((), (), s32[]{:S(2)}) async-start(), calls=%async_computation.8 | async-start | bytes 8650752 | tf_op jit(solution)/shard_map/all_gather | solution.py:110
  10.3 311.2 %all-gather.14.cloned.1.call-start = ((), (), s32[]{:S(2)}) async-start(), calls=%async_computation.9 | async-start | bytes 8650752 | tf_op jit(solution)/shard_map/all_gather | solution.py:110
  15.5 119.1 %copy-start.3 = (pred[1024,1024]{0,1:T(8,128)(4,1)}, pred[1024,1024]{0,1:T(8,128)(4,1)S(1)}, u32[]{:S(2)}) copy-start(pred[1024,1024]{0,1:T(8,128)(4,1)S(1)} %broadcast_compare_fusion) | copy-start | bytes 3145732
  19.1 81.7 %copy-start.14 = (f32[2,1024,64]{1,2,0:T(8,128)}, f32[2,1024,64]{1,2,0:T(8,128)S(1)}, u32[]{:S(2)}) copy-start(f32[2,1024,64]{1,2,0:T(8,128)S(1)} %get-tuple-element.110) | copy-start | bytes 1572868
  19.1 81.7 %copy-start.16 = (f32[2,1024,64]{1,2,0:T(8,128)}, f32[2,1024,64]{1,2,0:T(8,128)S(1)}, u32[]{:S(2)}) copy-start(f32[2,1024,64]{1,2,0:T(8,128)S(1)} %get-tuple-element.111) | copy-start | bytes 1572868
  153.5 38.8 %all-to-all-start = ((bf16[2,1024,256]{2,0,1:T(2,128)(2,1)}), bf16[2,1024,256]{2,0,1:T(2,128)(2,1)S(1)}, u32[]{:S(2)}, u32[]{:S(2)}) async-start(bf16[2,1024,256]{2,0,1:T(2,128)(2,1)} %copy.94), calls=%async_computation | async-start | bytes 2097152 | tf_op jit(solution)/shard_map/all_to_all | solution.py:157
  157.2 387.4 %reduce-scatter.9.cloned.1.call-start = ((), (), s32[]{:S(2)}) async-start(), calls=%async_computation.13 | async-start | bytes 8650752 | tf_op jit(solution)/shard_map/reduce_scatter | solution.py:116
  194.6 47.6 %copy-start.40 = (f32[1024]{0:T(1024)S(1)}, f32[1024]{0:T(1024)}, u32[]{:S(2)}) copy-start(f32[1024]{0:T(1024)} %param.24) | copy-start | bytes 12292
  242.2 79.4 %copy-start.39 = (f32[1024]{0:T(1024)S(1)}, f32[1024]{0:T(1024)}, u32[]{:S(2)}) copy-start(f32[1024]{0:T(1024)} %param.28) | copy-start | bytes 12292
  358.6 293.8 %reduce-scatter.11.cloned.1.call-start = ((), (), s32[]{:S(2)}) async-start(), calls=%async_computation.15 | async-start | bytes 8650752 | tf_op jit(solution)/shard_map/reduce_scatter | solution.py:116
  388.8 33.5 %all-to-all-start.1 = ((bf16[2,256,1024]{1,0,2:T(2,128)(2,1)}), bf16[2,256,1024]{1,0,2:T(2,128)(2,1)}, u32[]{:S(2)}, u32[]{:S(2)}) async-start(bf16[2,256,1024]{1,0,2:T(2,128)(2,1)} %copy.98), calls=%async_computation.1 | async-start | bytes 2097152 | tf_op jit(solution)/shard_map/all_to_all | solution.py:193
  393.1 322.8 %all-reduce.4.cloned.1.call-start = ((), (), s32[]{:S(2)}) async-start(), calls=%async_computation.11 | async-start | bytes 3145728 | tf_op jit(solution)/shard_map/psum | solution.py:211
  532.8 317.7 %reduce-scatter.7.cloned.1.call-start = ((), (), s32[]{:S(2)}) async-start(), calls=%async_computation.12 | async-start | bytes 2162688 | tf_op jit(solution)/shard_map/reduce_scatter | solution.py:116
  536.9 394.7 %reduce-scatter.5.cloned.1.call-start = ((), (), s32[]{:S(2)}) async-start(), calls=%async_computation.10 | async-start | bytes 5242880 | tf_op jit(solution)/shard_map/reduce_scatter | solution.py:208
  544.5 108.1 %copy-start.20 = (bf16[512,1024]{1,0:T(8,128)(2,1)S(1)}, bf16[512,1024]{1,0:T(8,128)(2,1)}, u32[]{:S(2)}) copy-start(bf16[512,1024]{1,0:T(8,128)(2,1)} %get-tuple-element.96) | copy-start | bytes 3145732
  544.5 110.4 %copy-start.33 = (f32[1024]{0:T(1024)S(1)}, f32[1024]{0:T(1024)}, u32[]{:S(2)}) copy-start(f32[1024]{0:T(1024)} %get-tuple-element.82) | copy-start | bytes 12292
  544.5 110.4 %copy-start.32 = (f32[1024]{0:T(1024)S(1)}, f32[1024]{0:T(1024)}, u32[]{:S(2)}) copy-start(f32[1024]{0:T(1024)} %get-tuple-element.87) | copy-start | bytes 12292
  544.5 417.9 %all-gather.16.cloned.1.call-start = ((), (), s32[]{:S(2)}) async-start(), calls=%async_computation.14 | async-start | bytes 2359296 | tf_op jit(solution)/shard_map/all_gather | solution.py:119
  545.1 447.2 %all-gather.18.cloned.1.call-start = ((), (), s32[]{:S(2)}) async-start(), calls=%async_computation.16 | async-start | bytes 2359296 | tf_op jit(solution)/shard_map/all_gather | solution.py:119
  652.5 476.3 %all-reduce.6.cloned.1.call-start = ((), (), s32[]{:S(2)}) async-start(), calls=%async_computation.17 | async-start | bytes 2359296 | tf_op jit(solution)/shard_map/psum | solution.py:227
  962.3 168.9 %copy-start.1 = (bf16[1024,1024]{1,0:T(8,128)(2,1)S(1)}, bf16[1024,1024]{1,0:T(8,128)(2,1)}, u32[]{:S(2)}) copy-start(bf16[1024,1024]{1,0:T(8,128)(2,1)} %param.25) | copy-start | bytes 6291460
  (33 other events, 337.6 us)
Sparse Core Ops, SparseCore 0:
  9.6 82.8 all-gather.7
  95.9 55.3 all-gather.9
  154.7 87.4 all-gather.11
  245.5 76.0 all-gather.13
  358.8 147.1 reduce-scatter.8
  508.1 144.3 reduce-scatter.10
  656.3 59.5 all-reduce.3
  718.8 131.6 reduce-scatter.6
  853.5 78.0 reduce-scatter.4
  933.5 28.7 all-gather.15
  964.4 27.8 all-gather.17
  999.0 129.6 all-reduce.5

commit v2 on v1

--- a/solution.py
+++ b/solution.py
@@ -1,8 +1,11 @@
+import functools
 import math
 
 import jax
 import jax.numpy as jnp
 from jax import lax
+from jax.experimental import pallas as pl
+from jax.experimental.pallas import tpu as pltpu
 from jax.sharding import Mesh
 from jax.sharding import PartitionSpec as P
 
@@ -101,22 +104,496 @@
     return (grad_queries, grad_keys, grad_values)
 
 
-def piece_of(shard):
-    rows = shard.shape[0] // 8
-    return lax.dynamic_slice_in_dim(shard, lax.axis_index(CELL) * rows, rows, 0)
-
-
-def gather_all(shard, zsize):
-    whole = lax.all_gather(piece_of(shard), ("z",) + CELL, axis=0, tiled=True)
-    return whole.reshape((zsize,) + shard.shape)
-
-
-def reduce_all(partial):
-    rows = partial.shape[0] * partial.shape[1]
-    piece = lax.psum_scatter(
-        partial.reshape(rows, partial.shape[2]), ("z",) + CELL, scatter_dimension=0, tiled=True
-    )
-    return lax.all_gather(piece, CELL, axis=0, tiled=True)
+MESH_ID = pl.DeviceIdType.MESH
+HBM = pl.BlockSpec(memory_space=pl.ANY)
+
+
+def other(axis):
+    return {axis: 1 - lax.axis_index(axis)}
+
+
+def greet(zsize):
+    z = lax.axis_index("z")
+    barrier = pltpu.get_barrier_semaphore()
+    for axis in CELL:
+        pl.semaphore_signal(barrier, inc=1, device_id=other(axis), device_id_type=MESH_ID)
+
+    @pl.when(z > 0)
+    def _():
+        pl.semaphore_signal(barrier, inc=1, device_id={"z": z - 1}, device_id_type=MESH_ID)
+
+    @pl.when(z < zsize - 1)
+    def _():
+        pl.semaphore_signal(barrier, inc=1, device_id={"z": z + 1}, device_id_type=MESH_ID)
+
+    peers = len(CELL) + jnp.where(z > 0, 1, 0) + jnp.where(z < zsize - 1, 1, 0)
+    pl.semaphore_wait(barrier, peers)
+
+
+def remote(src, dst, send_sem, recv_sem, device):
+    return pltpu.make_async_remote_copy(
+        src_ref=src, dst_ref=dst, send_sem=send_sem, recv_sem=recv_sem, device_id=device, device_id_type=MESH_ID
+    )
+
+
+ORDERS = {"xy": ("x", "y"), "yx": ("y", "x")}
+
+
+def gather_kernel(zsize, orders, *refs):
+    n = len(orders)
+    tok, bias, shards = refs[0], refs[1], refs[2:2 + n]
+    tok_all, bias_all, wholes = refs[2 + n], refs[3 + n], refs[4 + n:4 + 2 * n]
+    local_sem, z_send, z_recv, p_send, p_recv = refs[4 + 2 * n:]
+    z = lax.axis_index("z")
+    c = lax.axis_index("core")
+    place = [(lax.axis_index(o[0]), lax.axis_index(o[1])) for o in orders]
+
+    local = []
+    for k in range(n):
+        local.append(pltpu.make_async_copy(shards[k], wholes[k].at[z], local_sem.at[k]))
+    local.append(pltpu.make_async_copy(tok, tok_all.at[z], local_sem.at[n]))
+    local.append(pltpu.make_async_copy(bias, bias_all.at[z], local_sem.at[n + 1]))
+    for copy in local:
+        copy.start()
+    greet(zsize)
+
+    def line(item, src, step, side):
+        to = z + 1 if side == 0 else z - 1
+        if item < n:
+            f, s = place[item]
+            own = shards[item].at[c, f, s]
+            dst = wholes[item].at[src, c, f, s]
+        else:
+            own = (tok, bias)[item - n]
+            dst = (tok_all, bias_all)[item - n].at[src]
+        return remote(
+            own if step == 0 else dst, dst, z_send.at[side, item, step], z_recv.at[side, item, step], {"z": to}
+        )
+
+    def exchange(k, src, stage, slot):
+        f, s = place[k]
+        whole = wholes[k]
+        ref = (whole.at[src, c, f, s], whole.at[src, c, f], whole.at[src, c])[stage]
+        axis = (orders[k][1], orders[k][0], "core")[stage]
+        return remote(ref, ref, p_send.at[slot, k, stage], p_recv.at[slot, k, stage], other(axis))
+
+    def valid_from(side, step):
+        return z - step - 1 >= 0 if side == 0 else z + step + 1 < zsize
+
+    def source(side, step):
+        return z - step - 1 if side == 0 else z + step + 1
+
+    def has_next(side):
+        return z < zsize - 1 if side == 0 else z > 0
+
+    for side in range(2):
+
+        @pl.when(has_next(side))
+        def _():
+            for item in range(n):
+                line(item, z, 0, side).start()
+
+    def stage_on(stage, step):
+        for side in range(2):
+
+            @pl.when(valid_from(side, step))
+            def _():
+                src = source(side, step)
+                slot = side * (zsize - 1) + step
+                for k in range(n):
+                    exchange(k, src, stage - 1, slot).wait_recv()
+                    if stage < 3:
+                        exchange(k, src, stage, slot).start()
+
+    def arrive(items, step):
+        for side in range(2):
+
+            @pl.when(valid_from(side, step))
+            def _():
+                src = source(side, step)
+                for item in items:
+                    line(item, src, step, side).wait_recv()
+                    if step + 1 < zsize - 1:
+
+                        @pl.when(has_next(side))
+                        def _():
+                            line(item, src, step + 1, side).start()
+
+                    if item < n:
+                        exchange(item, src, 0, side * (zsize - 1) + step).start()
+
+    for step in range(zsize - 1):
+        arrive(range(n), step)
+        if step == zsize - 2:
+            for side in range(2):
+
+                @pl.when(has_next(side))
+                def _():
+                    for item in range(n, n + 2):
+                        line(item, z, 0, side).start()
+
+        if step >= 1:
+            stage_on(1, step - 1)
+    for step in range(zsize - 1):
+        if step == 0:
+            stage_on(1, zsize - 2)
+        stage_on(2, step)
+        arrive(range(n, n + 2), step)
+    for step in range(zsize - 1):
+        stage_on(3, step)
+    for copy in local:
+        copy.wait()
+    for side in range(2):
+
+        @pl.when(has_next(side))
+        def _():
+            for item in range(n + 2):
+                line(item, z, 0, side).wait_send()
+
+        for step in range(zsize - 1):
+
+            @pl.when(valid_from(side, step))
+            def _():
+                src = source(side, step)
+                if step + 1 < zsize - 1:
+
+                    @pl.when(has_next(side))
+                    def _():
+                        for item in range(n + 2):
+                            line(item, src, step + 1, side).wait_send()
+
+                for k in range(n):
+                    for stage in range(3):
+                        exchange(k, src, stage, side * (zsize - 1) + step).wait_send()
+
+
+def gather_start(tokens, bias, weights, zsize):
+    orders = [ORDERS[o] for o, _ in weights]
+    shards = [w for _, w in weights]
+    n = len(shards)
+    stack = lambda a: jax.ShapeDtypeStruct((zsize,) + a.shape, a.dtype)
+    return pl.pallas_call(
+        functools.partial(gather_kernel, zsize, orders),
+        out_shape=[stack(tokens), stack(bias)] + [stack(w) for w in shards],
+        in_specs=[HBM] * (n + 2),
+        out_specs=[HBM] * (n + 2),
+        scratch_shapes=[
+            pltpu.SemaphoreType.DMA((n + 2,)),
+            pltpu.SemaphoreType.DMA((2, n + 2, zsize - 1)),
+            pltpu.SemaphoreType.DMA((2, n + 2, zsize - 1)),
+            pltpu.SemaphoreType.DMA((2 * (zsize - 1), n, 3)),
+            pltpu.SemaphoreType.DMA((2 * (zsize - 1), n, 3)),
+        ],
+        compiler_params=pltpu.CompilerParams(collective_id=0, has_side_effects=True),
+    )(tokens, bias, *shards)
+
+
+def add_rows(dst, src):
+    rows = dst.shape[0]
+    step = min(rows, 32)
+
+    def body(i, carry):
+        at = pl.ds(pl.multiple_of(i * step, step), step)
+        dst[at, :] = dst[at, :] + src[at, :]
+        return carry
+
+    lax.fori_loop(0, rows // step, body, 0)
+
+
+def reduce_kernel(zsize, orders, *refs):
+    n = len(orders)
+    m = n - 2
+    parts, back, small = refs[:n], refs[n], refs[n + 1]
+    outs, back_out, small_out = refs[n + 2:2 * n + 2], refs[2 * n + 2], refs[2 * n + 3]
+    pos = 2 * n + 4
+    mine, got_c, got_1, got_2 = (refs[pos + i * n:pos + (i + 1) * n] for i in range(4))
+    pos += 4 * n
+    got_z = refs[pos:pos + m + 1]
+    pos += m + 1
+    back_mine, small_mine, small_got, small_line, small_total, part_line, part_total = refs[pos:pos + 7]
+    (local_sem, send, recv, z_send, z_recv, s_send, s_recv, t_send, t_recv, g_send, g_recv, end_sem) = refs[pos + 7:]
+    z = lax.axis_index("z")
+    c = lax.axis_index("core")
+    place = [(lax.axis_index(o[0]), lax.axis_index(o[1])) for o in orders]
+    turn = []
+    for i in range(zsize // 2):
+        turn += [i, zsize - 1 - i]
+    few = parts[m].shape[0]
+    groups = [[(m, b) for b in range(few)] + [(m + 1, 0)]] + [[(k, b) for k in range(m)] for b in turn]
+    steps = [kb for group in groups for kb in group]
+
+    def load(k, b):
+        return pltpu.make_async_copy(parts[k].at[b, c], mine[k].at[b], local_sem.at[k, b])
+
+    def load_back(b):
+        return pltpu.make_async_copy(back.at[b], back_mine.at[b], local_sem.at[n, b])
+
+    load_small = pltpu.make_async_copy(small, small_mine.at[0], local_sem.at[n + 1, 0])
+
+    def half(k, b, stage):
+        f, s = place[k]
+        if stage == 0:
+            src, dst, axis = parts[k].at[b, 1 - c], got_c[k].at[b], "core"
+        elif stage == 1:
+            src, dst, axis = mine[k].at[b, 1 - f], got_1[k].at[b], orders[k][0]
+        else:
+            src, dst, axis = mine[k].at[b, f, 1 - s], got_2[k].at[b], orders[k][1]
+        return remote(src, dst, send.at[stage, k, b], recv.at[stage, k, b], other(axis))
+
+    def own(k, b):
+        if k == m:
+            return back_mine.at[b]
+        f, s = place[k]
+        return mine[k].at[b, f, s]
+
+    def hop(k, b, side):
+        to = z + 1 if side == 0 else z - 1
+        at = b if side == 0 else jnp.where(b == z - 1, zsize, b)
+        return remote(own(k, b), got_z[k].at[at], z_send.at[k, b], z_recv.at[k, at], {"z": to})
+
+    def take(k, b, side):
+        at = b if side == 0 else jnp.where(b == z, zsize, b)
+        ref = got_z[k].at[at]
+        sender = z - 1 if side == 0 else z + 1
+        remote(own(k, b), ref, z_send.at[k, b], z_recv.at[k, at], {"z": sender}).wait_recv()
+        add_rows(own(k, b), ref)
+
+    def line_step(ks, b, hops):
+        for side in range(2):
+            here = z == hops if side == 0 else z == zsize - 1 - hops
+            goes = jnp.logical_and(here, z < b) if side == 0 else jnp.logical_and(here, z > b)
+            if hops:
+                ends = jnp.logical_and(here, z == b)
+
+                @pl.when(jnp.logical_or(goes, ends))
+                def _():
+                    for k in ks:
+                        take(k, b, side)
+
+            @pl.when(goes)
+            def _():
+                for k in ks:
+                    hop(k, b, side).start()
+
+    def small_swap(stage):
+        return remote(
+            small_mine.at[stage], small_got.at[stage], s_send.at[stage], s_recv.at[stage], other(CELL[stage])
+        )
+
+    def small_step(stage):
+        small_swap(stage).wait_recv()
+        small_mine[stage + 1] = small_mine[stage] + small_got[stage]
+        if stage < 2:
+            small_swap(stage + 1).start()
+
+    last = len(CELL)
+    last_part = own(m + 1, 0)
+
+    def total_copy(item, way):
+        line, total = ((small_line, small_total), (part_line, part_total))[item]
+        src = (small_mine.at[last], last_part)[item] if way == 0 else total
+        dst = line if way == 0 else total
+        to = z + 1 if way == 0 else z - 1
+        return remote(src, dst, t_send.at[item, way], t_recv.at[item, way], {"z": to})
+
+    def total_step(tick):
+        if 0 <= tick < zsize:
+
+            @pl.when(z == tick)
+            def _():
+                if tick > 0:
+                    for item in range(2):
+                        total_copy(item, 0).wait_recv()
+                    small_mine[last] = small_mine[last] + small_line[...]
+                    add_rows(last_part, part_line)
+                if tick < zsize - 1:
+                    for item in range(2):
+                        total_copy(item, 0).start()
+                else:
+                    small_total[...] = small_mine[last]
+                    part_total[...] = last_part[...]
+
+        back_tick = tick - (zsize - 1)
+        if 0 <= back_tick < zsize:
+
+            @pl.when(z == zsize - 1 - back_tick)
+            def _():
+                if back_tick > 0:
+                    for item in range(2):
+                        total_copy(item, 1).wait_recv()
+                if back_tick < zsize - 1:
+                    for item in range(2):
+                        total_copy(item, 1).start()
+
+    for b in turn:
+        load_back(b).start()
+    load_small.start()
+    for k, b in steps:
+        load(k, b).start()
+    greet(zsize)
+    for k, b in groups[0]:
+        half(k, b, 0).start()
+    for b in turn:
+        load_back(b).wait()
+    for b in turn:
+        line_step([m], b, 0)
+    load_small.wait()
+    small_swap(0).start()
+    for k, b in steps[len(groups[0]):]:
+        half(k, b, 0).start()
+
+    def stage_1(k, b):
+        f, s = place[k]
+        load(k, b).wait()
+        half(k, b, 0).wait_recv()
+        for i in range(2):
+            add_rows(mine[k].at[b, 1 - f, i], got_c[k].at[b, 1 - f, i])
+        half(k, b, 1).start()
+        for i in range(2):
+            add_rows(mine[k].at[b, f, i], got_c[k].at[b, f, i])
+
+    def stage_2(k, b):
+        f, s = place[k]
+        half(k, b, 1).wait_recv()
+        add_rows(mine[k].at[b, f, 1 - s], got_1[k].at[b, 1 - s])
+        half(k, b, 2).start()
+        add_rows(mine[k].at[b, f, s], got_1[k].at[b, s])
+
+    def stage_3(k, b):
+        f, s = place[k]
+        half(k, b, 2).wait_recv()
+        add_rows(mine[k].at[b, f, s], got_2[k].at[b])
+
+    def result(k, b):
+        return part_total if k == m + 1 else own(k, b) if k != m else mine[m].at[b, place[m][0], place[m][1]]
+
+    def out_of(k, b):
+        return outs[k].at[b] if k == m else outs[k]
+
+    def put(k, b, slot):
+        f, s = place[k]
+        return pltpu.make_async_copy(result(k, b), out_of(k, b).at[c, f, s], end_sem.at[slot])
+
+    def spread(k, b, stage, slot):
+        f, s = place[k]
+        out = out_of(k, b)
+        dst = (out.at[c, f, s], out.at[c, f], out.at[c])[stage]
+        src = result(k, b) if stage == 0 else dst
+        axis = (orders[k][1], orders[k][0], "core")[stage]
+        return remote(src, dst, g_send.at[slot, stage], g_recv.at[slot, stage], other(axis))
+
+    first = [(m, b, b) for b in range(few)]
+    rest = [(k, z, few + k) for k in range(m)] + [(m + 1, 0, few + m)]
+
+    def spread_start(items):
+        for k, b, slot in items:
+            spread(k, b, 0, slot).start()
+            put(k, b, slot).start()
+
+    def spread_on(items, stage):
+        for k, b, slot in items:
+            if stage == 1:
+                put(k, b, slot).wait()
+            spread(k, b, stage - 1, slot).wait_recv()
+            if stage < 3:
+                spread(k, b, stage, slot).start()
+
+    ks = list(range(m))
+    small_tick = 3
+    back_ticks = [2 + i + (1 if i > 1 else 0) for i in range(zsize)]
+    for tick in range(len(groups) + zsize + 2):
+        if tick < len(groups):
+            for k, b in groups[tick]:
+                stage_1(k, b)
+        if 1 <= tick <= len(groups):
+            for k, b in groups[tick - 1]:
+                stage_2(k, b)
+        if 2 <= tick <= len(groups) + 1:
+            for k, b in groups[tick - 2]:
+                stage_3(k, b)
+        if 1 <= tick <= 3:
+            small_step(tick - 1)
+        for i in range(1, zsize):
+            if tick == back_ticks[i - 1]:
+                for b in turn:
+                    line_step([m], b, i)
+        for j, b in enumerate(turn):
+            hops = tick - 3 - j
+            if 0 <= hops < zsize:
+                line_step(ks, b, hops)
+        total_step(tick - small_tick)
+        if tick == 4:
+            spread_start(first)
+        if 5 <= tick <= 7:
+            spread_on(first, tick - 4)
+    for tick in range(len(groups) + zsize + 2 - small_tick, 2 * zsize):
+        total_step(tick)
+    finish_back = pltpu.make_async_copy(back_mine.at[z], back_out, local_sem.at[n, 0])
+    finish_back.start()
+    finish_small = pltpu.make_async_copy(small_total, small_out, local_sem.at[n + 1, 0])
+    finish_small.start()
+    spread_start(rest)
+    for stage in (1, 2, 3):
+        spread_on(rest, stage)
+    finish_back.wait()
+    finish_small.wait()
+    for b in range(zsize):
+
+        @pl.when(z != b)
+        def _():
+            for k in range(m + 1):
+                hop(k, b, 0).wait_send()
+
+    for way in range(2):
+
+        @pl.when(z < zsize - 1 if way == 0 else z > 0)
+        def _():
+            for item in range(2):
+                total_copy(item, way).wait_send()
+
+    for k, b in steps:
+        for stage in range(3):
+            half(k, b, stage).wait_send()
+    for stage in range(3):
+        small_swap(stage).wait_send()
+    for k, b, slot in first + rest:
+        for stage in range(3):
+            spread(k, b, stage, slot).wait_send()
+
+
+def reduce_end(parts, cell_part, all_part, back, small, zsize):
+    orders = [ORDERS[o] for o, _ in parts + [cell_part, all_part]]
+    arrays = [a for _, a in parts + [cell_part, all_part]]
+    n = len(arrays)
+    shapes = [a.shape for a in arrays]
+    like = jax.ShapeDtypeStruct
+    outs = [like(s if i == n - 2 else s[1:], bf16) for i, s in enumerate(shapes)]
+    outs += [like(back.shape[1:], bf16), like(small.shape, f32)]
+    scratch = [pltpu.VMEM((s[0],) + s[2:], bf16) for s in shapes]
+    scratch += [pltpu.VMEM((s[0],) + s[2:], bf16) for s in shapes]
+    scratch += [pltpu.VMEM((s[0],) + s[3:], bf16) for s in shapes]
+    scratch += [pltpu.VMEM((s[0],) + s[4:], bf16) for s in shapes]
+    scratch += [pltpu.VMEM((zsize + 1,) + s[4:], bf16) for s in shapes[:-2]]
+    scratch += [pltpu.VMEM((zsize + 1,) + back.shape[1:], bf16), pltpu.VMEM(back.shape, bf16)]
+    scratch += [pltpu.VMEM((4,) + small.shape, f32), pltpu.VMEM((3,) + small.shape, f32)]
+    scratch += [pltpu.VMEM(small.shape, f32)] * 2 + [pltpu.VMEM(shapes[-1][4:], bf16)] * 2
+    dma = pltpu.SemaphoreType.DMA
+    most = max(zsize, shapes[-2][0])
+    ends = n - 1 + shapes[-2][0]
+    scratch += [
+        dma((n + 2, most)), dma((3, n, most)), dma((3, n, most)), dma((n - 1, zsize)), dma((n - 1, zsize + 1)),
+        dma((3,)), dma((3,)), dma((2, 2)), dma((2, 2)), dma((ends, 3)), dma((ends, 3)), dma((ends,)),
+    ]
+    return pl.pallas_call(
+        functools.partial(reduce_kernel, zsize, orders),
+        out_shape=outs,
+        in_specs=[HBM] * (n + 2),
+        out_specs=[HBM] * (n + 2),
+        scratch_shapes=scratch,
+        compiler_params=pltpu.CompilerParams(
+            collective_id=1, has_side_effects=True, vmem_limit_bytes=60 * 1024 * 1024
+        ),
+    )(*arrays, back, small)
 
 
 def per_device(blocks, tokens, segments, qkv_weight, qkv_bias, out_weight, out_bias, gain_one, shift_one,
@@ -140,11 +617,23 @@
     def join_heads(field):
         return field.transpose(0, 2, 1, 3).reshape(groups, length, head_cols)
 
-    whole_tokens = lax.all_gather(tokens, "z", axis=1, tiled=True)
-    out_all = gather_all(out_weight, zsize).reshape(model_width, model_width)
-    up_all = gather_all(up_weight, zsize)
-    down_all = gather_all(down_weight, zsize)
-    full_up_bias = lax.all_gather(up_bias, "z", axis=0, tiled=False)
+    def cut(array, rows_at):
+        shape = array.shape
+        return array.reshape(shape[:rows_at] + (2, 2, 2, shape[rows_at] // 8) + shape[rows_at + 1:])
+
+    token_rows = tokens.reshape(rows, model_width)
+    token_blocks, bias_blocks, out_all, up_all, down_all = gather_start(
+        token_rows,
+        up_bias.reshape(8, units_here // 8),
+        [("xy", cut(out_weight, 0)), ("xy", cut(up_weight, 0)), ("yx", cut(down_weight, 0))],
+        zsize,
+    )
+    whole_tokens = token_blocks.reshape(zsize, groups, local_rows, model_width).transpose(1, 0, 2, 3)
+    whole_tokens = whole_tokens.reshape(groups, length, model_width)
+    out_all = out_all.reshape(model_width, model_width)
+    up_all = up_all.reshape(zsize, model_width, units_here)
+    down_all = down_all.reshape(zsize, units_here, model_width)
+    full_up_bias = bias_blocks.reshape(zsize, units_here)
 
     projected = jnp.einsum("gld,cde->cgle", whole_tokens, qkv_weight, preferred_element_type=f32)
     projected = projected + qkv_bias[:, None, None, :]
@@ -205,15 +694,7 @@
     qkv_bias_grad = jnp.sum(grad_qkv.astype(f32), axis=(1, 2))
     qkv_weight_grad = jnp.einsum("gld,cgle->cde", whole_tokens, grad_qkv, preferred_element_type=f32)
     input_back = jnp.einsum("cgle,cde->gld", grad_qkv, qkv_weight, preferred_element_type=f32).astype(bf16)
-    input_back = lax.psum_scatter(input_back, "z", scatter_dimension=1, tiled=True)
-    tokens_grad = grad_first.reshape(groups, local_rows, model_width) + input_back.astype(f32)
-
-    qkv_weight_grad = lax.psum(qkv_weight_grad.astype(bf16), DP).astype(f32)
-    down_grad = reduce_all(down_grad)
-    up_grad = reduce_all(up_grad)
-    out_grad_w = reduce_all(out_grad_w.reshape(zsize, head_cols, model_width))
-    if blocks > 1:
-        down_grad, up_grad, out_grad_w = lax.psum((down_grad, up_grad, out_grad_w), ("xb", "yb"))
+    back = input_back.reshape(groups, zsize, local_rows, model_width).transpose(1, 0, 2, 3)
     small = jnp.concatenate(
         [
             out_bias_grad, gain_one_grad, shift_one_grad, down_bias_grad, gain_two_grad, shift_two_grad,
@@ -223,8 +704,34 @@
             ).reshape(-1),
         ]
     )
-    small = lax.psum(small, ALL)
-    proj_grad = lax.psum(proj_grad, ALL)
+    proj_cols = proj_grad.shape[1]
+    proj_grad = jnp.pad(proj_grad.astype(bf16), ((0, 0), (0, -proj_cols % 128)))
+    out_grad_w, up_grad, down_grad, qkv_weight_grad, proj_grad, back, small = reduce_end(
+        [
+            ("xy", cut(out_grad_w.reshape(zsize, head_cols, model_width), 1)),
+            ("xy", cut(up_grad, 1)),
+            ("yx", cut(down_grad, 1)),
+        ],
+        ("yx", cut(qkv_weight_grad.astype(bf16), 1)),
+        ("xy", cut(proj_grad[None], 1)),
+        back.reshape(zsize, rows, model_width),
+        small.reshape(8, -1),
+        zsize,
+    )
+    tokens_grad = grad_first.reshape(groups, local_rows, model_width) + back.astype(f32).reshape(
+        groups, local_rows, model_width
+    )
+    qkv_weight_grad = qkv_weight_grad.reshape(qkv_weight.shape)
+    proj_grad = proj_grad.reshape(model_width, -1)[:, :proj_cols].astype(f32)
+    out_grad_w = out_grad_w.reshape(out_weight.shape)
+    up_grad = up_grad.reshape(up_weight.shape)
+    down_grad = down_grad.reshape(down_weight.shape)
+    if blocks > 1:
+        down_grad, up_grad, out_grad_w, qkv_weight_grad = lax.psum(
+            (down_grad, up_grad, out_grad_w, qkv_weight_grad), ("xb", "yb")
+        )
+        small, proj_grad = lax.psum((small, proj_grad), ("xb", "yb"))
+    small = small.reshape(-1)
     base = 6 * model_width
     vec = [small[i * model_width:(i + 1) * model_width] for i in range(6)]
     up_bias_grad = lax.dynamic_slice(small, (base + zi * units_here,), (units_here,))
@@ -236,7 +743,7 @@
         result_low.reshape(shape3),
         embedded.reshape(groups, local_rows, -1),
         tokens_grad,
-        qkv_weight_grad,
+        qkv_weight_grad.astype(f32),
         qkv_bias_grad,
         out_grad_w.astype(f32),
         vec[0], vec[1], vec[2],

time: 1150 us -> 678 us (0.59)
  waiting for transfers between devices: 701 us -> 28.7 us
  Pallas kernels: 0 us -> 341 us
  blocking collectives: 91.7 us -> 0 us
  matrix products: 208 us -> 183 us
  between operations: 15.2 us -> 1.85 us
    pallas_call x0 -> x2, Pallas kernels: none -> 341 us  [the longest x1 178 us: gather_start(): pl.pallas_call(functools.partial(gather_kernel, zsize, orders), out_shape...]
    reduce_scatter x4 -> x0, waiting for transfers between devices: 304 us -> none  [the longest x3 239 us: reduce_all(): lax.psum_scatter(partial.reshape(rows, partial.shape[2]), ('z',) + CELL,...]
    all_gather x6 -> x0, waiting for transfers between devices: 221 us -> none  [the longest x3 94 us: gather_all(): whole = lax.all_gather(piece_of(shard), ('z',) + CELL, axis=0, tiled=True)]
    psum x2 -> x0, waiting for transfers between devices: 146 us -> none  [the longest x1 132 us: per_device(): proj_grad = lax.psum(proj_grad, ALL)]
    all_gather x2 -> x0, blocking collectives: 49.2 us -> none  [the longest x1 34.1 us: per_device(): full_up_bias = lax.all_gather(up_bias, 'z', axis=0, tiled=False)]
    psum x1 -> x0, blocking collectives: 42.5 us -> none  [per_device(): small = lax.psum(small, ALL)]
    all_to_all x1, waiting for transfers between devices: 29.2 us -> 4.25 us  [per_device(): lax.all_to_all(grad_mixed, 'z', split_axis=2, concat_axis=1, tiled=True)]
    all_to_all x1, waiting for transfers between devices: 0.01 us -> 24.5 us  [per_device(): lax.all_to_all(mixed, 'z', split_axis=1, concat_axis=2, tiled=True)]
  transfers between devices with their start and end apart: 14 -> 2, of which waited for: 11 -> 2; matrix products, arithmetic and copies ran while one was open for 24% -> 3% of each run, Pallas kernels for 0% -> 0%
where the time goes in v2:
time: 678 us; the launch traced here: 672 us
  Pallas kernels  341 us (50%)
  matrix products  183 us (27%)
  other arithmetic  70.9 us (10%)
  local copies, waits for them, and re-layouts  36.1 us (5%)
  waiting for transfers between devices  28.7 us (4%)
  starting transfers between devices  10.2 us (2%)
    pallas_call x1, Pallas kernels, gather_start(): pl.pallas_call(functools.partial(gather_kernel, zsize, orders), out_shape...  178 us
    pallas_call x1, Pallas kernels, reduce_end(): pl.pallas_call(functools.partial(reduce_kernel, zsize, orders), out_shape...  163 us
    dot_general x1, matrix products, per_device(): jnp.einsum('nd,zdf->znf', normed_low, up_all, preferred_element_type=f32)  25.9 us
    convert_element_type x2, other arithmetic, attend_back(): grad_scores = (probs * (grad_probs - row_inner)).astype(bf16)  24.5 us
    all_to_all x1, waiting for transfers between devices, per_device(): lax.all_to_all(mixed, 'z', split_axis=1, concat_axis=2, tiled=True)  24.5 us
    dot_general x2, matrix products, attend_back(): jnp.einsum('hqd,hkd->hqk', grad_mixed, values_low, preferred_element_type...  24 us
    dot_general x2, matrix products, attend_back(): jnp.einsum('hqk,hqd->hkd', probs.astype(bf16), grad_mixed, preferred_elem...  20.2 us
    reduce_sum x2, other arithmetic, attend(): row_total = jnp.sum(shifted, axis=-1, keepdims=True)  17.8 us
  transfers between devices with their start and end apart: 2, of which 2 were waited for; matrix products, arithmetic and copies ran while one was open for 3% of the time, Pallas kernels for 0%

profile of v2, /device:TPU:1, one launch (start us, length us, event | category | flops | bytes accessed | tf_op | source)
XLA Modules:
  0.0 671.9 jit_solution(15969386514223003521)
XLA Ops:
  2.4 177.6 %shard_map.288 = (bf16[4,512,1024]{2,1,0:T(8,128)(2,1)}, f32[4,8,128]{2,1,0:T(8,128)}, bf16[4,2,2,2,32,1024]{5,4,3,2,1,0:T(8,128)(2,1)}, bf16[4,2,2,2,128,1024]{...) custom-call(bf16[512,1024]{1,0:T(8,128)(2,1)} %bitcast.358, f32[8,128]{1,0:T(8,128)} %bitcast.377, ...), custom_call_target="tpu_custom_call" | custom-call | tf_op jit(solution)/shard_map/pallas_call | solution.py:275
  197.8 7.3 %select_reduce_fusion = (f32[4,1024]{1,0:T(4,128)S(1)}, f32[4,1024,1024]{1,2,0:T(8,128)}) fusion(pred[1024,1024]{0,1:T(8,128)(4,1)S(1)} %broadcast_compare_fusion, bf16[2,4,1024,64]{2,3,1,0:T(8,128)(2,1)S(1)} %get-tuple-element.129, bf16[2,4,1024,64]{2,3,1,0:T(8,128)(2,1)S(1)} %get-tuple-element.130), kind=kOutput, calls=%fused_computation.12 | convolution fusion | flops 545255424 | bytes 18890752 | tf_op jit(solution)/shard_map/hqd,hkd->hqk/dot_general | solution.py:78
  205.1 7.3 %select_reduce_fusion.1 = (f32[4,1024]{1,0:T(4,128)S(1)}, f32[4,1024,1024]{1,2,0:T(8,128)}) fusion(pred[1024,1024]{0,1:T(8,128)(4,1)S(1)} %broadcast_compare_fusion.1, bf16[2,4,1024,64]{2,3,1,0:T(8,128)(2,1)S(1)} %get-tuple-element.129, bf16[2,4,1024,64]{2,3,1,0:T(8,128)(2,1)S(1)} %get-tuple-element.130), kind=kOutput, calls=%fused_computation.13 | convolution fusion | flops 545255424 | bytes 18890752 | tf_op jit(solution)/shard_map/hqd,hkd->hqk/dot_general | solution.py:78
  212.3 9.0 %fusion.1 = f32[4,1024]{1,0:T(4,128)S(1)} fusion(f32[4,1024,1024]{1,2,0:T(8,128)} %get-tuple-element.146, f32[4,1024]{1,0:T(4,128)S(1)} %get-tuple-element.145, pred[1024,1024]{0,1:T(8,128)(4,1)} %copy-done.3), kind=kLoop, calls=%fused_computation.11 | loop fusion | flops 12578816 | bytes 17858560 | tf_op jit(solution)/shard_map/reduce_sum | solution.py:88
  221.4 8.6 %fusion.59 = bf16[1,4,1024,64]{2,3,1,0:T(8,128)(2,1)S(1)} fusion(f32[4,1024,1024]{1,2,0:T(8,128)} %get-tuple-element.146, f32[4,1024]{1,0:T(4,128)S(1)} %fusion.1, f32[4,1024]{1,0:T(4,128)S(1)} %get-tuple-element.145, pred[1024,1024]{0,1:T(8,128)(4,1)} %copy-done.3, bf16[2,4,1024,64]{2,3,1,0:T(8,128)(2,1)} %bitcast.325), kind=kOutput, calls=%fused_computation.126 | convolution fusion | flops 553910272 | bytes 18907136 | tf_op jit(solution)/shard_map/hqk,hkd->hqd/dot_general | solution.py:90
  229.9 8.8 %fusion = f32[4,1024]{1,0:T(4,128)S(1)} fusion(f32[4,1024,1024]{1,2,0:T(8,128)} %get-tuple-element.148, f32[4,1024]{1,0:T(4,128)S(1)} %get-tuple-element.147, pred[1024,1024]{0,1:T(8,128)(4,1)S(1)} %broadcast_compare_fusion.1), kind=kLoop, calls=%fused_computation.10 | loop fusion | flops 12578816 | bytes 17858560 | tf_op jit(solution)/shard_map/reduce_sum | solution.py:88
  238.7 8.2 %fusion.58 = bf16[1,4,1024,64]{2,3,1,0:T(8,128)(2,1)S(1)} fusion(f32[4,1024,1024]{1,2,0:T(8,128)} %get-tuple-element.148, f32[4,1024]{1,0:T(4,128)S(1)} %fusion, f32[4,1024]{1,0:T(4,128)S(1)} %get-tuple-element.147, pred[1024,1024]{0,1:T(8,128)(4,1)S(1)} %broadcast_compare_fusion.1, bf16[2,4,1024,64]{2,3,1,0:T(8,128)(2,1)} %bitcast.326), kind=kOutput, calls=%fused_computation.125 | convolution fusion | flops 553910272 | bytes 18907136 | tf_op jit(solution)/shard_map/hqk,hkd->hqd/dot_general | solution.py:90
  249.1 6.0 all-to-all-start
  255.9 24.5 %all-to-all-done = bf16[2,1024,256]{2,0,1:T(2,128)(2,1)S(1)} async-done(((bf16[2,1024,256]{2,0,1:T(2,128)(2,1)}), bf16[2,1024,256]{2,0,1:T(2,128)(2,1)S(1)}, u32[]{:S(2)}, u32[]{:S(2)}) %all-to-all-start) | async-done | bytes 1048608 | tf_op jit(solution)/shard_map/all_to_all | solution.py:646
  285.0 25.9 %fusion.13 = (bf16[4,512,1024]{2,1,0:T(8,128)(2,1)S(1)}, f32[4,512,1024]{2,1,0:T(8,128)}, f32[4,1024,512]{1,2,0:T(8,128)}) fusion(f32[4,1024]{1,0:T(4,128)S(1)} %bitcast.373, bf16[4,1024,1024]{2,1,0:T(8,128)(2,1)S(1)} %bitcast.382, f32[512,1024]{1,0:T(8,128)S(1)} %get-tuple-element.150, f32[1024]{0:T(1024)S(1)} %copy-done.51, f32[1024]{0:T(1024)S(1)} %copy-done.44, ...), kind=kOutput, calls=%fused_computation.34 | convolution fusion | flops 4436000768 | bytes 31485952 | tf_op jit(solution)/shard_map/nd,zdf->znf/dot_general | solution.py:653
  311.0 9.0 %fusion.96 = (f32[512]{0:T(512)S(1)}, f32[512,1024]{1,0:T(8,128)S(1)}) fusion(f32[1024]{0:T(1024)S(1)} %copy-done.50, bf16[4,512,1024]{2,1,0:T(8,128)(2,1)S(1)} %get-tuple-element.116, bf16[4,1024,1024]{2,1,0:T(8,128)(2,1)} %bitcast.383, f32[1024]{0:T(1024)S(1)} %copy-done.51, f32[1024]{0:T(1024)S(1)} %copy-done.44, f32[512]{0:T(512)S(1)} %add_rsqrt_fusion.1, ...), kind=kOutput, calls=%fused_computation.202 | convolution fusion | flops 4298636800 | bytes 16795648 | tf_op jit(solution)/shard_map/znf,zfd->nd/dot_general | solution.py:657
  324.2 13.5 %convert_reduce_fusion = (f32[4,1024]{1,0:T(4,128)S(1)}, bf16[4,512,1024]{2,1,0:T(8,128)(2,1)S(1)}) fusion(f32[4,512,1024]{2,1,0:T(8,128)} %get-tuple-element.117, bf16[4,1024,1024]{2,1,0:T(8,128)(2,1)} %bitcast.384, f32[512,1024]{1,0:T(8,128)S(1)} %get-tuple-element.113, f32[4,1024,512]{1,2,0:T(8,128)} %get-tuple-element.151, f32[4,1024]{1,0:T(4,128)S(1)} %bitcast.374), kind=kOutput, calls=%fused_computation.35 | convolution fusion | flops 4331139072 | bytes 31490048 | tf_op jit(solution)/shard_map/nd,zfd->znf/dot_general | solution.py:671
  337.7 9.4 %multiply_reduce_fusion.3 = (f32[1024]{0:T(1024)S(1)}, f32[512]{0:T(512)S(1)}, f32[512]{0:T(512)S(1)}, f32[1024]{0:T(1024)S(1)}, f32[512,1024]{1,0:T(8,128)S(1)}) fusion(f32[512,1024]{1,0:T(8,128)S(1)} %get-tuple-element.150, f32[512]{0:T(512)S(1)} %add_rsqrt_fusion.1, f32[512]{0:T(512)S(1)} %broadcast_multiply_fusion.7, f32[1024]{0:T(1024)S(1)} %copy-done.44, ...), kind=kOutput, calls=%fused_computation.91 | convolution fusion | flops 4300207104 | bytes 18894848 | tf_op jit(solution)/shard_map/znf,zdf->nd/dot_general | solution.py:675
  362.8 10.8 %convolution_convert_fusion = bf16[4,1024,1024]{2,1,0:T(8,128)(2,1)} fusion(bf16[4,512,1024]{2,1,0:T(8,128)(2,1)} %copy-done.52, f32[512,1024]{1,0:T(8,128)} %copy-done.26), kind=kOutput, calls=%fused_computation.55 | convolution fusion | flops 4299685888 | bytes 14680064 | tf_op jit(solution)/shard_map/znf,nd->zfd/dot_general | solution.py:670
  373.6 8.1 %convolution_convert_fusion.1 = bf16[4,1024,1024]{1,2,0:T(8,128)(2,1)} fusion(bf16[4,512,1024]{2,1,0:T(8,128)(2,1)S(1)} %copy-done.54, f32[512,1024]{1,0:T(8,128)S(1)} %copy-done.18, f32[1024]{0:T(1024)S(1)} %copy-done.51, f32[1024]{0:T(1024)S(1)} %copy-done.44, f32[512]{0:T(512)S(1)} %add_rsqrt_fusion.1, f32[512]{0:T(512)S(1)} %broadcast_multiply_fusion.7), kind=kOutput, calls=%fused_computation.56 | convolution fusion | flops 4301783040 | bytes 14692352 | tf_op jit(solution)/shard_map/nd,znf->zdf/dot_general | solution.py:674
  391.9 9.7 %fusion.60 = bf16[1,4,1024,64]{2,3,1,0:T(8,128)(2,1)S(1)} fusion(f32[4,1024,1024]{1,2,0:T(8,128)} %get-tuple-element.146, f32[4,1024]{1,0:T(4,128)S(1)} %log_add_fusion, pred[1024,1024]{0,1:T(8,128)(4,1)S(1)} %copy-done.4, bf16[2,4,1024,64]{2,3,1,0:T(8,128)(2,1)} %bitcast.329), kind=kOutput, calls=%fused_computation.127 | convolution fusion | flops 549715968 | bytes 18890752 | tf_op jit(solution)/shard_map/hqk,hqd->hkd/dot_general | solution.py:98
  401.6 12.0 %multiply_reduce_fusion = (f32[4,1024]{1,0:T(4,128)S(1)}, f32[4,1024,1024]{1,2,0:T(8,128)}) fusion(f32[4,1024,1024]{1,2,0:T(8,128)} %get-tuple-element.146, f32[4,1024]{1,0:T(4,128)S(1)} %log_add_fusion, pred[1024,1024]{0,1:T(8,128)(4,1)S(1)} %copy-done.4, bf16[2,4,1024,64]{2,3,1,0:T(8,128)(2,1)} %bitcast.327, bf16[2,4,1024,64]{2,3,1,0:T(8,128)(2,1)} %bitcast.330), kind=kOutput, calls=%fused_computation.1 | convolution fusion | flops 553644032 | bytes 35684352 | tf_op jit(solution)/shard_map/hqd,hkd->hqk/dot_general | solution.py:99
  413.6 12.2 %multiply_convert_fusion = bf16[4,1024,1024]{1,2,0:T(8,128)(2,1)S(1)} fusion(f32[4,1024,1024]{1,2,0:T(8,128)} %get-tuple-element.157, f32[4,1024,1024]{1,2,0:T(8,128)} %get-tuple-element.146, f32[4,1024]{1,0:T(4,128)S(1)} %get-tuple-element.156, f32[4,1024]{1,0:T(4,128)S(1)} %log_add_fusion, pred[1024,1024]{0,1:T(8,128)(4,1)S(1)} %copy-done.4), kind=kLoop, calls=%fused_computation | loop fusion | flops 20971520 | bytes 43024384 | tf_op jit(solution)/shard_map/convert_element_type | solution.py:101
  432.1 10.5 %fusion.63 = bf16[1,4,1024,64]{2,3,1,0:T(8,128)(2,1)} fusion(f32[4,1024,1024]{1,2,0:T(8,128)} %get-tuple-element.148, f32[4,1024]{1,0:T(4,128)S(1)} %copy-done.33, pred[1024,1024]{0,1:T(8,128)(4,1)S(1)} %copy-done.2, bf16[2,4,1024,64]{2,3,1,0:T(8,128)(2,1)} %bitcast.331), kind=kOutput, calls=%fused_computation.128 | convolution fusion | flops 549715968 | bytes 18890752 | tf_op jit(solution)/shard_map/hqk,hqd->hkd/dot_general | solution.py:98
  442.6 12.0 %multiply_reduce_fusion.1 = (f32[4,1024]{1,0:T(4,128)S(1)}, f32[4,1024,1024]{1,2,0:T(8,128)}) fusion(f32[4,1024,1024]{1,2,0:T(8,128)} %get-tuple-element.148, f32[4,1024]{1,0:T(4,128)S(1)} %copy-done.33, pred[1024,1024]{0,1:T(8,128)(4,1)S(1)} %copy-done.2, bf16[2,4,1024,64]{2,3,1,0:T(8,128)(2,1)} %bitcast.328, bf16[2,4,1024,64]{2,3,1,0:T(8,128)(2,1)} %bitcast.332), kind=kOutput, calls=%fused_computation.4 | convolution fusion | flops 553644032 | bytes 35684352 | tf_op jit(solution)/shard_map/hqd,hkd->hqk/dot_general | solution.py:99
  454.6 12.3 %multiply_convert_fusion.1 = bf16[4,1024,1024]{1,2,0:T(8,128)(2,1)S(1)} fusion(f32[4,1024,1024]{1,2,0:T(8,128)} %get-tuple-element.159, f32[4,1024,1024]{1,2,0:T(8,128)} %get-tuple-element.148, f32[4,1024]{1,0:T(4,128)S(1)} %get-tuple-element.158, f32[4,1024]{1,0:T(4,128)S(1)} %copy-done.33, pred[1024,1024]{0,1:T(8,128)(4,1)S(1)} %copy-done.2), kind=kLoop, calls=%fused_computation.3 | loop fusion | flops 20971520 | bytes 43024384 | tf_op jit(solution)/shard_map/convert_element_type | solution.py:101
  475.6 5.1 bitcast_convert_fusion
  486.4 4.6 copy.115
  491.0 163.1 %shard_map.289 = (bf16[2,2,2,32,1024]{4,3,2,1,0:T(8,128)(2,1)}, bf16[2,2,2,128,1024]{4,3,2,1,0:T(8,128)(2,1)}, bf16[2,2,2,128,1024]{4,3,2,1,0:T(8,128)(2,1)}, bf...) custom-call(bf16[4,2,2,2,32,1024]{5,4,3,2,1,0:T(8,128)(2,1)} %bitcas, ...), custom_call_target="tpu_custom_call" | custom-call | tf_op jit(solution)/shard_map/pallas_call | solution.py:587
  (206 shorter events, 94.8 us)
Async XLA Ops:
  0.6 182.0 %copy-start = (bf16[3,1024,256]{2,1,0:T(8,128)(2,1)S(1)}, bf16[3,1024,256]{2,1,0:T(8,128)(2,1)}, u32[]{:S(2)}) copy-start(bf16[3,1024,256]{2,1,0:T(8,128)(2,1)} %param.19) | copy-start | bytes 4718596
  192.4 46.3 %copy-start.1 = (pred[1024,1024]{0,1:T(8,128)(4,1)}, pred[1024,1024]{0,1:T(8,128)(4,1)S(1)}, u32[]{:S(2)}) copy-start(pred[1024,1024]{0,1:T(8,128)(4,1)S(1)} %broadcast_compare_fusion.1) | copy-start | bytes 3145732
  212.3 26.4 %copy-start.34 = (f32[4,1024]{1,0:T(4,128)}, f32[4,1024]{1,0:T(4,128)S(1)}, u32[]{:S(2)}) copy-start(f32[4,1024]{1,0:T(4,128)S(1)} %get-tuple-element.147) | copy-start | bytes 49156
  221.3 8.6 %copy-start.36 = (f32[4,1024]{1,0:T(4,128)}, f32[4,1024]{1,0:T(4,128)S(1)}, u32[]{:S(2)}) copy-start(f32[4,1024]{1,0:T(4,128)S(1)} %fusion.1) | copy-start | bytes 49156
  238.7 8.2 %copy-start.38 = (f32[4,1024]{1,0:T(4,128)}, f32[4,1024]{1,0:T(4,128)S(1)}, u32[]{:S(2)}) copy-start(f32[4,1024]{1,0:T(4,128)S(1)} %fusion) | copy-start | bytes 49156
  246.9 8.2 %copy-start.32 = (bf16[2,256,288]{1,2,0:T(8,128)(2,1)S(1)}, bf16[2,256,288]{1,2,0:T(8,128)(2,1)}, u32[]{:S(2)}) copy-start(bf16[2,256,288]{1,2,0:T(8,128)(2,1)} %param.33) | copy-start | bytes 884740
  247.1 8.2 %copy-start.35 = (f32[4,1024]{1,0:T(4,128)S(1)}, f32[4,1024]{1,0:T(4,128)}, u32[]{:S(2)}) copy-start(f32[4,1024]{1,0:T(4,128)} %copy-done.34) | copy-start | bytes 49156
  249.1 32.4 %copy-start.49 = (f32[1024]{0:T(1024)S(1)}, f32[1024]{0:T(1024)}, u32[]{:S(2)}) copy-start(f32[1024]{0:T(1024)} %param.22) | copy-start | bytes 12292
  249.1 31.2 %all-to-all-start = ((bf16[2,1024,256]{2,0,1:T(2,128)(2,1)}), bf16[2,1024,256]{2,0,1:T(2,128)(2,1)S(1)}, u32[]{:S(2)}, u32[]{:S(2)}) async-start(bf16[2,1024,256]{2,0,1:T(2,128)(2,1)} %copy.98), calls=%async_computation | async-start | bytes 2097152 | tf_op jit(solution)/shard_map/all_to_all | solution.py:646
  283.6 63.5 %copy-start.17 = (f32[512,1024]{1,0:T(8,128)}, f32[512,1024]{1,0:T(8,128)S(1)}, u32[]{:S(2)}) copy-start(f32[512,1024]{1,0:T(8,128)S(1)} %get-tuple-element.150) | copy-start | bytes 6291460
  285.0 25.9 %copy-start.50 = (f32[1024]{0:T(1024)S(1)}, f32[1024]{0:T(1024)}, u32[]{:S(2)}) copy-start(f32[1024]{0:T(1024)} %param.28) | copy-start | bytes 12292
  310.9 9.0 %copy-start.52 = (bf16[4,512,1024]{2,1,0:T(8,128)(2,1)}, bf16[4,512,1024]{2,1,0:T(8,128)(2,1)S(1)}, u32[]{:S(2)}) copy-start(bf16[4,512,1024]{2,1,0:T(8,128)(2,1)S(1)} %get-tuple-element.116) | copy-start | bytes 12582916
  310.9 9.4 %copy-start.42 = (f32[1024]{0:T(1024)S(1)}, f32[1024]{0:T(1024)}, u32[]{:S(2)}) copy-start(f32[1024]{0:T(1024)} %param.29) | copy-start | bytes 12292
  310.9 9.4 %copy-start.46 = (bf16[2,256,1024]{2,1,0:T(8,128)(2,1)S(1)}, bf16[2,256,1024]{2,1,0:T(8,128)(2,1)}, u32[]{:S(2)}) copy-start(bf16[2,256,1024]{2,1,0:T(8,128)(2,1)} %param.32) | copy-start | bytes 3145732
  311.0 9.4 %copy-start.47 = (bf16[1024,288]{0,1:T(8,128)(2,1)S(1)}, bf16[1024,288]{0,1:T(8,128)(2,1)}, u32[]{:S(2)}) copy-start(bf16[1024,288]{0,1:T(8,128)(2,1)} %param.31) | copy-start | bytes 1769476
  322.7 15.0 %copy-start.26 = (f32[512,1024]{1,0:T(8,128)}, f32[512,1024]{1,0:T(8,128)S(1)}, u32[]{:S(2)}) copy-start(f32[512,1024]{1,0:T(8,128)S(1)} %get-tuple-element.113) | copy-start | bytes 6291460
  337.7 9.5 %copy-start.53 = (bf16[4,512,1024]{2,1,0:T(8,128)(2,1)}, bf16[4,512,1024]{2,1,0:T(8,128)(2,1)S(1)}, u32[]{:S(2)}) copy-start(bf16[4,512,1024]{2,1,0:T(8,128)(2,1)S(1)} %get-tuple-element.161) | copy-start | bytes 12582916
  356.4 29.5 %all-to-all-start.1 = ((bf16[2,256,1024]{1,0,2:T(2,128)(2,1)}), bf16[2,256,1024]{1,0,2:T(2,128)(2,1)}, u32[]{:S(2)}, u32[]{:S(2)}) async-start(bf16[2,256,1024]{1,0,2:T(2,128)(2,1)} %copy.104), calls=%async_computation.1 | async-start | bytes 2097152 | tf_op jit(solution)/shard_map/all_to_all | solution.py:682
  362.8 10.8 %copy-start.18 = (f32[512,1024]{1,0:T(8,128)S(1)}, f32[512,1024]{1,0:T(8,128)}, u32[]{:S(2)}) copy-start(f32[512,1024]{1,0:T(8,128)} %copy-done.17) | copy-start | bytes 6291460
  362.8 10.8 %copy-start.54 = (bf16[4,512,1024]{2,1,0:T(8,128)(2,1)S(1)}, bf16[4,512,1024]{2,1,0:T(8,128)(2,1)}, u32[]{:S(2)}) copy-start(bf16[4,512,1024]{2,1,0:T(8,128)(2,1)} %copy-done.53) | copy-start | bytes 12582916
  381.7 10.2 %copy-start.4 = (pred[1024,1024]{0,1:T(8,128)(4,1)S(1)}, pred[1024,1024]{0,1:T(8,128)(4,1)}, u32[]{:S(2)}) copy-start(pred[1024,1024]{0,1:T(8,128)(4,1)} %copy-done.3) | copy-start | bytes 3145732
  413.6 12.3 %copy-start.11 = (bf16[2,4,1024,64]{2,3,1,0:T(8,128)(2,1)S(1)}, bf16[2,4,1024,64]{2,3,1,0:T(8,128)(2,1)}, u32[]{:S(2)}) copy-start(bf16[2,4,1024,64]{2,3,1,0:T(8,128)(2,1)} %copy-done.10) | copy-start | bytes 3145732
  454.6 12.3 %copy-start.12 = (bf16[2,4,1024,64]{2,3,1,0:T(8,128)(2,1)S(1)}, bf16[2,4,1024,64]{2,3,1,0:T(8,128)(2,1)}, u32[]{:S(2)}) copy-start(bf16[2,4,1024,64]{2,3,1,0:T(8,128)(2,1)} %copy-done.10) | copy-start | bytes 3145732
  491.0 163.1 %copy-start.16 = (f32[512,1024]{1,0:T(8,128)S(1)}, f32[512,1024]{1,0:T(8,128)}, u32[]{:S(2)}) copy-start(f32[512,1024]{1,0:T(8,128)} %copy-done.15) | copy-start | bytes 6291460
  (35 other events, 120.3 us)

commit v3 on v2

--- a/solution.py
+++ b/solution.py
@@ -43,18 +43,6 @@
     return (jnp.cos(angles), jnp.sin(angles))
 
 
-def rotate(field, cosine, sine):
-    half_dim = field.shape[-1] // 2
-    rotated = jnp.concatenate([-field[..., half_dim:], field[..., :half_dim]], axis=-1)
-    return field * cosine + rotated * sine
-
-
-def rotate_back(field, cosine, sine):
-    half_dim = field.shape[-1] // 2
-    rotated = jnp.concatenate([-field[..., half_dim:], field[..., :half_dim]], axis=-1)
-    return field * cosine - rotated * sine
-
-
 def norm_forward(field, gain, shift):
     row_mean = jnp.mean(field, axis=-1, keepdims=True)
     centred = field - row_mean
@@ -74,34 +62,247 @@
     return (grad_input, jnp.sum(upstream * scaled, axis=0), jnp.sum(upstream, axis=0))
 
 
-def masked_scores(queries, keys, seg_row):
-    scores = jnp.einsum("hqd,hkd->hqk", queries, keys, preferred_element_type=f32)
-    same_doc = seg_row[:, None] == seg_row[None, :]
-    return jnp.where(same_doc[None], scores, -1000000000.0)
-
-
-def attend(inputs):
-    queries, keys, values_low, seg_row = inputs
-    scores = masked_scores(queries, keys, seg_row)
-    row_peak = jnp.max(scores, axis=-1, keepdims=True)
-    shifted = jnp.exp(scores - row_peak)
-    row_total = jnp.sum(shifted, axis=-1, keepdims=True)
-    probs = (shifted / row_total).astype(bf16)
-    mixed_heads = jnp.einsum("hqk,hkd->hqd", probs, values_low, preferred_element_type=f32)
-    return (mixed_heads, row_peak + jnp.log(row_total))
-
-
-def attend_back(inputs):
-    queries, keys, values_low, seg_row, log_total, grad_mixed = inputs
-    scores = masked_scores(queries, keys, seg_row)
-    probs = jnp.exp(scores - log_total)
-    grad_values = jnp.einsum("hqk,hqd->hkd", probs.astype(bf16), grad_mixed, preferred_element_type=f32)
-    grad_probs = jnp.einsum("hqd,hkd->hqk", grad_mixed, values_low, preferred_element_type=f32)
-    row_inner = jnp.sum(probs * grad_probs, axis=-1, keepdims=True)
-    grad_scores = (probs * (grad_probs - row_inner)).astype(bf16)
-    grad_queries = jnp.einsum("hqk,hkd->hqd", grad_scores, keys, preferred_element_type=f32)
-    grad_keys = jnp.einsum("hqk,hqd->hkd", grad_scores, queries, preferred_element_type=f32)
-    return (grad_queries, grad_keys, grad_values)
+BLOCK = 256
+
+
+def turn_halves(field, sign_sine):
+    lane = lax.broadcasted_iota(jnp.int32, field.shape, 1)
+    half = HEAD_DIM // 2
+    width = field.shape[1]
+    swapped = jnp.where(lane % HEAD_DIM < half, pltpu.roll(field, width - half, 1), pltpu.roll(field, half, 1))
+    return swapped * sign_sine
+
+
+def scores_of(keys, queries):
+    return lax.dot_general(keys, queries, (((1,), (1,)), ((), ())), preferred_element_type=f32)
+
+
+def attend_kernel(group, lo_ref, hi_ref, tok_ref, w_ref, b_ref, cos_ref, sin_ref, seg_ref, mixed_ref, q_ref, k_ref, v_ref,
+                  lse_ref, vt_ref, m_ref, l_ref, acc_ref):
+    zsize, _, rows, _ = tok_ref.shape
+    length = zsize * rows
+    heads = q_ref.shape[1]
+    pair = 2 * HEAD_DIM
+    scale = HEAD_DIM ** (-0.5)
+
+    def project(i, carry):
+        at = pl.ds(pl.multiple_of(i * rows, rows), rows)
+        x = tok_ref[i, 0]
+        lane = lax.broadcasted_iota(jnp.int32, (rows, pair), 1)
+        doc = seg_ref[0, at, :]
+        same = lane - HEAD_DIM == doc
+        low = lane < HEAD_DIM
+        feature = lane < HEAD_DIM + 4
+        extra_q = jnp.where(same, 1.0, 0.0)
+        extra_k = jnp.where(jnp.logical_and(feature, jnp.logical_not(same)), -1e9, 0.0)
+        cosine = cos_ref[0, at, :]
+        sine = sin_ref[0, at, :]
+        for c in range(3):
+            field = jnp.dot(x, w_ref[c], preferred_element_type=f32) + b_ref[c:c + 1, :]
+            for j in range(heads // 2):
+                part = field[:, j * pair:(j + 1) * pair]
+                if c < 2:
+                    part = part * cosine + turn_halves(part, sine)
+                if c == 0:
+                    part = part * scale
+                for h in range(2):
+                    one = part if h == 0 else pltpu.roll(part, HEAD_DIM, 1)
+                    head = 2 * j + h
+                    if c == 0:
+                        q_ref[0, head, at, :] = jnp.where(low, one, extra_q).astype(bf16)
+                    elif c == 1:
+                        k_ref[0, head, at, :] = jnp.where(low, one, extra_k).astype(bf16)
+                    else:
+                        one = jnp.where(low, one, 0.0)
+                        v_ref[0, head, at, :] = one.astype(bf16)
+                        vt_ref[head, :, at] = one.T[:HEAD_DIM].astype(bf16)
+        return carry
+
+    lax.fori_loop(0, zsize, project, 0)
+
+    def query_block(i, carry):
+        at = pl.ds(pl.multiple_of(i * BLOCK, BLOCK), BLOCK)
+        m_ref[...] = jnp.full(m_ref.shape, -1e30, f32)
+        l_ref[...] = jnp.zeros(l_ref.shape, f32)
+        acc_ref[...] = jnp.zeros(acc_ref.shape, f32)
+
+        def key_block(j, carry):
+            keys_at = pl.ds(pl.multiple_of(j * BLOCK, BLOCK), BLOCK)
+            for h in range(heads):
+                st = scores_of(k_ref[0, h, keys_at, :], q_ref[0, h, at, :])
+                peak = m_ref[h:h + 1, :]
+                new = jnp.maximum(peak, jnp.max(st, axis=0, keepdims=True))
+                p = jnp.exp(st - new)
+                old = jnp.exp(peak - new)
+                m_ref[h:h + 1, :] = new
+                l_ref[h:h + 1, :] = l_ref[h:h + 1, :] * old + jnp.sum(p, axis=0, keepdims=True)
+                acc_ref[h] = acc_ref[h] * old + jnp.dot(
+                    vt_ref[h, :, keys_at], p.astype(bf16), preferred_element_type=f32
+                )
+            return carry
+
+        lax.fori_loop(lo_ref[group, i], hi_ref[group, i], key_block, 0)
+        out = [acc_ref[h] / l_ref[h:h + 1, :] for h in range(heads)]
+        for j in range(heads // 2):
+            both = jnp.concatenate([out[2 * j], out[2 * j + 1]], axis=0)
+            mixed_ref[0, at, j * pair:(j + 1) * pair] = both.T.astype(bf16)
+        lse_ref[0, :, at] = m_ref[...] + jnp.log(l_ref[...])
+        return carry
+
+    lax.fori_loop(0, length // BLOCK, query_block, 0)
+
+
+def attend_forward(group, bounds, tokens, weight, bias, cosine, sine, docs):
+    zsize, _, rows, width = tokens.shape
+    length = zsize * rows
+    cols = weight.shape[2]
+    heads = cols // HEAD_DIM
+    pair = 2 * HEAD_DIM
+    whole = lambda shape: pl.BlockSpec(shape, lambda i, *_: (0,) * len(shape))
+    of_group = lambda shape: pl.BlockSpec(shape, lambda i, *_: (group,) + (0,) * (len(shape) - 1))
+    like = jax.ShapeDtypeStruct
+    return pl.pallas_call(
+        functools.partial(attend_kernel, group),
+        grid_spec=pltpu.PrefetchScalarGridSpec(
+            num_scalar_prefetch=2,
+            grid=(1,),
+            in_specs=[
+                pl.BlockSpec((zsize, 1, rows, width), lambda i, *_: (0, group, 0, 0)),
+                whole(weight.shape), whole(bias.shape),
+                of_group((1, length, pair)), of_group((1, length, pair)), of_group((1, length, 1)),
+            ],
+            out_specs=[
+                whole((1, length, cols)),
+                whole((1, heads, length, pair)), whole((1, heads, length, pair)), whole((1, heads, length, pair)),
+                whole((1, heads, length)),
+            ],
+            scratch_shapes=[
+                pltpu.VMEM((heads, HEAD_DIM, length), bf16),
+                pltpu.VMEM((heads, BLOCK), f32), pltpu.VMEM((heads, BLOCK), f32),
+                pltpu.VMEM((heads, HEAD_DIM, BLOCK), f32),
+            ],
+        ),
+        out_shape=[
+            like((1, length, cols), bf16),
+            like((1, heads, length, pair), bf16), like((1, heads, length, pair), bf16),
+            like((1, heads, length, pair), bf16), like((1, heads, length), f32),
+        ],
+        compiler_params=pltpu.CompilerParams(vmem_limit_bytes=48 * 1024 * 1024),
+        cost_estimate=pl.CostEstimate(
+            flops=2 * length * width * 3 * cols + 4 * length * length * cols,
+            bytes_accessed=2 * length * width + 6 * width * cols + 8 * length * cols,
+            transcendentals=length * length * heads,
+        ),
+    )(*bounds, tokens, weight, bias, cosine, sine, docs)
+
+
+def attend_back_kernel(group, lo_ref, hi_ref, q_ref, k_ref, v_ref, lse_ref, mixed_ref, do_ref, cos_ref, sin_ref,
+                       grad_ref, sum_ref, dox_ref, kt_ref, delta_ref, dk_ref, dv_ref, dqt_ref):
+    heads, length = q_ref.shape[1], q_ref.shape[2]
+    pair = 2 * HEAD_DIM
+    scale = HEAD_DIM ** (-0.5)
+    blocks = length // BLOCK
+
+    def prepare(i, carry):
+        at = pl.ds(pl.multiple_of(i * BLOCK, BLOCK), BLOCK)
+        low = lax.broadcasted_iota(jnp.int32, (BLOCK, pair), 1) < HEAD_DIM
+        for j in range(heads // 2):
+            upstream = do_ref[0, at, j * pair:(j + 1) * pair].astype(f32)
+            product = (upstream * mixed_ref[0, at, j * pair:(j + 1) * pair].astype(f32)).T
+            for h in range(2):
+                head = 2 * j + h
+                one = upstream if h == 0 else pltpu.roll(upstream, HEAD_DIM, 1)
+                dox_ref[head, at, :] = jnp.where(low, one, 0.0).astype(bf16)
+                delta_ref[head:head + 1, at] = jnp.sum(
+                    product[h * HEAD_DIM:(h + 1) * HEAD_DIM], axis=0, keepdims=True
+                )
+                kt_ref[head, :, at] = k_ref[0, head, at, :].astype(f32).T[:HEAD_DIM].astype(bf16)
+                dk_ref[head, at, :] = jnp.zeros((BLOCK, pair), f32)
+                dv_ref[head, at, :] = jnp.zeros((BLOCK, pair), f32)
+        return carry
+
+    lax.fori_loop(0, blocks, prepare, 0)
+    sum_ref[...] = jnp.zeros(sum_ref.shape, f32)
+
+    def put(c, j, at, field):
+        low = field.astype(bf16)
+        grad_ref[c, 0, at, j * pair:(j + 1) * pair] = low
+        cols = pl.ds(j * pair, pair)
+        sum_ref[c:c + 1, cols] = sum_ref[c:c + 1, cols] + jnp.sum(low.astype(f32), axis=0, keepdims=True)
+
+    def back(field, at):
+        return field * cos_ref[0, at, :] - turn_halves(field, sin_ref[0, at, :])
+
+    def query_block(i, carry):
+        at = pl.ds(pl.multiple_of(i * BLOCK, BLOCK), BLOCK)
+        dqt_ref[...] = jnp.zeros(dqt_ref.shape, f32)
+
+        def key_block(j, carry):
+            keys_at = pl.ds(pl.multiple_of(j * BLOCK, BLOCK), BLOCK)
+            for h in range(heads):
+                queries = q_ref[0, h, at, :]
+                upstream = dox_ref[h, at, :]
+                st = scores_of(k_ref[0, h, keys_at, :], queries)
+                p = jnp.exp(st - lse_ref[0, h:h + 1, at])
+                dp = scores_of(v_ref[0, h, keys_at, :], upstream)
+                ds = (p * (dp - delta_ref[h:h + 1, at])).astype(bf16)
+                dv_ref[h, keys_at, :] = dv_ref[h, keys_at, :] + jnp.dot(
+                    p.astype(bf16), upstream, preferred_element_type=f32
+                )
+                dk_ref[h, keys_at, :] = dk_ref[h, keys_at, :] + jnp.dot(ds, queries, preferred_element_type=f32)
+                dqt_ref[h] = dqt_ref[h] + jnp.dot(kt_ref[h, :, keys_at], ds, preferred_element_type=f32)
+            return carry
+
+        lax.fori_loop(lo_ref[group, i], hi_ref[group, i], key_block, 0)
+        for j in range(heads // 2):
+            both = jnp.concatenate([dqt_ref[2 * j], dqt_ref[2 * j + 1]], axis=0)
+            put(0, j, at, back(both.T * scale, at))
+        return carry
+
+    lax.fori_loop(0, blocks, query_block, 0)
+
+    def finish(i, carry):
+        at = pl.ds(pl.multiple_of(i * BLOCK, BLOCK), BLOCK)
+        low = lax.broadcasted_iota(jnp.int32, (BLOCK, pair), 1) < HEAD_DIM
+        for j in range(heads // 2):
+            field = jnp.where(low, dk_ref[2 * j, at, :], pltpu.roll(dk_ref[2 * j + 1, at, :], HEAD_DIM, 1))
+            put(1, j, at, back(field, at))
+            field = jnp.where(low, dv_ref[2 * j, at, :], pltpu.roll(dv_ref[2 * j + 1, at, :], HEAD_DIM, 1))
+            put(2, j, at, field)
+        return carry
+
+    lax.fori_loop(0, blocks, finish, 0)
+
+
+def attend_backward(group, bounds, kept, mixed, upstream, cosine, sine):
+    queries, keys, values, lse = kept
+    _, heads, length, pair = queries.shape
+    cols = heads * HEAD_DIM
+    whole = lambda shape: pl.BlockSpec(shape, lambda i, *_: (0,) * len(shape))
+    of_group = lambda shape: pl.BlockSpec(shape, lambda i, *_: (group,) + (0,) * (len(shape) - 1))
+    like = jax.ShapeDtypeStruct
+    wide = (heads, length, pair)
+    return pl.pallas_call(
+        functools.partial(attend_back_kernel, group),
+        grid_spec=pltpu.PrefetchScalarGridSpec(
+            num_scalar_prefetch=2,
+            grid=(1,),
+            in_specs=[
+                whole(queries.shape), whole(keys.shape), whole(values.shape), whole(lse.shape), whole(mixed.shape),
+                of_group((1, length, cols)), of_group((1, length, pair)), of_group((1, length, pair)),
+            ],
+            out_specs=[whole((3, 1, length, cols)), whole((8, cols))],
+            scratch_shapes=[
+                pltpu.VMEM(wide, bf16), pltpu.VMEM((heads, HEAD_DIM, length), bf16), pltpu.VMEM((heads, length), f32),
+                pltpu.VMEM(wide, f32), pltpu.VMEM(wide, f32), pltpu.VMEM((heads, HEAD_DIM, BLOCK), f32),
+            ],
+        ),
+        out_shape=[like((3, 1, length, cols), bf16), like((8, cols), f32)],
+        compiler_params=pltpu.CompilerParams(vmem_limit_bytes=48 * 1024 * 1024),
+        cost_estimate=pl.CostEstimate(
+            flops=10 * length * length * cols, bytes_accessed=24 * length * cols, transcendentals=length * length * heads
+        ),
+    )(*bounds, queries, keys, values, lse, mixed, upstream, cosine, sine)
 
 
 MESH_ID = pl.DeviceIdType.MESH
@@ -136,6 +337,79 @@
     )
 
 
+def swap_kernel(zsize, to_rows, *refs):
+    sources, target = refs[:-4], refs[-4]
+    held, local_sem, send, recv = refs[-3], refs[-2], refs[-1].at[0], refs[-1].at[1]
+    groups = target.shape[0]
+    rows, cols = (target.shape[1], target.shape[2] // zsize) if to_rows else (target.shape[1] // zsize, target.shape[2])
+    z = lax.axis_index("z")
+
+    def source(g, peer):
+        if to_rows:
+            return sources[g].at[0, pl.ds(pl.multiple_of(peer * rows, rows), rows), :]
+        return sources[0].at[g, :, pl.ds(pl.multiple_of(peer * cols, cols), cols)]
+
+    def place(g, peer):
+        if to_rows:
+            return target.at[g, :, pl.ds(pl.multiple_of(peer * cols, cols), cols)]
+        return target.at[g, pl.ds(pl.multiple_of(peer * rows, rows), rows), :]
+
+    def copy_to(g, step):
+        peer = lax.rem(z + step, zsize)
+        return remote(source(g, peer), place(g, z), send.at[step, g], recv.at[step, g], {"z": peer})
+
+    def copy_from(g, step):
+        peer = lax.rem(z + zsize - step, zsize)
+        return remote(source(g, peer), place(g, peer), send.at[step, g], recv.at[step, g], {"z": peer})
+
+    into = [pltpu.make_async_copy(source(g, z), held.at[g], local_sem.at[0, g]) for g in range(groups)]
+    onward = [pltpu.make_async_copy(held.at[g], place(g, z), local_sem.at[1, g]) for g in range(groups)]
+    for copy in into:
+        copy.start()
+    barrier = pltpu.get_barrier_semaphore()
+    for step in range(1, zsize):
+        peer = lax.rem(z + step, zsize)
+        pl.semaphore_signal(barrier, inc=1, device_id={"z": peer}, device_id_type=MESH_ID)
+    pl.semaphore_wait(barrier, zsize - 1)
+    for g in range(groups):
+        for step in range(1, zsize):
+            copy_to(g, step).start()
+    for g in range(groups):
+        into[g].wait()
+        onward[g].start()
+    for g in range(groups):
+        for step in range(1, zsize):
+            copy_from(g, step).wait_recv()
+        onward[g].wait()
+    for g in range(groups):
+        for step in range(1, zsize):
+            copy_to(g, step).wait_send()
+
+
+def swap(sources, zsize, to_rows):
+    if to_rows:
+        groups, rows, cols = len(sources), sources[0].shape[1] // zsize, sources[0].shape[2]
+        shape = (groups, rows, zsize * cols)
+    else:
+        groups, rows, cols = sources[0].shape
+        cols //= zsize
+        shape = (groups, zsize * rows, cols)
+    return pl.pallas_call(
+        functools.partial(swap_kernel, zsize, to_rows),
+        out_shape=jax.ShapeDtypeStruct(shape, bf16),
+        in_specs=[HBM] * len(sources),
+        out_specs=HBM,
+        scratch_shapes=[
+            pltpu.VMEM((groups, rows, cols), bf16),
+            pltpu.SemaphoreType.DMA((2, groups)),
+            pltpu.SemaphoreType.DMA((2, zsize, groups)),
+        ],
+        compiler_params=pltpu.CompilerParams(
+            collective_id=2 if to_rows else 3, has_side_effects=True, vmem_limit_bytes=8 * 1024 * 1024
+        ),
+    )(*sources)
+
+
 ORDERS = {"xy": ("x", "y"), "yx": ("y", "x")}
 
 
@@ -143,17 +417,17 @@
     n = len(orders)
     tok, bias, shards = refs[0], refs[1], refs[2:2 + n]
     tok_all, bias_all, wholes = refs[2 + n], refs[3 + n], refs[4 + n:4 + 2 * n]
-    local_sem, z_send, z_recv, p_send, p_recv = refs[4 + 2 * n:]
+    held = refs[4 + 2 * n:6 + 3 * n]
+    local_sem, z_send, z_recv, p_send, p_recv = refs[6 + 3 * n:]
     z = lax.axis_index("z")
     c = lax.axis_index("core")
     place = [(lax.axis_index(o[0]), lax.axis_index(o[1])) for o in orders]
 
-    local = []
-    for k in range(n):
-        local.append(pltpu.make_async_copy(shards[k], wholes[k].at[z], local_sem.at[k]))
-    local.append(pltpu.make_async_copy(tok, tok_all.at[z], local_sem.at[n]))
-    local.append(pltpu.make_async_copy(bias, bias_all.at[z], local_sem.at[n + 1]))
-    for copy in local:
+    sources = list(shards) + [tok, bias]
+    targets = list(wholes) + [tok_all, bias_all]
+    into = [pltpu.make_async_copy(sources[i], held[i], local_sem.at[0, i]) for i in range(n + 2)]
+    local = [pltpu.make_async_copy(held[i], targets[i].at[z], local_sem.at[1, i]) for i in range(n + 2)]
+    for copy in into:
         copy.start()
     greet(zsize)
 
@@ -222,6 +496,9 @@
                     if item < n:
                         exchange(item, src, 0, side * (zsize - 1) + step).start()
 
+    for copy, onward in zip(into, local):
+        copy.wait()
+        onward.start()
     for step in range(zsize - 1):
         arrive(range(n), step)
         if step == zsize - 2:
@@ -277,14 +554,16 @@
         out_shape=[stack(tokens), stack(bias)] + [stack(w) for w in shards],
         in_specs=[HBM] * (n + 2),
         out_specs=[HBM] * (n + 2),
-        scratch_shapes=[
-            pltpu.SemaphoreType.DMA((n + 2,)),
+        scratch_shapes=[pltpu.VMEM(a.shape, a.dtype) for a in shards + [tokens, bias]] + [
+            pltpu.SemaphoreType.DMA((2, n + 2)),
             pltpu.SemaphoreType.DMA((2, n + 2, zsize - 1)),
             pltpu.SemaphoreType.DMA((2, n + 2, zsize - 1)),
             pltpu.SemaphoreType.DMA((2 * (zsize - 1), n, 3)),
             pltpu.SemaphoreType.DMA((2 * (zsize - 1), n, 3)),
         ],
-        compiler_params=pltpu.CompilerParams(collective_id=0, has_side_effects=True),
+        compiler_params=pltpu.CompilerParams(
+            collective_id=0, has_side_effects=True, vmem_limit_bytes=32 * 1024 * 1024
+        ),
     )(tokens, bias, *shards)
 
 
@@ -601,21 +880,22 @@
     groups, local_rows, model_width = tokens.shape
     length = segments.shape[1]
     zsize = length // local_rows
-    heads_here = qkv_weight.shape[2] // HEAD_DIM
     head_cols = qkv_weight.shape[2]
     units_here = up_weight.shape[1]
     rows = groups * local_rows
     zi = lax.axis_index("z")
-    q_scale = HEAD_DIM ** (-0.5)
     cosine, sine = rotary_tables(doc_positions(segments), HEAD_DIM)
-    cosine = cosine[:, None]
-    sine = sine[:, None]
-
-    def split_heads(field):
-        return field.reshape(groups, length, heads_here, HEAD_DIM).transpose(0, 2, 1, 3)
-
-    def join_heads(field):
-        return field.transpose(0, 2, 1, 3).reshape(groups, length, head_cols)
+    half = HEAD_DIM // 2
+    signs = jnp.where(jnp.arange(2 * HEAD_DIM) % HEAD_DIM < half, -1.0, 1.0)
+    cosine = jnp.concatenate([cosine, cosine], axis=-1)
+    sine = jnp.concatenate([sine, sine], axis=-1) * signs
+    firsts = segments[:, ::BLOCK]
+    lasts = segments[:, BLOCK - 1::BLOCK]
+    bounds = (
+        jnp.sum(segments[:, None, :] < firsts[:, :, None], axis=2, dtype=jnp.int32) // BLOCK,
+        (jnp.sum(segments[:, None, :] <= lasts[:, :, None], axis=2, dtype=jnp.int32) + BLOCK - 1) // BLOCK,
+    )
+    docs = segments[:, :, None]
 
     def cut(array, rows_at):
         shape = array.shape
@@ -628,22 +908,16 @@
         [("xy", cut(out_weight, 0)), ("xy", cut(up_weight, 0)), ("yx", cut(down_weight, 0))],
         zsize,
     )
-    whole_tokens = token_blocks.reshape(zsize, groups, local_rows, model_width).transpose(1, 0, 2, 3)
-    whole_tokens = whole_tokens.reshape(groups, length, model_width)
+    token_blocks = token_blocks.reshape(zsize, groups, local_rows, model_width)
     out_all = out_all.reshape(model_width, model_width)
     up_all = up_all.reshape(zsize, model_width, units_here)
     down_all = down_all.reshape(zsize, units_here, model_width)
     full_up_bias = bias_blocks.reshape(zsize, units_here)
 
-    projected = jnp.einsum("gld,cde->cgle", whole_tokens, qkv_weight, preferred_element_type=f32)
-    projected = projected + qkv_bias[:, None, None, :]
-    queries = (rotate(split_heads(projected[0]), cosine, sine) * q_scale).astype(bf16)
-    keys = rotate(split_heads(projected[1]), cosine, sine).astype(bf16)
-    values_low = split_heads(projected[2]).astype(bf16)
-    got = [attend((queries[g], keys[g], values_low[g], segments[g])) for g in range(groups)]
-    log_total = [g[1] for g in got]
-    mixed = join_heads(jnp.stack([g[0] for g in got])).astype(bf16)
-    mixed = lax.all_to_all(mixed, "z", split_axis=1, concat_axis=2, tiled=True).reshape(rows, model_width)
+    heads = [
+        attend_forward(g, bounds, token_blocks, qkv_weight, qkv_bias, cosine, sine, docs) for g in range(groups)
+    ]
+    mixed = swap([h[0] for h in heads], zsize, True).reshape(rows, model_width)
 
     first_sum = tokens.reshape(rows, model_width).astype(f32) + (
         jnp.dot(mixed, out_all, preferred_element_type=f32) + out_bias
@@ -679,22 +953,15 @@
     out_grad_w = jnp.einsum("nh,nd->hd", mixed, first_low, preferred_element_type=f32).astype(bf16)
     grad_mixed = jnp.einsum("nd,hd->nh", first_low, out_all, preferred_element_type=f32).astype(bf16)
     grad_mixed = grad_mixed.reshape(groups, local_rows, model_width)
-    grad_mixed = lax.all_to_all(grad_mixed, "z", split_axis=2, concat_axis=1, tiled=True)
-    grad_mixed = split_heads(grad_mixed)
+    upstream = swap([grad_mixed], zsize, False)
     back = [
-        attend_back((queries[g], keys[g], values_low[g], segments[g], log_total[g], grad_mixed[g]))
-        for g in range(groups)
+        attend_backward(g, bounds, heads[g][1:], heads[g][0], upstream, cosine, sine) for g in range(groups)
     ]
-    grad_queries = rotate_back(jnp.stack([b[0] for b in back]) * q_scale, cosine, sine)
-    grad_keys = rotate_back(jnp.stack([b[1] for b in back]), cosine, sine)
-    grad_values = jnp.stack([b[2] for b in back])
-    grad_qkv = jnp.stack(
-        [join_heads(grad_queries), join_heads(grad_keys), join_heads(grad_values)]
-    ).astype(bf16)
-    qkv_bias_grad = jnp.sum(grad_qkv.astype(f32), axis=(1, 2))
-    qkv_weight_grad = jnp.einsum("gld,cgle->cde", whole_tokens, grad_qkv, preferred_element_type=f32)
-    input_back = jnp.einsum("cgle,cde->gld", grad_qkv, qkv_weight, preferred_element_type=f32).astype(bf16)
-    back = input_back.reshape(groups, zsize, local_rows, model_width).transpose(1, 0, 2, 3)
+    grad_qkv = jnp.concatenate([b[0] for b in back], axis=1)
+    qkv_bias_grad = sum(b[1] for b in back)[:3]
+    by_z = grad_qkv.reshape(3, groups, zsize, local_rows, head_cols)
+    qkv_weight_grad = jnp.einsum("zgld,cgzle->cde", token_blocks, by_z, preferred_element_type=f32)
+    input_back = jnp.einsum("cgzle,cde->zgld", by_z, qkv_weight, preferred_element_type=f32).astype(bf16)
     small = jnp.concatenate(
         [
             out_bias_grad, gain_one_grad, shift_one_grad, down_bias_grad, gain_two_grad, shift_two_grad,
@@ -714,7 +981,7 @@
         ],
         ("yx", cut(qkv_weight_grad.astype(bf16), 1)),
         ("xy", cut(proj_grad[None], 1)),
-        back.reshape(zsize, rows, model_width),
+        input_back.reshape(zsize, rows, model_width),
         small.reshape(8, -1),
         zsize,
     )

time: 678 us -> 556 us (0.82)
  matrix products: 183 us -> 89.6 us
  Pallas kernels: 341 us -> 400 us
  other arithmetic: 70.9 us -> 29.1 us
  waiting for transfers between devices: 28.7 us -> 0 us
  starting transfers between devices: 10.2 us -> 0 us
    pallas_call x0 -> x6, Pallas kernels: none -> 122 us  [the longest x2 47.2 us: swap(): pl.pallas_call(functools.partial(swap_kernel, zsize, to_rows), out_shape=...]
    dot_general x15 -> x2, matrix products: 98 us -> 8.57 us  [the longest x1 4.53 us: per_device(): jnp.einsum('zgld,cgzle->cde', token_blocks, by_z, preferred_element_type=...]
    pallas_call x1, Pallas kernels: 178 us -> 110 us  [gather_start(): pl.pallas_call(functools.partial(gather_kernel, zsize, orders), out_shape...]
    all_to_all x2 -> x0, waiting for transfers between devices: 28.7 us -> none  [the longest x1 24.5 us: per_device(): lax.all_to_all(mixed, 'z', split_axis=1, concat_axis=2, tiled=True)]
    convert_element_type x3 -> x0, other arithmetic: 25.8 us -> none  [the longest x2 24.5 us: attend_back(): grad_scores = (probs * (grad_probs - row_inner)).astype(bf16)]
    reduce_sum x3 -> x1, other arithmetic: 18.3 us -> 0.23 us  [per_device(): jnp.sum(segments[:, None, :] <= lasts[:, :, None], axis=2, dtype=jnp.int32)]
    unnamed x127 -> x128, local copies, waits for them, and re-layouts: 6.51 us -> 18.9 us
    reshape x3 -> x0, local copies, waits for them, and re-layouts: 11.2 us -> none  [the longest x1 4.64 us: per_device(): input_back.reshape(groups, zsize, local_rows, model_width)]
  transfers between devices with their start and end apart: 2 -> 0, of which waited for: 2 -> 0; matrix products, arithmetic and copies ran while one was open for 3% -> 0% of each run, Pallas kernels for 0% -> 0%
where the time goes in v3:
time: 556 us; the launch traced here: 550 us
  Pallas kernels  400 us (72%)
  matrix products  89.6 us (16%)
  local copies, waits for them, and re-layouts  29.6 us (5%)
  other arithmetic  29.1 us (5%)
    pallas_call x1, Pallas kernels, reduce_end(): pl.pallas_call(functools.partial(reduce_kernel, zsize, orders), out_shape...  168 us
    pallas_call x1, Pallas kernels, gather_start(): pl.pallas_call(functools.partial(gather_kernel, zsize, orders), out_shape...  110 us
    pallas_call x2, Pallas kernels, swap(): pl.pallas_call(functools.partial(swap_kernel, zsize, to_rows), out_shape=...  47.2 us
    pallas_call x2, Pallas kernels, attend_forward(): pl.pallas_call(functools.partial(attend_kernel, group), grid_spec=pltpu.P...  39 us
    pallas_call x2, Pallas kernels, attend_backward(): pl.pallas_call(functools.partial(attend_back_kernel, group), grid_spec=pl...  36.1 us
    dot_general x1, matrix products, per_device(): jnp.einsum('nd,zdf->znf', normed_low, up_all, preferred_element_type=f32)  26 us
    unnamed x128, local copies, waits for them, and re-layouts  18.9 us
    dot_general x1, matrix products, per_device(): jnp.einsum('nd,zfd->znf', second_low, down_all, preferred_element_type=f32)  14 us

profile of v3, /device:TPU:1, one launch (start us, length us, event | category | flops | bytes accessed | tf_op | source)
XLA Modules:
  0.0 550.2 jit_solution(4706725751802949211)
XLA Ops:
  3.1 4.0 fusion.37
  8.8 110.0 %shard_map.288 = (bf16[4,512,1024]{2,1,0:T(8,128)(2,1)S(1)}, f32[4,8,128]{2,1,0:T(8,128)S(1)}, bf16[4,2,2,2,32,1024]{5,4,3,2,1,0:T(8,128)(2,1)S(1)}, bf16[4,2,2,...) custom-call(bf16[512,1024]{1,0:T(8,128)(2,1)S(1)} %bitcast.219, f32[8,128]{1,0:T(8,128)S(1)} %bitcast.226, ...), custom_call_target="tpu_custom_call" | custom-call | tf_op jit(solution)/shard_map/pallas_call | solution.py:552
  118.8 3.2 copy-done.9
  128.4 19.4 %shard_map.290 = (bf16[1,1024,256]{2,1,0:T(8,128)(2,1)S(1)}, bf16[1,4,1024,128]{3,2,1,0:T(8,128)(2,1)S(1)}, bf16[1,4,1024,128]{3,2,1,0:T(8,128)(2,1)S(1)}, bf16[...) custom-call(s32[2,4]{1,0:T(2,128)S(1)} %get-tuple-element.152.lo_ref, s32[2,4]{1,0:T(2,128)S(1)} %get-tuple-element.151.hi_ref, ...), custom_call_target="tpu_custom_call" | custom-call | flops 2684354560 | bytes 5767168 | tf_op jit(solution)/shard_map/pallas_call | solution.py:164
  150.9 19.6 %shard_map.289 = (bf16[1,1024,256]{2,1,0:T(8,128)(2,1)S(1)}, bf16[1,4,1024,128]{3,2,1,0:T(8,128)(2,1)S(1)}, bf16[1,4,1024,128]{3,2,1,0:T(8,128)(2,1)S(1)}, bf16[...) custom-call(s32[2,4]{1,0:T(2,128)S(1)} %get-tuple-element.152.lo_ref, s32[2,4]{1,0:T(2,128)S(1)} %get-tuple-element.151.hi_ref, ...), custom_call_target="tpu_custom_call" | custom-call | flops 2684354560 | bytes 5767168 | tf_op jit(solution)/shard_map/pallas_call | solution.py:164
  173.4 22.8 %shard_map.291 = bf16[2,256,1024]{2,1,0:T(8,128)(2,1)S(1)} custom-call(bf16[1,1024,256]{2,1,0:T(8,128)(2,1)S(1)} %get-tuple-element.43.refs_0_.mixed_ref, bf16[1,1024,256]{2,1,0:T(8,128)(2,1)S(1)} %get-tuple-element.44.refs_1_.mixed_ref), custom_call_target="tpu_custom_call" | custom-call | tf_op jit(solution)/shard_map/pallas_call | solution.py:397
  198.1 26.0 %fusion.9 = (bf16[4,512,1024]{2,1,0:T(8,128)(2,1)S(1)}, f32[4,512,1024]{2,1,0:T(8,128)}, f32[4,1024,512]{1,2,0:T(8,128)}) fusion(f32[4,1024]{1,0:T(4,128)S(1)} %bitcast.255, bf16[4,1024,1024]{2,1,0:T(8,128)(2,1)S(1)} %bitcast.229, f32[512,1024]{1,0:T(8,128)S(1)} %get-tuple-element.143, f32[1024]{0:T(1024)S(1)} %copy-done.50, f32[1024]{0:T(1024)S(1)} %copy-done.45, ...), kind=kOutput, calls=%fused_computation.18 | convolution fusion | flops 4436000768 | bytes 31485952 | tf_op jit(solution)/shard_map/nd,zdf->znf/dot_general | solution.py:927
  224.3 4.8 fusion.52
  231.4 2.5 convert_reduce_fusion.1
  233.9 14.0 %convert_reduce_fusion = (f32[4,1024]{1,0:T(4,128)S(1)}, bf16[4,512,1024]{2,1,0:T(8,128)(2,1)}) fusion(f32[4,512,1024]{2,1,0:T(8,128)} %get-tuple-element.131, bf16[4,1024,1024]{2,1,0:T(8,128)(2,1)} %bitcast.259, f32[512,1024]{1,0:T(8,128)} %get-tuple-element.127, f32[4,1024,512]{1,2,0:T(8,128)} %get-tuple-element.144, f32[4,1024]{1,0:T(4,128)S(1)} %bitcast.256), kind=kOutput, calls=%fused_computation.19 | convolution fusion | flops 4331139072 | bytes 31490048 | tf_op jit(solution)/shard_map/nd,zfd->znf/dot_general | solution.py:945
  247.9 9.9 %multiply_reduce_fusion.1 = (f32[1024]{0:T(1024)}, f32[512]{0:T(512)S(1)}, f32[512]{0:T(512)S(1)}, f32[1024]{0:T(1024)}, f32[512,1024]{1,0:T(8,128)}) fusion(f32[512,1024]{1,0:T(8,128)} %copy-done.27, f32[512]{0:T(512)S(1)} %add_rsqrt_fusion.1, f32[512]{0:T(512)S(1)} %broadcast_multiply_fusion.6, f32[1024]{0:T(1024)S(1)} %copy-done.45, ...), kind=kOutput, calls=%fused_computation.49 | convolution fusion | flops 4300207104 | bytes 18894848 | tf_op jit(solution)/shard_map/znf,zdf->nd/dot_general | solution.py:949
  261.4 24.4 %shard_map.292.do_ref = bf16[2,1024,256]{2,1,0:T(8,128)(2,1)S(1)} custom-call(bf16[2,256,1024]{2,1,0:T(8,128)(2,1)S(1)} %bitcast.223), custom_call_target="tpu_custom_call" | custom-call | tf_op jit(solution)/shard_map/pallas_call | solution.py:397
  285.9 18.2 %shard_map.293 = (bf16[3,1,1024,256]{3,2,1,0:T(8,128)(2,1)}, f32[8,256]{1,0:T(8,128)S(1)}) custom-call(s32[2,4]{1,0:T(2,128)S(1)} %get-tuple-element.152.lo_ref, s32[2,4]{1,0:T(2,128)S(1)} %get-tuple-element.151.hi_ref, bf16[1,4,1024,128]{3,2,1,0:T(8,128)(2,1)S(1)} %copy-done.22, bf16[1,4,1024,128]{3,2,1,0:T(8,128)(2,1)S(1)} %copy-done.24, ...), custom_call_target="tpu_custom_call" | custom-call | flops 2684354560 | bytes 6291456 | tf_op jit(solution)/shard_map/pallas_call | solution.py:285
  304.1 17.9 %shard_map.294 = (bf16[3,1,1024,256]{3,2,1,0:T(8,128)(2,1)}, f32[8,256]{1,0:T(8,128)S(1)}) custom-call(s32[2,4]{1,0:T(2,128)S(1)} %get-tuple-element.152.lo_ref, s32[2,4]{1,0:T(2,128)S(1)} %get-tuple-element.151.hi_ref, bf16[1,4,1024,128]{3,2,1,0:T(8,128)(2,1)S(1)} %copy-done.16, bf16[1,4,1024,128]{3,2,1,0:T(8,128)(2,1)S(1)} %copy-done.18, ...), custom_call_target="tpu_custom_call" | custom-call | flops 2684354560 | bytes 6291456 | tf_op jit(solution)/shard_map/pallas_call | solution.py:285
  326.7 4.0 fusion.29
  330.8 2.6 copy.103
  334.4 4.5 fusion.31
  339.0 2.6 copy.63
  341.6 9.2 %convolution_convert_fusion = bf16[4,1024,1024]{2,1,0:T(8,128)(2,1)} fusion(bf16[4,512,1024]{2,1,0:T(8,128)(2,1)} %copy-done.52, f32[512,1024]{1,0:T(8,128)S(1)} %copy-done.34), kind=kOutput, calls=%fused_computation.33 | convolution fusion | flops 4299685888 | bytes 14680064 | tf_op jit(solution)/shard_map/znf,nd->zfd/dot_general | solution.py:944
  350.9 8.1 %convolution_convert_fusion.1 = bf16[4,1024,1024]{1,2,0:T(8,128)(2,1)} fusion(bf16[4,512,1024]{2,1,0:T(8,128)(2,1)S(1)} %copy-done.53, f32[512,1024]{1,0:T(8,128)S(1)} %copy-done.29, f32[1024]{0:T(1024)S(1)} %copy-done.51, f32[1024]{0:T(1024)S(1)} %copy-done.45, f32[512]{0:T(512)S(1)} %add_rsqrt_fusion.1, f32[512]{0:T(512)S(1)} %broadcast_multiply_fusion.6), kind=kOutput, calls=%fused_computation.34 | convolution fusion | flops 4301783040 | bytes 14692352 | tf_op jit(solution)/shard_map/nd,znf->zdf/dot_general | solution.py:948
  359.0 2.6 convolution_convert_fusion.2
  365.3 168.0 %shard_map.295 = (bf16[2,2,2,32,1024]{4,3,2,1,0:T(8,128)(2,1)}, bf16[2,2,2,128,1024]{4,3,2,1,0:T(8,128)(2,1)}, bf16[2,2,2,128,1024]{4,3,2,1,0:T(8,128)(2,1)}, bf...) custom-call(bf16[4,2,2,2,32,1024]{5,4,3,2,1,0:T(8,128)(2,1)} %bitcas, ...), custom_call_target="tpu_custom_call" | custom-call | tf_op jit(solution)/shard_map/pallas_call | solution.py:866
  533.3 4.2 bitcast_convert_fusion.2
  537.6 2.6 bitcast_convert_fusion.3
  (179 shorter events, 43.2 us)
Async XLA Ops:
  0.6 228.8 %copy-start = (bf16[1024,288]{0,1:T(8,128)(2,1)S(1)}, bf16[1024,288]{0,1:T(8,128)(2,1)}, u32[]{:S(2)}) copy-start(bf16[1024,288]{0,1:T(8,128)(2,1)} %param.31) | copy-start | bytes 1769476
  7.2 118.2 %copy-start.41 = (s32[2,1024]{1,0:T(2,128)S(1)}, s32[2,1024]{1,0:T(2,128)}, u32[]{:S(2)}) copy-start(s32[2,1024]{1,0:T(2,128)} %param.18) | copy-start | bytes 24580
  8.7 118.4 %copy-start.14 = (f32[3,256]{1,0:T(4,128)S(1)}, f32[3,256]{1,0:T(4,128)}, u32[]{:S(2)}) copy-start(f32[3,256]{1,0:T(4,128)} %b_ref.3) | copy-start | bytes 9220
  150.9 45.4 %copy-start.13 = (bf16[4,2,2,2,32,1024]{5,4,3,2,1,0:T(8,128)(2,1)S(1)}, bf16[4,2,2,2,32,1024]{5,4,3,2,1,0:T(8,128)(2,1)}, u32[]{:S(2)}) copy-start(bf16[4,2,2,2,32,1024]{5,4,3,2,1,0:T(8,128)(2,1)} %copy-done.12) | copy-start | bytes 6291460
  150.9 45.4 %copy-start.48 = (f32[1024]{0:T(1024)S(1)}, f32[1024]{0:T(1024)}, u32[]{:S(2)}) copy-start(f32[1024]{0:T(1024)} %param.22) | copy-start | bytes 12292
  150.9 47.2 %slice-start = ((s8[8388608]{0:T(1024)(128)(4,1)}), s8[4194304]{0:T(1024)(128)(4,1)S(1)}, s32[]{:S(2)}) async-start(s8[8388608]{0:T(1024)(128)(4,1)} %bitcast.227), calls=%async_computation | async-start | bytes 8388608
  173.4 24.6 %slice-start.1 = ((s8[8388608]{0:T(1024)(128)(4,1)}), s8[4194304]{0:T(1024)(128)(4,1)S(1)}, s32[]{:S(2)}) async-start(s8[8388608]{0:T(1024)(128)(4,1)} %bitcast.227), calls=%async_computation.1 | async-start | bytes 8388608
  196.3 27.9 %slice-start.2 = ((s8[8388608]{0:T(1024)(128)(4,1)}), s8[4194304]{0:T(1024)(128)(4,1)S(1)}, s32[]{:S(2)}) async-start(s8[8388608]{0:T(1024)(128)(4,1)} %bitcast.260), calls=%async_computation.2 | async-start | bytes 8388608
  197.7 26.5 %copy-start.27 = (f32[512,1024]{1,0:T(8,128)}, f32[512,1024]{1,0:T(8,128)S(1)}, u32[]{:S(2)}) copy-start(f32[512,1024]{1,0:T(8,128)S(1)} %get-tuple-element.143) | copy-start | bytes 6291460
  198.1 26.1 %slice-start.3 = ((s8[8388608]{0:T(1024)(128)(4,1)}), s8[4194304]{0:T(1024)(128)(4,1)S(1)}, s32[]{:S(2)}) async-start(s8[8388608]{0:T(1024)(128)(4,1)} %bitcast.260), calls=%async_computation.3 | async-start | bytes 8388608
  198.1 26.1 %copy-start.49 = (f32[1024]{0:T(1024)S(1)}, f32[1024]{0:T(1024)}, u32[]{:S(2)}) copy-start(f32[1024]{0:T(1024)} %param.28) | copy-start | bytes 12292
  247.9 9.9 %copy-start.28 = (f32[512,1024]{1,0:T(8,128)S(1)}, f32[512,1024]{1,0:T(8,128)}, u32[]{:S(2)}) copy-start(f32[512,1024]{1,0:T(8,128)} %copy-done.27) | copy-start | bytes 6291460
  260.1 25.8 %copy-start.30 = (f32[512,1024]{1,0:T(8,128)}, f32[512,1024]{1,0:T(8,128)S(1)}, u32[]{:S(2)}) copy-start(f32[512,1024]{1,0:T(8,128)S(1)} %get-tuple-element.129) | copy-start | bytes 6291460
  260.1 25.8 %copy-start.22 = (bf16[1,4,1024,128]{3,2,1,0:T(8,128)(2,1)S(1)}, bf16[1,4,1024,128]{3,2,1,0:T(8,128)(2,1)}, u32[]{:S(2)}) copy-start(bf16[1,4,1024,128]{3,2,1,0:T(8,128)(2,1)} %copy-done.21) | copy-start | bytes 3145732
  260.1 25.8 %copy-start.24 = (bf16[1,4,1024,128]{3,2,1,0:T(8,128)(2,1)S(1)}, bf16[1,4,1024,128]{3,2,1,0:T(8,128)(2,1)}, u32[]{:S(2)}) copy-start(bf16[1,4,1024,128]{3,2,1,0:T(8,128)(2,1)} %copy-done.23) | copy-start | bytes 3145732
  260.1 25.8 %copy-start.26 = (bf16[1,4,1024,128]{3,2,1,0:T(8,128)(2,1)S(1)}, bf16[1,4,1024,128]{3,2,1,0:T(8,128)(2,1)}, u32[]{:S(2)}) copy-start(bf16[1,4,1024,128]{3,2,1,0:T(8,128)(2,1)} %copy-done.25) | copy-start | bytes 3145732
  285.9 18.2 %copy-start.16 = (bf16[1,4,1024,128]{3,2,1,0:T(8,128)(2,1)S(1)}, bf16[1,4,1024,128]{3,2,1,0:T(8,128)(2,1)}, u32[]{:S(2)}) copy-start(bf16[1,4,1024,128]{3,2,1,0:T(8,128)(2,1)} %copy-done.15) | copy-start | bytes 3145732
  285.9 18.2 %copy-start.18 = (bf16[1,4,1024,128]{3,2,1,0:T(8,128)(2,1)S(1)}, bf16[1,4,1024,128]{3,2,1,0:T(8,128)(2,1)}, u32[]{:S(2)}) copy-start(bf16[1,4,1024,128]{3,2,1,0:T(8,128)(2,1)} %copy-done.17) | copy-start | bytes 3145732
  285.9 18.2 %copy-start.20 = (bf16[1,4,1024,128]{3,2,1,0:T(8,128)(2,1)S(1)}, bf16[1,4,1024,128]{3,2,1,0:T(8,128)(2,1)}, u32[]{:S(2)}) copy-start(bf16[1,4,1024,128]{3,2,1,0:T(8,128)(2,1)} %copy-done.19) | copy-start | bytes 3145732
  304.1 20.7 %copy-start.36 = (bf16[3,1,1024,256]{3,2,1,0:T(8,128)(2,1)S(1)}, bf16[3,1,1024,256]{3,2,1,0:T(8,128)(2,1)}, u32[]{:S(2)}) copy-start(bf16[3,1,1024,256]{3,2,1,0:T(8,128)(2,1)} %get-tuple-element.53) | copy-start | bytes 4718596
  341.6 9.3 %copy-start.29 = (f32[512,1024]{1,0:T(8,128)S(1)}, f32[512,1024]{1,0:T(8,128)}, u32[]{:S(2)}) copy-start(f32[512,1024]{1,0:T(8,128)} %copy-done.27) | copy-start | bytes 6291460
  341.6 9.3 %copy-start.51 = (f32[1024]{0:T(1024)S(1)}, f32[1024]{0:T(1024)}, u32[]{:S(2)}) copy-start(f32[1024]{0:T(1024)} %param.24) | copy-start | bytes 12292
  341.6 9.3 %copy-start.53 = (bf16[4,512,1024]{2,1,0:T(8,128)(2,1)S(1)}, bf16[4,512,1024]{2,1,0:T(8,128)(2,1)}, u32[]{:S(2)}) copy-start(bf16[4,512,1024]{2,1,0:T(8,128)(2,1)} %get-tuple-element.150) | copy-start | bytes 12582916
  350.9 8.1 %copy-start.6 = (bf16[2,256,1024]{2,1,0:T(8,128)(2,1)S(1)}, bf16[2,256,1024]{2,1,0:T(8,128)(2,1)}, u32[]{:S(2)}) copy-start(bf16[2,256,1024]{2,1,0:T(8,128)(2,1)} %copy-done.5) | copy-start | bytes 3145732
  (34 other events, 120.4 us)

commit v4 on v3

--- a/solution.py
+++ b/solution.py
@@ -77,8 +77,9 @@
     return lax.dot_general(keys, queries, (((1,), (1,)), ((), ())), preferred_element_type=f32)
 
 
-def attend_kernel(group, lo_ref, hi_ref, tok_ref, w_ref, b_ref, cos_ref, sin_ref, seg_ref, mixed_ref, q_ref, k_ref, v_ref,
+def attend_kernel(lo_ref, hi_ref, tok_ref, w_ref, b_ref, cos_ref, sin_ref, seg_ref, mixed_ref, q_ref, k_ref, v_ref,
                   lse_ref, vt_ref, m_ref, l_ref, acc_ref):
+    group = pl.program_id(0)
     zsize, _, rows, _ = tok_ref.shape
     length = zsize * rows
     heads = q_ref.shape[1]
@@ -152,29 +153,29 @@
     lax.fori_loop(0, length // BLOCK, query_block, 0)
 
 
-def attend_forward(group, bounds, tokens, weight, bias, cosine, sine, docs):
-    zsize, _, rows, width = tokens.shape
+def attend_forward(bounds, tokens, weight, bias, cosine, sine, docs):
+    zsize, groups, rows, width = tokens.shape
     length = zsize * rows
     cols = weight.shape[2]
     heads = cols // HEAD_DIM
     pair = 2 * HEAD_DIM
     whole = lambda shape: pl.BlockSpec(shape, lambda i, *_: (0,) * len(shape))
-    of_group = lambda shape: pl.BlockSpec(shape, lambda i, *_: (group,) + (0,) * (len(shape) - 1))
+    of_group = lambda shape: pl.BlockSpec(shape, lambda i, *_: (i,) + (0,) * (len(shape) - 1))
     like = jax.ShapeDtypeStruct
     return pl.pallas_call(
-        functools.partial(attend_kernel, group),
+        attend_kernel,
         grid_spec=pltpu.PrefetchScalarGridSpec(
             num_scalar_prefetch=2,
-            grid=(1,),
+            grid=(groups,),
             in_specs=[
-                pl.BlockSpec((zsize, 1, rows, width), lambda i, *_: (0, group, 0, 0)),
+                pl.BlockSpec((zsize, 1, rows, width), lambda i, *_: (0, i, 0, 0)),
                 whole(weight.shape), whole(bias.shape),
                 of_group((1, length, pair)), of_group((1, length, pair)), of_group((1, length, 1)),
             ],
             out_specs=[
-                whole((1, length, cols)),
-                whole((1, heads, length, pair)), whole((1, heads, length, pair)), whole((1, heads, length, pair)),
-                whole((1, heads, length)),
+                of_group((1, length, cols)),
+                of_group((1, heads, length, pair)), of_group((1, heads, length, pair)), of_group((1, heads, length, pair)),
+                of_group((1, heads, length)),
             ],
             scratch_shapes=[
                 pltpu.VMEM((heads, HEAD_DIM, length), bf16),
@@ -183,21 +184,22 @@
             ],
         ),
         out_shape=[
-            like((1, length, cols), bf16),
-            like((1, heads, length, pair), bf16), like((1, heads, length, pair), bf16),
-            like((1, heads, length, pair), bf16), like((1, heads, length), f32),
+            like((groups, length, cols), bf16),
+            like((groups, heads, length, pair), bf16), like((groups, heads, length, pair), bf16),
+            like((groups, heads, length, pair), bf16), like((groups, heads, length), f32),
         ],
         compiler_params=pltpu.CompilerParams(vmem_limit_bytes=48 * 1024 * 1024),
         cost_estimate=pl.CostEstimate(
-            flops=2 * length * width * 3 * cols + 4 * length * length * cols,
+            flops=groups * (2 * length * width * 3 * cols + 4 * length * length * cols),
             bytes_accessed=2 * length * width + 6 * width * cols + 8 * length * cols,
             transcendentals=length * length * heads,
         ),
     )(*bounds, tokens, weight, bias, cosine, sine, docs)
 
 
-def attend_back_kernel(group, lo_ref, hi_ref, q_ref, k_ref, v_ref, lse_ref, mixed_ref, do_ref, cos_ref, sin_ref,
+def attend_back_kernel(lo_ref, hi_ref, q_ref, k_ref, v_ref, lse_ref, mixed_ref, do_ref, cos_ref, sin_ref,
                        grad_ref, sum_ref, dox_ref, kt_ref, delta_ref, dk_ref, dv_ref, dqt_ref):
+    group = pl.program_id(0)
     heads, length = q_ref.shape[1], q_ref.shape[2]
     pair = 2 * HEAD_DIM
     scale = HEAD_DIM ** (-0.5)
@@ -222,7 +224,9 @@
         return carry
 
     lax.fori_loop(0, blocks, prepare, 0)
-    sum_ref[...] = jnp.zeros(sum_ref.shape, f32)
+    @pl.when(group == 0)
+    def _():
+        sum_ref[...] = jnp.zeros(sum_ref.shape, f32)
 
     def put(c, j, at, field):
         low = field.astype(bf16)
@@ -274,33 +278,35 @@
     lax.fori_loop(0, blocks, finish, 0)
 
 
-def attend_backward(group, bounds, kept, mixed, upstream, cosine, sine):
+def attend_backward(bounds, kept, mixed, upstream, cosine, sine):
     queries, keys, values, lse = kept
-    _, heads, length, pair = queries.shape
+    groups, heads, length, pair = queries.shape
     cols = heads * HEAD_DIM
     whole = lambda shape: pl.BlockSpec(shape, lambda i, *_: (0,) * len(shape))
-    of_group = lambda shape: pl.BlockSpec(shape, lambda i, *_: (group,) + (0,) * (len(shape) - 1))
+    of_group = lambda shape: pl.BlockSpec(shape, lambda i, *_: (i,) + (0,) * (len(shape) - 1))
     like = jax.ShapeDtypeStruct
     wide = (heads, length, pair)
     return pl.pallas_call(
-        functools.partial(attend_back_kernel, group),
+        attend_back_kernel,
         grid_spec=pltpu.PrefetchScalarGridSpec(
             num_scalar_prefetch=2,
-            grid=(1,),
-            in_specs=[
-                whole(queries.shape), whole(keys.shape), whole(values.shape), whole(lse.shape), whole(mixed.shape),
+            grid=(groups,),
+            in_specs=[of_group((1,) + wide)] * 3 + [
+                of_group((1, heads, length)), of_group((1, length, cols)),
                 of_group((1, length, cols)), of_group((1, length, pair)), of_group((1, length, pair)),
             ],
-            out_specs=[whole((3, 1, length, cols)), whole((8, cols))],
+            out_specs=[
+                pl.BlockSpec((3, 1, length, cols), lambda i, *_: (0, i, 0, 0)), whole((8, cols)),
+            ],
             scratch_shapes=[
                 pltpu.VMEM(wide, bf16), pltpu.VMEM((heads, HEAD_DIM, length), bf16), pltpu.VMEM((heads, length), f32),
                 pltpu.VMEM(wide, f32), pltpu.VMEM(wide, f32), pltpu.VMEM((heads, HEAD_DIM, BLOCK), f32),
             ],
         ),
-        out_shape=[like((3, 1, length, cols), bf16), like((8, cols), f32)],
+        out_shape=[like((3, groups, length, cols), bf16), like((8, cols), f32)],
         compiler_params=pltpu.CompilerParams(vmem_limit_bytes=48 * 1024 * 1024),
         cost_estimate=pl.CostEstimate(
-            flops=10 * length * length * cols, bytes_accessed=24 * length * cols, transcendentals=length * length * heads
+            flops=groups * 10 * length * length * cols, bytes_accessed=24 * length * cols, transcendentals=length * length * heads
         ),
     )(*bounds, queries, keys, values, lse, mixed, upstream, cosine, sine)
 
@@ -337,17 +343,15 @@
     )
 
 
-def swap_kernel(zsize, to_rows, *refs):
-    sources, target = refs[:-4], refs[-4]
-    held, local_sem, send, recv = refs[-3], refs[-2], refs[-1].at[0], refs[-1].at[1]
+def swap_kernel(zsize, to_rows, origin, target, held, local_sem, send, recv):
     groups = target.shape[0]
     rows, cols = (target.shape[1], target.shape[2] // zsize) if to_rows else (target.shape[1] // zsize, target.shape[2])
     z = lax.axis_index("z")
 
     def source(g, peer):
         if to_rows:
-            return sources[g].at[0, pl.ds(pl.multiple_of(peer * rows, rows), rows), :]
-        return sources[0].at[g, :, pl.ds(pl.multiple_of(peer * cols, cols), cols)]
+            return origin.at[g, pl.ds(pl.multiple_of(peer * rows, rows), rows), :]
+        return origin.at[g, :, pl.ds(pl.multiple_of(peer * cols, cols), cols)]
 
     def place(g, peer):
         if to_rows:
@@ -386,28 +390,29 @@
             copy_to(g, step).wait_send()
 
 
-def swap(sources, zsize, to_rows):
+def swap(array, zsize, to_rows):
+    groups, rows, cols = array.shape
     if to_rows:
-        groups, rows, cols = len(sources), sources[0].shape[1] // zsize, sources[0].shape[2]
+        rows //= zsize
         shape = (groups, rows, zsize * cols)
     else:
-        groups, rows, cols = sources[0].shape
         cols //= zsize
         shape = (groups, zsize * rows, cols)
     return pl.pallas_call(
         functools.partial(swap_kernel, zsize, to_rows),
         out_shape=jax.ShapeDtypeStruct(shape, bf16),
-        in_specs=[HBM] * len(sources),
+        in_specs=[HBM],
         out_specs=HBM,
         scratch_shapes=[
             pltpu.VMEM((groups, rows, cols), bf16),
             pltpu.SemaphoreType.DMA((2, groups)),
-            pltpu.SemaphoreType.DMA((2, zsize, groups)),
+            pltpu.SemaphoreType.DMA((zsize, groups)),
+            pltpu.SemaphoreType.DMA((zsize, groups)),
         ],
         compiler_params=pltpu.CompilerParams(
             collective_id=2 if to_rows else 3, has_side_effects=True, vmem_limit_bytes=8 * 1024 * 1024
         ),
-    )(*sources)
+    )(array)
 
 
 ORDERS = {"xy": ("x", "y"), "yx": ("y", "x")}
@@ -579,35 +584,45 @@
     lax.fori_loop(0, rows // step, body, 0)
 
 
-def reduce_kernel(zsize, orders, *refs):
-    n = len(orders)
-    m = n - 2
-    parts, back, small = refs[:n], refs[n], refs[n + 1]
-    outs, back_out, small_out = refs[n + 2:2 * n + 2], refs[2 * n + 2], refs[2 * n + 3]
-    pos = 2 * n + 4
-    mine, got_c, got_1, got_2 = (refs[pos + i * n:pos + (i + 1) * n] for i in range(4))
-    pos += 4 * n
-    got_z = refs[pos:pos + m + 1]
-    pos += m + 1
-    back_mine, small_mine, small_got, small_line, small_total, part_line, part_total = refs[pos:pos + 7]
-    (local_sem, send, recv, z_send, z_recv, s_send, s_recv, t_send, t_recv, g_send, g_recv, end_sem) = refs[pos + 7:]
+def reduce_kernel(zsize, orders, w, *refs):
+    n = 3
+    p = len(orders) - n
+    items = n + p
+    pieces, came, refs = refs[:p], refs[p:2 * p], refs[2 * p:]
+    parts, backs, small = refs[:n], refs[n:n + w], refs[n + w]
+    pos = n + w + 1
+    piece_out, part_out, back_out = refs[pos:pos + p], refs[pos + p:pos + p + n], refs[pos + p + n:pos + p + n + w]
+    small_out = refs[pos + p + n + w]
+    outs = list(part_out) + list(piece_out)
+    pos += p + n + w + 1
+    mine = refs[pos:pos + items + w]
+    pos += items + w
+    got_c, got_1, got_2 = refs[pos:pos + n], refs[pos + n:pos + n + items], refs[pos + n + items:pos + n + 2 * items]
+    pos += n + 2 * items
+    lines = [0] + list(range(n, items + w))
+    line_backs = list(range(items, items + w))
+    got_z = dict(zip(lines, refs[pos:pos + len(lines)]))
+    pos += len(lines)
+    small_mine, small_got, small_line, small_total, part_line, part_total = refs[pos:pos + 6]
+    (local_sem, send, recv, z_send, z_recv, s_send, s_recv, t_send, t_recv, g_send, g_recv, end_sem) = refs[pos + 6:]
     z = lax.axis_index("z")
     c = lax.axis_index("core")
+    orders = orders[p:] + orders[:p]
     place = [(lax.axis_index(o[0]), lax.axis_index(o[1])) for o in orders]
     turn = []
     for i in range(zsize // 2):
         turn += [i, zsize - 1 - i]
-    few = parts[m].shape[0]
-    groups = [[(m, b) for b in range(few)] + [(m + 1, 0)]] + [[(k, b) for k in range(m)] for b in turn]
-    steps = [kb for group in groups for kb in group]
+    few = parts[1].shape[0]
+    steps = [(1, b) for b in range(few)] + [(2, 0)] + [(0, b) for b in turn]
 
     def load(k, b):
-        return pltpu.make_async_copy(parts[k].at[b, c], mine[k].at[b], local_sem.at[k, b])
-
-    def load_back(b):
-        return pltpu.make_async_copy(back.at[b], back_mine.at[b], local_sem.at[n, b])
-
-    load_small = pltpu.make_async_copy(small, small_mine.at[0], local_sem.at[n + 1, 0])
+        src = parts[k].at[b, c] if k < n else pieces[k - n].at[b] if k < items else backs[k - items].at[b]
+        return pltpu.make_async_copy(src, mine[k].at[b], local_sem.at[k, b])
+
+    def load_came(k, b):
+        return pltpu.make_async_copy(came[k - n].at[b], got_1[k].at[b], local_sem.at[items + w + 1 + k - n, b])
+
+    load_small = pltpu.make_async_copy(small, small_mine.at[0], local_sem.at[items + w, 0])
 
     def half(k, b, stage):
         f, s = place[k]
@@ -616,14 +631,15 @@
         elif stage == 1:
             src, dst, axis = mine[k].at[b, 1 - f], got_1[k].at[b], orders[k][0]
         else:
-            src, dst, axis = mine[k].at[b, f, 1 - s], got_2[k].at[b], orders[k][1]
+            held = mine[k].at[b, f] if k < n else mine[k].at[b]
+            src, dst, axis = held.at[1 - s], got_2[k].at[b], orders[k][1]
         return remote(src, dst, send.at[stage, k, b], recv.at[stage, k, b], other(axis))
 
     def own(k, b):
-        if k == m:
-            return back_mine.at[b]
+        if k >= items:
+            return mine[k].at[b]
         f, s = place[k]
-        return mine[k].at[b, f, s]
+        return mine[k].at[b, s] if k >= n else mine[k].at[b, f, s]
 
     def hop(k, b, side):
         to = z + 1 if side == 0 else z - 1
@@ -637,22 +653,28 @@
         remote(own(k, b), ref, z_send.at[k, b], z_recv.at[k, at], {"z": sender}).wait_recv()
         add_rows(own(k, b), ref)
 
-    def line_step(ks, b, hops):
+    def line_start(ks, messages):
         for side in range(2):
-            here = z == hops if side == 0 else z == zsize - 1 - hops
-            goes = jnp.logical_and(here, z < b) if side == 0 else jnp.logical_and(here, z > b)
-            if hops:
-                ends = jnp.logical_and(here, z == b)
-
-                @pl.when(jnp.logical_or(goes, ends))
+
+            @pl.when(z == (0 if side == 0 else zsize - 1))
+            def _():
+                for i in messages:
+                    for k in ks:
+                        hop(k, zsize - 1 - i if side == 0 else i, side).start()
+
+    def line_slot(ks, slot):
+        for i in range(slot):
+            for side in range(2):
+                b = zsize - 1 - i if side == 0 else i
+
+                @pl.when(z == (slot - i if side == 0 else zsize - 1 - slot + i))
                 def _():
                     for k in ks:
                         take(k, b, side)
 
-            @pl.when(goes)
-            def _():
-                for k in ks:
-                    hop(k, b, side).start()
+                        @pl.when(z < b if side == 0 else z > b)
+                        def _():
+                            hop(k, b, side).start()
 
     def small_swap(stage):
         return remote(
@@ -666,7 +688,7 @@
             small_swap(stage + 1).start()
 
     last = len(CELL)
-    last_part = own(m + 1, 0)
+    last_part = own(2, 0)
 
     def total_copy(item, way):
         line, total = ((small_line, small_total), (part_line, part_total))[item]
@@ -704,22 +726,26 @@
                     for item in range(2):
                         total_copy(item, 1).start()
 
+    line_pieces = list(range(n, items))
+    piece_steps = [(k, b) for b in turn for k in line_pieces]
     for b in turn:
-        load_back(b).start()
-    load_small.start()
+        for k in line_backs:
+            load(k, b).start()
+    for k, b in piece_steps:
+        load(k, b).start()
+        load_came(k, b).start()
     for k, b in steps:
         load(k, b).start()
+    load_small.start()
     greet(zsize)
-    for k, b in groups[0]:
+    for k, b in steps:
         half(k, b, 0).start()
     for b in turn:
-        load_back(b).wait()
-    for b in turn:
-        line_step([m], b, 0)
+        for k in line_backs:
+            load(k, b).wait()
+    line_start(line_backs, [0])
     load_small.wait()
     small_swap(0).start()
-    for k, b in steps[len(groups[0]):]:
-        half(k, b, 0).start()
 
     def stage_1(k, b):
         f, s = place[k]
@@ -733,21 +759,25 @@
 
     def stage_2(k, b):
         f, s = place[k]
-        half(k, b, 1).wait_recv()
-        add_rows(mine[k].at[b, f, 1 - s], got_1[k].at[b, 1 - s])
+        held = mine[k].at[b, f] if k < n else mine[k].at[b]
+        if k < n:
+            half(k, b, 1).wait_recv()
+        else:
+            load(k, b).wait()
+            load_came(k, b).wait()
+        add_rows(held.at[1 - s], got_1[k].at[b, 1 - s])
         half(k, b, 2).start()
-        add_rows(mine[k].at[b, f, s], got_1[k].at[b, s])
+        add_rows(held.at[s], got_1[k].at[b, s])
 
     def stage_3(k, b):
-        f, s = place[k]
         half(k, b, 2).wait_recv()
-        add_rows(mine[k].at[b, f, s], got_2[k].at[b])
+        add_rows(own(k, b), got_2[k].at[b])
 
     def result(k, b):
-        return part_total if k == m + 1 else own(k, b) if k != m else mine[m].at[b, place[m][0], place[m][1]]
+        return part_total if k == 2 else own(k, b)
 
     def out_of(k, b):
-        return outs[k].at[b] if k == m else outs[k]
+        return outs[k].at[b] if k == 1 else outs[k]
 
     def put(k, b, slot):
         f, s = place[k]
@@ -761,67 +791,104 @@
         axis = (orders[k][1], orders[k][0], "core")[stage]
         return remote(src, dst, g_send.at[slot, stage], g_recv.at[slot, stage], other(axis))
 
-    first = [(m, b, b) for b in range(few)]
-    rest = [(k, z, few + k) for k in range(m)] + [(m + 1, 0, few + m)]
-
-    def spread_start(items):
-        for k, b, slot in items:
-            spread(k, b, 0, slot).start()
-            put(k, b, slot).start()
-
-    def spread_on(items, stage):
-        for k, b, slot in items:
+    spreads = [
+        [(1, b, b) for b in range(few)],
+        [(k, z, few + k - n) for k in line_pieces],
+        [(0, z, few + p), (2, 0, few + p + 1)],
+    ]
+
+    def spread_step(group, stage):
+        for k, b, slot in spreads[group]:
+            if stage == 0:
+                spread(k, b, 0, slot).start()
+                put(k, b, slot).start()
+                continue
             if stage == 1:
                 put(k, b, slot).wait()
             spread(k, b, stage - 1, slot).wait_recv()
             if stage < 3:
                 spread(k, b, stage, slot).start()
 
-    ks = list(range(m))
-    small_tick = 3
-    back_ticks = [2 + i + (1 if i > 1 else 0) for i in range(zsize)]
-    for tick in range(len(groups) + zsize + 2):
-        if tick < len(groups):
-            for k, b in groups[tick]:
-                stage_1(k, b)
-        if 1 <= tick <= len(groups):
-            for k, b in groups[tick - 1]:
-                stage_2(k, b)
-        if 2 <= tick <= len(groups) + 1:
-            for k, b in groups[tick - 2]:
-                stage_3(k, b)
-        if 1 <= tick <= 3:
-            small_step(tick - 1)
-        for i in range(1, zsize):
-            if tick == back_ticks[i - 1]:
-                for b in turn:
-                    line_step([m], b, i)
-        for j, b in enumerate(turn):
-            hops = tick - 3 - j
-            if 0 <= hops < zsize:
-                line_step(ks, b, hops)
-        total_step(tick - small_tick)
-        if tick == 4:
-            spread_start(first)
-        if 5 <= tick <= 7:
-            spread_on(first, tick - 4)
-    for tick in range(len(groups) + zsize + 2 - small_tick, 2 * zsize):
+    def sent(ks):
+        for b in range(zsize):
+
+            @pl.when(z != b)
+            def _():
+                for k in ks:
+                    hop(k, b, 0).wait_send()
+
+    at_end = jnp.logical_or(z == 0, z == zsize - 1)
+    for k, b in piece_steps:
+        stage_2(k, b)
+    for k, b in steps:
+        stage_1(k, b)
+    small_step(0)
+    for k, b in piece_steps:
+        stage_3(k, b)
+    line_start(line_pieces, range(zsize - 1))
+    for k, b in steps:
+        stage_2(k, b)
+    small_step(1)
+    line_slot(line_backs, 1)
+    for k, b in steps:
+        stage_3(k, b)
+    small_step(2)
+    spread_step(0, 0)
+    line_start([0], range(zsize - 1))
+    total_step(0)
+
+    @pl.when(at_end)
+    def _():
+        sent(line_pieces)
+
+    line_start(line_backs, range(1, zsize - 1))
+    ticks = list(range(1, 2 * zsize - 1))
+    later = [(0, 1), (0, 2), (0, 3)]
+
+    def fill(group_stages, count):
+        for _ in range(count):
+            if group_stages:
+                spread_step(*group_stages.pop(0))
+
+    for slot in range(1, zsize):
+        line_slot(line_pieces, slot)
+        total_step(ticks.pop(0))
+        fill(later, 1)
+        if slot >= 2:
+            line_slot([0], slot - 1)
+    fill(later, 3)
+    spread_step(1, 0)
+    later = [(1, 1), (1, 2), (1, 3)]
+    total_step(ticks.pop(0))
+    line_slot([0], zsize - 1)
+    for slot in range(2, zsize - 1):
+        line_slot(line_backs, slot)
+        fill(later, 1)
+    for tick in ticks:
         total_step(tick)
-    finish_back = pltpu.make_async_copy(back_mine.at[z], back_out, local_sem.at[n, 0])
-    finish_back.start()
-    finish_small = pltpu.make_async_copy(small_total, small_out, local_sem.at[n + 1, 0])
+    spread_step(2, 0)
+    fill(later, 1)
+    spread_step(2, 1)
+    fill(later, 1)
+    spread_step(2, 2)
+    fill(later, 3)
+    line_slot(line_backs, zsize - 1)
+    finish_back = [
+        pltpu.make_async_copy(mine[k].at[z], back_out[k - items], local_sem.at[k, 0]) for k in line_backs
+    ]
+    for copy in finish_back:
+        copy.start()
+    finish_small = pltpu.make_async_copy(small_total, small_out, local_sem.at[items + w, 0])
     finish_small.start()
-    spread_start(rest)
-    for stage in (1, 2, 3):
-        spread_on(rest, stage)
-    finish_back.wait()
+    spread_step(2, 3)
+    for copy in finish_back:
+        copy.wait()
     finish_small.wait()
-    for b in range(zsize):
-
-        @pl.when(z != b)
-        def _():
-            for k in range(m + 1):
-                hop(k, b, 0).wait_send()
+    sent([0] + line_backs)
+
+    @pl.when(jnp.logical_not(at_end))
+    def _():
+        sent(line_pieces)
 
     for way in range(2):
 
@@ -833,46 +900,186 @@
     for k, b in steps:
         for stage in range(3):
             half(k, b, stage).wait_send()
+    for k, b in piece_steps:
+        half(k, b, 2).wait_send()
     for stage in range(3):
         small_swap(stage).wait_send()
-    for k, b, slot in first + rest:
-        for stage in range(3):
-            spread(k, b, stage, slot).wait_send()
-
-
-def reduce_end(parts, cell_part, all_part, back, small, zsize):
-    orders = [ORDERS[o] for o, _ in parts + [cell_part, all_part]]
-    arrays = [a for _, a in parts + [cell_part, all_part]]
-    n = len(arrays)
+    for group in spreads:
+        for k, b, slot in group:
+            for stage in range(3):
+                spread(k, b, stage, slot).wait_send()
+
+
+def reduce_end(pieces, parts, backs, small, zsize):
+    orders = [ORDERS[o[0]] for o in pieces + parts]
+    piece_arrays = [a for _, a, _ in pieces]
+    came = [a for _, _, a in pieces]
+    arrays = [a for _, a in parts]
+    p, n, w = len(pieces), len(parts), len(backs)
     shapes = [a.shape for a in arrays]
     like = jax.ShapeDtypeStruct
-    outs = [like(s if i == n - 2 else s[1:], bf16) for i, s in enumerate(shapes)]
-    outs += [like(back.shape[1:], bf16), like(small.shape, f32)]
-    scratch = [pltpu.VMEM((s[0],) + s[2:], bf16) for s in shapes]
-    scratch += [pltpu.VMEM((s[0],) + s[2:], bf16) for s in shapes]
-    scratch += [pltpu.VMEM((s[0],) + s[3:], bf16) for s in shapes]
-    scratch += [pltpu.VMEM((s[0],) + s[4:], bf16) for s in shapes]
-    scratch += [pltpu.VMEM((zsize + 1,) + s[4:], bf16) for s in shapes[:-2]]
-    scratch += [pltpu.VMEM((zsize + 1,) + back.shape[1:], bf16), pltpu.VMEM(back.shape, bf16)]
+    outs = [like((2, 2, 2) + a.shape[2:], bf16) for a in piece_arrays]
+    outs += [like(s if i == 1 else s[1:], bf16) for i, s in enumerate(shapes)]
+    outs += [like(a.shape[1:], bf16) for a in backs] + [like(small.shape, f32)]
+    held = lambda shape: pltpu.VMEM(shape, bf16)
+    scratch = [held((s[0],) + s[2:]) for s in shapes]
+    scratch += [held(a.shape) for a in piece_arrays + backs]
+    scratch += [held((s[0],) + s[2:]) for s in shapes]
+    scratch += [held((s[0],) + s[3:]) for s in shapes] + [held(a.shape) for a in piece_arrays]
+    scratch += [held((s[0],) + s[4:]) for s in shapes] + [held(a.shape[:1] + a.shape[2:]) for a in piece_arrays]
+    scratch += [held((zsize + 1,) + shapes[0][4:])]
+    scratch += [held((zsize + 1,) + a.shape[2:]) for a in piece_arrays] + [held((zsize + 1,) + a.shape[1:]) for a in backs]
     scratch += [pltpu.VMEM((4,) + small.shape, f32), pltpu.VMEM((3,) + small.shape, f32)]
-    scratch += [pltpu.VMEM(small.shape, f32)] * 2 + [pltpu.VMEM(shapes[-1][4:], bf16)] * 2
+    scratch += [pltpu.VMEM(small.shape, f32)] * 2 + [held(shapes[2][4:])] * 2
     dma = pltpu.SemaphoreType.DMA
-    most = max(zsize, shapes[-2][0])
-    ends = n - 1 + shapes[-2][0]
+    most = max(zsize, shapes[1][0])
+    ends = shapes[1][0] + p + 2
     scratch += [
-        dma((n + 2, most)), dma((3, n, most)), dma((3, n, most)), dma((n - 1, zsize)), dma((n - 1, zsize + 1)),
+        dma((n + 2 * p + w + 1, most)), dma((3, n + p, most)), dma((3, n + p, most)),
+        dma((n + p + w, zsize)), dma((n + p + w, zsize + 1)),
         dma((3,)), dma((3,)), dma((2, 2)), dma((2, 2)), dma((ends, 3)), dma((ends, 3)), dma((ends,)),
     ]
     return pl.pallas_call(
-        functools.partial(reduce_kernel, zsize, orders),
+        functools.partial(reduce_kernel, zsize, orders, w),
         out_shape=outs,
-        in_specs=[HBM] * (n + 2),
-        out_specs=[HBM] * (n + 2),
+        in_specs=[HBM] * (n + 2 * p + w + 1),
+        out_specs=[HBM] * (n + p + w + 1),
         scratch_shapes=scratch,
         compiler_params=pltpu.CompilerParams(
-            collective_id=1, has_side_effects=True, vmem_limit_bytes=60 * 1024 * 1024
+            collective_id=1, has_side_effects=True, vmem_limit_bytes=48 * 1024 * 1024
         ),
-    )(*arrays, back, small)
+    )(*piece_arrays, *came, *arrays, *backs, small)
+
+
+def gelu_pair(v):
+    size = jnp.abs(v)
+    t = 1.0 / (1.0 + (0.3275911 * 0.5 ** 0.5) * size)
+    bell = jnp.exp(-0.5 * (v * v))
+    poly = t * (0.254829592 + t * (-0.284496736 + t * (1.421413741 + t * (-1.453152027 + t * 1.061405429))))
+    tail = 0.5 * poly * bell
+    cdf = jnp.where(v >= 0.0, 1.0 - tail, tail)
+    return v * cdf, cdf + v * (bell * (1.0 / (2.0 * math.pi) ** 0.5))
+
+
+def ffn_kernel(x_ref, up_ref, bias_ref, down_ref, active_ref, slope_ref, sum_ref):
+    rows = x_ref.shape[0]
+    part = rows // 2
+
+    @pl.when(pl.program_id(0) == 0)
+    def _():
+        sum_ref[...] = jnp.zeros(sum_ref.shape, f32)
+
+    for i in range(2):
+        at = pl.ds(i * part, part)
+        hidden = jnp.dot(x_ref[at, :], up_ref[0], preferred_element_type=f32) + bias_ref[0]
+        active, slope = gelu_pair(hidden)
+        active = active.astype(bf16)
+        active_ref[0, at, :] = active
+        slope_ref[0, at, :] = slope.astype(bf16)
+        sum_ref[at, :] += jnp.dot(active, down_ref[0], preferred_element_type=f32)
+
+
+def ffn_forward(normed_low, up_all, up_bias, down_all):
+    zsize, width, units = up_all.shape
+    rows = normed_low.shape[0]
+    tile = units // 2
+    like = jax.ShapeDtypeStruct
+    tiles = pl.BlockSpec((1, rows, tile), lambda s: (s // 2, 0, s % 2))
+    return pl.pallas_call(
+        ffn_kernel,
+        grid=(2 * zsize,),
+        in_specs=[
+            pl.BlockSpec((rows, width), lambda s: (0, 0)),
+            pl.BlockSpec((1, width, tile), lambda s: (s // 2, 0, s % 2)),
+            pl.BlockSpec((1, 1, tile), lambda s: (s // 2, 0, s % 2)),
+            pl.BlockSpec((1, tile, width), lambda s: (s // 2, s % 2, 0)),
+        ],
+        out_specs=[tiles, tiles, pl.BlockSpec((rows, width), lambda s: (0, 0))],
+        out_shape=[
+            like((zsize, rows, units), bf16), like((zsize, rows, units), bf16), like((rows, width), f32),
+        ],
+        compiler_params=pltpu.CompilerParams(vmem_limit_bytes=40 * 1024 * 1024),
+    )(normed_low, up_all, up_bias[:, None, :], down_all)
+
+
+def ffn_back_kernel(core_ref, second_ref, normed_ref, up_ref, down_ref, active_ref, slope_ref,
+                    give_up_ref, keep_up_ref, give_down_ref, keep_down_ref, back_ref, bias_ref, turned_ref):
+    s = pl.program_id(0)
+    half = turned_ref.shape[0] // 2
+    c = core_ref[0]
+
+    @pl.when(s == 0)
+    def _():
+        back_ref[...] = jnp.zeros(back_ref.shape, f32)
+        turned_ref[...] = normed_ref[...].T
+
+    second = second_ref[...]
+    upstream = lax.dot_general(second, down_ref[0], (((1,), (1,)), ((), ())), preferred_element_type=f32)
+    grad = (upstream * slope_ref[0].astype(f32)).astype(bf16)
+    bias_ref[0] = jnp.sum(grad.astype(f32), axis=0, keepdims=True)
+    down = lax.dot_general(active_ref[0], second, (((0,), (0,)), ((), ())), preferred_element_type=f32).astype(bf16)
+
+    @pl.when(s % 2 == 0)
+    def _():
+        give_down_ref[0] = down
+
+    @pl.when(s % 2 == 1)
+    def _():
+        keep_down_ref[0] = down
+
+    back_ref[...] += lax.dot_general(grad, up_ref[0], (((1,), (1,)), ((), ())), preferred_element_type=f32)
+    give = turned_ref[pl.ds(pl.multiple_of((1 - c) * half, half), half), :]
+    give_up_ref[0] = jnp.dot(give, grad, preferred_element_type=f32).astype(bf16)
+    keep = turned_ref[pl.ds(pl.multiple_of(c * half, half), half), :]
+    keep_up_ref[0] = jnp.dot(keep, grad, preferred_element_type=f32).astype(bf16)
+
+
+def ffn_backward(core, second_low, normed_low, up_all, down_all, active, slope):
+    zsize, width, units = up_all.shape
+    rows = normed_low.shape[0]
+    tile = units // 2
+    like = jax.ShapeDtypeStruct
+    part = lambda s, c: (1 - c[0] + (2 * c[0] - 1) * (s % 2))
+    whole = pl.BlockSpec((rows, width), lambda s, c: (0, 0))
+    tiles = pl.BlockSpec((1, rows, tile), lambda s, c: (s // 2, 0, part(s, c)))
+    up_half = pl.BlockSpec((1, width // 2, tile), lambda s, c: (s // 2, 0, part(s, c)))
+    down_half = pl.BlockSpec((1, tile, width), lambda s, c: (s // 2, 0, 0))
+    return pl.pallas_call(
+        ffn_back_kernel,
+        grid_spec=pltpu.PrefetchScalarGridSpec(
+            num_scalar_prefetch=1,
+            grid=(2 * zsize,),
+            in_specs=[
+                whole, whole,
+                pl.BlockSpec((1, width, tile), lambda s, c: (s // 2, 0, part(s, c))),
+                pl.BlockSpec((1, tile, width), lambda s, c: (s // 2, part(s, c), 0)),
+                tiles, tiles,
+            ],
+            out_specs=[
+                up_half, up_half, down_half, down_half, whole,
+                pl.BlockSpec((1, 1, tile), lambda s, c: (s // 2, 0, part(s, c))),
+            ],
+            scratch_shapes=[pltpu.VMEM((width, rows), bf16)],
+        ),
+        out_shape=[
+            like((zsize, width // 2, units), bf16), like((zsize, width // 2, units), bf16),
+            like((zsize, tile, width), bf16), like((zsize, tile, width), bf16),
+            like((rows, width), f32), like((zsize, 1, units), f32),
+        ],
+        compiler_params=pltpu.CompilerParams(vmem_limit_bytes=40 * 1024 * 1024),
+    )(core, second_low, normed_low, up_all, down_all, active, slope)
+
+
+PAIR = [(0, 1), (1, 0)]
+
+
+def first_halving(got, keep, order):
+    zsize, half, cols = keep.shape
+    shape = (zsize, 2, 2, half // 4, cols)
+    got, keep = got.reshape(shape), keep.reshape(shape)
+    i = lax.axis_index(ORDERS[order][0])
+    pick = lambda array, j: lax.dynamic_index_in_dim(array, j, 1, keepdims=False)
+    return pick(keep, 1 - i) + pick(got, 1 - i), pick(keep, i) + pick(got, i)
 
 
 def per_device(blocks, tokens, segments, qkv_weight, qkv_bias, out_weight, out_bias, gain_one, shift_one,
@@ -914,21 +1121,15 @@
     down_all = down_all.reshape(zsize, units_here, model_width)
     full_up_bias = bias_blocks.reshape(zsize, units_here)
 
-    heads = [
-        attend_forward(g, bounds, token_blocks, qkv_weight, qkv_bias, cosine, sine, docs) for g in range(groups)
-    ]
-    mixed = swap([h[0] for h in heads], zsize, True).reshape(rows, model_width)
+    own_mixed, *kept = attend_forward(bounds, token_blocks, qkv_weight, qkv_bias, cosine, sine, docs)
+    mixed = swap(own_mixed, zsize, True).reshape(rows, model_width)
 
     first_sum = tokens.reshape(rows, model_width).astype(f32) + (
         jnp.dot(mixed, out_all, preferred_element_type=f32) + out_bias
     )
     normed, scaled_one, inv_one = norm_forward(first_sum, gain_one, shift_one)
     normed_low = normed.astype(bf16)
-    hidden = jnp.einsum("nd,zdf->znf", normed_low, up_all, preferred_element_type=f32)
-    hidden = hidden + full_up_bias[:, None, :]
-    active, gelu_pull = jax.vjp(lambda field: jax.nn.gelu(field, approximate=False), hidden)
-    active = active.astype(bf16)
-    ffn = jnp.einsum("znf,zfd->nd", active, down_all, preferred_element_type=f32)
+    active, slope, ffn = ffn_forward(normed_low, up_all, full_up_bias, down_all)
     second_sum = normed + (ffn + down_bias)
     result, scaled_two, inv_two = norm_forward(second_sum, gain_two, shift_two)
     result_low = result.astype(bf16)
@@ -941,27 +1142,34 @@
     grad_second, gain_two_grad, shift_two_grad = norm_backward(grad_result, scaled_two, inv_two, gain_two)
     second_low = grad_second.astype(bf16)
     down_bias_grad = jnp.sum(second_low.astype(f32), axis=0)
-    down_grad = jnp.einsum("znf,nd->zfd", active, second_low, preferred_element_type=f32).astype(bf16)
-    grad_active = jnp.einsum("nd,zfd->znf", second_low, down_all, preferred_element_type=f32)
-    grad_hidden = gelu_pull(grad_active)[0].astype(bf16)
-    up_bias_grad = jnp.sum(grad_hidden.astype(f32), axis=1)
-    up_grad = jnp.einsum("nd,znf->zdf", normed_low, grad_hidden, preferred_element_type=f32).astype(bf16)
-    grad_normed = grad_second + jnp.einsum("znf,zdf->nd", grad_hidden, up_all, preferred_element_type=f32)
+    core = lax.axis_index("core").reshape(1)
+    give_up, keep_up, give_down, keep_down, ffn_back, up_bias_grad = ffn_backward(
+        core, second_low, normed_low, up_all, down_all, active, slope
+    )
+    got_down = lax.ppermute(give_down, "core", PAIR)
+    got_up = lax.ppermute(give_up, "core", PAIR)
+    grad_normed = grad_second + ffn_back
     grad_first, gain_one_grad, shift_one_grad = norm_backward(grad_normed, scaled_one, inv_one, gain_one)
     first_low = grad_first.astype(bf16)
     out_bias_grad = jnp.sum(first_low.astype(f32), axis=0)
     out_grad_w = jnp.einsum("nh,nd->hd", mixed, first_low, preferred_element_type=f32).astype(bf16)
     grad_mixed = jnp.einsum("nd,hd->nh", first_low, out_all, preferred_element_type=f32).astype(bf16)
     grad_mixed = grad_mixed.reshape(groups, local_rows, model_width)
-    upstream = swap([grad_mixed], zsize, False)
-    back = [
-        attend_backward(g, bounds, heads[g][1:], heads[g][0], upstream, cosine, sine) for g in range(groups)
-    ]
-    grad_qkv = jnp.concatenate([b[0] for b in back], axis=1)
-    qkv_bias_grad = sum(b[1] for b in back)[:3]
+    upstream = swap(grad_mixed, zsize, False)
+    send_down, keep_down = first_halving(got_down, keep_down, "yx")
+    send_up, keep_up = first_halving(got_up, keep_up, "xy")
+    upstream, send_down, send_up = lax.optimization_barrier((upstream, send_down, send_up))
+    got_down = lax.ppermute(send_down, ORDERS["yx"][0], PAIR)
+    got_up = lax.ppermute(send_up, ORDERS["xy"][0], PAIR)
+    grad_qkv, qkv_bias_grad = attend_backward(bounds, kept, own_mixed, upstream, cosine, sine)
+    grad_qkv, got_down, got_up = lax.optimization_barrier((grad_qkv, got_down, got_up))
+    qkv_bias_grad = qkv_bias_grad[:3]
     by_z = grad_qkv.reshape(3, groups, zsize, local_rows, head_cols)
     qkv_weight_grad = jnp.einsum("zgld,cgzle->cde", token_blocks, by_z, preferred_element_type=f32)
-    input_back = jnp.einsum("cgzle,cde->zgld", by_z, qkv_weight, preferred_element_type=f32).astype(bf16)
+    backs = [
+        jnp.einsum("czle,cde->zld", by_z[:, g], qkv_weight, preferred_element_type=f32).astype(bf16)
+        for g in range(groups)
+    ]
     small = jnp.concatenate(
         [
             out_bias_grad, gain_one_grad, shift_one_grad, down_bias_grad, gain_two_grad, shift_two_grad,
@@ -973,21 +1181,18 @@
     )
     proj_cols = proj_grad.shape[1]
     proj_grad = jnp.pad(proj_grad.astype(bf16), ((0, 0), (0, -proj_cols % 128)))
-    out_grad_w, up_grad, down_grad, qkv_weight_grad, proj_grad, back, small = reduce_end(
+    up_grad, down_grad, out_grad_w, qkv_weight_grad, proj_grad, *back, small = reduce_end(
+        [("xy", keep_up, got_up), ("yx", keep_down, got_down)],
         [
             ("xy", cut(out_grad_w.reshape(zsize, head_cols, model_width), 1)),
-            ("xy", cut(up_grad, 1)),
-            ("yx", cut(down_grad, 1)),
+            ("yx", cut(qkv_weight_grad.astype(bf16), 1)),
+            ("xy", cut(proj_grad[None], 1)),
         ],
-        ("yx", cut(qkv_weight_grad.astype(bf16), 1)),
-        ("xy", cut(proj_grad[None], 1)),
-        input_back.reshape(zsize, rows, model_width),
+        backs,
         small.reshape(8, -1),
         zsize,
     )
-    tokens_grad = grad_first.reshape(groups, local_rows, model_width) + back.astype(f32).reshape(
-        groups, local_rows, model_width
-    )
+    tokens_grad = grad_first.reshape(groups, local_rows, model_width) + jnp.stack(back).astype(f32)
     qkv_weight_grad = qkv_weight_grad.reshape(qkv_weight.shape)
     proj_grad = proj_grad.reshape(model_width, -1)[:, :proj_cols].astype(f32)
     out_grad_w = out_grad_w.reshape(out_weight.shape)

time: 556 us -> 543 us (0.977)
  matrix products: 89.6 us -> 23 us
  Pallas kernels: 400 us -> 422 us
  other arithmetic: 29.1 us -> 48.1 us
  local copies, waits for them, and re-layouts: 29.6 us -> 40.5 us
  starting transfers between devices: 0 us -> 6.85 us
    dot_general x7 -> x2, matrix products: 76 us -> 6.3 us  [per_device(): jnp.einsum('czle,cde->zld', by_z[:, g], qkv_weight, preferred_element_typ...]
    pallas_call x5, Pallas kernels: 243 us -> 265 us  [the longest x1 143 us: reduce_end(): pl.pallas_call(functools.partial(reduce_kernel, zsize, orders, w), out_sh...]
    add x0 -> x2, other arithmetic: none -> 11 us  [first_halving(): return (pick(keep, 1 - i) + pick(got, 1 - i), pick(keep, i) + pick(got, i))]
    unnamed x128 -> x104, local copies, waits for them, and re-layouts: 18.9 us -> 26.8 us
    ppermute x0 -> x4, starting transfers between devices: none -> 6.85 us  [the longest x1 4.37 us: per_device(): got_up = lax.ppermute(send_up, ORDERS['xy'][0], PAIR)]
  transfers between devices with their start and end apart: 0 -> 4, of which waited for: 0 -> 0; matrix products, arithmetic and copies ran while one was open for 0% -> 6% of each run, Pallas kernels for 0% -> 11%
where the time goes in v4:
time: 543 us; the launch traced here: 542 us
  Pallas kernels  422 us (78%)
  other arithmetic  48.1 us (9%)
  local copies, waits for them, and re-layouts  40.5 us (7%)
  matrix products  23 us (4%)
  starting transfers between devices  6.85 us (1%)
    pallas_call x1, Pallas kernels, reduce_end(): pl.pallas_call(functools.partial(reduce_kernel, zsize, orders, w), out_sh...  143 us
    pallas_call x1, Pallas kernels, gather_start(): pl.pallas_call(functools.partial(gather_kernel, zsize, orders), out_shape...  110 us
    pallas_call x2, Pallas kernels, swap(): pl.pallas_call(functools.partial(swap_kernel, zsize, to_rows), out_shape=...  46.4 us
    pallas_call x1, Pallas kernels, attend_forward(): pl.pallas_call(attend_kernel, grid_spec=pltpu.PrefetchScalarGridSpec(num_...  40.1 us
    pallas_call x1, Pallas kernels, attend_backward(): pl.pallas_call(attend_back_kernel, grid_spec=pltpu.PrefetchScalarGridSpec...  36.2 us
    unnamed x104, local copies, waits for them, and re-layouts  26.8 us
    pallas_call x1, Pallas kernels, ffn_backward(): pl.pallas_call(ffn_back_kernel, grid_spec=pltpu.PrefetchScalarGridSpec(nu...  26.2 us
    pallas_call x1, Pallas kernels, ffn_forward(): pl.pallas_call(ffn_kernel, grid=(2 * zsize,), in_specs=[pl.BlockSpec((row...  19.8 us
  transfers between devices with their start and end apart: 4, of which 0 were waited for; matrix products, arithmetic and copies ran while one was open for 6% of the time, Pallas kernels for 11%

profile of v4, /device:TPU:1, one launch (start us, length us, event | category | flops | bytes accessed | tf_op | source)
XLA Modules:
  0.0 541.5 jit_solution(13856685958373240914)
XLA Ops:
  4.6 4.8 fusion.15
  11.1 2.9 pad_maximum_fusion.1
  14.6 110.0 %shard_map.288 = (bf16[4,512,1024]{2,1,0:T(8,128)(2,1)S(1)}, f32[4,8,128]{2,1,0:T(8,128)S(1)}, bf16[4,2,2,2,32,1024]{5,4,3,2,1,0:T(8,128)(2,1)S(1)}, bf16[4,2,2,...) custom-call(bf16[512,1024]{1,0:T(8,128)(2,1)S(1)} %bitcast.150, f32[8,128]{1,0:T(8,128)S(1)} %bitcast.161, ...), custom_call_target="tpu_custom_call" | custom-call | tf_op jit(solution)/shard_map/pallas_call | solution.py:557
  124.6 3.2 copy-done.1
  132.0 40.1 %shard_map.289 = (bf16[2,1024,256]{2,1,0:T(8,128)(2,1)S(1)}, bf16[2,4,1024,128]{3,2,1,0:T(8,128)(2,1)}, bf16[2,4,1024,128]{3,2,1,0:T(8,128)(2,1)}, bf16[2,4,1024,128]{3,2,1,0:T(8,128)(2,1)}, f32[2,4,1024]{2,1,0:T(4,128)S(1)}) custom-call(s32[2,4]{1,0:T(2,128)S(1)} %get-tuple-element.172.lo_ref, s32[2,4]{1,0:T(2,128)S(1)} %get-tuple-element.171.hi_ref, ...), custom_call_target="tpu_custom_call" | custom-call | flops 5368709120 | bytes 5767168 | tf_op jit(solution)/shard_map/pallas_call | solution.py:165
  172.2 22.8 %shard_map.290 = bf16[2,256,1024]{2,1,0:T(8,128)(2,1)S(1)} custom-call(bf16[2,1024,256]{2,1,0:T(8,128)(2,1)S(1)} %get-tuple-element.52.origin.mixed_ref), custom_call_target="tpu_custom_call" | custom-call | tf_op jit(solution)/shard_map/pallas_call | solution.py:401
  197.6 19.8 %shard_map.291 = (bf16[4,512,1024]{2,1,0:T(8,128)(2,1)S(1)}, bf16[4,512,1024]{2,1,0:T(8,128)(2,1)S(1)}, f32[512,1024]{1,0:T(8,128)S(1)}) custom-call(bf16[512,1024]{1,0:T(8,128)(2,1)S(1)} %fusion.9.x_ref.normed_ref, bf16[4,1024,1024]{2,1,0:T(8,128)(2,1)} %bitcast.144, f32[4,1,1024]{2,1,0:T(1,128)S(1)} %bitcast.159, bf16[4,1024,1024]{2,1,0:T(8,128)(2,1)} %bitcast.166), custom_call_target="tpu_custom_call" | custom-call | tf_op jit(solution)/shard_map/pallas_call | solution.py:988
  223.4 2.6 multiply_reduce_fusion
  226.1 4.8 convert_reduce_fusion
  230.9 26.2 %shard_map.292 = (bf16[4,512,1024]{2,1,0:T(8,128)(2,1)}, bf16[4,512,1024]{2,1,0:T(8,128)(2,1)S(1)}, bf16[4,512,1024]{2,1,0:T(8,128)(2,1)}, bf16[4,512,1024]{2,1,...) custom-call(s32[1]{0:T(128)} %bitcast.14.core_ref, ...), custom_call_target="tpu_custom_call" | custom-call | tf_op jit(solution)/shard_map/pallas_call | solution.py:1047
  262.9 4.1 multiply_reduce_fusion.1
  269.9 23.5 %shard_map.293.do_ref = bf16[2,1024,256]{2,1,0:T(8,128)(2,1)S(1)} custom-call(bf16[2,256,1024]{2,1,0:T(8,128)(2,1)S(1)} %bitcast.154), custom_call_target="tpu_custom_call" | custom-call | tf_op jit(solution)/shard_map/pallas_call | solution.py:401
  295.7 6.1 %fusion.6 = (bf16[4,2,128,1024]{3,2,1,0:T(8,128)(2,1)}, bf16[4,2,128,1024]{3,2,1,0:T(8,128)(2,1)}) fusion(bf16[4,2,2,128,1024]{4,3,2,1,0:T(8,128)(2,1)} %bitcast.20, s32[]{:T(128)S(6)} %select_n.64, bf16[4,2,2,128,1024]{4,3,2,1,0:T(8,128)(2,1)} %bitcast.170, s32[]{:T(128)S(6)} %select_n.63), kind=kLoop, calls=%fused_computation.13 | loop fusion | flops 2097152 | bytes 12582920 | tf_op jit(solution)/shard_map/add | solution.py:1082
  301.8 4.9 fusion.5
  306.7 4.4 collective-permute-start.3
  321.7 4.4 convolution_convert_fusion
  326.1 36.2 %shard_map.294 = (bf16[3,2,1024,256]{3,2,1,0:T(8,128)(2,1)}, f32[8,256]{1,0:T(8,128)S(1)}) custom-call(s32[2,4]{1,0:T(2,128)S(1)} %get-tuple-element.172.lo_ref, s32[2,4]{1,0:T(2,128)S(1)} %get-tuple-element.171.hi_ref, bf16[2,4,1024,128]{3,2,1,0:T(8,128)(2,1)} %get-tuple-element.65.q_ref, bf16[2,4,1024,128]{3,2,1,0:T(8,128)(2,1)} %get-tuple-element.66.k_ref, ...), custom_call_target="tpu_custom_call" | custom-call | flops 5368709120 | bytes 6291456 | tf_op jit(solution)/shard_map/pallas_call | solution.py:289
  366.2 3.1 bitcast_convert_fusion.refs_8_
  369.4 3.2 bitcast_convert_fusion.1.refs_7_
  373.3 4.5 fusion.12
  380.4 143.0 %shard_map.295 = (bf16[2,2,2,128,1024]{4,3,2,1,0:T(8,128)(2,1)}, bf16[2,2,2,128,1024]{4,3,2,1,0:T(8,128)(2,1)}, bf16[2,2,2,32,1024]{4,3,2,1,0:T(8,128)(2,1)S(1)}...) custom-call(bf16[4,2,128,1024]{3,2,1,0:T(8,128)(2,1)} %get-tuple-ele, ...), custom_call_target="tpu_custom_call" | custom-call | tf_op jit(solution)/shard_map/pallas_call | solution.py:942
  523.5 4.3 bitcast_convert_fusion.3
  527.8 2.6 bitcast_convert_fusion.4
  538.2 3.4 convert_add_fusion.1
  (159 shorter events, 55.2 us)
Async XLA Ops:
  0.6 221.9 %copy-start = (bf16[1024,288]{0,1:T(8,128)(2,1)S(1)}, bf16[1024,288]{0,1:T(8,128)(2,1)}, u32[]{:S(2)}) copy-start(bf16[1024,288]{0,1:T(8,128)(2,1)} %param.31) | copy-start | bytes 1769476
  4.3 5.2 copy-start.38
  4.6 9.4 %copy-start.19 = (bf16[256,1024]{1,0:T(8,128)(2,1)S(1)}, bf16[256,1024]{1,0:T(8,128)(2,1)}, u32[]{:S(2)}) copy-start(bf16[256,1024]{1,0:T(8,128)(2,1)} %param.21) | copy-start | bytes 1572868
  9.5 4.6 copy-start.9
  14.1 115.8 %copy-start.10 = (f32[2,1024,128]{2,1,0:T(8,128)}, f32[2,1024,128]{2,1,0:T(8,128)S(1)}, u32[]{:S(2)}) copy-start(f32[2,1024,128]{2,1,0:T(8,128)S(1)} %get-tuple-element.174.sin_ref) | copy-start | bytes 3145732
  14.6 115.3 %copy-start.18 = (s32[2,1024,1]{2,1,0:T(8,128)S(1)}, s32[2,1024,1]{2,1,0:T(8,128)}, u32[]{:S(2)}) copy-start(s32[2,1024,1]{2,1,0:T(8,128)} %copy.59.seg_ref) | copy-start | bytes 24580
  14.6 115.3 %copy-start.29 = (f32[3,256]{1,0:T(4,128)S(1)}, f32[3,256]{1,0:T(4,128)}, u32[]{:S(2)}) copy-start(f32[3,256]{1,0:T(4,128)} %b_ref.1) | copy-start | bytes 9220
  129.8 65.2 %copy-start.25 = (bf16[4,2,2,2,32,1024]{5,4,3,2,1,0:T(8,128)(2,1)}, bf16[4,2,2,2,32,1024]{5,4,3,2,1,0:T(8,128)(2,1)S(1)}, u32[]{:S(2)}) copy-start(bf16[4,2,2,2,32,1024]{5,4,3,2,1,0:T(8,128)(2,1)S(1)} %get-tuple-element.53) | copy-start | bytes 6291460
  172.1 24.3 %copy-start.12 = (bf16[2,1024,256]{2,1,0:T(8,128)(2,1)}, bf16[2,1024,256]{2,1,0:T(8,128)(2,1)S(1)}, u32[]{:S(2)}) copy-start(bf16[2,1024,256]{2,1,0:T(8,128)(2,1)S(1)} %get-tuple-element.52.origin.mixed_ref) | copy-start | bytes 3145732
  172.2 22.9 %copy-start.45 = (f32[1024]{0:T(1024)S(1)}, f32[1024]{0:T(1024)}, u32[]{:S(2)}) copy-start(f32[1024]{0:T(1024)} %param.22) | copy-start | bytes 12292
  196.4 23.0 %copy-start.30 = (f32[512,1024]{1,0:T(8,128)}, f32[512,1024]{1,0:T(8,128)S(1)}, u32[]{:S(2)}) copy-start(f32[512,1024]{1,0:T(8,128)S(1)} %get-tuple-element.169) | copy-start | bytes 6291460
  197.6 21.8 %copy-start.43 = (f32[1024]{0:T(1024)S(1)}, f32[1024]{0:T(1024)}, u32[]{:S(2)}) copy-start(f32[1024]{0:T(1024)} %param.28) | copy-start | bytes 12292
  221.4 4.7 copy-start.32
  260.4 35.3 %collective-permute-start.1 = (bf16[4,512,1024]{2,1,0:T(8,128)(2,1)}, bf16[4,512,1024]{2,1,0:T(8,128)(2,1)}, u32[]{:S(2)}, u32[]{:S(2)}) collective-permute-start(bf16[4,512,1024]{2,1,0:T(8,128)(2,1)} %get-tuple-element.64), channel_id=1, source_target_pairs={{0,4},{4,0},{1,5},{5,1},{2,6},{6,2},{3,7},{7,3},{8,12},{12,8},{9,1... | collective-permute-start | bytes 12582920 | tf_op jit(solution)/shard_map/ppermute | solution.py:1149
  262.9 38.9 %collective-permute-start = (bf16[4,512,1024]{2,1,0:T(8,128)(2,1)}, bf16[4,512,1024]{2,1,0:T(8,128)(2,1)}, u32[]{:S(2)}, u32[]{:S(2)}) collective-permute-start(bf16[4,512,1024]{2,1,0:T(8,128)(2,1)} %get-tuple-element.62), channel_id=1, source_target_pairs={{0,4},{4,0},{1,5},{5,1},{2,6},{6,2},{3,7},{7,3},{8,12},{12,8},{9,1... | collective-permute-start | bytes 12582920 | tf_op jit(solution)/shard_map/ppermute | solution.py:1150
  269.9 24.5 %copy-start.34 = (bf16[512,1024]{1,0:T(8,128)(2,1)S(1)}, bf16[512,1024]{1,0:T(8,128)(2,1)}, u32[]{:S(2)}) copy-start(bf16[512,1024]{1,0:T(8,128)(2,1)} %get-tuple-element.158) | copy-start | bytes 3145732
  295.7 6.1 %copy-start.3 = (bf16[4,512,1024]{2,1,0:T(8,128)(2,1)S(1)}, bf16[4,512,1024]{2,1,0:T(8,128)(2,1)}, u32[]{:S(2)}) copy-start(bf16[4,512,1024]{2,1,0:T(8,128)(2,1)} %copy-done.2) | copy-start | bytes 12582916
  306.7 57.2 %collective-permute-start.2 = (bf16[4,2,128,1024]{3,2,1,0:T(8,128)(2,1)}, bf16[4,2,128,1024]{3,2,1,0:T(8,128)(2,1)}, u32[]{:S(2)}, u32[]{:S(2)}) collective-permute-start(bf16[4,2,128,1024]{3,2,1,0:T(8,128)(2,1)} %get-tuple-element.71), channel_id=1, source_target_pairs={{0,8},{8,0},{1,9},{9,1},{2,10},{10,2},{3,11},{11,3},{4,12},{12,4},... | collective-permute-start | bytes 6291464 | tf_op jit(solution)/shard_map/ppermute | solution.py:1162
  306.7 57.2 %collective-permute-start.3 = (bf16[4,2,128,1024]{3,2,1,0:T(8,128)(2,1)}, bf16[4,2,128,1024]{3,2,1,0:T(8,128)(2,1)}, u32[]{:S(2)}, u32[]{:S(2)}) collective-permute-start(bf16[4,2,128,1024]{3,2,1,0:T(8,128)(2,1)} %get-tuple-element.72), channel_id=1, source_target_pairs={{0,16},{16,0},{1,17},{17,1},{2,18},{18,2},{3,19},{19,3},{4,20},{20... | collective-permute-start | bytes 6291464 | tf_op jit(solution)/shard_map/ppermute | solution.py:1163
  312.3 9.4 %copy-start.15 = (bf16[2,256,1024]{2,1,0:T(8,128)(2,1)S(1)}, bf16[2,256,1024]{2,1,0:T(8,128)(2,1)}, u32[]{:S(2)}) copy-start(bf16[2,256,1024]{2,1,0:T(8,128)(2,1)} %copy-done.14) | copy-start | bytes 3145732
  321.7 4.4 copy-start.11
  321.7 4.4 copy-start.13
  321.7 4.4 copy-start.17
  523.5 4.3 copy-start.20
  (26 other events, 60.5 us)

commit v5 on v4

--- a/solution.py
+++ b/solution.py
@@ -16,31 +16,27 @@
 ALL = DP + ("z",)
 f32 = jnp.float32
 bf16 = jnp.bfloat16
+VMEM = 60 * 1024 * 1024
 
 
 def doc_positions(segment_rows):
-    length = segment_rows.shape[-1]
-    row_index = jnp.broadcast_to(jnp.arange(length, dtype=jnp.int32), segment_rows.shape)
-    change = jnp.concatenate(
-        [
-            jnp.ones(segment_rows.shape[:-1] + (1,), jnp.bool_),
-            segment_rows[..., 1:] != segment_rows[..., :-1],
-        ],
-        axis=-1,
-    )
-    doc_start = lax.cummax(
-        jnp.where(change, row_index, jnp.zeros_like(row_index)), axis=segment_rows.ndim - 1
-    )
-    return row_index - doc_start
-
-
-def rotary_tables(positions, head_dim):
-    half_dim = head_dim // 2
-    exponent = jnp.arange(half_dim, dtype=f32) * (2.0 / head_dim)
+    below = segment_rows[:, None, :] < jnp.arange(4, dtype=jnp.int32)[None, :, None]
+    starts = jnp.sum(below, axis=2, dtype=jnp.int32)
+    row_index = jnp.arange(segment_rows.shape[1], dtype=jnp.int32)[None]
+    start = starts[:, 3:4]
+    for doc in (2, 1, 0):
+        start = jnp.where(segment_rows == doc, starts[:, doc:doc + 1], start)
+    return row_index - start
+
+
+def rotary_tables(positions):
+    half_dim = HEAD_DIM // 2
+    lane = jnp.arange(2 * HEAD_DIM, dtype=jnp.int32)
+    exponent = (lane % half_dim).astype(f32) * (2.0 / HEAD_DIM)
     frequency = jnp.exp(-exponent * math.log(10000.0))
+    sign = jnp.where(lane % HEAD_DIM < half_dim, -1.0, 1.0)
     angles = positions.astype(f32)[..., None] * frequency
-    angles = jnp.concatenate([angles, angles], axis=-1)
-    return (jnp.cos(angles), jnp.sin(angles))
+    return (jnp.cos(angles), jnp.sin(angles) * sign)
 
 
 def norm_forward(field, gain, shift):
@@ -129,17 +125,18 @@
 
         def key_block(j, carry):
             keys_at = pl.ds(pl.multiple_of(j * BLOCK, BLOCK), BLOCK)
+            st = [scores_of(k_ref[0, h, keys_at, :], q_ref[0, h, at, :]) for h in range(heads)]
+            peak = m_ref[...]
+            new = jnp.maximum(peak, jnp.concatenate([jnp.max(t, axis=0, keepdims=True) for t in st], axis=0))
+            p = [jnp.exp(st[h] - new[h:h + 1, :]) for h in range(heads)]
+            old = jnp.exp(peak - new)
+            m_ref[...] = new
+            l_ref[...] = l_ref[...] * old + jnp.concatenate([jnp.sum(t, axis=0, keepdims=True) for t in p], axis=0)
+            part = [
+                jnp.dot(vt_ref[h, :, keys_at], p[h].astype(bf16), preferred_element_type=f32) for h in range(heads)
+            ]
             for h in range(heads):
-                st = scores_of(k_ref[0, h, keys_at, :], q_ref[0, h, at, :])
-                peak = m_ref[h:h + 1, :]
-                new = jnp.maximum(peak, jnp.max(st, axis=0, keepdims=True))
-                p = jnp.exp(st - new)
-                old = jnp.exp(peak - new)
-                m_ref[h:h + 1, :] = new
-                l_ref[h:h + 1, :] = l_ref[h:h + 1, :] * old + jnp.sum(p, axis=0, keepdims=True)
-                acc_ref[h] = acc_ref[h] * old + jnp.dot(
-                    vt_ref[h, :, keys_at], p.astype(bf16), preferred_element_type=f32
-                )
+                acc_ref[h] = acc_ref[h] * old[h:h + 1, :] + part[h]
             return carry
 
         lax.fori_loop(lo_ref[group, i], hi_ref[group, i], key_block, 0)
@@ -188,7 +185,7 @@
             like((groups, heads, length, pair), bf16), like((groups, heads, length, pair), bf16),
             like((groups, heads, length, pair), bf16), like((groups, heads, length), f32),
         ],
-        compiler_params=pltpu.CompilerParams(vmem_limit_bytes=48 * 1024 * 1024),
+        compiler_params=pltpu.CompilerParams(vmem_limit_bytes=VMEM),
         cost_estimate=pl.CostEstimate(
             flops=groups * (2 * length * width * 3 * cols + 4 * length * length * cols),
             bytes_accessed=2 * length * width + 6 * width * cols + 8 * length * cols,
@@ -197,40 +194,41 @@
     )(*bounds, tokens, weight, bias, cosine, sine, docs)
 
 
-def attend_back_kernel(lo_ref, hi_ref, q_ref, k_ref, v_ref, lse_ref, mixed_ref, do_ref, cos_ref, sin_ref,
-                       grad_ref, sum_ref, dox_ref, kt_ref, delta_ref, dk_ref, dv_ref, dqt_ref):
+def attend_back_kernel(lo_ref, hi_ref, z_ref, q_ref, k_ref, v_ref, lse_ref, mixed_ref, cos_ref, sin_ref, tok_ref, w_ref, *refs):
+    do_refs, refs = refs[:tok_ref.shape[0]], refs[tok_ref.shape[0]:]
+    (back_ref, wgrad_ref, sum_ref, grad_ref, wsum_ref, dox_ref, kt_ref, delta_ref, dk_ref, dv_ref, dqt_ref) = refs
     group = pl.program_id(0)
     heads, length = q_ref.shape[1], q_ref.shape[2]
     pair = 2 * HEAD_DIM
     scale = HEAD_DIM ** (-0.5)
     blocks = length // BLOCK
 
-    def prepare(i, carry):
-        at = pl.ds(pl.multiple_of(i * BLOCK, BLOCK), BLOCK)
-        low = lax.broadcasted_iota(jnp.int32, (BLOCK, pair), 1) < HEAD_DIM
+    zsize, _, rows, _ = tok_ref.shape
+    low_half = lax.broadcasted_iota(jnp.int32, (rows, pair), 1) < HEAD_DIM
+    for step in range(zsize):
+        at = pl.ds(pl.multiple_of(lax.rem(z_ref[0] + zsize - step, zsize) * rows, rows), rows)
         for j in range(heads // 2):
-            upstream = do_ref[0, at, j * pair:(j + 1) * pair].astype(f32)
+            upstream = do_refs[step][0, :, j * pair:(j + 1) * pair].astype(f32)
             product = (upstream * mixed_ref[0, at, j * pair:(j + 1) * pair].astype(f32)).T
             for h in range(2):
                 head = 2 * j + h
                 one = upstream if h == 0 else pltpu.roll(upstream, HEAD_DIM, 1)
-                dox_ref[head, at, :] = jnp.where(low, one, 0.0).astype(bf16)
+                dox_ref[head, at, :] = jnp.where(low_half, one, 0.0).astype(bf16)
                 delta_ref[head:head + 1, at] = jnp.sum(
                     product[h * HEAD_DIM:(h + 1) * HEAD_DIM], axis=0, keepdims=True
                 )
                 kt_ref[head, :, at] = k_ref[0, head, at, :].astype(f32).T[:HEAD_DIM].astype(bf16)
-                dk_ref[head, at, :] = jnp.zeros((BLOCK, pair), f32)
-                dv_ref[head, at, :] = jnp.zeros((BLOCK, pair), f32)
-        return carry
-
-    lax.fori_loop(0, blocks, prepare, 0)
+                dk_ref[head, at, :] = jnp.zeros((rows, pair), f32)
+                dv_ref[head, at, :] = jnp.zeros((rows, pair), f32)
+
     @pl.when(group == 0)
     def _():
         sum_ref[...] = jnp.zeros(sum_ref.shape, f32)
+        wsum_ref[...] = jnp.zeros(wsum_ref.shape, f32)
 
     def put(c, j, at, field):
         low = field.astype(bf16)
-        grad_ref[c, 0, at, j * pair:(j + 1) * pair] = low
+        grad_ref[c, at, j * pair:(j + 1) * pair] = low
         cols = pl.ds(j * pair, pair)
         sum_ref[c:c + 1, cols] = sum_ref[c:c + 1, cols] + jnp.sum(low.astype(f32), axis=0, keepdims=True)
 
@@ -243,18 +241,20 @@
 
         def key_block(j, carry):
             keys_at = pl.ds(pl.multiple_of(j * BLOCK, BLOCK), BLOCK)
-            for h in range(heads):
-                queries = q_ref[0, h, at, :]
-                upstream = dox_ref[h, at, :]
-                st = scores_of(k_ref[0, h, keys_at, :], queries)
-                p = jnp.exp(st - lse_ref[0, h:h + 1, at])
-                dp = scores_of(v_ref[0, h, keys_at, :], upstream)
-                ds = (p * (dp - delta_ref[h:h + 1, at])).astype(bf16)
-                dv_ref[h, keys_at, :] = dv_ref[h, keys_at, :] + jnp.dot(
-                    p.astype(bf16), upstream, preferred_element_type=f32
-                )
-                dk_ref[h, keys_at, :] = dk_ref[h, keys_at, :] + jnp.dot(ds, queries, preferred_element_type=f32)
-                dqt_ref[h] = dqt_ref[h] + jnp.dot(kt_ref[h, :, keys_at], ds, preferred_element_type=f32)
+            every = range(heads)
+            queries = [q_ref[0, h, at, :] for h in every]
+            upstream = [dox_ref[h, at, :] for h in every]
+            st = [scores_of(k_ref[0, h, keys_at, :], queries[h]) for h in every]
+            dp = [scores_of(v_ref[0, h, keys_at, :], upstream[h]) for h in every]
+            p = [jnp.exp(st[h] - lse_ref[0, h:h + 1, at]) for h in every]
+            ds = [(p[h] * (dp[h] - delta_ref[h:h + 1, at])).astype(bf16) for h in every]
+            dv = [jnp.dot(p[h].astype(bf16), upstream[h], preferred_element_type=f32) for h in every]
+            dk = [jnp.dot(ds[h], queries[h], preferred_element_type=f32) for h in every]
+            dq = [jnp.dot(kt_ref[h, :, keys_at], ds[h], preferred_element_type=f32) for h in every]
+            for h in every:
+                dv_ref[h, keys_at, :] = dv_ref[h, keys_at, :] + dv[h]
+                dk_ref[h, keys_at, :] = dk_ref[h, keys_at, :] + dk[h]
+                dqt_ref[h] = dqt_ref[h] + dq[h]
             return carry
 
         lax.fori_loop(lo_ref[group, i], hi_ref[group, i], key_block, 0)
@@ -277,10 +277,29 @@
 
     lax.fori_loop(0, blocks, finish, 0)
 
-
-def attend_backward(bounds, kept, mixed, upstream, cosine, sine):
+    def onward(i, carry):
+        at = pl.ds(pl.multiple_of(i * rows, rows), rows)
+        total = None
+        x = tok_ref[i, 0]
+        for c in range(3):
+            grad = grad_ref[c, at, :]
+            part = lax.dot_general(grad, w_ref[c], (((1,), (1,)), ((), ())), preferred_element_type=f32)
+            total = part if total is None else total + part
+            wsum_ref[c] += lax.dot_general(x, grad, (((0,), (0,)), ((), ())), preferred_element_type=f32)
+        back_ref[0, i] = total.astype(bf16)
+        return carry
+
+    lax.fori_loop(0, zsize, onward, 0)
+
+    @pl.when(group == pl.num_programs(0) - 1)
+    def _():
+        wgrad_ref[...] = wsum_ref[...].astype(bf16)
+
+
+def attend_backward(bounds, zi, kept, mixed, upstream, cosine, sine, tokens, weight):
     queries, keys, values, lse = kept
     groups, heads, length, pair = queries.shape
+    zsize, _, rows, width = tokens.shape
     cols = heads * HEAD_DIM
     whole = lambda shape: pl.BlockSpec(shape, lambda i, *_: (0,) * len(shape))
     of_group = lambda shape: pl.BlockSpec(shape, lambda i, *_: (i,) + (0,) * (len(shape) - 1))
@@ -289,26 +308,28 @@
     return pl.pallas_call(
         attend_back_kernel,
         grid_spec=pltpu.PrefetchScalarGridSpec(
-            num_scalar_prefetch=2,
+            num_scalar_prefetch=3,
             grid=(groups,),
             in_specs=[of_group((1,) + wide)] * 3 + [
                 of_group((1, heads, length)), of_group((1, length, cols)),
-                of_group((1, length, cols)), of_group((1, length, pair)), of_group((1, length, pair)),
-            ],
-            out_specs=[
-                pl.BlockSpec((3, 1, length, cols), lambda i, *_: (0, i, 0, 0)), whole((8, cols)),
-            ],
+                of_group((1, length, pair)), of_group((1, length, pair)),
+                pl.BlockSpec((zsize, 1, rows, width), lambda i, *_: (0, i, 0, 0)), whole(weight.shape),
+            ] + [of_group((1, rows, cols))] * zsize,
+            out_specs=[of_group((1, zsize, rows, width)), whole(weight.shape), whole((8, cols))],
             scratch_shapes=[
+                pltpu.VMEM((3, length, cols), bf16), pltpu.VMEM(weight.shape, f32),
                 pltpu.VMEM(wide, bf16), pltpu.VMEM((heads, HEAD_DIM, length), bf16), pltpu.VMEM((heads, length), f32),
                 pltpu.VMEM(wide, f32), pltpu.VMEM(wide, f32), pltpu.VMEM((heads, HEAD_DIM, BLOCK), f32),
             ],
         ),
-        out_shape=[like((3, groups, length, cols), bf16), like((8, cols), f32)],
-        compiler_params=pltpu.CompilerParams(vmem_limit_bytes=48 * 1024 * 1024),
+        out_shape=[
+            like((groups, zsize, rows, width), bf16), like(weight.shape, bf16), like((8, cols), f32),
+        ],
+        compiler_params=pltpu.CompilerParams(vmem_limit_bytes=VMEM),
         cost_estimate=pl.CostEstimate(
             flops=groups * 10 * length * length * cols, bytes_accessed=24 * length * cols, transcendentals=length * length * heads
         ),
-    )(*bounds, queries, keys, values, lse, mixed, upstream, cosine, sine)
+    )(*bounds, zi.reshape(1), queries, keys, values, lse, mixed, cosine, sine, tokens, weight, *upstream)
 
 
 MESH_ID = pl.DeviceIdType.MESH
@@ -410,7 +431,7 @@
             pltpu.SemaphoreType.DMA((zsize, groups)),
         ],
         compiler_params=pltpu.CompilerParams(
-            collective_id=2 if to_rows else 3, has_side_effects=True, vmem_limit_bytes=8 * 1024 * 1024
+            collective_id=2 if to_rows else 3, has_side_effects=True, vmem_limit_bytes=VMEM
         ),
     )(array)
 
@@ -567,7 +588,7 @@
             pltpu.SemaphoreType.DMA((2 * (zsize - 1), n, 3)),
         ],
         compiler_params=pltpu.CompilerParams(
-            collective_id=0, has_side_effects=True, vmem_limit_bytes=32 * 1024 * 1024
+            collective_id=0, has_side_effects=True, vmem_limit_bytes=VMEM
         ),
     )(tokens, bias, *shards)
 
@@ -589,12 +610,12 @@
     p = len(orders) - n
     items = n + p
     pieces, came, refs = refs[:p], refs[p:2 * p], refs[2 * p:]
-    parts, backs, small = refs[:n], refs[n:n + w], refs[n + w]
-    pos = n + w + 1
-    piece_out, part_out, back_out = refs[pos:pos + p], refs[pos + p:pos + p + n], refs[pos + p + n:pos + p + n + w]
-    small_out = refs[pos + p + n + w]
+    parts, backs, small = refs[:n], refs[n], refs[n + 1]
+    pos = n + 2
+    piece_out, part_out, back_out = refs[pos:pos + p], refs[pos + p:pos + p + n], refs[pos + p + n]
+    small_out = refs[pos + p + n + 1]
     outs = list(part_out) + list(piece_out)
-    pos += p + n + w + 1
+    pos += p + n + 2
     mine = refs[pos:pos + items + w]
     pos += items + w
     got_c, got_1, got_2 = refs[pos:pos + n], refs[pos + n:pos + n + items], refs[pos + n + items:pos + n + 2 * items]
@@ -616,7 +637,7 @@
     steps = [(1, b) for b in range(few)] + [(2, 0)] + [(0, b) for b in turn]
 
     def load(k, b):
-        src = parts[k].at[b, c] if k < n else pieces[k - n].at[b] if k < items else backs[k - items].at[b]
+        src = parts[k].at[b, c] if k < n else pieces[k - n].at[b] if k < items else backs.at[k - items, b]
         return pltpu.make_async_copy(src, mine[k].at[b], local_sem.at[k, b])
 
     def load_came(k, b):
@@ -874,7 +895,7 @@
     fill(later, 3)
     line_slot(line_backs, zsize - 1)
     finish_back = [
-        pltpu.make_async_copy(mine[k].at[z], back_out[k - items], local_sem.at[k, 0]) for k in line_backs
+        pltpu.make_async_copy(mine[k].at[z], back_out.at[k - items], local_sem.at[k, 0]) for k in line_backs
     ]
     for copy in finish_back:
         copy.start()
@@ -915,20 +936,20 @@
     piece_arrays = [a for _, a, _ in pieces]
     came = [a for _, _, a in pieces]
     arrays = [a for _, a in parts]
-    p, n, w = len(pieces), len(parts), len(backs)
+    p, n, w = len(pieces), len(parts), backs.shape[0]
     shapes = [a.shape for a in arrays]
     like = jax.ShapeDtypeStruct
     outs = [like((2, 2, 2) + a.shape[2:], bf16) for a in piece_arrays]
     outs += [like(s if i == 1 else s[1:], bf16) for i, s in enumerate(shapes)]
-    outs += [like(a.shape[1:], bf16) for a in backs] + [like(small.shape, f32)]
+    outs += [like((w,) + backs.shape[2:], bf16), like(small.shape, f32)]
     held = lambda shape: pltpu.VMEM(shape, bf16)
     scratch = [held((s[0],) + s[2:]) for s in shapes]
-    scratch += [held(a.shape) for a in piece_arrays + backs]
+    scratch += [held(a.shape) for a in piece_arrays] + [held(backs.shape[1:])] * w
     scratch += [held((s[0],) + s[2:]) for s in shapes]
     scratch += [held((s[0],) + s[3:]) for s in shapes] + [held(a.shape) for a in piece_arrays]
     scratch += [held((s[0],) + s[4:]) for s in shapes] + [held(a.shape[:1] + a.shape[2:]) for a in piece_arrays]
     scratch += [held((zsize + 1,) + shapes[0][4:])]
-    scratch += [held((zsize + 1,) + a.shape[2:]) for a in piece_arrays] + [held((zsize + 1,) + a.shape[1:]) for a in backs]
+    scratch += [held((zsize + 1,) + a.shape[2:]) for a in piece_arrays] + [held((zsize + 1,) + backs.shape[2:])] * w
     scratch += [pltpu.VMEM((4,) + small.shape, f32), pltpu.VMEM((3,) + small.shape, f32)]
     scratch += [pltpu.VMEM(small.shape, f32)] * 2 + [held(shapes[2][4:])] * 2
     dma = pltpu.SemaphoreType.DMA
@@ -942,13 +963,13 @@
     return pl.pallas_call(
         functools.partial(reduce_kernel, zsize, orders, w),
         out_shape=outs,
-        in_specs=[HBM] * (n + 2 * p + w + 1),
-        out_specs=[HBM] * (n + p + w + 1),
+        in_specs=[HBM] * (n + 2 * p + 2),
+        out_specs=[HBM] * (n + p + 2),
         scratch_shapes=scratch,
         compiler_params=pltpu.CompilerParams(
-            collective_id=1, has_side_effects=True, vmem_limit_bytes=48 * 1024 * 1024
+            collective_id=1, has_side_effects=True, vmem_limit_bytes=VMEM
         ),
-    )(*piece_arrays, *came, *arrays, *backs, small)
+    )(*piece_arrays, *came, *arrays, backs, small)
 
 
 def gelu_pair(v):
@@ -998,7 +1019,7 @@
         out_shape=[
             like((zsize, rows, units), bf16), like((zsize, rows, units), bf16), like((rows, width), f32),
         ],
-        compiler_params=pltpu.CompilerParams(vmem_limit_bytes=40 * 1024 * 1024),
+        compiler_params=pltpu.CompilerParams(vmem_limit_bytes=VMEM),
     )(normed_low, up_all, up_bias[:, None, :], down_all)
 
 
@@ -1066,7 +1087,7 @@
             like((zsize, tile, width), bf16), like((zsize, tile, width), bf16),
             like((rows, width), f32), like((zsize, 1, units), f32),
         ],
-        compiler_params=pltpu.CompilerParams(vmem_limit_bytes=40 * 1024 * 1024),
+        compiler_params=pltpu.CompilerParams(vmem_limit_bytes=VMEM),
     )(core, second_low, normed_low, up_all, down_all, active, slope)
 
 
@@ -1080,6 +1101,32 @@
     i = lax.axis_index(ORDERS[order][0])
     pick = lambda array, j: lax.dynamic_index_in_dim(array, j, 1, keepdims=False)
     return pick(keep, 1 - i) + pick(got, 1 - i), pick(keep, i) + pick(got, i)
+
+
+def widen_kernel(up_ref, down_ref, out_ref, qkv_ref, first_ref, back_ref, up_o, down_o, out_o, qkv_o, first_o):
+    for source, target in ((up_ref, up_o), (down_ref, down_o), (out_ref, out_o), (qkv_ref, qkv_o)):
+        target[...] = source[...].astype(f32)
+    first_o[...] = first_ref[...] + back_ref[...].astype(f32)
+
+
+def widen(up, down, out, qkv, first, back):
+    steps = 8
+
+    def rows_of(array):
+        return pl.BlockSpec((array.shape[0] // steps, array.shape[1]), lambda i: (i, 0))
+
+    arrays = [up, down, out]
+    specs = [rows_of(a) for a in arrays]
+    specs.append(pl.BlockSpec((3, qkv.shape[1] // steps, qkv.shape[2]), lambda i: (0, i, 0)))
+    specs.append(rows_of(first))
+    return pl.pallas_call(
+        widen_kernel,
+        grid=(steps,),
+        in_specs=specs + [rows_of(back)],
+        out_specs=specs,
+        out_shape=[jax.ShapeDtypeStruct(a.shape, f32) for a in arrays + [qkv, first]],
+        compiler_params=pltpu.CompilerParams(vmem_limit_bytes=VMEM),
+    )(up, down, out, qkv, first, back)
 
 
 def per_device(blocks, tokens, segments, qkv_weight, qkv_bias, out_weight, out_bias, gain_one, shift_one,
@@ -1091,11 +1138,7 @@
     units_here = up_weight.shape[1]
     rows = groups * local_rows
     zi = lax.axis_index("z")
-    cosine, sine = rotary_tables(doc_positions(segments), HEAD_DIM)
-    half = HEAD_DIM // 2
-    signs = jnp.where(jnp.arange(2 * HEAD_DIM) % HEAD_DIM < half, -1.0, 1.0)
-    cosine = jnp.concatenate([cosine, cosine], axis=-1)
-    sine = jnp.concatenate([sine, sine], axis=-1) * signs
+    cosine, sine = rotary_tables(doc_positions(segments))
     firsts = segments[:, ::BLOCK]
     lasts = segments[:, BLOCK - 1::BLOCK]
     bounds = (
@@ -1155,21 +1198,21 @@
     out_grad_w = jnp.einsum("nh,nd->hd", mixed, first_low, preferred_element_type=f32).astype(bf16)
     grad_mixed = jnp.einsum("nd,hd->nh", first_low, out_all, preferred_element_type=f32).astype(bf16)
     grad_mixed = grad_mixed.reshape(groups, local_rows, model_width)
-    upstream = swap(grad_mixed, zsize, False)
+    upstream = []
+    for step in range(zsize):
+        part = lax.dynamic_slice_in_dim(grad_mixed, lax.rem(zi + step, zsize) * head_cols, head_cols, 2)
+        ring = [(i, (i + step) % zsize) for i in range(zsize)]
+        upstream.append(lax.ppermute(part, "z", ring) if step else part)
     send_down, keep_down = first_halving(got_down, keep_down, "yx")
     send_up, keep_up = first_halving(got_up, keep_up, "xy")
-    upstream, send_down, send_up = lax.optimization_barrier((upstream, send_down, send_up))
+    upstream, send_down, send_up = lax.optimization_barrier((tuple(upstream), send_down, send_up))
     got_down = lax.ppermute(send_down, ORDERS["yx"][0], PAIR)
     got_up = lax.ppermute(send_up, ORDERS["xy"][0], PAIR)
-    grad_qkv, qkv_bias_grad = attend_backward(bounds, kept, own_mixed, upstream, cosine, sine)
-    grad_qkv, got_down, got_up = lax.optimization_barrier((grad_qkv, got_down, got_up))
+    backs, qkv_weight_grad, qkv_bias_grad = attend_backward(
+        bounds, zi, kept, own_mixed, upstream, cosine, sine, token_blocks, qkv_weight
+    )
+    backs, got_down, got_up = lax.optimization_barrier((backs, got_down, got_up))
     qkv_bias_grad = qkv_bias_grad[:3]
-    by_z = grad_qkv.reshape(3, groups, zsize, local_rows, head_cols)
-    qkv_weight_grad = jnp.einsum("zgld,cgzle->cde", token_blocks, by_z, preferred_element_type=f32)
-    backs = [
-        jnp.einsum("czle,cde->zld", by_z[:, g], qkv_weight, preferred_element_type=f32).astype(bf16)
-        for g in range(groups)
-    ]
     small = jnp.concatenate(
         [
             out_bias_grad, gain_one_grad, shift_one_grad, down_bias_grad, gain_two_grad, shift_two_grad,
@@ -1181,18 +1224,17 @@
     )
     proj_cols = proj_grad.shape[1]
     proj_grad = jnp.pad(proj_grad.astype(bf16), ((0, 0), (0, -proj_cols % 128)))
-    up_grad, down_grad, out_grad_w, qkv_weight_grad, proj_grad, *back, small = reduce_end(
+    up_grad, down_grad, out_grad_w, qkv_weight_grad, proj_grad, back, small = reduce_end(
         [("xy", keep_up, got_up), ("yx", keep_down, got_down)],
         [
             ("xy", cut(out_grad_w.reshape(zsize, head_cols, model_width), 1)),
-            ("yx", cut(qkv_weight_grad.astype(bf16), 1)),
+            ("yx", cut(qkv_weight_grad, 1)),
             ("xy", cut(proj_grad[None], 1)),
         ],
         backs,
         small.reshape(8, -1),
         zsize,
     )
-    tokens_grad = grad_first.reshape(groups, local_rows, model_width) + jnp.stack(back).astype(f32)
     qkv_weight_grad = qkv_weight_grad.reshape(qkv_weight.shape)
     proj_grad = proj_grad.reshape(model_width, -1)[:, :proj_cols].astype(f32)
     out_grad_w = out_grad_w.reshape(out_weight.shape)
@@ -1204,6 +1246,9 @@
         )
         small, proj_grad = lax.psum((small, proj_grad), ("xb", "yb"))
     small = small.reshape(-1)
+    up_grad, down_grad, out_grad_w, qkv_weight_grad, tokens_grad = widen(
+        up_grad, down_grad, out_grad_w, qkv_weight_grad, grad_first, back.reshape(rows, model_width)
+    )
     base = 6 * model_width
     vec = [small[i * model_width:(i + 1) * model_width] for i in range(6)]
     up_bias_grad = lax.dynamic_slice(small, (base + zi * units_here,), (units_here,))
@@ -1214,14 +1259,14 @@
     return (
         result_low.reshape(shape3),
         embedded.reshape(groups, local_rows, -1),
-        tokens_grad,
-        qkv_weight_grad.astype(f32),
+        tokens_grad.reshape(shape3),
+        qkv_weight_grad,
         qkv_bias_grad,
-        out_grad_w.astype(f32),
+        out_grad_w,
         vec[0], vec[1], vec[2],
-        up_grad.astype(f32),
+        up_grad,
         up_bias_grad,
-        down_grad.astype(f32),
+        down_grad,
         vec[3], vec[4], vec[5],
         proj_grad,
     )

time: 543 us -> 490 us (0.902)
  local copies, waits for them, and re-layouts: 40.5 us -> 16.2 us
  other arithmetic: 48.1 us -> 33 us
  Pallas kernels: 422 us -> 408 us
  matrix products: 23 us -> 13.9 us
  waiting for transfers between devices: 0.01 us -> 5.44 us
    pallas_call x2 -> x1, Pallas kernels: 46.4 us -> 22.8 us  [swap(): pl.pallas_call(functools.partial(swap_kernel, zsize, to_rows), out_shape=...]
    unnamed x104 -> x51, local copies, waits for them, and re-layouts: 26.8 us -> 6.62 us
    dot_general x3 -> x0, matrix products: 10.8 us -> none  [the longest x2 6.3 us: per_device(): jnp.einsum('czle,cde->zld', by_z[:, g], qkv_weight, preferred_element_typ...]
    pallas_call x1, Pallas kernels: 40.1 us -> 29.5 us  [attend_forward(): pl.pallas_call(attend_kernel, grid_spec=pltpu.PrefetchScalarGridSpec(num_...]
    pallas_call x0 -> x1, Pallas kernels: none -> 10.1 us  [widen(): pl.pallas_call(widen_kernel, grid=(steps,), in_specs=specs + [rows_of(bac...]
    convert_element_type x4 -> x0, other arithmetic: 10.1 us -> none  [the longest x1 4.3 us: per_device(): down_grad.astype(f32)]
  transfers between devices with their start and end apart: 4 -> 7, of which waited for: 0 -> 1; matrix products, arithmetic and copies ran while one was open for 6% -> 6% of each run, Pallas kernels for 11% -> 8%
where the time goes in v5:
time: 490 us; the launch traced here: 487 us
  Pallas kernels  408 us (83%)
  other arithmetic  33 us (7%)
  local copies, waits for them, and re-layouts  16.2 us (3%)
  matrix products  13.9 us (3%)
  starting transfers between devices  9.38 us (2%)
  waiting for transfers between devices  5.44 us (1%)
    pallas_call x1, Pallas kernels, reduce_end(): pl.pallas_call(functools.partial(reduce_kernel, zsize, orders, w), out_sh...  147 us
    pallas_call x1, Pallas kernels, gather_start(): pl.pallas_call(functools.partial(gather_kernel, zsize, orders), out_shape...  110 us
    pallas_call x1, Pallas kernels, attend_backward(): pl.pallas_call(attend_back_kernel, grid_spec=pltpu.PrefetchScalarGridSpec...  39.8 us
    pallas_call x1, Pallas kernels, attend_forward(): pl.pallas_call(attend_kernel, grid_spec=pltpu.PrefetchScalarGridSpec(num_...  29.5 us
    pallas_call x1, Pallas kernels, ffn_backward(): pl.pallas_call(ffn_back_kernel, grid_spec=pltpu.PrefetchScalarGridSpec(nu...  27.9 us
    pallas_call x1, Pallas kernels, swap(): pl.pallas_call(functools.partial(swap_kernel, zsize, to_rows), out_shape=...  22.8 us
    pallas_call x1, Pallas kernels, ffn_forward(): pl.pallas_call(ffn_kernel, grid=(2 * zsize,), in_specs=[pl.BlockSpec((row...  21.2 us
    add x2, other arithmetic, first_halving(): return (pick(keep, 1 - i) + pick(got, 1 - i), pick(keep, i) + pick(got, i))  10.7 us
  transfers between devices with their start and end apart: 7, of which 1 were waited for; matrix products, arithmetic and copies ran while one was open for 6% of the time, Pallas kernels for 8%

profile of v5, /device:TPU:1, one launch (start us, length us, event | category | flops | bytes accessed | tf_op | source)
XLA Modules:
  0.0 487.0 jit_solution(2084767345020098350)
XLA Ops:
  3.4 2.0 copy.62.seg_ref
  6.8 5.5 %fusion.5 = (f32[2,1024,128]{2,1,0:T(8,128)}, f32[2,1024,128]{2,1,0:T(8,128)}) fusion(f32[128]{0:T(128)S(1)} %get-tuple-element.212, f32[128]{0:T(128)S(1)} %get-tuple-element.213, f32[2,1024]{1,0:T(2,128)S(1)} %fusion.7), kind=kLoop, calls=%fused_computation.34 | loop fusion | flops 524288 | bytes 2106368 | tf_op jit(solution)/shard_map/mul | solution.py:39
  12.4 109.6 %shard_map.288 = (bf16[4,512,1024]{2,1,0:T(8,128)(2,1)}, f32[4,8,128]{2,1,0:T(8,128)}, bf16[4,2,2,2,32,1024]{5,4,3,2,1,0:T(8,128)(2,1)}, bf16[4,2,2,2,128,1024]{...) custom-call(bf16[512,1024]{1,0:T(8,128)(2,1)} %bitcast.103, f32[8,128]{1,0:T(8,128)} %bitcast.119, ...), custom_call_target="tpu_custom_call" | custom-call | tf_op jit(solution)/shard_map/pallas_call | solution.py:578
  122.0 29.5 %shard_map.289 = (bf16[2,1024,256]{2,1,0:T(8,128)(2,1)}, bf16[2,4,1024,128]{3,2,1,0:T(8,128)(2,1)}, bf16[2,4,1024,128]{3,2,1,0:T(8,128)(2,1)}, bf16[2,4,1024,128]{3,2,1,0:T(8,128)(2,1)}, f32[2,4,1024]{2,1,0:T(4,128)}) custom-call(s32[2,4]{1,0:T(2,128)} %get-tuple-element.211.lo_ref, s32[2,4]{1,0:T(2,128)} %get-tuple-element.210.hi_ref, ...), custom_call_target="tpu_custom_call" | custom-call | flops 5368709120 | bytes 5767168 | tf_op jit(solution)/shard_map/pallas_call | solution.py:162
  151.5 22.8 %shard_map.290 = bf16[2,256,1024]{2,1,0:T(8,128)(2,1)} custom-call(bf16[2,1024,256]{2,1,0:T(8,128)(2,1)} %get-tuple-element.60.origin.mixed_ref), custom_call_target="tpu_custom_call" | custom-call | tf_op jit(solution)/shard_map/pallas_call | solution.py:422
  174.4 3.5 fusion.17
  180.0 21.2 %shard_map.291 = (bf16[4,512,1024]{2,1,0:T(8,128)(2,1)}, bf16[4,512,1024]{2,1,0:T(8,128)(2,1)}, f32[512,1024]{1,0:T(8,128)}) custom-call(bf16[512,1024]{1,0:T(8,128)(2,1)} %fusion.4.x_ref.normed_ref, bf16[4,1024,1024]{2,1,0:T(8,128)(2,1)} %bitcast.86, f32[4,1,1024]{2,1,0:T(1,128)} %bitcast.116, bf16[4,1024,1024]{2,1,0:T(8,128)(2,1)} %bitcast.88), custom_call_target="tpu_custom_call" | custom-call | tf_op jit(solution)/shard_map/pallas_call | solution.py:1009
  201.2 2.3 fusion.15
  205.6 2.6 multiply_reduce_fusion
  208.3 5.1 %convert_reduce_fusion = (f32[1024]{0:T(1024)S(1)}, bf16[512,1024]{1,0:T(8,128)(2,1)}, f32[512,1024]{1,0:T(8,128)}, bf16[512,1024]{1,0:T(8,128)(2,1)}) fusion(f32[512]{0:T(512)S(1)} %broadcast_multiply_fusion.2, f32[512,1024]{1,0:T(8,128)} %copy-done.1, f32[512]{0:T(512)S(1)} %broadcast_multiply_fusion.4, f32[512]{0:T(512)S(1)} %broadcast_multiply_fusion.3, ...), kind=kLoop, calls=%fused_computation.10 | loop fusion | flops 6814720 | bytes 8409088 | tf_op jit(solution)/shard_map/reduce_sum | solution.py:1187
  213.4 27.9 %shard_map.292 = (bf16[4,512,1024]{2,1,0:T(8,128)(2,1)}, bf16[4,512,1024]{2,1,0:T(8,128)(2,1)}, bf16[4,512,1024]{2,1,0:T(8,128)(2,1)}, bf16[4,512,1024]{2,1,0:T(...) custom-call(s32[1]{0:T(128)} %bitcast.13.core_ref, bf16[512,1024]{1,0:T(8,128)(2,1)} %get-tuple-element.182.second_ref, ...), custom_call_target="tpu_custom_call" | custom-call | tf_op jit(solution)/shard_map/pallas_call | solution.py:1068
  241.3 2.7 collective-permute-start.1
  244.1 3.2 multiply_reduce_fusion.1
  251.1 2.0 collective-permute-start.2
  256.5 6.0 %fusion.1 = (bf16[4,2,128,1024]{3,2,1,0:T(8,128)(2,1)}, bf16[4,2,128,1024]{3,2,1,0:T(8,128)(2,1)}) fusion(bf16[4,2,2,128,1024]{4,3,2,1,0:T(8,128)(2,1)} %bitcast.19, s32[]{:T(128)S(6)} %select_n.98, bf16[4,2,2,128,1024]{4,3,2,1,0:T(8,128)(2,1)} %bitcast.91, s32[]{:T(128)S(6)} %select_n.93), kind=kLoop, calls=%fused_computation.3 | loop fusion | flops 2097152 | bytes 12582920 | tf_op jit(solution)/shard_map/add | solution.py:1103
  262.5 4.7 fusion
  267.2 5.4 %collective-permute-done.3.refs_2_ = bf16[2,256,256]{2,1,0:T(8,128)(2,1)S(1)} collective-permute-done((bf16[2,256,256]{2,1,0:T(8,128)(2,1)S(1)}, bf16[2,256,256]{2,1,0:T(8,128)(2,1)S(1)}, u32[]{:S(2)}, u32[]{:S(2)}) %collective-permute-start.3) | collective-permute-done | bytes 262176 | tf_op jit(solution)/shard_map/ppermute | solution.py:1205
  272.7 1.5 collective-permute-start.5
  276.4 1.6 copy.84
  278.0 1.7 copy.89
  280.8 3.9 convolution_convert_fusion
  284.6 39.8 %shard_map.293 = (bf16[2,4,256,1024]{3,2,1,0:T(8,128)(2,1)}, bf16[3,1024,256]{2,1,0:T(8,128)(2,1)}, f32[8,256]{1,0:T(8,128)}) custom-call(s32[2,4]{1,0:T(2,128)} %get-tuple-element.211.lo_ref, s32[2,4]{1,0:T(2,128)} %get-tuple-element.210.hi_ref, s32[1]{0:T(128)} %bitcast.21.z_ref, bf16[2,4,1024,128]{3,2,1,0:T(8,128)(2,1)} %get-tuple-element.72.q_ref, ...), custom_call_target="tpu_custom_call" | custom-call | flops 5368709120 | bytes 6291456 | tf_op jit(solution)/shard_map/pallas_call | solution.py:308
  325.9 147.1 %shard_map.294 = (bf16[2,2,2,128,1024]{4,3,2,1,0:T(8,128)(2,1)}, bf16[2,2,2,128,1024]{4,3,2,1,0:T(8,128)(2,1)}, bf16[2,2,2,32,1024]{4,3,2,1,0:T(8,128)(2,1)}, bf...) custom-call(bf16[4,2,128,1024]{3,2,1,0:T(8,128)(2,1)} %get-tuple-ele, ...), custom_call_target="tpu_custom_call" | custom-call | tf_op jit(solution)/shard_map/pallas_call | solution.py:963
  476.8 10.1 %shard_map.295 = (f32[1024,1024]{1,0:T(8,128)}, f32[1024,1024]{1,0:T(8,128)}, f32[256,1024]{1,0:T(8,128)}, f32[3,1024,256]{2,1,0:T(8,128)}, f32[512,1024]{1,0:T(8,128)}) custom-call(bf16[1024,1024]{1,0:T(8,128)(2,1)} %bitcast.96, bf16[1024,1024]{1,0:T(8,128)(2,1)} %bitcast.97, bf16[256,1024]{1,0:T(8,128)(2,1)} %bitcast.111, bf16[3,1024,256]{2,1,0:T(8,128)(2,1)} %bitcast.99, ...), custom_call_target="tpu_custom_call" | custom-call | tf_op jit(solution)/shard_map/pallas_call | solution.py:1122
  (95 shorter events, 24.1 us)
Async XLA Ops:
  0.6 204.1 %copy-start = (bf16[1024,288]{0,1:T(8,128)(2,1)S(1)}, bf16[1024,288]{0,1:T(8,128)(2,1)}, u32[]{:S(2)}) copy-start(bf16[1024,288]{0,1:T(8,128)(2,1)} %param.31) | copy-start | bytes 1769476
  151.5 22.9 %copy-start.19 = (f32[1024]{0:T(1024)S(1)}, f32[1024]{0:T(1024)}, u32[]{:S(2)}) copy-start(f32[1024]{0:T(1024)} %param.22) | copy-start | bytes 12292
  180.0 21.2 %copy-start.13 = (f32[1024]{0:T(1024)S(1)}, f32[1024]{0:T(1024)}, u32[]{:S(2)}) copy-start(f32[1024]{0:T(1024)} %param.28) | copy-start | bytes 12292
  203.5 4.7 copy-start.1
  203.6 1.2 copy-start.11
  203.6 2.0 copy-start.15
  205.6 2.7 copy-start.12
  241.3 15.2 %collective-permute-start.1 = (bf16[4,512,1024]{2,1,0:T(8,128)(2,1)}, bf16[4,512,1024]{2,1,0:T(8,128)(2,1)}, u32[]{:S(2)}, u32[]{:S(2)}) collective-permute-start(bf16[4,512,1024]{2,1,0:T(8,128)(2,1)} %get-tuple-element.71), channel_id=1, source_target_pairs={{0,4},{4,0},{1,5},{5,1},{2,6},{6,2},{3,7},{7,3},{8,12},{12,8},{9,1... | collective-permute-start | bytes 12582920 | tf_op jit(solution)/shard_map/ppermute | solution.py:1192
  244.0 18.5 %collective-permute-start = (bf16[4,512,1024]{2,1,0:T(8,128)(2,1)}, bf16[4,512,1024]{2,1,0:T(8,128)(2,1)}, u32[]{:S(2)}, u32[]{:S(2)}) collective-permute-start(bf16[4,512,1024]{2,1,0:T(8,128)(2,1)} %get-tuple-element.69), channel_id=1, source_target_pairs={{0,4},{4,0},{1,5},{5,1},{2,6},{6,2},{3,7},{7,3},{8,12},{12,8},{9,1... | collective-permute-start | bytes 12582920 | tf_op jit(solution)/shard_map/ppermute | solution.py:1193
  247.3 1.6 copy-start.14
  248.0 2.2 copy-start.2
  250.2 5.1 %copy-start.5 = (bf16[512,1024]{1,0:T(8,128)(2,1)S(1)}, bf16[512,1024]{1,0:T(8,128)(2,1)}, u32[]{:S(2)}) copy-start(bf16[512,1024]{1,0:T(8,128)(2,1)} %get-tuple-element.193) | copy-start | bytes 3145732
  251.1 16.1 %collective-permute-start.2 = (bf16[2,256,256]{2,1,0:T(8,128)(2,1)}, bf16[2,256,256]{2,1,0:T(8,128)(2,1)S(1)}, u32[]{:S(2)}, u32[]{:S(2)}) collective-permute-start(bf16[2,256,256]{2,1,0:T(8,128)(2,1)} %get-tuple-element.196), channel_id=1, source_target_pairs={{0,1},{1,2},{2,3},{3,0},{4,5},{5,6},{6,7},{7,4},{8,9},{9,10},{10,1... | collective-permute-start | bytes 786440 | tf_op jit(solution)/shard_map/ppermute | solution.py:1205
  253.2 19.5 %collective-permute-start.3 = (bf16[2,256,256]{2,1,0:T(8,128)(2,1)S(1)}, bf16[2,256,256]{2,1,0:T(8,128)(2,1)S(1)}, u32[]{:S(2)}, u32[]{:S(2)}) collective-permute-start(bf16[2,256,256]{2,1,0:T(8,128)(2,1)S(1)} %get-tuple-element.195), channel_id=1, source_target_pairs={{0,2},{1,3},{2,0},{3,1},{4,6},{5,7},{6,4},{7,5},{8,10},{9,11},{10,... | collective-permute-start | bytes 786440 | tf_op jit(solution)/shard_map/ppermute | solution.py:1205
  254.3 18.4 %collective-permute-start.4 = (bf16[2,256,256]{2,1,0:T(8,128)(2,1)S(1)}, bf16[2,256,256]{2,1,0:T(8,128)(2,1)S(1)}, u32[]{:S(2)}, u32[]{:S(2)}) collective-permute-start(bf16[2,256,256]{2,1,0:T(8,128)(2,1)S(1)} %get-tuple-element.194), channel_id=1, source_target_pairs={{0,3},{1,0},{2,1},{3,2},{4,7},{5,4},{6,5},{7,6},{8,11},{9,8},{10,9... | collective-permute-start | bytes 786440 | tf_op jit(solution)/shard_map/ppermute | solution.py:1205
  256.5 6.0 %copy-start.4 = (bf16[4,512,1024]{2,1,0:T(8,128)(2,1)S(1)}, bf16[4,512,1024]{2,1,0:T(8,128)(2,1)}, u32[]{:S(2)}) copy-start(bf16[4,512,1024]{2,1,0:T(8,128)(2,1)} %get-tuple-element.68) | copy-start | bytes 12582916
  267.2 7.9 %copy-start.16 = (bf16[2,256,256]{2,1,0:T(8,128)(2,1)}, bf16[2,256,256]{2,1,0:T(8,128)(2,1)S(1)}, u32[]{:S(2)}) copy-start(bf16[2,256,256]{2,1,0:T(8,128)(2,1)S(1)} %collective-permute-done.2.refs_1_) | copy-start | bytes 786436
  272.6 2.5 copy-start.17
  272.7 2.5 copy-start.18
  272.7 53.2 %collective-permute-start.5 = (bf16[4,2,128,1024]{3,2,1,0:T(8,128)(2,1)}, bf16[4,2,128,1024]{3,2,1,0:T(8,128)(2,1)}, u32[]{:S(2)}, u32[]{:S(2)}) collective-permute-start(bf16[4,2,128,1024]{3,2,1,0:T(8,128)(2,1)} %get-tuple-element.82), channel_id=1, source_target_pairs={{0,8},{8,0},{1,9},{9,1},{2,10},{10,2},{3,11},{11,3},{4,12},{12,4},... | collective-permute-start | bytes 6291464 | tf_op jit(solution)/shard_map/ppermute | solution.py:1209
  274.2 51.7 %collective-permute-start.6 = (bf16[4,2,128,1024]{3,2,1,0:T(8,128)(2,1)}, bf16[4,2,128,1024]{3,2,1,0:T(8,128)(2,1)}, u32[]{:S(2)}, u32[]{:S(2)}) collective-permute-start(bf16[4,2,128,1024]{3,2,1,0:T(8,128)(2,1)} %get-tuple-element.83), channel_id=1, source_target_pairs={{0,16},{16,0},{1,17},{17,1},{2,18},{18,2},{3,19},{19,3},{4,20},{20... | collective-permute-start | bytes 6291464 | tf_op jit(solution)/shard_map/ppermute | solution.py:1210
  276.4 4.3 copy-start.9
  276.4 4.3 copy-start.3
  472.9 2.6 copy-start.8
  (3 other events, 2.5 us)

commit v6 on v5

--- a/solution.py
+++ b/solution.py
@@ -194,16 +194,18 @@
     )(*bounds, tokens, weight, bias, cosine, sine, docs)
 
 
-def attend_back_kernel(lo_ref, hi_ref, z_ref, q_ref, k_ref, v_ref, lse_ref, mixed_ref, cos_ref, sin_ref, tok_ref, w_ref, *refs):
-    do_refs, refs = refs[:tok_ref.shape[0]], refs[tok_ref.shape[0]:]
-    (back_ref, wgrad_ref, sum_ref, grad_ref, wsum_ref, dox_ref, kt_ref, delta_ref, dk_ref, dv_ref, dqt_ref) = refs
-    group = pl.program_id(0)
+def attend_back_kernel(group, last, lo_ref, hi_ref, z_ref, q_ref, k_ref, v_ref, lse_ref, mixed_ref, cos_ref, sin_ref, tok_ref, w_ref, *refs):
+    zsize, _, rows, _ = tok_ref.shape
+    do_refs, refs = refs[:zsize], refs[zsize:]
+    if group:
+        before_ref, refs = refs[0], refs[1:]
+    back_refs, refs = refs[:1 if last else zsize], refs[1 if last else zsize:]
+    wgrad_ref, sum_ref, grad_ref, wsum_ref, dox_ref, kt_ref, delta_ref, dk_ref, dv_ref, dqt_ref = refs
     heads, length = q_ref.shape[1], q_ref.shape[2]
     pair = 2 * HEAD_DIM
     scale = HEAD_DIM ** (-0.5)
     blocks = length // BLOCK
 
-    zsize, _, rows, _ = tok_ref.shape
     low_half = lax.broadcasted_iota(jnp.int32, (rows, pair), 1) < HEAD_DIM
     for step in range(zsize):
         at = pl.ds(pl.multiple_of(lax.rem(z_ref[0] + zsize - step, zsize) * rows, rows), rows)
@@ -221,10 +223,8 @@
                 dk_ref[head, at, :] = jnp.zeros((rows, pair), f32)
                 dv_ref[head, at, :] = jnp.zeros((rows, pair), f32)
 
-    @pl.when(group == 0)
-    def _():
-        sum_ref[...] = jnp.zeros(sum_ref.shape, f32)
-        wsum_ref[...] = jnp.zeros(wsum_ref.shape, f32)
+    sum_ref[...] = jnp.zeros(sum_ref.shape, f32)
+    wsum_ref[...] = before_ref[...] if group else jnp.zeros(wsum_ref.shape, f32)
 
     def put(c, j, at, field):
         low = field.astype(bf16)
@@ -277,7 +277,7 @@
 
     lax.fori_loop(0, blocks, finish, 0)
 
-    def onward(i, carry):
+    def onward(i, target):
         at = pl.ds(pl.multiple_of(i * rows, rows), rows)
         total = None
         x = tok_ref[i, 0]
@@ -286,50 +286,56 @@
             part = lax.dot_general(grad, w_ref[c], (((1,), (1,)), ((), ())), preferred_element_type=f32)
             total = part if total is None else total + part
             wsum_ref[c] += lax.dot_general(x, grad, (((0,), (0,)), ((), ())), preferred_element_type=f32)
-        back_ref[0, i] = total.astype(bf16)
-        return carry
-
-    lax.fori_loop(0, zsize, onward, 0)
-
-    @pl.when(group == pl.num_programs(0) - 1)
-    def _():
-        wgrad_ref[...] = wsum_ref[...].astype(bf16)
-
-
-def attend_backward(bounds, zi, kept, mixed, upstream, cosine, sine, tokens, weight):
+        target[...] = total.astype(bf16)
+
+    for step in range(zsize):
+        if last:
+            onward(step, back_refs[0].at[0, step])
+        else:
+            onward(lax.rem(z_ref[0] + step, zsize), back_refs[step])
+    wgrad_ref[...] = wsum_ref[...].astype(wgrad_ref.dtype)
+
+
+def attend_backward(group, before, bounds, zi, kept, mixed, upstream, cosine, sine, tokens, weight):
     queries, keys, values, lse = kept
     groups, heads, length, pair = queries.shape
     zsize, _, rows, width = tokens.shape
     cols = heads * HEAD_DIM
+    last = group == groups - 1
     whole = lambda shape: pl.BlockSpec(shape, lambda i, *_: (0,) * len(shape))
-    of_group = lambda shape: pl.BlockSpec(shape, lambda i, *_: (i,) + (0,) * (len(shape) - 1))
+    of_group = lambda shape: pl.BlockSpec(shape, lambda i, *_: (group,) + (0,) * (len(shape) - 1))
     like = jax.ShapeDtypeStruct
     wide = (heads, length, pair)
     return pl.pallas_call(
-        attend_back_kernel,
+        functools.partial(attend_back_kernel, group, last),
         grid_spec=pltpu.PrefetchScalarGridSpec(
             num_scalar_prefetch=3,
-            grid=(groups,),
+            grid=(1,),
             in_specs=[of_group((1,) + wide)] * 3 + [
                 of_group((1, heads, length)), of_group((1, length, cols)),
                 of_group((1, length, pair)), of_group((1, length, pair)),
-                pl.BlockSpec((zsize, 1, rows, width), lambda i, *_: (0, i, 0, 0)), whole(weight.shape),
-            ] + [of_group((1, rows, cols))] * zsize,
-            out_specs=[of_group((1, zsize, rows, width)), whole(weight.shape), whole((8, cols))],
+                pl.BlockSpec((zsize, 1, rows, width), lambda i, *_: (0, group, 0, 0)), whole(weight.shape),
+            ] + [of_group((1, rows, cols))] * zsize + [whole(weight.shape)] * (group > 0),
+            out_specs=([whole((1, zsize, rows, width))] if last else [whole((rows, width))] * zsize) + [
+                whole(weight.shape), whole((8, cols)),
+            ],
             scratch_shapes=[
                 pltpu.VMEM((3, length, cols), bf16), pltpu.VMEM(weight.shape, f32),
                 pltpu.VMEM(wide, bf16), pltpu.VMEM((heads, HEAD_DIM, length), bf16), pltpu.VMEM((heads, length), f32),
                 pltpu.VMEM(wide, f32), pltpu.VMEM(wide, f32), pltpu.VMEM((heads, HEAD_DIM, BLOCK), f32),
             ],
         ),
-        out_shape=[
-            like((groups, zsize, rows, width), bf16), like(weight.shape, bf16), like((8, cols), f32),
+        out_shape=([like((1, zsize, rows, width), bf16)] if last else [like((rows, width), bf16)] * zsize) + [
+            like(weight.shape, bf16 if last else f32), like((8, cols), f32),
         ],
         compiler_params=pltpu.CompilerParams(vmem_limit_bytes=VMEM),
         cost_estimate=pl.CostEstimate(
-            flops=groups * 10 * length * length * cols, bytes_accessed=24 * length * cols, transcendentals=length * length * heads
+            flops=0 if last else 40 * length * length * cols,
+            bytes_accessed=0 if last else 48 * length * cols,
+            transcendentals=0 if last else 2 * length * length * heads,
         ),
-    )(*bounds, zi.reshape(1), queries, keys, values, lse, mixed, cosine, sine, tokens, weight, *upstream)
+    )(*bounds, zi.reshape(1), queries, keys, values, lse, mixed, cosine, sine, tokens, weight, *upstream,
+      *([before] if group else []))
 
 
 MESH_ID = pl.DeviceIdType.MESH
@@ -844,9 +850,16 @@
     for k, b in steps:
         stage_1(k, b)
     small_step(0)
-    for k, b in piece_steps:
-        stage_3(k, b)
-    line_start(line_pieces, range(zsize - 1))
+    for b in turn:
+        for k in line_pieces:
+            stage_3(k, b)
+        for side in range(2):
+
+            @pl.when(jnp.logical_and(z == (0 if side == 0 else zsize - 1), z != b))
+            def _():
+                for k in line_pieces:
+                    hop(k, b, side).start()
+
     for k, b in steps:
         stage_2(k, b)
     small_step(1)
@@ -1106,7 +1119,7 @@
 def widen_kernel(up_ref, down_ref, out_ref, qkv_ref, first_ref, back_ref, up_o, down_o, out_o, qkv_o, first_o):
     for source, target in ((up_ref, up_o), (down_ref, down_o), (out_ref, out_o), (qkv_ref, qkv_o)):
         target[...] = source[...].astype(f32)
-    first_o[...] = first_ref[...] + back_ref[...].astype(f32)
+    first_o[...] = first_ref[...] + back_ref[...]
 
 
 def widen(up, down, out, qkv, first, back):
@@ -1205,14 +1218,21 @@
         upstream.append(lax.ppermute(part, "z", ring) if step else part)
     send_down, keep_down = first_halving(got_down, keep_down, "yx")
     send_up, keep_up = first_halving(got_up, keep_up, "xy")
-    upstream, send_down, send_up = lax.optimization_barrier((tuple(upstream), send_down, send_up))
     got_down = lax.ppermute(send_down, ORDERS["yx"][0], PAIR)
     got_up = lax.ppermute(send_up, ORDERS["xy"][0], PAIR)
-    backs, qkv_weight_grad, qkv_bias_grad = attend_backward(
-        bounds, zi, kept, own_mixed, upstream, cosine, sine, token_blocks, qkv_weight
-    )
-    backs, got_down, got_up = lax.optimization_barrier((backs, got_down, got_up))
-    qkv_bias_grad = qkv_bias_grad[:3]
+    qkv_weight_grad, qkv_bias_grad, early = None, 0.0, []
+    for g in range(groups):
+        *backs, qkv_weight_grad, bias_part = attend_backward(
+            g, qkv_weight_grad, bounds, zi, kept, own_mixed, upstream, cosine, sine, token_blocks, qkv_weight
+        )
+        qkv_bias_grad = qkv_bias_grad + bias_part[:3]
+        if g < groups - 1:
+            early.append([
+                lax.ppermute(part, "z", [(i, (i + step) % zsize) for i in range(zsize)]) if step else part
+                for step, part in enumerate(backs)
+            ])
+    backs, got_down, got_up = lax.optimization_barrier((backs[0], got_down, got_up))
+
     small = jnp.concatenate(
         [
             out_bias_grad, gain_one_grad, shift_one_grad, down_bias_grad, gain_two_grad, shift_two_grad,
@@ -1235,6 +1255,7 @@
         small.reshape(8, -1),
         zsize,
     )
+    back, early = lax.optimization_barrier((back, early))
     qkv_weight_grad = qkv_weight_grad.reshape(qkv_weight.shape)
     proj_grad = proj_grad.reshape(model_width, -1)[:, :proj_cols].astype(f32)
     out_grad_w = out_grad_w.reshape(out_weight.shape)
@@ -1247,7 +1268,8 @@
         small, proj_grad = lax.psum((small, proj_grad), ("xb", "yb"))
     small = small.reshape(-1)
     up_grad, down_grad, out_grad_w, qkv_weight_grad, tokens_grad = widen(
-        up_grad, down_grad, out_grad_w, qkv_weight_grad, grad_first, back.reshape(rows, model_width)
+        up_grad, down_grad, out_grad_w, qkv_weight_grad, grad_first,
+        jnp.concatenate([sum(part.astype(f32) for part in parts) for parts in early] + [back[0].astype(f32)]),
     )
     base = 6 * model_width
     vec = [small[i * model_width:(i + 1) * model_width] for i in range(6)]

time: 490 us -> 471 us (0.961)
  Pallas kernels: 408 us -> 389 us
  starting transfers between devices: 9.38 us -> 16 us
  waiting for transfers between devices: 5.44 us -> 0.03 us
  other arithmetic: 33 us -> 38 us
    pallas_call x1, Pallas kernels: 147 us -> 121 us  [reduce_end(): pl.pallas_call(functools.partial(reduce_kernel, zsize, orders, w), out_sh...]
    ppermute x0 -> x3, starting transfers between devices: none -> 6.46 us  [per_device(): lax.ppermute(part, 'z', [(i, (i + step) % zsize) for i in range(zsize)])]
    pallas_call x1 -> x2, Pallas kernels: 39.8 us -> 45.7 us  [attend_backward(): pl.pallas_call(functools.partial(attend_back_kernel, group, last), grid_s...]
    ppermute x3, waiting for transfers between devices: 5.43 us -> 0.01 us  [per_device(): upstream.append(lax.ppermute(part, 'z', ring) if step else part)]
  transfers between devices with their start and end apart: 7 -> 10, of which waited for: 1 -> 0; matrix products, arithmetic and copies ran while one was open for 6% -> 5% of each run, Pallas kernels for 8% -> 35%
where the time goes in v6:
time: 471 us; the launch traced here: 469 us
  Pallas kernels  389 us (83%)
  other arithmetic  38 us (8%)
  starting transfers between devices  16 us (3%)
  local copies, waits for them, and re-layouts  13.6 us (3%)
  matrix products  11 us (2%)
    pallas_call x1, Pallas kernels, reduce_end(): pl.pallas_call(functools.partial(reduce_kernel, zsize, orders, w), out_sh...  121 us
    pallas_call x1, Pallas kernels, gather_start(): pl.pallas_call(functools.partial(gather_kernel, zsize, orders), out_shape...  110 us
    pallas_call x2, Pallas kernels, attend_backward(): pl.pallas_call(functools.partial(attend_back_kernel, group, last), grid_s...  45.7 us
    pallas_call x1, Pallas kernels, attend_forward(): pl.pallas_call(attend_kernel, grid_spec=pltpu.PrefetchScalarGridSpec(num_...  29.9 us
    pallas_call x1, Pallas kernels, ffn_backward(): pl.pallas_call(ffn_back_kernel, grid_spec=pltpu.PrefetchScalarGridSpec(nu...  28 us
    pallas_call x1, Pallas kernels, swap(): pl.pallas_call(functools.partial(swap_kernel, zsize, to_rows), out_shape=...  22.8 us
    pallas_call x1, Pallas kernels, ffn_forward(): pl.pallas_call(ffn_kernel, grid=(2 * zsize,), in_specs=[pl.BlockSpec((row...  21.2 us
    add x2, other arithmetic, first_halving(): return (pick(keep, 1 - i) + pick(got, 1 - i), pick(keep, i) + pick(got, i))  10.8 us
  transfers between devices with their start and end apart: 10, of which 0 were waited for; matrix products, arithmetic and copies ran while one was open for 5% of the time, Pallas kernels for 35%

profile of v6, /device:TPU:1, one launch (start us, length us, event | category | flops | bytes accessed | tf_op | source)
XLA Modules:
  0.0 468.6 jit_solution(10800580875174912345)
XLA Ops:
  3.4 2.0 copy.62.seg_ref
  6.8 5.5 %fusion.5 = (f32[2,1024,128]{2,1,0:T(8,128)}, f32[2,1024,128]{2,1,0:T(8,128)}) fusion(f32[128]{0:T(128)S(1)} %get-tuple-element.222, f32[128]{0:T(128)S(1)} %get-tuple-element.223, f32[2,1024]{1,0:T(2,128)S(1)} %fusion.7), kind=kLoop, calls=%fused_computation.35 | loop fusion | flops 524288 | bytes 2106368 | tf_op jit(solution)/shard_map/mul | solution.py:39
  12.4 109.6 %shard_map.288 = (bf16[4,512,1024]{2,1,0:T(8,128)(2,1)}, f32[4,8,128]{2,1,0:T(8,128)}, bf16[4,2,2,2,32,1024]{5,4,3,2,1,0:T(8,128)(2,1)}, bf16[4,2,2,2,128,1024]{...) custom-call(bf16[512,1024]{1,0:T(8,128)(2,1)} %bitcast.108, f32[8,128]{1,0:T(8,128)} %bitcast.123, ...), custom_call_target="tpu_custom_call" | custom-call | tf_op jit(solution)/shard_map/pallas_call | solution.py:584
  122.0 29.9 %shard_map.289 = (bf16[2,1024,256]{2,1,0:T(8,128)(2,1)}, bf16[2,4,1024,128]{3,2,1,0:T(8,128)(2,1)}, bf16[2,4,1024,128]{3,2,1,0:T(8,128)(2,1)}, bf16[2,4,1024,128]{3,2,1,0:T(8,128)(2,1)}, f32[2,4,1024]{2,1,0:T(4,128)}) custom-call(s32[2,4]{1,0:T(2,128)} %get-tuple-element.221.lo_ref, s32[2,4]{1,0:T(2,128)} %get-tuple-element.220.hi_ref, ...), custom_call_target="tpu_custom_call" | custom-call | flops 5368709120 | bytes 5767168 | tf_op jit(solution)/shard_map/pallas_call | solution.py:162
  151.8 22.8 %shard_map.290 = bf16[2,256,1024]{2,1,0:T(8,128)(2,1)} custom-call(bf16[2,1024,256]{2,1,0:T(8,128)(2,1)} %get-tuple-element.65.origin.mixed_ref), custom_call_target="tpu_custom_call" | custom-call | tf_op jit(solution)/shard_map/pallas_call | solution.py:428
  174.7 3.5 fusion.17
  180.3 21.2 %shard_map.291 = (bf16[4,512,1024]{2,1,0:T(8,128)(2,1)}, bf16[4,512,1024]{2,1,0:T(8,128)(2,1)}, f32[512,1024]{1,0:T(8,128)}) custom-call(bf16[512,1024]{1,0:T(8,128)(2,1)} %fusion.4.x_ref.normed_ref, bf16[4,1024,1024]{2,1,0:T(8,128)(2,1)} %bitcast.88, f32[4,1,1024]{2,1,0:T(1,128)} %bitcast.120, bf16[4,1024,1024]{2,1,0:T(8,128)(2,1)} %bitcast.90), custom_call_target="tpu_custom_call" | custom-call | tf_op jit(solution)/shard_map/pallas_call | solution.py:1022
  201.6 2.3 fusion.15
  205.9 2.6 multiply_reduce_fusion
  208.6 5.1 %convert_reduce_fusion = (f32[1024]{0:T(1024)S(1)}, bf16[512,1024]{1,0:T(8,128)(2,1)}, f32[512,1024]{1,0:T(8,128)}, bf16[512,1024]{1,0:T(8,128)(2,1)}) fusion(f32[512]{0:T(512)S(1)} %broadcast_multiply_fusion.2, f32[512,1024]{1,0:T(8,128)} %copy-done.2, f32[512]{0:T(512)S(1)} %broadcast_multiply_fusion.4, f32[512]{0:T(512)S(1)} %broadcast_multiply_fusion.3, ...), kind=kLoop, calls=%fused_computation.11 | loop fusion | flops 6814720 | bytes 8409088 | tf_op jit(solution)/shard_map/reduce_sum | solution.py:1200
  213.7 28.0 %shard_map.292 = (bf16[4,512,1024]{2,1,0:T(8,128)(2,1)}, bf16[4,512,1024]{2,1,0:T(8,128)(2,1)}, bf16[4,512,1024]{2,1,0:T(8,128)(2,1)}, bf16[4,512,1024]{2,1,0:T(...) custom-call(s32[1]{0:T(128)} %bitcast.13.core_ref, bf16[512,1024]{1,0:T(8,128)(2,1)} %get-tuple-element.192.second_ref, ...), custom_call_target="tpu_custom_call" | custom-call | tf_op jit(solution)/shard_map/pallas_call | solution.py:1081
  241.8 2.7 collective-permute-start.1
  244.5 3.2 multiply_reduce_fusion.1
  251.7 2.0 collective-permute-start.2
  258.9 6.0 %fusion.1 = (bf16[4,2,128,1024]{3,2,1,0:T(8,128)(2,1)}, bf16[4,2,128,1024]{3,2,1,0:T(8,128)(2,1)}) fusion(bf16[4,2,2,128,1024]{4,3,2,1,0:T(8,128)(2,1)} %bitcast.19, s32[]{:T(128)S(6)} %select_n.98, bf16[4,2,2,128,1024]{4,3,2,1,0:T(8,128)(2,1)} %bitcast.93, s32[]{:T(128)S(6)} %select_n.93), kind=kLoop, calls=%fused_computation.4 | loop fusion | flops 2097152 | bytes 12582920 | tf_op jit(solution)/shard_map/add | solution.py:1116
  264.9 2.6 collective-permute-start.5
  267.6 4.8 %fusion = (bf16[4,2,128,1024]{3,2,1,0:T(8,128)(2,1)}, bf16[4,2,128,1024]{3,2,1,0:T(8,128)(2,1)}) fusion(bf16[4,2,2,128,1024]{4,3,2,1,0:T(8,128)(2,1)} %bitcast.16, s32[]{:T(128)S(6)} %select_n.99, bf16[4,2,2,128,1024]{4,3,2,1,0:T(8,128)(2,1)S(1)} %bitcast.92, s32[]{:T(128)S(6)} %select_n.92), kind=kLoop, calls=%fused_computation.2 | loop fusion | flops 2097152 | bytes 12582920 | tf_op jit(solution)/shard_map/add | solution.py:1116
  272.4 2.6 convolution_convert_fusion
  275.0 23.3 %shard_map.293 = (bf16[256,1024]{1,0:T(8,128)(2,1)}, bf16[256,1024]{1,0:T(8,128)(2,1)}, bf16[256,1024]{1,0:T(8,128)(2,1)}, bf16[256,1024]{1,0:T(8,128)(2,1)}, f32[3,1024,256]{2,1,0:T(8,128)}, /*index=5*/f32[8,256]{1,0:T(8,128)}) custom-call(s32[2,4]{1,0:T(2,128)} %get-tuple-element.221.lo_ref, s32[2,4]{1,0:T(2,128)} %get-tuple-element.220.hi_ref, ...), custom_call_target="tpu_custom_call" | custom-call | flops 10737418240 | bytes 12582912 | tf_op jit(solution)/shard_map/pallas_call | solution.py:309
  298.3 4.3 collective-permute-start.7
  302.9 1.8 collective-permute-start.9
  304.7 22.5 %shard_map.294 = (bf16[1,4,256,1024]{3,2,1,0:T(8,128)(2,1)}, bf16[3,1024,256]{2,1,0:T(8,128)(2,1)}, f32[8,256]{1,0:T(8,128)}) custom-call(s32[2,4]{1,0:T(2,128)} %get-tuple-element.221.lo_ref, s32[2,4]{1,0:T(2,128)} %get-tuple-element.220.hi_ref, s32[1]{0:T(128)} %bitcast.21.z_ref, bf16[2,4,1024,128]{3,2,1,0:T(8,128)(2,1)} %get-tuple-element.77.q_ref, ...), custom_call_target="tpu_custom_call" | custom-call | tf_op jit(solution)/shard_map/pallas_call | solution.py:309
  330.0 120.6 %shard_map.295 = (bf16[2,2,2,128,1024]{4,3,2,1,0:T(8,128)(2,1)}, bf16[2,2,2,128,1024]{4,3,2,1,0:T(8,128)(2,1)}, bf16[2,2,2,32,1024]{4,3,2,1,0:T(8,128)(2,1)}, bf...) custom-call(bf16[4,2,128,1024]{3,2,1,0:T(8,128)(2,1)} %get-tuple-ele, ...), custom_call_target="tpu_custom_call" | custom-call | tf_op jit(solution)/shard_map/pallas_call | solution.py:976
  457.6 10.7 %shard_map.296 = (f32[1024,1024]{1,0:T(8,128)}, f32[1024,1024]{1,0:T(8,128)}, f32[256,1024]{1,0:T(8,128)}, f32[3,1024,256]{2,1,0:T(8,128)}, f32[512,1024]{1,0:T(8,128)}) custom-call(bf16[1024,1024]{1,0:T(8,128)(2,1)} %bitcast.100, bf16[1024,1024]{1,0:T(8,128)(2,1)} %bitcast.101, bf16[256,1024]{1,0:T(8,128)(2,1)} %bitcast.115, ...), custom_call_target="tpu_custom_call" | custom-call | tf_op jit(solution)/shard_map/pallas_call | solution.py:1135
  (115 shorter events, 27.5 us)
Async XLA Ops:
  0.6 204.4 %copy-start = (bf16[1024,288]{0,1:T(8,128)(2,1)S(1)}, bf16[1024,288]{0,1:T(8,128)(2,1)}, u32[]{:S(2)}) copy-start(bf16[1024,288]{0,1:T(8,128)(2,1)} %param.31) | copy-start | bytes 1769476
  151.8 22.9 %copy-start.24 = (f32[1024]{0:T(1024)S(1)}, f32[1024]{0:T(1024)}, u32[]{:S(2)}) copy-start(f32[1024]{0:T(1024)} %param.22) | copy-start | bytes 12292
  180.3 21.2 %copy-start.20 = (f32[1024]{0:T(1024)S(1)}, f32[1024]{0:T(1024)}, u32[]{:S(2)}) copy-start(f32[1024]{0:T(1024)} %param.28) | copy-start | bytes 12292
  203.9 4.7 %copy-start.2 = (f32[512,1024]{1,0:T(8,128)}, f32[512,1024]{1,0:T(8,128)S(1)}, u32[]{:S(2)}) copy-start(f32[512,1024]{1,0:T(8,128)S(1)} %get-tuple-element.198) | copy-start | bytes 6291460
  205.9 2.6 copy-start.19
  241.8 17.1 %collective-permute-start.1 = (bf16[4,512,1024]{2,1,0:T(8,128)(2,1)}, bf16[4,512,1024]{2,1,0:T(8,128)(2,1)}, u32[]{:S(2)}, u32[]{:S(2)}) collective-permute-start(bf16[4,512,1024]{2,1,0:T(8,128)(2,1)} %get-tuple-element.76), channel_id=1, source_target_pairs={{0,4},{4,0},{1,5},{5,1},{2,6},{6,2},{3,7},{7,3},{8,12},{12,8},{9,1... | collective-permute-start | bytes 12582920 | tf_op jit(solution)/shard_map/ppermute | solution.py:1205
  244.5 23.1 %collective-permute-start = (bf16[4,512,1024]{2,1,0:T(8,128)(2,1)}, bf16[4,512,1024]{2,1,0:T(8,128)(2,1)}, u32[]{:S(2)}, u32[]{:S(2)}) collective-permute-start(bf16[4,512,1024]{2,1,0:T(8,128)(2,1)} %get-tuple-element.74), channel_id=1, source_target_pairs={{0,4},{4,0},{1,5},{5,1},{2,6},{6,2},{3,7},{7,3},{8,12},{12,8},{9,1... | collective-permute-start | bytes 12582920 | tf_op jit(solution)/shard_map/ppermute | solution.py:1206
  250.6 5.1 %copy-start.6 = (bf16[512,1024]{1,0:T(8,128)(2,1)S(1)}, bf16[512,1024]{1,0:T(8,128)(2,1)}, u32[]{:S(2)}) copy-start(bf16[512,1024]{1,0:T(8,128)(2,1)} %get-tuple-element.203) | copy-start | bytes 3145732
  251.7 23.3 %collective-permute-start.2 = (bf16[2,256,256]{2,1,0:T(8,128)(2,1)}, bf16[2,256,256]{2,1,0:T(8,128)(2,1)}, u32[]{:S(2)}, u32[]{:S(2)}) collective-permute-start(bf16[2,256,256]{2,1,0:T(8,128)(2,1)} %get-tuple-element.206), channel_id=1, source_target_pairs={{0,1},{1,2},{2,3},{3,0},{4,5},{5,6},{6,7},{7,4},{8,9},{9,10},{10,1... | collective-permute-start | bytes 786440 | tf_op jit(solution)/shard_map/ppermute | solution.py:1218
  253.7 21.3 %collective-permute-start.3 = (bf16[2,256,256]{2,1,0:T(8,128)(2,1)}, bf16[2,256,256]{2,1,0:T(8,128)(2,1)}, u32[]{:S(2)}, u32[]{:S(2)}) collective-permute-start(bf16[2,256,256]{2,1,0:T(8,128)(2,1)} %get-tuple-element.205), channel_id=1, source_target_pairs={{0,2},{1,3},{2,0},{3,1},{4,6},{5,7},{6,4},{7,5},{8,10},{9,11},{10,... | collective-permute-start | bytes 786440 | tf_op jit(solution)/shard_map/ppermute | solution.py:1218
  254.8 20.2 %collective-permute-start.4 = (bf16[2,256,256]{2,1,0:T(8,128)(2,1)}, bf16[2,256,256]{2,1,0:T(8,128)(2,1)}, u32[]{:S(2)}, u32[]{:S(2)}) collective-permute-start(bf16[2,256,256]{2,1,0:T(8,128)(2,1)} %get-tuple-element.204), channel_id=1, source_target_pairs={{0,3},{1,0},{2,1},{3,2},{4,7},{5,4},{6,5},{7,6},{8,11},{9,8},{10,9... | collective-permute-start | bytes 786440 | tf_op jit(solution)/shard_map/ppermute | solution.py:1218
  258.9 8.7 %copy-start.5 = (bf16[4,512,1024]{2,1,0:T(8,128)(2,1)S(1)}, bf16[4,512,1024]{2,1,0:T(8,128)(2,1)}, u32[]{:S(2)}) copy-start(bf16[4,512,1024]{2,1,0:T(8,128)(2,1)} %get-tuple-element.73) | copy-start | bytes 12582916
  264.9 63.7 %collective-permute-start.5 = (bf16[4,2,128,1024]{3,2,1,0:T(8,128)(2,1)}, bf16[4,2,128,1024]{3,2,1,0:T(8,128)(2,1)S(1)}, u32[]{:S(2)}, u32[]{:S(2)}) collective-permute-start(bf16[4,2,128,1024]{3,2,1,0:T(8,128)(2,1)} %get-tuple-element.201), channel_id=1, source_target_pairs={{0,8},{8,0},{1,9},{9,1},{2,10},{10,2},{3,11},{11,3},{4,12},{12,4},... | collective-permute-start | bytes 6291464 | tf_op jit(solution)/shard_map/ppermute | solution.py:1221
  267.5 4.8 %copy-start.4 = (f32[512,1024]{1,0:T(8,128)S(1)}, f32[512,1024]{1,0:T(8,128)}, u32[]{:S(2)}) copy-start(f32[512,1024]{1,0:T(8,128)} %copy-done.3) | copy-start | bytes 6291460
  267.6 4.8 %copy-start.8 = (bf16[2,256,1024]{2,1,0:T(8,128)(2,1)S(1)}, bf16[2,256,1024]{2,1,0:T(8,128)(2,1)}, u32[]{:S(2)}) copy-start(bf16[2,256,1024]{2,1,0:T(8,128)(2,1)} %shard_map.290) | copy-start | bytes 3145732
  272.4 56.3 %collective-permute-start.6 = (bf16[4,2,128,1024]{3,2,1,0:T(8,128)(2,1)}, bf16[4,2,128,1024]{3,2,1,0:T(8,128)(2,1)}, u32[]{:S(2)}, u32[]{:S(2)}) collective-permute-start(bf16[4,2,128,1024]{3,2,1,0:T(8,128)(2,1)} %get-tuple-element.199), channel_id=1, source_target_pairs={{0,16},{16,0},{1,17},{17,1},{2,18},{18,2},{3,19},{19,3},{4,20},{20... | collective-permute-start | bytes 6291464 | tf_op jit(solution)/shard_map/ppermute | solution.py:1222
  275.0 29.7 %copy-start.16 = (f32[4,1,1024]{2,1,0:T(1,128)S(1)}, f32[4,1,1024]{2,1,0:T(1,128)}, u32[]{:S(2)}) copy-start(f32[4,1,1024]{2,1,0:T(1,128)} %get-tuple-element.88) | copy-start | bytes 49156
  298.3 152.3 %collective-permute-start.7 = (bf16[256,1024]{1,0:T(8,128)(2,1)}, bf16[256,1024]{1,0:T(8,128)(2,1)S(1)}, u32[]{:S(2)}, u32[]{:S(2)}) collective-permute-start(bf16[256,1024]{1,0:T(8,128)(2,1)} %get-tuple-element.97), channel_id=1, source_target_pairs={{0,1},{1,2},{2,3},{3,0},{4,5},{5,6},{6,7},{7,4},{8,9},{9,10},{10,1... | collective-permute-start | bytes 1572872 | tf_op jit(solution)/shard_map/ppermute | solution.py:1231
  302.6 148.0 %collective-permute-start.8 = (bf16[256,1024]{1,0:T(8,128)(2,1)}, bf16[256,1024]{1,0:T(8,128)(2,1)S(1)}, u32[]{:S(2)}, u32[]{:S(2)}) collective-permute-start(bf16[256,1024]{1,0:T(8,128)(2,1)} %get-tuple-element.98), channel_id=1, source_target_pairs={{0,2},{1,3},{2,0},{3,1},{4,6},{5,7},{6,4},{7,5},{8,10},{9,11},{10,... | collective-permute-start | bytes 1572872 | tf_op jit(solution)/shard_map/ppermute | solution.py:1231
  302.9 147.7 %collective-permute-start.9 = (bf16[256,1024]{1,0:T(8,128)(2,1)}, bf16[256,1024]{1,0:T(8,128)(2,1)}, u32[]{:S(2)}, u32[]{:S(2)}) collective-permute-start(bf16[256,1024]{1,0:T(8,128)(2,1)} %get-tuple-element.99), channel_id=1, source_target_pairs={{0,3},{1,0},{2,1},{3,2},{4,7},{5,4},{6,5},{7,6},{8,11},{9,8},{10,9... | collective-permute-start | bytes 1572872 | tf_op jit(solution)/shard_map/ppermute | solution.py:1231
  304.7 22.5 %copy-start.21 = (f32[8,256]{1,0:T(8,128)S(1)}, f32[8,256]{1,0:T(8,128)}, u32[]{:S(2)}) copy-start(f32[8,256]{1,0:T(8,128)} %get-tuple-element.89) | copy-start | bytes 24580
  450.6 2.9 copy-start.15
  450.6 4.2 copy-start.10
  457.6 10.7 %copy-start.1 = (bf16[1024,288]{0,1:T(8,128)(2,1)S(1)}, bf16[1024,288]{0,1:T(8,128)(2,1)}, u32[]{:S(2)}) copy-start(bf16[1024,288]{0,1:T(8,128)(2,1)} %param.31) | copy-start | bytes 1769476
  (11 other events, 16.3 us)

commit v7 on v6

--- a/solution.py
+++ b/solution.py
@@ -73,9 +73,8 @@
     return lax.dot_general(keys, queries, (((1,), (1,)), ((), ())), preferred_element_type=f32)
 
 
-def attend_kernel(lo_ref, hi_ref, tok_ref, w_ref, b_ref, cos_ref, sin_ref, seg_ref, mixed_ref, q_ref, k_ref, v_ref,
+def attend_kernel(group, lo_ref, hi_ref, tok_ref, w_ref, b_ref, cos_ref, sin_ref, seg_ref, mixed_ref, q_ref, k_ref, v_ref,
                   lse_ref, vt_ref, m_ref, l_ref, acc_ref):
-    group = pl.program_id(0)
     zsize, _, rows, _ = tok_ref.shape
     length = zsize * rows
     heads = q_ref.shape[1]
@@ -150,29 +149,29 @@
     lax.fori_loop(0, length // BLOCK, query_block, 0)
 
 
-def attend_forward(bounds, tokens, weight, bias, cosine, sine, docs):
-    zsize, groups, rows, width = tokens.shape
+def attend_forward(group, bounds, tokens, weight, bias, cosine, sine, docs):
+    zsize, _, rows, width = tokens.shape
     length = zsize * rows
     cols = weight.shape[2]
     heads = cols // HEAD_DIM
     pair = 2 * HEAD_DIM
     whole = lambda shape: pl.BlockSpec(shape, lambda i, *_: (0,) * len(shape))
-    of_group = lambda shape: pl.BlockSpec(shape, lambda i, *_: (i,) + (0,) * (len(shape) - 1))
+    of_group = lambda shape: pl.BlockSpec(shape, lambda i, *_: (group,) + (0,) * (len(shape) - 1))
     like = jax.ShapeDtypeStruct
     return pl.pallas_call(
-        attend_kernel,
+        functools.partial(attend_kernel, group),
         grid_spec=pltpu.PrefetchScalarGridSpec(
             num_scalar_prefetch=2,
-            grid=(groups,),
+            grid=(1,),
             in_specs=[
-                pl.BlockSpec((zsize, 1, rows, width), lambda i, *_: (0, i, 0, 0)),
+                pl.BlockSpec((zsize, 1, rows, width), lambda i, *_: (0, group, 0, 0)),
                 whole(weight.shape), whole(bias.shape),
                 of_group((1, length, pair)), of_group((1, length, pair)), of_group((1, length, 1)),
             ],
             out_specs=[
-                of_group((1, length, cols)),
-                of_group((1, heads, length, pair)), of_group((1, heads, length, pair)), of_group((1, heads, length, pair)),
-                of_group((1, heads, length)),
+                whole((1, length, cols)),
+                whole((1, heads, length, pair)), whole((1, heads, length, pair)), whole((1, heads, length, pair)),
+                whole((1, heads, length)),
             ],
             scratch_shapes=[
                 pltpu.VMEM((heads, HEAD_DIM, length), bf16),
@@ -181,13 +180,13 @@
             ],
         ),
         out_shape=[
-            like((groups, length, cols), bf16),
-            like((groups, heads, length, pair), bf16), like((groups, heads, length, pair), bf16),
-            like((groups, heads, length, pair), bf16), like((groups, heads, length), f32),
+            like((1, length, cols), bf16),
+            like((1, heads, length, pair), bf16), like((1, heads, length, pair), bf16),
+            like((1, heads, length, pair), bf16), like((1, heads, length), f32),
         ],
         compiler_params=pltpu.CompilerParams(vmem_limit_bytes=VMEM),
         cost_estimate=pl.CostEstimate(
-            flops=groups * (2 * length * width * 3 * cols + 4 * length * length * cols),
+            flops=2 * length * width * 3 * cols + 4 * length * length * cols,
             bytes_accessed=2 * length * width + 6 * width * cols + 8 * length * cols,
             transcendentals=length * length * heads,
         ),
@@ -298,8 +297,8 @@
 
 def attend_backward(group, before, bounds, zi, kept, mixed, upstream, cosine, sine, tokens, weight):
     queries, keys, values, lse = kept
-    groups, heads, length, pair = queries.shape
-    zsize, _, rows, width = tokens.shape
+    _, heads, length, pair = queries.shape
+    zsize, groups, rows, width = tokens.shape
     cols = heads * HEAD_DIM
     last = group == groups - 1
     whole = lambda shape: pl.BlockSpec(shape, lambda i, *_: (0,) * len(shape))
@@ -311,11 +310,11 @@
         grid_spec=pltpu.PrefetchScalarGridSpec(
             num_scalar_prefetch=3,
             grid=(1,),
-            in_specs=[of_group((1,) + wide)] * 3 + [
-                of_group((1, heads, length)), of_group((1, length, cols)),
+            in_specs=[whole((1,) + wide)] * 3 + [
+                whole((1, heads, length)), whole((1, length, cols)),
                 of_group((1, length, pair)), of_group((1, length, pair)),
                 pl.BlockSpec((zsize, 1, rows, width), lambda i, *_: (0, group, 0, 0)), whole(weight.shape),
-            ] + [of_group((1, rows, cols))] * zsize + [whole(weight.shape)] * (group > 0),
+            ] + [whole((1, rows, cols))] * zsize + [whole(weight.shape)] * (group > 0),
             out_specs=([whole((1, zsize, rows, width))] if last else [whole((rows, width))] * zsize) + [
                 whole(weight.shape), whole((8, cols)),
             ],
@@ -368,78 +367,6 @@
     return pltpu.make_async_remote_copy(
         src_ref=src, dst_ref=dst, send_sem=send_sem, recv_sem=recv_sem, device_id=device, device_id_type=MESH_ID
     )
-
-
-def swap_kernel(zsize, to_rows, origin, target, held, local_sem, send, recv):
-    groups = target.shape[0]
-    rows, cols = (target.shape[1], target.shape[2] // zsize) if to_rows else (target.shape[1] // zsize, target.shape[2])
-    z = lax.axis_index("z")
-
-    def source(g, peer):
-        if to_rows:
-            return origin.at[g, pl.ds(pl.multiple_of(peer * rows, rows), rows), :]
-        return origin.at[g, :, pl.ds(pl.multiple_of(peer * cols, cols), cols)]
-
-    def place(g, peer):
-        if to_rows:
-            return target.at[g, :, pl.ds(pl.multiple_of(peer * cols, cols), cols)]
-        return target.at[g, pl.ds(pl.multiple_of(peer * rows, rows), rows), :]
-
-    def copy_to(g, step):
-        peer = lax.rem(z + step, zsize)
-        return remote(source(g, peer), place(g, z), send.at[step, g], recv.at[step, g], {"z": peer})
-
-    def copy_from(g, step):
-        peer = lax.rem(z + zsize - step, zsize)
-        return remote(source(g, peer), place(g, peer), send.at[step, g], recv.at[step, g], {"z": peer})
-
-    into = [pltpu.make_async_copy(source(g, z), held.at[g], local_sem.at[0, g]) for g in range(groups)]
-    onward = [pltpu.make_async_copy(held.at[g], place(g, z), local_sem.at[1, g]) for g in range(groups)]
-    for copy in into:
-        copy.start()
-    barrier = pltpu.get_barrier_semaphore()
-    for step in range(1, zsize):
-        peer = lax.rem(z + step, zsize)
-        pl.semaphore_signal(barrier, inc=1, device_id={"z": peer}, device_id_type=MESH_ID)
-    pl.semaphore_wait(barrier, zsize - 1)
-    for g in range(groups):
-        for step in range(1, zsize):
-            copy_to(g, step).start()
-    for g in range(groups):
-        into[g].wait()
-        onward[g].start()
-    for g in range(groups):
-        for step in range(1, zsize):
-            copy_from(g, step).wait_recv()
-        onward[g].wait()
-    for g in range(groups):
-        for step in range(1, zsize):
-            copy_to(g, step).wait_send()
-
-
-def swap(array, zsize, to_rows):
-    groups, rows, cols = array.shape
-    if to_rows:
-        rows //= zsize
-        shape = (groups, rows, zsize * cols)
-    else:
-        cols //= zsize
-        shape = (groups, zsize * rows, cols)
-    return pl.pallas_call(
-        functools.partial(swap_kernel, zsize, to_rows),
-        out_shape=jax.ShapeDtypeStruct(shape, bf16),
-        in_specs=[HBM],
-        out_specs=HBM,
-        scratch_shapes=[
-            pltpu.VMEM((groups, rows, cols), bf16),
-            pltpu.SemaphoreType.DMA((2, groups)),
-            pltpu.SemaphoreType.DMA((zsize, groups)),
-            pltpu.SemaphoreType.DMA((zsize, groups)),
-        ],
-        compiler_params=pltpu.CompilerParams(
-            collective_id=2 if to_rows else 3, has_side_effects=True, vmem_limit_bytes=VMEM
-        ),
-    )(array)
 
 
 ORDERS = {"xy": ("x", "y"), "yx": ("y", "x")}
@@ -601,7 +528,7 @@
 
 def add_rows(dst, src):
     rows = dst.shape[0]
-    step = min(rows, 32)
+    step = math.gcd(rows, 32)
 
     def body(i, carry):
         at = pl.ds(pl.multiple_of(i * step, step), step)
@@ -995,16 +922,43 @@
     return v * cdf, cdf + v * (bell * (1.0 / (2.0 * math.pi) ** 0.5))
 
 
-def ffn_kernel(x_ref, up_ref, bias_ref, down_ref, active_ref, slope_ref, sum_ref):
-    rows = x_ref.shape[0]
-    part = rows // 2
+def norm_rows(field):
+    mean = jnp.mean(field, axis=-1, keepdims=True)
+    centred = field - mean
+    inv_std = lax.rsqrt(jnp.mean(centred * centred, axis=-1, keepdims=True) + eps)
+    return centred * inv_std, inv_std
+
+
+def ffn_kernel(zsize, groups, z_ref, tok_ref, out_ref, out_bias_ref, gain_one_ref, shift_one_ref, up_ref, bias_ref, down_ref,
+               down_bias_ref, gain_two_ref, shift_two_ref, proj_ref, dy_ref, de_ref, *refs):
+    pieces = refs[:zsize * groups]
+    (active_ref, slope_ref, mixed_ref, x_ref, scaled_ref, inv_ref, result_ref, embed_ref, grad_ref, low_ref, proj_grad_ref,
+     vec_ref, normed_ref, sum_ref) = refs[zsize * groups:]
+    rows, width = x_ref.shape
+    local = rows // groups
+    cols = width // zsize
+    chunk = 128
+    heads = proj_ref.shape[0]
 
     @pl.when(pl.program_id(0) == 0)
     def _():
+        for g in range(groups):
+            for step in range(zsize):
+                at = lax.rem(z_ref[0] + zsize - step, zsize) * cols
+                mixed_ref[pl.ds(g * local, local), pl.ds(pl.multiple_of(at, cols), cols)] = pieces[g * zsize + step][0]
+        for i in range(rows // chunk):
+            at = pl.ds(i * chunk, chunk)
+            attended = jnp.dot(mixed_ref[at, :], out_ref[...], preferred_element_type=f32) + out_bias_ref[...]
+            scaled, inv_std = norm_rows(tok_ref[at, :].astype(f32) + attended)
+            normed = scaled * gain_one_ref[...] + shift_one_ref[...]
+            scaled_ref[at, :] = scaled
+            inv_ref[at, :] = inv_std
+            normed_ref[at, :] = normed
+            x_ref[at, :] = normed.astype(bf16)
         sum_ref[...] = jnp.zeros(sum_ref.shape, f32)
 
     for i in range(2):
-        at = pl.ds(i * part, part)
+        at = pl.ds(i * (rows // 2), rows // 2)
         hidden = jnp.dot(x_ref[at, :], up_ref[0], preferred_element_type=f32) + bias_ref[0]
         active, slope = gelu_pair(hidden)
         active = active.astype(bf16)
@@ -1012,28 +966,78 @@
         slope_ref[0, at, :] = slope.astype(bf16)
         sum_ref[at, :] += jnp.dot(active, down_ref[0], preferred_element_type=f32)
 
-
-def ffn_forward(normed_low, up_all, up_bias, down_all):
+    @pl.when(pl.program_id(0) == pl.num_programs(0) - 1)
+    def _():
+        total = [jnp.zeros((1, width), f32)] * 3
+        for i in range(rows // chunk):
+            at = pl.ds(i * chunk, chunk)
+            scaled, inv_std = norm_rows(normed_ref[at, :] + (sum_ref[at, :] + down_bias_ref[...]))
+            result_ref[at, :] = (scaled * gain_two_ref[...] + shift_two_ref[...]).astype(bf16)
+            g, inner = i * chunk // local, i * chunk % local
+            upstream = dy_ref[at, :].astype(f32) + lax.dot_general(
+                de_ref[g, :, inner:inner + chunk], proj_ref[...], (((0,), (0,)), ((), ())), preferred_element_type=f32
+            )
+            grad_scaled = upstream * gain_two_ref[...]
+            grad = inv_std * (
+                grad_scaled
+                - jnp.mean(grad_scaled, axis=-1, keepdims=True)
+                - scaled * jnp.mean(grad_scaled * scaled, axis=-1, keepdims=True)
+            )
+            grad_ref[at, :] = grad
+            low = grad.astype(bf16)
+            low_ref[at, :] = low
+            for n, field in enumerate((low.astype(f32), upstream * scaled, upstream)):
+                total[n] = total[n] + jnp.sum(field, axis=0, keepdims=True)
+        vec_ref[...] = jnp.zeros(vec_ref.shape, f32)
+        for n in range(3):
+            vec_ref[n:n + 1, :] = total[n]
+        proj_grad = jnp.zeros((heads, width), f32)
+        for g in range(groups):
+            result = result_ref[pl.ds(g * local, local), :]
+            embed_ref[g] = lax.dot_general(
+                proj_ref[...], result, (((1,), (1,)), ((), ())), preferred_element_type=f32
+            ).astype(bf16)
+            proj_grad = proj_grad + jnp.dot(de_ref[g], result, preferred_element_type=f32)
+        proj_grad_ref[...] = jnp.zeros(proj_grad_ref.shape, bf16)
+        proj_grad_ref[pl.ds(0, heads), :] = proj_grad.astype(bf16)
+
+
+def ffn_forward(zi, tokens, pieces, out_all, one, up_all, up_bias, down_all, two, proj, dy, de):
     zsize, width, units = up_all.shape
-    rows = normed_low.shape[0]
+    rows = tokens.shape[0]
+    groups, heads, local = de.shape
     tile = units // 2
     like = jax.ShapeDtypeStruct
-    tiles = pl.BlockSpec((1, rows, tile), lambda s: (s // 2, 0, s % 2))
+    whole = lambda shape: pl.BlockSpec(shape, lambda s, z: (0,) * len(shape))
+    tiles = pl.BlockSpec((1, rows, tile), lambda s, z: (s // 2, 0, s % 2))
+    field, row = whole((rows, width)), whole((1, width))
+    padded = heads + -heads % 128
     return pl.pallas_call(
-        ffn_kernel,
-        grid=(2 * zsize,),
-        in_specs=[
-            pl.BlockSpec((rows, width), lambda s: (0, 0)),
-            pl.BlockSpec((1, width, tile), lambda s: (s // 2, 0, s % 2)),
-            pl.BlockSpec((1, 1, tile), lambda s: (s // 2, 0, s % 2)),
-            pl.BlockSpec((1, tile, width), lambda s: (s // 2, s % 2, 0)),
-        ],
-        out_specs=[tiles, tiles, pl.BlockSpec((rows, width), lambda s: (0, 0))],
+        functools.partial(ffn_kernel, zsize, groups),
+        grid_spec=pltpu.PrefetchScalarGridSpec(
+            num_scalar_prefetch=1,
+            grid=(2 * zsize,),
+            in_specs=[
+                field, whole((width, width)), row, row, row,
+                pl.BlockSpec((1, width, tile), lambda s, z: (s // 2, 0, s % 2)),
+                pl.BlockSpec((1, 1, tile), lambda s, z: (s // 2, 0, s % 2)),
+                pl.BlockSpec((1, tile, width), lambda s, z: (s // 2, s % 2, 0)),
+                row, row, row, whole(proj.shape), field, whole(de.shape),
+            ] + [whole(p.shape) for p in pieces],
+            out_specs=[
+                tiles, tiles, field, field, field, whole((rows, 1)), field, whole(de.shape), field, field,
+                whole((padded, width)), whole((8, width)),
+            ],
+            scratch_shapes=[pltpu.VMEM((rows, width), f32), pltpu.VMEM((rows, width), f32)],
+        ),
         out_shape=[
-            like((zsize, rows, units), bf16), like((zsize, rows, units), bf16), like((rows, width), f32),
+            like((zsize, rows, units), bf16), like((zsize, rows, units), bf16), like((rows, width), bf16),
+            like((rows, width), bf16), like((rows, width), f32), like((rows, 1), f32), like((rows, width), bf16),
+            like(de.shape, bf16), like((rows, width), f32), like((rows, width), bf16), like((padded, width), bf16),
+            like((8, width), f32),
         ],
         compiler_params=pltpu.CompilerParams(vmem_limit_bytes=VMEM),
-    )(normed_low, up_all, up_bias[:, None, :], down_all)
+    )(zi.reshape(1), tokens, out_all, *one, up_all, up_bias[:, None, :], down_all, *two, proj, dy, de, *pieces)
 
 
 def ffn_back_kernel(core_ref, second_ref, normed_ref, up_ref, down_ref, active_ref, slope_ref,
@@ -1116,30 +1120,45 @@
     return pick(keep, 1 - i) + pick(got, 1 - i), pick(keep, i) + pick(got, i)
 
 
-def widen_kernel(up_ref, down_ref, out_ref, qkv_ref, first_ref, back_ref, up_o, down_o, out_o, qkv_o, first_o):
+def widen_kernel(counts, up_ref, down_ref, out_ref, qkv_ref, first_ref, *refs):
+    parts, (up_o, down_o, out_o, qkv_o, first_o) = refs[:-5], refs[-5:]
     for source, target in ((up_ref, up_o), (down_ref, down_o), (out_ref, out_o), (qkv_ref, qkv_o)):
         target[...] = source[...].astype(f32)
-    first_o[...] = first_ref[...] + back_ref[...]
-
-
-def widen(up, down, out, qkv, first, back):
+    per_group = pl.num_programs(0) // len(counts)
+    for g, count in enumerate(counts):
+        own, parts = parts[:count], parts[count:]
+
+        @pl.when(pl.program_id(0) // per_group == g)
+        def _():
+            total = first_ref[...]
+            for part in own:
+                total = total + part[...].astype(f32)
+            first_o[...] = total
+
+
+def widen(up, down, out, qkv, first, parts):
     steps = 8
+    per_group = steps // len(parts)
 
     def rows_of(array):
         return pl.BlockSpec((array.shape[0] // steps, array.shape[1]), lambda i: (i, 0))
+
+    def of_group(g):
+        block = first.shape[0] // steps
+        return pl.BlockSpec((block, first.shape[1]), lambda i: (jnp.clip(i - g * per_group, 0, per_group - 1), 0))
 
     arrays = [up, down, out]
     specs = [rows_of(a) for a in arrays]
     specs.append(pl.BlockSpec((3, qkv.shape[1] // steps, qkv.shape[2]), lambda i: (0, i, 0)))
     specs.append(rows_of(first))
     return pl.pallas_call(
-        widen_kernel,
+        functools.partial(widen_kernel, [len(p) for p in parts]),
         grid=(steps,),
-        in_specs=specs + [rows_of(back)],
+        in_specs=specs + [of_group(g) for g, own in enumerate(parts) for _ in own],
         out_specs=specs,
         out_shape=[jax.ShapeDtypeStruct(a.shape, f32) for a in arrays + [qkv, first]],
         compiler_params=pltpu.CompilerParams(vmem_limit_bytes=VMEM),
-    )(up, down, out, qkv, first, back)
+    )(up, down, out, qkv, first, *[part for own in parts for part in own])
 
 
 def per_device(blocks, tokens, segments, qkv_weight, qkv_bias, out_weight, out_bias, gain_one, shift_one,
@@ -1177,27 +1196,27 @@
     down_all = down_all.reshape(zsize, units_here, model_width)
     full_up_bias = bias_blocks.reshape(zsize, units_here)
 
-    own_mixed, *kept = attend_forward(bounds, token_blocks, qkv_weight, qkv_bias, cosine, sine, docs)
-    mixed = swap(own_mixed, zsize, True).reshape(rows, model_width)
-
-    first_sum = tokens.reshape(rows, model_width).astype(f32) + (
-        jnp.dot(mixed, out_all, preferred_element_type=f32) + out_bias
+    def ring(step):
+        return [(i, (i + step) % zsize) for i in range(zsize)]
+
+    def exchange(array, size, axis):
+        parts = []
+        for step in range(zsize):
+            part = lax.dynamic_slice_in_dim(array, lax.rem(zi + step, zsize) * size, size, axis)
+            parts.append(lax.ppermute(part, "z", ring(step)) if step else part)
+        return parts
+
+    kept, pieces = [], []
+    for g in range(groups):
+        kept.append(attend_forward(g, bounds, token_blocks, qkv_weight, qkv_bias, cosine, sine, docs))
+        pieces += exchange(kept[g][0], local_rows, 1)
+    flat = lambda vector: vector.reshape(1, model_width)
+    (active, slope, mixed, normed_low, scaled_one, inv_one, result_low, embedded, grad_second, second_low, proj_grad,
+     vec_two) = ffn_forward(
+        zi, token_rows, pieces, out_all, [flat(v) for v in (out_bias, gain_one, shift_one)], up_all, full_up_bias,
+        down_all, [flat(v) for v in (down_bias, gain_two, shift_two)], proj_weight.T,
+        out_grad.reshape(rows, model_width), embed_grad.transpose(0, 2, 1),
     )
-    normed, scaled_one, inv_one = norm_forward(first_sum, gain_one, shift_one)
-    normed_low = normed.astype(bf16)
-    active, slope, ffn = ffn_forward(normed_low, up_all, full_up_bias, down_all)
-    second_sum = normed + (ffn + down_bias)
-    result, scaled_two, inv_two = norm_forward(second_sum, gain_two, shift_two)
-    result_low = result.astype(bf16)
-    embedded = jnp.dot(result_low, proj_weight, preferred_element_type=f32).astype(bf16)
-    embed_rows = embed_grad.reshape(rows, -1)
-    grad_result = out_grad.reshape(rows, model_width).astype(f32) + jnp.einsum(
-        "np,dp->nd", embed_rows, proj_weight, preferred_element_type=f32
-    )
-    proj_grad = jnp.einsum("nd,np->dp", result_low, embed_rows, preferred_element_type=f32)
-    grad_second, gain_two_grad, shift_two_grad = norm_backward(grad_result, scaled_two, inv_two, gain_two)
-    second_low = grad_second.astype(bf16)
-    down_bias_grad = jnp.sum(second_low.astype(f32), axis=0)
     core = lax.axis_index("core").reshape(1)
     give_up, keep_up, give_down, keep_down, ffn_back, up_bias_grad = ffn_backward(
         core, second_low, normed_low, up_all, down_all, active, slope
@@ -1211,39 +1230,30 @@
     out_grad_w = jnp.einsum("nh,nd->hd", mixed, first_low, preferred_element_type=f32).astype(bf16)
     grad_mixed = jnp.einsum("nd,hd->nh", first_low, out_all, preferred_element_type=f32).astype(bf16)
     grad_mixed = grad_mixed.reshape(groups, local_rows, model_width)
-    upstream = []
-    for step in range(zsize):
-        part = lax.dynamic_slice_in_dim(grad_mixed, lax.rem(zi + step, zsize) * head_cols, head_cols, 2)
-        ring = [(i, (i + step) % zsize) for i in range(zsize)]
-        upstream.append(lax.ppermute(part, "z", ring) if step else part)
+    upstream = [exchange(grad_mixed[g:g + 1], head_cols, 2) for g in range(groups)]
     send_down, keep_down = first_halving(got_down, keep_down, "yx")
     send_up, keep_up = first_halving(got_up, keep_up, "xy")
+    upstream[0], send_down, send_up = lax.optimization_barrier((upstream[0], send_down, send_up))
     got_down = lax.ppermute(send_down, ORDERS["yx"][0], PAIR)
     got_up = lax.ppermute(send_up, ORDERS["xy"][0], PAIR)
     qkv_weight_grad, qkv_bias_grad, early = None, 0.0, []
     for g in range(groups):
         *backs, qkv_weight_grad, bias_part = attend_backward(
-            g, qkv_weight_grad, bounds, zi, kept, own_mixed, upstream, cosine, sine, token_blocks, qkv_weight
+            g, qkv_weight_grad, bounds, zi, kept[g][1:], kept[g][0], upstream[g], cosine, sine, token_blocks, qkv_weight
         )
         qkv_bias_grad = qkv_bias_grad + bias_part[:3]
         if g < groups - 1:
             early.append([
-                lax.ppermute(part, "z", [(i, (i + step) % zsize) for i in range(zsize)]) if step else part
+                lax.ppermute(part, "z", ring(step)) if step else part
                 for step, part in enumerate(backs)
             ])
-    backs, got_down, got_up = lax.optimization_barrier((backs[0], got_down, got_up))
-
-    small = jnp.concatenate(
-        [
-            out_bias_grad, gain_one_grad, shift_one_grad, down_bias_grad, gain_two_grad, shift_two_grad,
-            up_bias_grad.reshape(-1),
-            lax.dynamic_update_slice(
-                jnp.zeros((zsize, 3 * head_cols), f32), qkv_bias_grad.reshape(1, -1), (zi, 0)
-            ).reshape(-1),
-        ]
+    backs, got_down, got_up, qkv_bias_grad = lax.optimization_barrier((backs[0], got_down, got_up, qkv_bias_grad))
+
+    vec_one = jnp.pad(jnp.stack([out_bias_grad, gain_one_grad, shift_one_grad]), ((0, 5), (0, 0)))
+    placed = lax.dynamic_update_slice(
+        jnp.zeros((zsize, 3 * head_cols), f32), qkv_bias_grad.reshape(1, -1), (zi, 0)
     )
-    proj_cols = proj_grad.shape[1]
-    proj_grad = jnp.pad(proj_grad.astype(bf16), ((0, 0), (0, -proj_cols % 128)))
+    small = jnp.concatenate([vec_one, vec_two, up_bias_grad.reshape(8, -1), placed.reshape(8, -1)], axis=1)
     up_grad, down_grad, out_grad_w, qkv_weight_grad, proj_grad, back, small = reduce_end(
         [("xy", keep_up, got_up), ("yx", keep_down, got_down)],
         [
@@ -1252,12 +1262,11 @@
             ("xy", cut(proj_grad[None], 1)),
         ],
         backs,
-        small.reshape(8, -1),
+        small,
         zsize,
     )
-    back, early = lax.optimization_barrier((back, early))
     qkv_weight_grad = qkv_weight_grad.reshape(qkv_weight.shape)
-    proj_grad = proj_grad.reshape(model_width, -1)[:, :proj_cols].astype(f32)
+    proj_grad = proj_grad.reshape(-1, model_width)[:proj_weight.shape[1]].astype(f32).T
     out_grad_w = out_grad_w.reshape(out_weight.shape)
     up_grad = up_grad.reshape(up_weight.shape)
     down_grad = down_grad.reshape(down_weight.shape)
@@ -1266,21 +1275,19 @@
             (down_grad, up_grad, out_grad_w, qkv_weight_grad), ("xb", "yb")
         )
         small, proj_grad = lax.psum((small, proj_grad), ("xb", "yb"))
-    small = small.reshape(-1)
     up_grad, down_grad, out_grad_w, qkv_weight_grad, tokens_grad = widen(
-        up_grad, down_grad, out_grad_w, qkv_weight_grad, grad_first,
-        jnp.concatenate([sum(part.astype(f32) for part in parts) for parts in early] + [back[0].astype(f32)]),
+        up_grad, down_grad, out_grad_w, qkv_weight_grad, grad_first, early + [[back[0]]]
     )
-    base = 6 * model_width
-    vec = [small[i * model_width:(i + 1) * model_width] for i in range(6)]
-    up_bias_grad = lax.dynamic_slice(small, (base + zi * units_here,), (units_here,))
-    qkv_bias_grad = lax.dynamic_slice(
-        small, (base + zsize * units_here + zi * 3 * head_cols,), (3 * head_cols,)
-    ).reshape(3, head_cols)
+    base = 2 * model_width
+    vec = list(small[:3, :model_width]) + list(small[:3, model_width:base])
+    split = base + zsize * units_here // 8
+    up_bias_grad = lax.dynamic_slice(small[:, base:split].reshape(-1), (zi * units_here,), (units_here,))
+    qkv_bias_grad = lax.dynamic_slice(small[:, split:].reshape(-1), (zi * 3 * head_cols,), (3 * head_cols,))
+    qkv_bias_grad = qkv_bias_grad.reshape(3, head_cols)
     shape3 = (groups, local_rows, model_width)
     return (
         result_low.reshape(shape3),
-        embedded.reshape(groups, local_rows, -1),
+        embedded.transpose(0, 2, 1),
         tokens_grad.reshape(shape3),
         qkv_weight_grad,
         qkv_bias_grad,

time: 471 us -> 462 us (0.981)
  other arithmetic: 38 us -> 24.9 us
  Pallas kernels: 389 us -> 376 us
  waiting for transfers between devices: 0.03 us -> 9.36 us
  starting transfers between devices: 16 us -> 22.3 us
  matrix products: 11 us -> 5.15 us
    ppermute x6 -> x15, waiting for transfers between devices: 0.02 us -> 9.35 us  [the longest x12 9.34 us: exchange(): parts.append(lax.ppermute(part, 'z', ring(step)) if step else part)]
    pallas_call x4, Pallas kernels: 84.6 us -> 75.6 us  [the longest x2 34 us: attend_forward(): pl.pallas_call(functools.partial(attend_kernel, group), grid_spec=pltpu.P...]
    reduce_sum x4 -> x0, other arithmetic: 8.1 us -> none  [the longest x1 5.11 us: per_device(): down_bias_grad = jnp.sum(second_low.astype(f32), axis=0)]
    dot_general x4 -> x0, matrix products: 7.13 us -> none  [the longest x1 3.53 us: per_device(): jnp.dot(mixed, out_all, preferred_element_type=f32) + out_bias]
    ppermute x6 -> x15, starting transfers between devices: 10.6 us -> 15.6 us  [the longest x12 12 us: exchange(): parts.append(lax.ppermute(part, 'z', ring(step)) if step else part)]
  transfers between devices with their start and end apart: 10 -> 19, of which waited for: 0 -> 3; matrix products, arithmetic and copies ran while one was open for 5% -> 7% of each run, Pallas kernels for 35% -> 39%
where the time goes in v7:
time: 462 us; the launch traced here: 455 us
  Pallas kernels  376 us (81%)
  other arithmetic  24.9 us (5%)
  starting transfers between devices  22.3 us (5%)
  local copies, waits for them, and re-layouts  16.4 us (4%)
  waiting for transfers between devices  9.36 us (2%)
  matrix products  5.15 us (1%)
    pallas_call x1, Pallas kernels, reduce_end(): pl.pallas_call(functools.partial(reduce_kernel, zsize, orders, w), out_sh...  116 us
    pallas_call x1, Pallas kernels, gather_start(): pl.pallas_call(functools.partial(gather_kernel, zsize, orders), out_shape...  110 us
    pallas_call x2, Pallas kernels, attend_backward(): pl.pallas_call(functools.partial(attend_back_kernel, group, last), grid_s...  45.6 us
    pallas_call x2, Pallas kernels, attend_forward(): pl.pallas_call(functools.partial(attend_kernel, group), grid_spec=pltpu.P...  34 us
    pallas_call x1, Pallas kernels, ffn_forward(): pl.pallas_call(functools.partial(ffn_kernel, zsize, groups), grid_spec=pl...  30.6 us
    pallas_call x1, Pallas kernels, ffn_backward(): pl.pallas_call(ffn_back_kernel, grid_spec=pltpu.PrefetchScalarGridSpec(nu...  28.3 us
    ppermute x12, starting transfers between devices, exchange(): parts.append(lax.ppermute(part, 'z', ring(step)) if step else part)  12 us
    pallas_call x1, Pallas kernels, widen(): pl.pallas_call(functools.partial(widen_kernel, [len(p) for p in parts]),...  10.9 us
  transfers between devices with their start and end apart: 19, of which 3 were waited for; matrix products, arithmetic and copies ran while one was open for 7% of the time, Pallas kernels for 39%

profile of v7, /device:TPU:1, one launch (start us, length us, event | category | flops | bytes accessed | tf_op | source)
XLA Modules:
  0.0 455.1 jit_solution(2107625460704519872)
XLA Ops:
  3.4 2.0 copy.53.seg_ref
  6.8 5.5 %fusion.4 = (f32[2,1024,128]{2,1,0:T(8,128)}, f32[2,1024,128]{2,1,0:T(8,128)}) fusion(f32[128]{0:T(128)S(1)} %get-tuple-element.190, f32[128]{0:T(128)S(1)} %get-tuple-element.191, f32[2,1024]{1,0:T(2,128)S(1)} %fusion.6), kind=kLoop, calls=%fused_computation.18 | loop fusion | flops 524288 | bytes 2106368 | tf_op jit(solution)/shard_map/mul | solution.py:39
  12.3 109.6 %shard_map.288 = (bf16[4,512,1024]{2,1,0:T(8,128)(2,1)}, f32[4,8,128]{2,1,0:T(8,128)}, bf16[4,2,2,2,32,1024]{5,4,3,2,1,0:T(8,128)(2,1)}, bf16[4,2,2,2,128,1024]{...) custom-call(bf16[512,1024]{1,0:T(8,128)(2,1)} %bitcast.111, f32[8,128]{1,0:T(8,128)} %bitcast.143, ...), custom_call_target="tpu_custom_call" | custom-call | tf_op jit(solution)/shard_map/pallas_call | solution.py:511
  121.9 17.7 %shard_map.290 = (bf16[1,1024,256]{2,1,0:T(8,128)(2,1)}, bf16[1,4,1024,128]{3,2,1,0:T(8,128)(2,1)}, bf16[1,4,1024,128]{3,2,1,0:T(8,128)(2,1)}, bf16[1,4,1024,128]{3,2,1,0:T(8,128)(2,1)}, f32[1,4,1024]{2,1,0:T(4,128)}) custom-call(s32[2,4]{1,0:T(2,128)} %get-tuple-element.189.lo_ref, s32[2,4]{1,0:T(2,128)} %get-tuple-element.188.hi_ref, ...), custom_call_target="tpu_custom_call" | custom-call | flops 2684354560 | bytes 5767168 | tf_op jit(solution)/shard_map/pallas_call | solution.py:161
  139.7 1.8 constant_dynamic-slice_fusion
  142.9 16.3 %shard_map.289 = (bf16[1,1024,256]{2,1,0:T(8,128)(2,1)}, bf16[1,4,1024,128]{3,2,1,0:T(8,128)(2,1)}, bf16[1,4,1024,128]{3,2,1,0:T(8,128)(2,1)}, bf16[1,4,1024,128]{3,2,1,0:T(8,128)(2,1)}, f32[1,4,1024]{2,1,0:T(4,128)}) custom-call(s32[2,4]{1,0:T(2,128)} %get-tuple-element.189.lo_ref, s32[2,4]{1,0:T(2,128)} %get-tuple-element.188.hi_ref, ...), custom_call_target="tpu_custom_call" | custom-call | flops 2684354560 | bytes 5767168 | tf_op jit(solution)/shard_map/pallas_call | solution.py:161
  159.2 1.8 constant_dynamic-slice_fusion.4
  161.0 2.6 collective-permute-start.2
  165.5 7.9 %collective-permute-done.1.refs_2_ = bf16[1,256,256]{2,1,0:T(8,128)(2,1)S(1)} collective-permute-done((bf16[1,256,256]{2,1,0:T(8,128)(2,1)S(1)}, bf16[1,256,256]{2,1,0:T(8,128)(2,1)S(1)}, u32[]{:S(2)}, u32[]{:S(2)}) %collective-permute-start.1) | collective-permute-done | bytes 131104 | tf_op jit(solution)/shard_map/ppermute | solution.py:1206
  174.1 30.6 %shard_map.291 = (bf16[4,512,1024]{2,1,0:T(8,128)(2,1)}, bf16[4,512,1024]{2,1,0:T(8,128)(2,1)}, bf16[512,1024]{1,0:T(8,128)(2,1)}, bf16[512,1024]{1,0:T(8,128)(2...) custom-call(s32[1]{0:T(128)} %bitcast.z_ref, ...), custom_call_target="tpu_custom_call" | custom-call | tf_op jit(solution)/shard_map/pallas_call | solution.py:1015
  204.8 28.3 %shard_map.292 = (bf16[4,512,1024]{2,1,0:T(8,128)(2,1)}, bf16[4,512,1024]{2,1,0:T(8,128)(2,1)}, bf16[4,512,1024]{2,1,0:T(8,128)(2,1)}, bf16[4,512,1024]{2,1,0:T(...) custom-call(s32[1]{0:T(128)} %bitcast.23.core_ref, bf16[512,1024]{1,0:T(8,128)(2,1)} %get-tuple-element.89.second_ref, ...), custom_call_target="tpu_custom_call" | custom-call | tf_op jit(solution)/shard_map/pallas_call | solution.py:1085
  233.1 4.2 collective-permute-start.6
  237.5 3.3 multiply_reduce_fusion
  247.7 4.8 %fusion = (bf16[4,2,128,1024]{3,2,1,0:T(8,128)(2,1)}, bf16[4,2,128,1024]{3,2,1,0:T(8,128)(2,1)}) fusion(bf16[4,2,2,128,1024]{4,3,2,1,0:T(8,128)(2,1)} %bitcast.25, s32[]{:T(128)S(6)} %select_n.111, bf16[4,2,2,128,1024]{4,3,2,1,0:T(8,128)(2,1)S(1)} %bitcast.110, s32[]{:T(128)S(6)} %select_n.108), kind=kLoop, calls=%fused_computation.1 | loop fusion | flops 2097152 | bytes 12582920 | tf_op jit(solution)/shard_map/add | solution.py:1120
  252.5 4.7 %fusion.1 = (bf16[4,2,128,1024]{3,2,1,0:T(8,128)(2,1)}, bf16[4,2,128,1024]{3,2,1,0:T(8,128)(2,1)}) fusion(bf16[4,2,2,128,1024]{4,3,2,1,0:T(8,128)(2,1)} %bitcast.28, s32[]{:T(128)S(6)} %select_n.110, bf16[4,2,2,128,1024]{4,3,2,1,0:T(8,128)(2,1)S(1)} %bitcast.109, s32[]{:T(128)S(6)} %select_n.109), kind=kLoop, calls=%fused_computation.3 | loop fusion | flops 2097152 | bytes 12582920 | tf_op jit(solution)/shard_map/add | solution.py:1120
  258.1 2.4 collective-permute-start.14
  265.1 3.8 convolution_convert_fusion
  268.9 21.5 %shard_map.293 = (bf16[256,1024]{1,0:T(8,128)(2,1)}, bf16[256,1024]{1,0:T(8,128)(2,1)}, bf16[256,1024]{1,0:T(8,128)(2,1)}, bf16[256,1024]{1,0:T(8,128)(2,1)}, f32[3,1024,256]{2,1,0:T(8,128)}, /*index=5*/f32[8,256]{1,0:T(8,128)}) custom-call(s32[2,4]{1,0:T(2,128)} %get-tuple-element.189.lo_ref, s32[2,4]{1,0:T(2,128)} %get-tuple-element.188.hi_ref, ...), custom_call_target="tpu_custom_call" | custom-call | flops 10737418240 | bytes 12582912 | tf_op jit(solution)/shard_map/pallas_call | solution.py:308
  290.8 2.1 collective-permute-start.17
  294.1 24.1 %shard_map.294 = (bf16[1,4,256,1024]{3,2,1,0:T(8,128)(2,1)}, bf16[3,1024,256]{2,1,0:T(8,128)(2,1)}, f32[8,256]{1,0:T(8,128)}) custom-call(s32[2,4]{1,0:T(2,128)} %get-tuple-element.189.lo_ref, s32[2,4]{1,0:T(2,128)} %get-tuple-element.188.hi_ref, s32[1]{0:T(128)} %bitcast.z_ref, bf16[1,4,1024,128]{3,2,1,0:T(8,128)(2,1)} %get-tuple-element.97.q_ref, ...), custom_call_target="tpu_custom_call" | custom-call | tf_op jit(solution)/shard_map/pallas_call | solution.py:308
  319.7 116.5 %shard_map.295 = (bf16[2,2,2,128,1024]{4,3,2,1,0:T(8,128)(2,1)}, bf16[2,2,2,128,1024]{4,3,2,1,0:T(8,128)(2,1)}, bf16[2,2,2,32,1024]{4,3,2,1,0:T(8,128)(2,1)}, bf...) custom-call(bf16[4,2,128,1024]{3,2,1,0:T(8,128)(2,1)} %get-tuple-ele, ...), custom_call_target="tpu_custom_call" | custom-call | tf_op jit(solution)/shard_map/pallas_call | solution.py:903
  438.8 1.5 fusion.15
  440.3 2.2 convert_bitcast_fusion
  443.7 10.9 %shard_map.296 = (f32[1024,1024]{1,0:T(8,128)}, f32[1024,1024]{1,0:T(8,128)}, f32[256,1024]{1,0:T(8,128)}, f32[3,1024,256]{2,1,0:T(8,128)}, f32[512,1024]{1,0:T(8,128)}) custom-call(bf16[1024,1024]{1,0:T(8,128)(2,1)} %bitcast.122, bf16[1024,1024]{1,0:T(8,128)(2,1)} %bitcast.123, bf16[256,1024]{1,0:T(8,128)(2,1)} %bitcast.130, ...), custom_call_target="tpu_custom_call" | custom-call | tf_op jit(solution)/shard_map/pallas_call | solution.py:1154
  (116 shorter events, 27.5 us)
Async XLA Ops:
  141.4 22.7 %collective-permute-start.5 = (bf16[1,256,256]{2,1,0:T(8,128)(2,1)S(1)}, bf16[1,256,256]{2,1,0:T(8,128)(2,1)S(1)}, u32[]{:S(2)}, u32[]{:S(2)}) collective-permute-start(bf16[1,256,256]{2,1,0:T(8,128)(2,1)S(1)} %get-tuple-element.172), channel_id=1, source_target_pairs={{0,3},{1,0},{2,1},{3,2},{4,7},{5,4},{6,5},{7,6},{8,11},{9,8},{10,9... | collective-permute-start | bytes 393224 | tf_op jit(solution)/shard_map/ppermute | solution.py:1206
  142.2 22.7 %collective-permute-start.4 = (bf16[1,256,256]{2,1,0:T(8,128)(2,1)S(1)}, bf16[1,256,256]{2,1,0:T(8,128)(2,1)S(1)}, u32[]{:S(2)}, u32[]{:S(2)}) collective-permute-start(bf16[1,256,256]{2,1,0:T(8,128)(2,1)S(1)} %get-tuple-element.173), channel_id=1, source_target_pairs={{0,2},{1,3},{2,0},{3,1},{4,6},{5,7},{6,4},{7,5},{8,10},{9,11},{10,... | collective-permute-start | bytes 393224 | tf_op jit(solution)/shard_map/ppermute | solution.py:1206
  142.2 22.7 %collective-permute-start.3 = (bf16[1,256,256]{2,1,0:T(8,128)(2,1)S(1)}, bf16[1,256,256]{2,1,0:T(8,128)(2,1)S(1)}, u32[]{:S(2)}, u32[]{:S(2)}) collective-permute-start(bf16[1,256,256]{2,1,0:T(8,128)(2,1)S(1)} %get-tuple-element.174), channel_id=1, source_target_pairs={{0,1},{1,2},{2,3},{3,0},{4,5},{5,6},{6,7},{7,4},{8,9},{9,10},{10,1... | collective-permute-start | bytes 393224 | tf_op jit(solution)/shard_map/ppermute | solution.py:1206
  161.0 4.5 collective-permute-start.2
  163.6 9.8 %collective-permute-start.1 = (bf16[1,256,256]{2,1,0:T(8,128)(2,1)S(1)}, bf16[1,256,256]{2,1,0:T(8,128)(2,1)S(1)}, u32[]{:S(2)}, u32[]{:S(2)}) collective-permute-start(bf16[1,256,256]{2,1,0:T(8,128)(2,1)S(1)} %get-tuple-element.177), channel_id=1, source_target_pairs={{0,2},{1,3},{2,0},{3,1},{4,6},{5,7},{6,4},{7,5},{8,10},{9,11},{10,... | collective-permute-start | bytes 393224 | tf_op jit(solution)/shard_map/ppermute | solution.py:1206
  164.2 9.2 %collective-permute-start = (bf16[1,256,256]{2,1,0:T(8,128)(2,1)S(1)}, bf16[1,256,256]{2,1,0:T(8,128)(2,1)S(1)}, u32[]{:S(2)}, u32[]{:S(2)}) collective-permute-start(bf16[1,256,256]{2,1,0:T(8,128)(2,1)S(1)} %get-tuple-element.178), channel_id=1, source_target_pairs={{0,1},{1,2},{2,3},{3,0},{4,5},{5,6},{6,7},{7,4},{8,9},{9,10},{10,1... | collective-permute-start | bytes 393224 | tf_op jit(solution)/shard_map/ppermute | solution.py:1206
  204.7 32.6 %copy-start.9 = (f32[512,1]{1,0:T(8,128)S(1)}, f32[512,1]{1,0:T(8,128)}, u32[]{:S(2)}) copy-start(f32[512,1]{1,0:T(8,128)} %get-tuple-element.101) | copy-start | bytes 6148
  204.7 32.8 %copy-start.1 = (f32[512,1024]{1,0:T(8,128)S(1)}, f32[512,1024]{1,0:T(8,128)}, u32[]{:S(2)}) copy-start(f32[512,1024]{1,0:T(8,128)} %get-tuple-element.104) | copy-start | bytes 6291460
  204.8 32.8 %copy-start.19 = (f32[1024]{0:T(1024)S(1)}, f32[1024]{0:T(1024)}, u32[]{:S(2)}) copy-start(f32[1024]{0:T(1024)} %param.23) | copy-start | bytes 12292
  233.1 14.6 %collective-permute-start.6 = (bf16[4,512,1024]{2,1,0:T(8,128)(2,1)}, bf16[4,512,1024]{2,1,0:T(8,128)(2,1)}, u32[]{:S(2)}, u32[]{:S(2)}) collective-permute-start(bf16[4,512,1024]{2,1,0:T(8,128)(2,1)} %get-tuple-element.94), channel_id=1, source_target_pairs={{0,4},{4,0},{1,5},{5,1},{2,6},{6,2},{3,7},{7,3},{8,12},{12,8},{9,1... | collective-permute-start | bytes 12582920 | tf_op jit(solution)/shard_map/ppermute | solution.py:1225
  237.3 15.2 %collective-permute-start.7 = (bf16[4,512,1024]{2,1,0:T(8,128)(2,1)}, bf16[4,512,1024]{2,1,0:T(8,128)(2,1)}, u32[]{:S(2)}, u32[]{:S(2)}) collective-permute-start(bf16[4,512,1024]{2,1,0:T(8,128)(2,1)} %get-tuple-element.96), channel_id=1, source_target_pairs={{0,4},{4,0},{1,5},{5,1},{2,6},{6,2},{3,7},{7,3},{8,12},{12,8},{9,1... | collective-permute-start | bytes 12582920 | tf_op jit(solution)/shard_map/ppermute | solution.py:1224
  244.8 12.3 %collective-permute-start.13 = (bf16[1,256,256]{2,1,0:T(8,128)(2,1)S(1)}, bf16[1,256,256]{2,1,0:T(8,128)(2,1)S(1)}, u32[]{:S(2)}, u32[]{:S(2)}) collective-permute-start(bf16[1,256,256]{2,1,0:T(8,128)(2,1)S(1)} %get-tuple-element.164), channel_id=1, source_target_pairs={{0,3},{1,0},{2,1},{3,2},{4,7},{5,4},{6,5},{7,6},{8,11},{9,8},{10,9... | collective-permute-start | bytes 393224 | tf_op jit(solution)/shard_map/ppermute | solution.py:1206
  245.5 12.6 %collective-permute-start.12 = (bf16[1,256,256]{2,1,0:T(8,128)(2,1)S(1)}, bf16[1,256,256]{2,1,0:T(8,128)(2,1)S(1)}, u32[]{:S(2)}, u32[]{:S(2)}) collective-permute-start(bf16[1,256,256]{2,1,0:T(8,128)(2,1)S(1)} %get-tuple-element.165), channel_id=1, source_target_pairs={{0,2},{1,3},{2,0},{3,1},{4,6},{5,7},{6,4},{7,5},{8,10},{9,11},{10,... | collective-permute-start | bytes 393224 | tf_op jit(solution)/shard_map/ppermute | solution.py:1206
  246.2 11.9 %collective-permute-start.11 = (bf16[1,256,256]{2,1,0:T(8,128)(2,1)S(1)}, bf16[1,256,256]{2,1,0:T(8,128)(2,1)S(1)}, u32[]{:S(2)}, u32[]{:S(2)}) collective-permute-start(bf16[1,256,256]{2,1,0:T(8,128)(2,1)S(1)} %get-tuple-element.166), channel_id=1, source_target_pairs={{0,1},{1,2},{2,3},{3,0},{4,5},{5,6},{6,7},{7,4},{8,9},{9,10},{10,1... | collective-permute-start | bytes 393224 | tf_op jit(solution)/shard_map/ppermute | solution.py:1206
  258.1 60.8 %collective-permute-start.14 = (bf16[4,2,128,1024]{3,2,1,0:T(8,128)(2,1)}, bf16[4,2,128,1024]{3,2,1,0:T(8,128)(2,1)}, u32[]{:S(2)}, u32[]{:S(2)}) collective-permute-start(bf16[4,2,128,1024]{3,2,1,0:T(8,128)(2,1)} %get-tuple-element.115), channel_id=1, source_target_pairs={{0,8},{8,0},{1,9},{9,1},{2,10},{10,2},{3,11},{11,3},{4,12},{12,4},... | collective-permute-start | bytes 6291464 | tf_op jit(solution)/shard_map/ppermute | solution.py:1237
  260.5 58.4 %collective-permute-start.15 = (bf16[4,2,128,1024]{3,2,1,0:T(8,128)(2,1)}, bf16[4,2,128,1024]{3,2,1,0:T(8,128)(2,1)}, u32[]{:S(2)}, u32[]{:S(2)}) collective-permute-start(bf16[4,2,128,1024]{3,2,1,0:T(8,128)(2,1)} %get-tuple-element.116), channel_id=1, source_target_pairs={{0,16},{16,0},{1,17},{17,1},{2,18},{18,2},{3,19},{19,3},{4,20},{20... | collective-permute-start | bytes 6291464 | tf_op jit(solution)/shard_map/ppermute | solution.py:1238
  261.3 29.1 %collective-permute-start.10 = (bf16[1,256,256]{2,1,0:T(8,128)(2,1)S(1)}, bf16[1,256,256]{2,1,0:T(8,128)(2,1)S(1)}, u32[]{:S(2)}, u32[]{:S(2)}) collective-permute-start(bf16[1,256,256]{2,1,0:T(8,128)(2,1)S(1)} %get-tuple-element.168), channel_id=1, source_target_pairs={{0,3},{1,0},{2,1},{3,2},{4,7},{5,4},{6,5},{7,6},{8,11},{9,8},{10,9... | collective-permute-start | bytes 393224 | tf_op jit(solution)/shard_map/ppermute | solution.py:1206
  262.2 28.6 %collective-permute-start.9 = (bf16[1,256,256]{2,1,0:T(8,128)(2,1)S(1)}, bf16[1,256,256]{2,1,0:T(8,128)(2,1)S(1)}, u32[]{:S(2)}, u32[]{:S(2)}) collective-permute-start(bf16[1,256,256]{2,1,0:T(8,128)(2,1)S(1)} %get-tuple-element.169), channel_id=1, source_target_pairs={{0,2},{1,3},{2,0},{3,1},{4,6},{5,7},{6,4},{7,5},{8,10},{9,11},{10,... | collective-permute-start | bytes 393224 | tf_op jit(solution)/shard_map/ppermute | solution.py:1206
  263.6 29.2 %collective-permute-start.8 = (bf16[1,256,256]{2,1,0:T(8,128)(2,1)S(1)}, bf16[1,256,256]{2,1,0:T(8,128)(2,1)S(1)}, u32[]{:S(2)}, u32[]{:S(2)}) collective-permute-start(bf16[1,256,256]{2,1,0:T(8,128)(2,1)S(1)} %get-tuple-element.170), channel_id=1, source_target_pairs={{0,1},{1,2},{2,3},{3,0},{4,5},{5,6},{6,7},{7,4},{8,9},{9,10},{10,1... | collective-permute-start | bytes 393224 | tf_op jit(solution)/shard_map/ppermute | solution.py:1206
  290.4 152.1 %collective-permute-start.16 = (bf16[256,1024]{1,0:T(8,128)(2,1)}, bf16[256,1024]{1,0:T(8,128)(2,1)S(1)}, u32[]{:S(2)}, u32[]{:S(2)}) collective-permute-start(bf16[256,1024]{1,0:T(8,128)(2,1)} %get-tuple-element.133), channel_id=1, source_target_pairs={{0,1},{1,2},{2,3},{3,0},{4,5},{5,6},{6,7},{7,4},{8,9},{9,10},{10,1... | collective-permute-start | bytes 1572872 | tf_op jit(solution)/shard_map/ppermute | solution.py:1247
  290.8 151.8 %collective-permute-start.17 = (bf16[256,1024]{1,0:T(8,128)(2,1)}, bf16[256,1024]{1,0:T(8,128)(2,1)S(1)}, u32[]{:S(2)}, u32[]{:S(2)}) collective-permute-start(bf16[256,1024]{1,0:T(8,128)(2,1)} %get-tuple-element.134), channel_id=1, source_target_pairs={{0,2},{1,3},{2,0},{3,1},{4,6},{5,7},{6,4},{7,5},{8,10},{9,11},{10,... | collective-permute-start | bytes 1572872 | tf_op jit(solution)/shard_map/ppermute | solution.py:1247
  292.8 149.8 %collective-permute-start.18 = (bf16[256,1024]{1,0:T(8,128)(2,1)}, bf16[256,1024]{1,0:T(8,128)(2,1)S(1)}, u32[]{:S(2)}, u32[]{:S(2)}) collective-permute-start(bf16[256,1024]{1,0:T(8,128)(2,1)} %get-tuple-element.135), channel_id=1, source_target_pairs={{0,3},{1,0},{2,1},{3,2},{4,7},{5,4},{6,5},{7,6},{8,11},{9,8},{10,9... | collective-permute-start | bytes 1572872 | tf_op jit(solution)/shard_map/ppermute | solution.py:1247
  294.1 24.1 %copy-start.22 = (f32[8,256]{1,0:T(8,128)S(1)}, f32[8,256]{1,0:T(8,128)}, u32[]{:S(2)}) copy-start(f32[8,256]{1,0:T(8,128)} %get-tuple-element.117) | copy-start | bytes 24580
  294.1 24.9 %copy-start.20 = (f32[8,1024]{1,0:T(8,128)S(1)}, f32[8,1024]{1,0:T(8,128)}, u32[]{:S(2)}) copy-start(f32[8,1024]{1,0:T(8,128)} %get-tuple-element.125) | copy-start | bytes 98308
  (21 other events, 126.5 us)

commit v8 on v7

--- a/solution.py
+++ b/solution.py
@@ -85,12 +85,10 @@
         at = pl.ds(pl.multiple_of(i * rows, rows), rows)
         x = tok_ref[i, 0]
         lane = lax.broadcasted_iota(jnp.int32, (rows, pair), 1)
-        doc = seg_ref[0, at, :]
-        same = lane - HEAD_DIM == doc
         low = lane < HEAD_DIM
-        feature = lane < HEAD_DIM + 4
-        extra_q = jnp.where(same, 1.0, 0.0)
-        extra_k = jnp.where(jnp.logical_and(feature, jnp.logical_not(same)), -1e9, 0.0)
+        doc = lax.broadcasted_iota(jnp.int32, (pair, rows), 0) - HEAD_DIM
+        extra_q = jnp.where(doc == seg_ref[group:group + 1, at], 1.0, 0.0).T
+        extra_k = jnp.where(lane < HEAD_DIM + 4, (extra_q - 1.0) * 1e9, 0.0)
         cosine = cos_ref[0, at, :]
         sine = sin_ref[0, at, :]
         for c in range(3):
@@ -166,7 +164,7 @@
             in_specs=[
                 pl.BlockSpec((zsize, 1, rows, width), lambda i, *_: (0, group, 0, 0)),
                 whole(weight.shape), whole(bias.shape),
-                of_group((1, length, pair)), of_group((1, length, pair)), of_group((1, length, 1)),
+                of_group((1, length, pair)), of_group((1, length, pair)), whole(docs.shape),
             ],
             out_specs=[
                 whole((1, length, cols)),
@@ -198,8 +196,7 @@
     do_refs, refs = refs[:zsize], refs[zsize:]
     if group:
         before_ref, refs = refs[0], refs[1:]
-    back_refs, refs = refs[:1 if last else zsize], refs[1 if last else zsize:]
-    wgrad_ref, sum_ref, grad_ref, wsum_ref, dox_ref, kt_ref, delta_ref, dk_ref, dv_ref, dqt_ref = refs
+    back_ref, wgrad_ref, sum_ref, grad_ref, wsum_ref, dox_ref, kt_ref, delta_ref, dk_ref, dv_ref, dqt_ref = refs
     heads, length = q_ref.shape[1], q_ref.shape[2]
     pair = 2 * HEAD_DIM
     scale = HEAD_DIM ** (-0.5)
@@ -276,7 +273,8 @@
 
     lax.fori_loop(0, blocks, finish, 0)
 
-    def onward(i, target):
+    def onward(slot, carry):
+        i = slot if last else lax.rem(z_ref[0] + slot, zsize)
         at = pl.ds(pl.multiple_of(i * rows, rows), rows)
         total = None
         x = tok_ref[i, 0]
@@ -285,13 +283,10 @@
             part = lax.dot_general(grad, w_ref[c], (((1,), (1,)), ((), ())), preferred_element_type=f32)
             total = part if total is None else total + part
             wsum_ref[c] += lax.dot_general(x, grad, (((0,), (0,)), ((), ())), preferred_element_type=f32)
-        target[...] = total.astype(bf16)
-
-    for step in range(zsize):
-        if last:
-            onward(step, back_refs[0].at[0, step])
-        else:
-            onward(lax.rem(z_ref[0] + step, zsize), back_refs[step])
+        back_ref[0, slot] = total.astype(bf16)
+        return carry
+
+    lax.fori_loop(0, zsize, onward, 0)
     wgrad_ref[...] = wsum_ref[...].astype(wgrad_ref.dtype)
 
 
@@ -315,17 +310,15 @@
                 of_group((1, length, pair)), of_group((1, length, pair)),
                 pl.BlockSpec((zsize, 1, rows, width), lambda i, *_: (0, group, 0, 0)), whole(weight.shape),
             ] + [whole((1, rows, cols))] * zsize + [whole(weight.shape)] * (group > 0),
-            out_specs=([whole((1, zsize, rows, width))] if last else [whole((rows, width))] * zsize) + [
-                whole(weight.shape), whole((8, cols)),
-            ],
+            out_specs=[whole((1, zsize, rows, width)), whole(weight.shape), whole((8, cols))],
             scratch_shapes=[
                 pltpu.VMEM((3, length, cols), bf16), pltpu.VMEM(weight.shape, f32),
                 pltpu.VMEM(wide, bf16), pltpu.VMEM((heads, HEAD_DIM, length), bf16), pltpu.VMEM((heads, length), f32),
                 pltpu.VMEM(wide, f32), pltpu.VMEM(wide, f32), pltpu.VMEM((heads, HEAD_DIM, BLOCK), f32),
             ],
         ),
-        out_shape=([like((1, zsize, rows, width), bf16)] if last else [like((rows, width), bf16)] * zsize) + [
-            like(weight.shape, bf16 if last else f32), like((8, cols), f32),
+        out_shape=[
+            like((1, zsize, rows, width), bf16), like(weight.shape, bf16 if last else f32), like((8, cols), f32),
         ],
         compiler_params=pltpu.CompilerParams(vmem_limit_bytes=VMEM),
         cost_estimate=pl.CostEstimate(
@@ -946,8 +939,8 @@
             for step in range(zsize):
                 at = lax.rem(z_ref[0] + zsize - step, zsize) * cols
                 mixed_ref[pl.ds(g * local, local), pl.ds(pl.multiple_of(at, cols), cols)] = pieces[g * zsize + step][0]
-        for i in range(rows // chunk):
-            at = pl.ds(i * chunk, chunk)
+        def first(i, carry):
+            at = pl.ds(pl.multiple_of(i * chunk, chunk), chunk)
             attended = jnp.dot(mixed_ref[at, :], out_ref[...], preferred_element_type=f32) + out_bias_ref[...]
             scaled, inv_std = norm_rows(tok_ref[at, :].astype(f32) + attended)
             normed = scaled * gain_one_ref[...] + shift_one_ref[...]
@@ -955,27 +948,30 @@
             inv_ref[at, :] = inv_std
             normed_ref[at, :] = normed
             x_ref[at, :] = normed.astype(bf16)
+            return carry
+
+        lax.fori_loop(0, rows // chunk, first, 0)
         sum_ref[...] = jnp.zeros(sum_ref.shape, f32)
 
-    for i in range(2):
-        at = pl.ds(i * (rows // 2), rows // 2)
-        hidden = jnp.dot(x_ref[at, :], up_ref[0], preferred_element_type=f32) + bias_ref[0]
-        active, slope = gelu_pair(hidden)
-        active = active.astype(bf16)
-        active_ref[0, at, :] = active
+    parts = [pl.ds(i * chunk, chunk) for i in range(rows // chunk)]
+    hidden = [jnp.dot(x_ref[at, :], up_ref[0], preferred_element_type=f32) + bias_ref[0] for at in parts]
+    for at, field in zip(parts, hidden):
+        active, slope = gelu_pair(field)
         slope_ref[0, at, :] = slope.astype(bf16)
-        sum_ref[at, :] += jnp.dot(active, down_ref[0], preferred_element_type=f32)
+        active_ref[0, :, at] = active.T.astype(bf16)
+        sum_ref[at, :] += jnp.dot(active.astype(bf16), down_ref[0], preferred_element_type=f32)
 
     @pl.when(pl.program_id(0) == pl.num_programs(0) - 1)
     def _():
-        total = [jnp.zeros((1, width), f32)] * 3
-        for i in range(rows // chunk):
-            at = pl.ds(i * chunk, chunk)
+        vec_ref[...] = jnp.zeros(vec_ref.shape, f32)
+
+        def second(i, carry):
+            at = pl.ds(pl.multiple_of(i * chunk, chunk), chunk)
             scaled, inv_std = norm_rows(normed_ref[at, :] + (sum_ref[at, :] + down_bias_ref[...]))
             result_ref[at, :] = (scaled * gain_two_ref[...] + shift_two_ref[...]).astype(bf16)
-            g, inner = i * chunk // local, i * chunk % local
+            g, inner = i // (local // chunk), lax.rem(i, local // chunk)
             upstream = dy_ref[at, :].astype(f32) + lax.dot_general(
-                de_ref[g, :, inner:inner + chunk], proj_ref[...], (((0,), (0,)), ((), ())), preferred_element_type=f32
+                de_ref[g, :, pl.ds(pl.multiple_of(inner * chunk, chunk), chunk)], proj_ref[...], (((0,), (0,)), ((), ())), preferred_element_type=f32
             )
             grad_scaled = upstream * gain_two_ref[...]
             grad = inv_std * (
@@ -987,10 +983,10 @@
             low = grad.astype(bf16)
             low_ref[at, :] = low
             for n, field in enumerate((low.astype(f32), upstream * scaled, upstream)):
-                total[n] = total[n] + jnp.sum(field, axis=0, keepdims=True)
-        vec_ref[...] = jnp.zeros(vec_ref.shape, f32)
-        for n in range(3):
-            vec_ref[n:n + 1, :] = total[n]
+                vec_ref[n:n + 1, :] = vec_ref[n:n + 1, :] + jnp.sum(field, axis=0, keepdims=True)
+            return carry
+
+        lax.fori_loop(0, rows // chunk, second, 0)
         proj_grad = jnp.zeros((heads, width), f32)
         for g in range(groups):
             result = result_ref[pl.ds(g * local, local), :]
@@ -1006,32 +1002,33 @@
     zsize, width, units = up_all.shape
     rows = tokens.shape[0]
     groups, heads, local = de.shape
-    tile = units // 2
+    tile = units
     like = jax.ShapeDtypeStruct
     whole = lambda shape: pl.BlockSpec(shape, lambda s, z: (0,) * len(shape))
-    tiles = pl.BlockSpec((1, rows, tile), lambda s, z: (s // 2, 0, s % 2))
+    tiles = pl.BlockSpec((1, rows, tile), lambda s, z: (s, 0, 0))
     field, row = whole((rows, width)), whole((1, width))
     padded = heads + -heads % 128
     return pl.pallas_call(
         functools.partial(ffn_kernel, zsize, groups),
         grid_spec=pltpu.PrefetchScalarGridSpec(
             num_scalar_prefetch=1,
-            grid=(2 * zsize,),
+            grid=(zsize,),
             in_specs=[
                 field, whole((width, width)), row, row, row,
-                pl.BlockSpec((1, width, tile), lambda s, z: (s // 2, 0, s % 2)),
-                pl.BlockSpec((1, 1, tile), lambda s, z: (s // 2, 0, s % 2)),
-                pl.BlockSpec((1, tile, width), lambda s, z: (s // 2, s % 2, 0)),
+                pl.BlockSpec((1, width, tile), lambda s, z: (s, 0, 0)),
+                pl.BlockSpec((1, 1, tile), lambda s, z: (s, 0, 0)),
+                pl.BlockSpec((1, tile, width), lambda s, z: (s, 0, 0)),
                 row, row, row, whole(proj.shape), field, whole(de.shape),
             ] + [whole(p.shape) for p in pieces],
             out_specs=[
-                tiles, tiles, field, field, field, whole((rows, 1)), field, whole(de.shape), field, field,
+                pl.BlockSpec((1, tile, rows), lambda s, z: (s, 0, 0)), tiles,
+                field, field, field, whole((rows, 1)), field, whole(de.shape), field, field,
                 whole((padded, width)), whole((8, width)),
             ],
             scratch_shapes=[pltpu.VMEM((rows, width), f32), pltpu.VMEM((rows, width), f32)],
         ),
         out_shape=[
-            like((zsize, rows, units), bf16), like((zsize, rows, units), bf16), like((rows, width), bf16),
+            like((zsize, units, rows), bf16), like((zsize, rows, units), bf16), like((rows, width), bf16),
             like((rows, width), bf16), like((rows, width), f32), like((rows, 1), f32), like((rows, width), bf16),
             like(de.shape, bf16), like((rows, width), f32), like((rows, width), bf16), like((padded, width), bf16),
             like((8, width), f32),
@@ -1055,53 +1052,43 @@
     upstream = lax.dot_general(second, down_ref[0], (((1,), (1,)), ((), ())), preferred_element_type=f32)
     grad = (upstream * slope_ref[0].astype(f32)).astype(bf16)
     bias_ref[0] = jnp.sum(grad.astype(f32), axis=0, keepdims=True)
-    down = lax.dot_general(active_ref[0], second, (((0,), (0,)), ((), ())), preferred_element_type=f32).astype(bf16)
-
-    @pl.when(s % 2 == 0)
-    def _():
-        give_down_ref[0] = down
-
-    @pl.when(s % 2 == 1)
-    def _():
-        keep_down_ref[0] = down
-
+    units = active_ref.shape[1] // 2
     back_ref[...] += lax.dot_general(grad, up_ref[0], (((1,), (1,)), ((), ())), preferred_element_type=f32)
-    give = turned_ref[pl.ds(pl.multiple_of((1 - c) * half, half), half), :]
-    give_up_ref[0] = jnp.dot(give, grad, preferred_element_type=f32).astype(bf16)
-    keep = turned_ref[pl.ds(pl.multiple_of(c * half, half), half), :]
-    keep_up_ref[0] = jnp.dot(keep, grad, preferred_element_type=f32).astype(bf16)
+    for who, down_to, up_to in ((1 - c, give_down_ref, give_up_ref), (c, keep_down_ref, keep_up_ref)):
+        active = active_ref[0, pl.ds(pl.multiple_of(who * units, units), units), :]
+        down_to[0] = jnp.dot(active, second, preferred_element_type=f32).astype(bf16)
+        turned = turned_ref[pl.ds(pl.multiple_of(who * half, half), half), :]
+        up_to[0] = jnp.dot(turned, grad, preferred_element_type=f32).astype(bf16)
 
 
 def ffn_backward(core, second_low, normed_low, up_all, down_all, active, slope):
     zsize, width, units = up_all.shape
     rows = normed_low.shape[0]
-    tile = units // 2
     like = jax.ShapeDtypeStruct
-    part = lambda s, c: (1 - c[0] + (2 * c[0] - 1) * (s % 2))
     whole = pl.BlockSpec((rows, width), lambda s, c: (0, 0))
-    tiles = pl.BlockSpec((1, rows, tile), lambda s, c: (s // 2, 0, part(s, c)))
-    up_half = pl.BlockSpec((1, width // 2, tile), lambda s, c: (s // 2, 0, part(s, c)))
-    down_half = pl.BlockSpec((1, tile, width), lambda s, c: (s // 2, 0, 0))
+    tiles = pl.BlockSpec((1, rows, units), lambda s, c: (s, 0, 0))
+    up_half = pl.BlockSpec((1, width // 2, units), lambda s, c: (s, 0, 0))
+    down_half = pl.BlockSpec((1, units // 2, width), lambda s, c: (s, 0, 0))
     return pl.pallas_call(
         ffn_back_kernel,
         grid_spec=pltpu.PrefetchScalarGridSpec(
             num_scalar_prefetch=1,
-            grid=(2 * zsize,),
+            grid=(zsize,),
             in_specs=[
                 whole, whole,
-                pl.BlockSpec((1, width, tile), lambda s, c: (s // 2, 0, part(s, c))),
-                pl.BlockSpec((1, tile, width), lambda s, c: (s // 2, part(s, c), 0)),
-                tiles, tiles,
+                pl.BlockSpec((1, width, units), lambda s, c: (s, 0, 0)),
+                pl.BlockSpec((1, units, width), lambda s, c: (s, 0, 0)),
+                pl.BlockSpec((1, units, rows), lambda s, c: (s, 0, 0)), tiles,
             ],
             out_specs=[
                 up_half, up_half, down_half, down_half, whole,
-                pl.BlockSpec((1, 1, tile), lambda s, c: (s // 2, 0, part(s, c))),
+                pl.BlockSpec((1, 1, units), lambda s, c: (s, 0, 0)),
             ],
             scratch_shapes=[pltpu.VMEM((width, rows), bf16)],
         ),
         out_shape=[
             like((zsize, width // 2, units), bf16), like((zsize, width // 2, units), bf16),
-            like((zsize, tile, width), bf16), like((zsize, tile, width), bf16),
+            like((zsize, units // 2, width), bf16), like((zsize, units // 2, width), bf16),
             like((rows, width), f32), like((zsize, 1, units), f32),
         ],
         compiler_params=pltpu.CompilerParams(vmem_limit_bytes=VMEM),
@@ -1171,13 +1158,12 @@
     rows = groups * local_rows
     zi = lax.axis_index("z")
     cosine, sine = rotary_tables(doc_positions(segments))
-    firsts = segments[:, ::BLOCK]
-    lasts = segments[:, BLOCK - 1::BLOCK]
+    starts = jnp.sum(segments[:, None, :] < jnp.arange(4, dtype=jnp.int32)[None, :, None], axis=2, dtype=jnp.int32)
+    edges = jnp.arange(length // BLOCK, dtype=jnp.int32)[None, :, None] * BLOCK
     bounds = (
-        jnp.sum(segments[:, None, :] < firsts[:, :, None], axis=2, dtype=jnp.int32) // BLOCK,
-        (jnp.sum(segments[:, None, :] <= lasts[:, :, None], axis=2, dtype=jnp.int32) + BLOCK - 1) // BLOCK,
+        jnp.max(jnp.where(starts[:, None, :] <= edges, starts[:, None, :], 0), axis=2) // BLOCK,
+        (jnp.min(jnp.where(starts[:, None, :] >= edges + BLOCK, starts[:, None, :], length), axis=2) + BLOCK - 1) // BLOCK,
     )
-    docs = segments[:, :, None]
 
     def cut(array, rows_at):
         shape = array.shape
@@ -1208,7 +1194,7 @@
 
     kept, pieces = [], []
     for g in range(groups):
-        kept.append(attend_forward(g, bounds, token_blocks, qkv_weight, qkv_bias, cosine, sine, docs))
+        kept.append(attend_forward(g, bounds, token_blocks, qkv_weight, qkv_bias, cosine, sine, segments))
         pieces += exchange(kept[g][0], local_rows, 1)
     flat = lambda vector: vector.reshape(1, model_width)
     (active, slope, mixed, normed_low, scaled_one, inv_one, result_low, embedded, grad_second, second_low, proj_grad,
@@ -1238,16 +1224,15 @@
     got_up = lax.ppermute(send_up, ORDERS["xy"][0], PAIR)
     qkv_weight_grad, qkv_bias_grad, early = None, 0.0, []
     for g in range(groups):
-        *backs, qkv_weight_grad, bias_part = attend_backward(
+        backs, qkv_weight_grad, bias_part = attend_backward(
             g, qkv_weight_grad, bounds, zi, kept[g][1:], kept[g][0], upstream[g], cosine, sine, token_blocks, qkv_weight
         )
         qkv_bias_grad = qkv_bias_grad + bias_part[:3]
         if g < groups - 1:
             early.append([
-                lax.ppermute(part, "z", ring(step)) if step else part
-                for step, part in enumerate(backs)
+                lax.ppermute(backs[0, step], "z", ring(step)) if step else backs[0, step] for step in range(zsize)
             ])
-    backs, got_down, got_up, qkv_bias_grad = lax.optimization_barrier((backs[0], got_down, got_up, qkv_bias_grad))
+    backs, got_down, got_up, qkv_bias_grad = lax.optimization_barrier((backs, got_down, got_up, qkv_bias_grad))
 
     vec_one = jnp.pad(jnp.stack([out_bias_grad, gain_one_grad, shift_one_grad]), ((0, 5), (0, 0)))
     placed = lax.dynamic_update_slice(

time: 462 us -> 451 us (0.976); the launches traced: 455 us -> 451 us
  transfers between devices with their start and end apart: 19 -> 19, of which waited for: 3 -> 3; matrix products, arithmetic and copies ran while one was open for 7% -> 7% of each run, Pallas kernels for 39% -> 40%
where the time goes in v8:
time: 451 us
  Pallas kernels  372 us (82%)
  other arithmetic  26.2 us (6%)
  starting transfers between devices  25.5 us (6%)
  local copies, waits for them, and re-layouts  15.6 us (3%)
  waiting for transfers between devices  6.69 us (1%)
    pallas_call x1, Pallas kernels, reduce_end(): pl.pallas_call(functools.partial(reduce_kernel, zsize, orders, w), out_sh...  117 us
    pallas_call x1, Pallas kernels, gather_start(): pl.pallas_call(functools.partial(gather_kernel, zsize, orders), out_shape...  110 us
    pallas_call x2, Pallas kernels, attend_backward(): pl.pallas_call(functools.partial(attend_back_kernel, group, last), grid_s...  46.1 us
    pallas_call x2, Pallas kernels, attend_forward(): pl.pallas_call(functools.partial(attend_kernel, group), grid_spec=pltpu.P...  32.2 us
    pallas_call x1, Pallas kernels, ffn_forward(): pl.pallas_call(functools.partial(ffn_kernel, zsize, groups), grid_spec=pl...  30.2 us
    pallas_call x1, Pallas kernels, ffn_backward(): pl.pallas_call(ffn_back_kernel, grid_spec=pltpu.PrefetchScalarGridSpec(nu...  25.8 us
    ppermute x12, starting transfers between devices, exchange(): parts.append(lax.ppermute(part, 'z', ring(step)) if step else part)  11.6 us
    pallas_call x1, Pallas kernels, widen(): pl.pallas_call(functools.partial(widen_kernel, [len(p) for p in parts]),...  10.9 us
  transfers between devices with their start and end apart: 19, of which 3 were waited for; matrix products, arithmetic and copies ran while one was open for 7% of the time, Pallas kernels for 40%

profile of v8, /device:TPU:1, one launch (start us, length us, event | category | flops | bytes accessed | tf_op | source)
XLA Modules:
  0.0 451.0 jit_solution(4391364183220407349)
XLA Ops:
  3.4 5.5 %fusion.4 = (f32[2,1024,128]{2,1,0:T(8,128)}, f32[2,1024,128]{2,1,0:T(8,128)}) fusion(f32[128]{0:T(128)S(1)} %get-tuple-element.185, f32[128]{0:T(128)S(1)} %get-tuple-element.186, f32[2,1024]{1,0:T(2,128)S(1)} %fusion.6), kind=kLoop, calls=%fused_computation.18 | loop fusion | flops 524288 | bytes 2106368 | tf_op jit(solution)/shard_map/mul | solution.py:39
  8.9 109.6 %shard_map.288 = (bf16[4,512,1024]{2,1,0:T(8,128)(2,1)}, f32[4,8,128]{2,1,0:T(8,128)}, bf16[4,2,2,2,32,1024]{5,4,3,2,1,0:T(8,128)(2,1)}, bf16[4,2,2,2,128,1024]{...) custom-call(bf16[512,1024]{1,0:T(8,128)(2,1)} %bitcast.118, f32[8,128]{1,0:T(8,128)} %bitcast.149, ...), custom_call_target="tpu_custom_call" | custom-call | tf_op jit(solution)/shard_map/pallas_call | solution.py:504
  118.5 16.1 %shard_map.290 = (bf16[1,1024,256]{2,1,0:T(8,128)(2,1)}, bf16[1,4,1024,128]{3,2,1,0:T(8,128)(2,1)}, bf16[1,4,1024,128]{3,2,1,0:T(8,128)(2,1)}, bf16[1,4,1024,128]{3,2,1,0:T(8,128)(2,1)}, f32[1,4,1024]{2,1,0:T(4,128)}) custom-call(s32[2,4]{1,0:T(2,128)} %get-tuple-element.188.lo_ref, s32[2,4]{1,0:T(2,128)} %get-tuple-element.187.hi_ref, ...), custom_call_target="tpu_custom_call" | custom-call | flops 2684354560 | bytes 5767168 | tf_op jit(solution)/shard_map/pallas_call | solution.py:159
  134.6 1.8 constant_dynamic-slice_fusion
  137.9 16.1 %shard_map.289 = (bf16[1,1024,256]{2,1,0:T(8,128)(2,1)}, bf16[1,4,1024,128]{3,2,1,0:T(8,128)(2,1)}, bf16[1,4,1024,128]{3,2,1,0:T(8,128)(2,1)}, bf16[1,4,1024,128]{3,2,1,0:T(8,128)(2,1)}, f32[1,4,1024]{2,1,0:T(4,128)}) custom-call(s32[2,4]{1,0:T(2,128)} %get-tuple-element.188.lo_ref, s32[2,4]{1,0:T(2,128)} %get-tuple-element.187.hi_ref, ...), custom_call_target="tpu_custom_call" | custom-call | flops 2684354560 | bytes 5767168 | tf_op jit(solution)/shard_map/pallas_call | solution.py:159
  153.9 1.8 constant_dynamic-slice_fusion.4
  155.7 2.6 collective-permute-start.2
  160.3 5.6 %collective-permute-done.1.refs_2_ = bf16[1,256,256]{2,1,0:T(8,128)(2,1)S(1)} collective-permute-done((bf16[1,256,256]{2,1,0:T(8,128)(2,1)S(1)}, bf16[1,256,256]{2,1,0:T(8,128)(2,1)S(1)}, u32[]{:S(2)}, u32[]{:S(2)}) %collective-permute-start.1) | collective-permute-done | bytes 131104 | tf_op jit(solution)/shard_map/ppermute | solution.py:1192
  166.5 30.2 %shard_map.291 = (bf16[4,1024,512]{2,1,0:T(8,128)(2,1)}, bf16[4,512,1024]{2,1,0:T(8,128)(2,1)}, bf16[512,1024]{1,0:T(8,128)(2,1)}, bf16[512,1024]{1,0:T(8,128)(2...) custom-call(s32[1]{0:T(128)} %bitcast.z_ref, ...), custom_call_target="tpu_custom_call" | custom-call | tf_op jit(solution)/shard_map/pallas_call | solution.py:1011
  196.8 25.8 %shard_map.292 = (bf16[4,512,1024]{2,1,0:T(8,128)(2,1)}, bf16[4,512,1024]{2,1,0:T(8,128)(2,1)}, bf16[4,512,1024]{2,1,0:T(8,128)(2,1)}, bf16[4,512,1024]{2,1,0:T(...) custom-call(s32[1]{0:T(128)} %bitcast.22.core_ref, bf16[512,1024]{1,0:T(8,128)(2,1)} %get-tuple-element.86.second_ref, ...), custom_call_target="tpu_custom_call" | custom-call | tf_op jit(solution)/shard_map/pallas_call | solution.py:1072
  222.6 7.7 %collective-permute-start.6 = (bf16[4,512,1024]{2,1,0:T(8,128)(2,1)}, bf16[4,512,1024]{2,1,0:T(8,128)(2,1)}, u32[]{:S(2)}, u32[]{:S(2)}) collective-permute-start(bf16[4,512,1024]{2,1,0:T(8,128)(2,1)} %get-tuple-element.91), channel_id=1, source_target_pairs={{0,4},{4,0},{1,5},{5,1},{2,6},{6,2},{3,7},{7,3},{8,12},{12,8},{9,1... | collective-permute-start | bytes 12582920 | tf_op jit(solution)/shard_map/ppermute | solution.py:1211
  231.3 3.2 multiply_reduce_fusion
  241.1 5.0 %fusion = (bf16[4,2,128,1024]{3,2,1,0:T(8,128)(2,1)}, bf16[4,2,128,1024]{3,2,1,0:T(8,128)(2,1)}) fusion(bf16[4,2,2,128,1024]{4,3,2,1,0:T(8,128)(2,1)} %bitcast.24, s32[]{:T(128)S(6)} %select_n.120, bf16[4,2,2,128,1024]{4,3,2,1,0:T(8,128)(2,1)S(1)} %bitcast.117, s32[]{:T(128)S(6)} %select_n.117), kind=kLoop, calls=%fused_computation.1 | loop fusion | flops 2097152 | bytes 12582920 | tf_op jit(solution)/shard_map/add | solution.py:1107
  246.2 5.0 %fusion.1 = (bf16[4,2,128,1024]{3,2,1,0:T(8,128)(2,1)}, bf16[4,2,128,1024]{3,2,1,0:T(8,128)(2,1)}) fusion(bf16[4,2,2,128,1024]{4,3,2,1,0:T(8,128)(2,1)} %bitcast.27, s32[]{:T(128)S(6)} %select_n.119, bf16[4,2,2,128,1024]{4,3,2,1,0:T(8,128)(2,1)S(1)} %bitcast.116, s32[]{:T(128)S(6)} %select_n.118), kind=kLoop, calls=%fused_computation.3 | loop fusion | flops 2097152 | bytes 12582920 | tf_op jit(solution)/shard_map/add | solution.py:1107
  251.6 2.7 collective-permute-start.14
  260.1 2.6 convolution_convert_fusion
  262.7 22.6 %shard_map.293 = (bf16[1,4,256,1024]{3,2,1,0:T(8,128)(2,1)}, f32[3,1024,256]{2,1,0:T(8,128)}, f32[8,256]{1,0:T(8,128)}) custom-call(s32[2,4]{1,0:T(2,128)} %get-tuple-element.188.lo_ref, s32[2,4]{1,0:T(2,128)} %get-tuple-element.187.hi_ref, s32[1]{0:T(128)} %bitcast.z_ref, bf16[1,4,1024,128]{3,2,1,0:T(8,128)(2,1)} %get-tuple-element.102.q_ref, ...), custom_call_target="tpu_custom_call" | custom-call | flops 10737418240 | bytes 12582912 | tf_op jit(solution)/shard_map/pallas_call | solution.py:303
  285.3 2.5 slice_bitcast_fusion
  287.8 1.8 collective-permute-start.18
  290.3 23.5 %shard_map.294 = (bf16[1,4,256,1024]{3,2,1,0:T(8,128)(2,1)}, bf16[3,1024,256]{2,1,0:T(8,128)(2,1)}, f32[8,256]{1,0:T(8,128)}) custom-call(s32[2,4]{1,0:T(2,128)} %get-tuple-element.188.lo_ref, s32[2,4]{1,0:T(2,128)} %get-tuple-element.187.hi_ref, s32[1]{0:T(128)} %bitcast.z_ref, bf16[1,4,1024,128]{3,2,1,0:T(8,128)(2,1)} %get-tuple-element.94.q_ref, ...), custom_call_target="tpu_custom_call" | custom-call | tf_op jit(solution)/shard_map/pallas_call | solution.py:303
  315.2 117.1 %shard_map.295 = (bf16[2,2,2,128,1024]{4,3,2,1,0:T(8,128)(2,1)}, bf16[2,2,2,128,1024]{4,3,2,1,0:T(8,128)(2,1)}, bf16[2,2,2,32,1024]{4,3,2,1,0:T(8,128)(2,1)}, bf...) custom-call(bf16[4,2,128,1024]{3,2,1,0:T(8,128)(2,1)} %get-tuple-ele, ...), custom_call_target="tpu_custom_call" | custom-call | tf_op jit(solution)/shard_map/pallas_call | solution.py:896
  435.0 1.5 fusion.15
  436.5 2.2 convert_bitcast_fusion
  439.9 10.9 %shard_map.296 = (f32[1024,1024]{1,0:T(8,128)}, f32[1024,1024]{1,0:T(8,128)}, f32[256,1024]{1,0:T(8,128)}, f32[3,1024,256]{2,1,0:T(8,128)}, f32[512,1024]{1,0:T(8,128)}) custom-call(bf16[1024,1024]{1,0:T(8,128)(2,1)} %bitcast.129, bf16[1024,1024]{1,0:T(8,128)(2,1)} %bitcast.130, bf16[256,1024]{1,0:T(8,128)(2,1)} %bitcast.137, ...), custom_call_target="tpu_custom_call" | custom-call | tf_op jit(solution)/shard_map/pallas_call | solution.py:1141
  (117 shorter events, 26.4 us)
Async XLA Ops:
  136.4 22.5 %collective-permute-start.5 = (bf16[1,256,256]{2,1,0:T(8,128)(2,1)S(1)}, bf16[1,256,256]{2,1,0:T(8,128)(2,1)S(1)}, u32[]{:S(2)}, u32[]{:S(2)}) collective-permute-start(bf16[1,256,256]{2,1,0:T(8,128)(2,1)S(1)} %get-tuple-element.169), channel_id=1, source_target_pairs={{0,3},{1,0},{2,1},{3,2},{4,7},{5,4},{6,5},{7,6},{8,11},{9,8},{10,9... | collective-permute-start | bytes 393224 | tf_op jit(solution)/shard_map/ppermute | solution.py:1192
  137.2 22.3 %collective-permute-start.4 = (bf16[1,256,256]{2,1,0:T(8,128)(2,1)S(1)}, bf16[1,256,256]{2,1,0:T(8,128)(2,1)S(1)}, u32[]{:S(2)}, u32[]{:S(2)}) collective-permute-start(bf16[1,256,256]{2,1,0:T(8,128)(2,1)S(1)} %get-tuple-element.170), channel_id=1, source_target_pairs={{0,2},{1,3},{2,0},{3,1},{4,6},{5,7},{6,4},{7,5},{8,10},{9,11},{10,... | collective-permute-start | bytes 393224 | tf_op jit(solution)/shard_map/ppermute | solution.py:1192
  137.2 22.3 %collective-permute-start.3 = (bf16[1,256,256]{2,1,0:T(8,128)(2,1)S(1)}, bf16[1,256,256]{2,1,0:T(8,128)(2,1)S(1)}, u32[]{:S(2)}, u32[]{:S(2)}) collective-permute-start(bf16[1,256,256]{2,1,0:T(8,128)(2,1)S(1)} %get-tuple-element.171), channel_id=1, source_target_pairs={{0,1},{1,2},{2,3},{3,0},{4,5},{5,6},{6,7},{7,4},{8,9},{9,10},{10,1... | collective-permute-start | bytes 393224 | tf_op jit(solution)/shard_map/ppermute | solution.py:1192
  155.7 4.6 %collective-permute-start.2 = (bf16[1,256,256]{2,1,0:T(8,128)(2,1)S(1)}, bf16[1,256,256]{2,1,0:T(8,128)(2,1)S(1)}, u32[]{:S(2)}, u32[]{:S(2)}) collective-permute-start(bf16[1,256,256]{2,1,0:T(8,128)(2,1)S(1)} %get-tuple-element.173), channel_id=1, source_target_pairs={{0,3},{1,0},{2,1},{3,2},{4,7},{5,4},{6,5},{7,6},{8,11},{9,8},{10,9... | collective-permute-start | bytes 393224 | tf_op jit(solution)/shard_map/ppermute | solution.py:1192
  158.3 7.5 %collective-permute-start.1 = (bf16[1,256,256]{2,1,0:T(8,128)(2,1)S(1)}, bf16[1,256,256]{2,1,0:T(8,128)(2,1)S(1)}, u32[]{:S(2)}, u32[]{:S(2)}) collective-permute-start(bf16[1,256,256]{2,1,0:T(8,128)(2,1)S(1)} %get-tuple-element.174), channel_id=1, source_target_pairs={{0,2},{1,3},{2,0},{3,1},{4,6},{5,7},{6,4},{7,5},{8,10},{9,11},{10,... | collective-permute-start | bytes 393224 | tf_op jit(solution)/shard_map/ppermute | solution.py:1192
  158.9 7.0 %collective-permute-start = (bf16[1,256,256]{2,1,0:T(8,128)(2,1)S(1)}, bf16[1,256,256]{2,1,0:T(8,128)(2,1)S(1)}, u32[]{:S(2)}, u32[]{:S(2)}) collective-permute-start(bf16[1,256,256]{2,1,0:T(8,128)(2,1)S(1)} %get-tuple-element.175), channel_id=1, source_target_pairs={{0,1},{1,2},{2,3},{3,0},{4,5},{5,6},{6,7},{7,4},{8,9},{9,10},{10,1... | collective-permute-start | bytes 393224 | tf_op jit(solution)/shard_map/ppermute | solution.py:1192
  196.7 33.6 %copy-start.9 = (f32[512,1]{1,0:T(8,128)S(1)}, f32[512,1]{1,0:T(8,128)}, u32[]{:S(2)}) copy-start(f32[512,1]{1,0:T(8,128)} %get-tuple-element.98) | copy-start | bytes 6148
  196.7 34.6 %copy-start.1 = (f32[512,1024]{1,0:T(8,128)S(1)}, f32[512,1024]{1,0:T(8,128)}, u32[]{:S(2)}) copy-start(f32[512,1024]{1,0:T(8,128)} %get-tuple-element.101) | copy-start | bytes 6291460
  196.8 34.6 %copy-start.19 = (f32[1024]{0:T(1024)S(1)}, f32[1024]{0:T(1024)}, u32[]{:S(2)}) copy-start(f32[1024]{0:T(1024)} %param.23) | copy-start | bytes 12292
  222.6 18.5 %collective-permute-start.6 = (bf16[4,512,1024]{2,1,0:T(8,128)(2,1)}, bf16[4,512,1024]{2,1,0:T(8,128)(2,1)}, u32[]{:S(2)}, u32[]{:S(2)}) collective-permute-start(bf16[4,512,1024]{2,1,0:T(8,128)(2,1)} %get-tuple-element.91), channel_id=1, source_target_pairs={{0,4},{4,0},{1,5},{5,1},{2,6},{6,2},{3,7},{7,3},{8,12},{12,8},{9,1... | collective-permute-start | bytes 12582920 | tf_op jit(solution)/shard_map/ppermute | solution.py:1211
  230.3 15.9 %collective-permute-start.7 = (bf16[4,512,1024]{2,1,0:T(8,128)(2,1)}, bf16[4,512,1024]{2,1,0:T(8,128)(2,1)}, u32[]{:S(2)}, u32[]{:S(2)}) collective-permute-start(bf16[4,512,1024]{2,1,0:T(8,128)(2,1)} %get-tuple-element.93), channel_id=1, source_target_pairs={{0,4},{4,0},{1,5},{5,1},{2,6},{6,2},{3,7},{7,3},{8,12},{12,8},{9,1... | collective-permute-start | bytes 12582920 | tf_op jit(solution)/shard_map/ppermute | solution.py:1210
  235.1 24.9 %copy-start = (f32[512,1024]{1,0:T(8,128)}, f32[512,1024]{1,0:T(8,128)S(1)}, u32[]{:S(2)}) copy-start(f32[512,1024]{1,0:T(8,128)S(1)} %get-tuple-element.149.first_ref) | copy-start | bytes 6291460
  238.5 12.7 %collective-permute-start.13 = (bf16[1,256,256]{2,1,0:T(8,128)(2,1)S(1)}, bf16[1,256,256]{2,1,0:T(8,128)(2,1)S(1)}, u32[]{:S(2)}, u32[]{:S(2)}) collective-permute-start(bf16[1,256,256]{2,1,0:T(8,128)(2,1)S(1)} %get-tuple-element.161), channel_id=1, source_target_pairs={{0,3},{1,0},{2,1},{3,2},{4,7},{5,4},{6,5},{7,6},{8,11},{9,8},{10,9... | collective-permute-start | bytes 393224 | tf_op jit(solution)/shard_map/ppermute | solution.py:1192
  239.2 12.4 %collective-permute-start.12 = (bf16[1,256,256]{2,1,0:T(8,128)(2,1)S(1)}, bf16[1,256,256]{2,1,0:T(8,128)(2,1)S(1)}, u32[]{:S(2)}, u32[]{:S(2)}) collective-permute-start(bf16[1,256,256]{2,1,0:T(8,128)(2,1)S(1)} %get-tuple-element.162), channel_id=1, source_target_pairs={{0,2},{1,3},{2,0},{3,1},{4,6},{5,7},{6,4},{7,5},{8,10},{9,11},{10,... | collective-permute-start | bytes 393224 | tf_op jit(solution)/shard_map/ppermute | solution.py:1192
  239.7 11.9 %collective-permute-start.11 = (bf16[1,256,256]{2,1,0:T(8,128)(2,1)S(1)}, bf16[1,256,256]{2,1,0:T(8,128)(2,1)S(1)}, u32[]{:S(2)}, u32[]{:S(2)}) collective-permute-start(bf16[1,256,256]{2,1,0:T(8,128)(2,1)S(1)} %get-tuple-element.163), channel_id=1, source_target_pairs={{0,1},{1,2},{2,3},{3,0},{4,5},{5,6},{6,7},{7,4},{8,9},{9,10},{10,1... | collective-permute-start | bytes 393224 | tf_op jit(solution)/shard_map/ppermute | solution.py:1192
  251.6 62.8 %collective-permute-start.14 = (bf16[4,2,128,1024]{3,2,1,0:T(8,128)(2,1)}, bf16[4,2,128,1024]{3,2,1,0:T(8,128)(2,1)}, u32[]{:S(2)}, u32[]{:S(2)}) collective-permute-start(bf16[4,2,128,1024]{3,2,1,0:T(8,128)(2,1)} %get-tuple-element.112), channel_id=1, source_target_pairs={{0,8},{8,0},{1,9},{9,1},{2,10},{10,2},{3,11},{11,3},{4,12},{12,4},... | collective-permute-start | bytes 6291464 | tf_op jit(solution)/shard_map/ppermute | solution.py:1223
  254.3 60.1 %collective-permute-start.15 = (bf16[4,2,128,1024]{3,2,1,0:T(8,128)(2,1)}, bf16[4,2,128,1024]{3,2,1,0:T(8,128)(2,1)}, u32[]{:S(2)}, u32[]{:S(2)}) collective-permute-start(bf16[4,2,128,1024]{3,2,1,0:T(8,128)(2,1)} %get-tuple-element.113), channel_id=1, source_target_pairs={{0,16},{16,0},{1,17},{17,1},{2,18},{18,2},{3,19},{19,3},{4,20},{20... | collective-permute-start | bytes 6291464 | tf_op jit(solution)/shard_map/ppermute | solution.py:1224
  256.3 31.5 %collective-permute-start.10 = (bf16[1,256,256]{2,1,0:T(8,128)(2,1)S(1)}, bf16[1,256,256]{2,1,0:T(8,128)(2,1)S(1)}, u32[]{:S(2)}, u32[]{:S(2)}) collective-permute-start(bf16[1,256,256]{2,1,0:T(8,128)(2,1)S(1)} %get-tuple-element.165), channel_id=1, source_target_pairs={{0,3},{1,0},{2,1},{3,2},{4,7},{5,4},{6,5},{7,6},{8,11},{9,8},{10,9... | collective-permute-start | bytes 393224 | tf_op jit(solution)/shard_map/ppermute | solution.py:1192
  257.7 31.8 %collective-permute-start.9 = (bf16[1,256,256]{2,1,0:T(8,128)(2,1)S(1)}, bf16[1,256,256]{2,1,0:T(8,128)(2,1)S(1)}, u32[]{:S(2)}, u32[]{:S(2)}) collective-permute-start(bf16[1,256,256]{2,1,0:T(8,128)(2,1)S(1)} %get-tuple-element.166), channel_id=1, source_target_pairs={{0,2},{1,3},{2,0},{3,1},{4,6},{5,7},{6,4},{7,5},{8,10},{9,11},{10,... | collective-permute-start | bytes 393224 | tf_op jit(solution)/shard_map/ppermute | solution.py:1192
  258.6 31.0 %collective-permute-start.8 = (bf16[1,256,256]{2,1,0:T(8,128)(2,1)S(1)}, bf16[1,256,256]{2,1,0:T(8,128)(2,1)S(1)}, u32[]{:S(2)}, u32[]{:S(2)}) collective-permute-start(bf16[1,256,256]{2,1,0:T(8,128)(2,1)S(1)} %get-tuple-element.167), channel_id=1, source_target_pairs={{0,1},{1,2},{2,3},{3,0},{4,5},{5,6},{6,7},{7,4},{8,9},{9,10},{10,1... | collective-permute-start | bytes 393224 | tf_op jit(solution)/shard_map/ppermute | solution.py:1192
  287.8 151.0 %collective-permute-start.18 = (bf16[256,1024]{1,0:T(8,128)(2,1)S(1)}, bf16[256,1024]{1,0:T(8,128)(2,1)S(1)}, u32[]{:S(2)}, u32[]{:S(2)}) collective-permute-start(bf16[256,1024]{1,0:T(8,128)(2,1)S(1)} %get-tuple-element.155), channel_id=1, source_target_pairs={{0,3},{1,0},{2,1},{3,2},{4,7},{5,4},{6,5},{7,6},{8,11},{9,8},{10,9... | collective-permute-start | bytes 1572872 | tf_op jit(solution)/shard_map/ppermute | solution.py:1233
  289.6 149.1 %collective-permute-start.17 = (bf16[256,1024]{1,0:T(8,128)(2,1)S(1)}, bf16[256,1024]{1,0:T(8,128)(2,1)S(1)}, u32[]{:S(2)}, u32[]{:S(2)}) collective-permute-start(bf16[256,1024]{1,0:T(8,128)(2,1)S(1)} %get-tuple-element.156), channel_id=1, source_target_pairs={{0,2},{1,3},{2,0},{3,1},{4,6},{5,7},{6,4},{7,5},{8,10},{9,11},{10,... | collective-permute-start | bytes 1572872 | tf_op jit(solution)/shard_map/ppermute | solution.py:1233
  289.6 149.1 %collective-permute-start.16 = (bf16[256,1024]{1,0:T(8,128)(2,1)S(1)}, bf16[256,1024]{1,0:T(8,128)(2,1)S(1)}, u32[]{:S(2)}, u32[]{:S(2)}) collective-permute-start(bf16[256,1024]{1,0:T(8,128)(2,1)S(1)} %get-tuple-element.157), channel_id=1, source_target_pairs={{0,1},{1,2},{2,3},{3,0},{4,5},{5,6},{6,7},{7,4},{8,9},{9,10},{10,1... | collective-permute-start | bytes 1572872 | tf_op jit(solution)/shard_map/ppermute | solution.py:1233
  290.3 24.3 %copy-start.20 = (f32[8,1024]{1,0:T(8,128)S(1)}, f32[8,1024]{1,0:T(8,128)}, u32[]{:S(2)}) copy-start(f32[8,1024]{1,0:T(8,128)} %get-tuple-element.122) | copy-start | bytes 98308
  (21 other events, 118.8 us)

commit v9 on v8

--- a/solution.py
+++ b/solution.py
@@ -191,12 +191,19 @@
     )(*bounds, tokens, weight, bias, cosine, sine, docs)
 
 
-def attend_back_kernel(group, last, lo_ref, hi_ref, z_ref, q_ref, k_ref, v_ref, lse_ref, mixed_ref, cos_ref, sin_ref, tok_ref, w_ref, *refs):
-    zsize, _, rows, _ = tok_ref.shape
+def attend_back_kernel(group, last, lo_ref, hi_ref, z_ref, q_ref, k_ref, v_ref, lse_ref, mixed_ref, cos_ref, sin_ref, tok_hbm, w_hbm, *refs):
+    zsize, _, rows, _ = tok_hbm.shape
     do_refs, refs = refs[:zsize], refs[zsize:]
     if group:
-        before_ref, refs = refs[0], refs[1:]
-    back_ref, wgrad_ref, sum_ref, grad_ref, wsum_ref, dox_ref, kt_ref, delta_ref, dk_ref, dv_ref, dqt_ref = refs
+        before_hbm, refs = refs[0], refs[1:]
+    back_ref, wgrad_ref, sum_ref, grad_ref, wsum_ref, dox_ref, kt_ref, delta_ref, dk_ref, dv_ref, dqt_ref, tok_ref, w_ref, sem = refs
+    late = [
+        pltpu.make_async_copy(tok_hbm.at[:, group], tok_ref, sem.at[0]), pltpu.make_async_copy(w_hbm, w_ref, sem.at[1]),
+    ]
+    if group:
+        late.append(pltpu.make_async_copy(before_hbm, wsum_ref, sem.at[2]))
+    for copy in late:
+        copy.start()
     heads, length = q_ref.shape[1], q_ref.shape[2]
     pair = 2 * HEAD_DIM
     scale = HEAD_DIM ** (-0.5)
@@ -220,7 +227,8 @@
                 dv_ref[head, at, :] = jnp.zeros((rows, pair), f32)
 
     sum_ref[...] = jnp.zeros(sum_ref.shape, f32)
-    wsum_ref[...] = before_ref[...] if group else jnp.zeros(wsum_ref.shape, f32)
+    if not group:
+        wsum_ref[...] = jnp.zeros(wsum_ref.shape, f32)
 
     def put(c, j, at, field):
         low = field.astype(bf16)
@@ -277,7 +285,7 @@
         i = slot if last else lax.rem(z_ref[0] + slot, zsize)
         at = pl.ds(pl.multiple_of(i * rows, rows), rows)
         total = None
-        x = tok_ref[i, 0]
+        x = tok_ref[i]
         for c in range(3):
             grad = grad_ref[c, at, :]
             part = lax.dot_general(grad, w_ref[c], (((1,), (1,)), ((), ())), preferred_element_type=f32)
@@ -286,6 +294,8 @@
         back_ref[0, slot] = total.astype(bf16)
         return carry
 
+    for copy in late:
+        copy.wait()
     lax.fori_loop(0, zsize, onward, 0)
     wgrad_ref[...] = wsum_ref[...].astype(wgrad_ref.dtype)
 
@@ -308,13 +318,14 @@
             in_specs=[whole((1,) + wide)] * 3 + [
                 whole((1, heads, length)), whole((1, length, cols)),
                 of_group((1, length, pair)), of_group((1, length, pair)),
-                pl.BlockSpec((zsize, 1, rows, width), lambda i, *_: (0, group, 0, 0)), whole(weight.shape),
-            ] + [whole((1, rows, cols))] * zsize + [whole(weight.shape)] * (group > 0),
+                HBM, HBM,
+            ] + [whole((1, rows, cols))] * zsize + [HBM] * (group > 0),
             out_specs=[whole((1, zsize, rows, width)), whole(weight.shape), whole((8, cols))],
             scratch_shapes=[
                 pltpu.VMEM((3, length, cols), bf16), pltpu.VMEM(weight.shape, f32),
                 pltpu.VMEM(wide, bf16), pltpu.VMEM((heads, HEAD_DIM, length), bf16), pltpu.VMEM((heads, length), f32),
                 pltpu.VMEM(wide, f32), pltpu.VMEM(wide, f32), pltpu.VMEM((heads, HEAD_DIM, BLOCK), f32),
+                pltpu.VMEM((zsize, rows, width), bf16), pltpu.VMEM(weight.shape, bf16), pltpu.SemaphoreType.DMA((3,)),
             ],
         ),
         out_shape=[
@@ -1124,7 +1135,7 @@
 
 
 def widen(up, down, out, qkv, first, parts):
-    steps = 8
+    steps = 4
     per_group = steps // len(parts)
 
     def rows_of(array):

time: 451 us -> 448 us (level)
  no operation moved by 1% of the time
where the time goes in v9:
time: 448 us; the launch traced here: 444 us
  Pallas kernels  368 us (82%)
  other arithmetic  26.2 us (6%)
  starting transfers between devices  22.7 us (5%)
  local copies, waits for them, and re-layouts  15.6 us (3%)
  waiting for transfers between devices  6.69 us (1%)
    pallas_call x1, Pallas kernels, reduce_end(): pl.pallas_call(functools.partial(reduce_kernel, zsize, orders, w), out_sh...  114 us
    pallas_call x1, Pallas kernels, gather_start(): pl.pallas_call(functools.partial(gather_kernel, zsize, orders), out_shape...  110 us
    pallas_call x2, Pallas kernels, attend_backward(): pl.pallas_call(functools.partial(attend_back_kernel, group, last), grid_s...  44.4 us
    pallas_call x2, Pallas kernels, attend_forward(): pl.pallas_call(functools.partial(attend_kernel, group), grid_spec=pltpu.P...  33.6 us
    pallas_call x1, Pallas kernels, ffn_forward(): pl.pallas_call(functools.partial(ffn_kernel, zsize, groups), grid_spec=pl...  30.2 us
    pallas_call x1, Pallas kernels, ffn_backward(): pl.pallas_call(ffn_back_kernel, grid_spec=pltpu.PrefetchScalarGridSpec(nu...  25.8 us
    ppermute x12, starting transfers between devices, exchange(): parts.append(lax.ppermute(part, 'z', ring(step)) if step else part)  11.7 us
    add x2, other arithmetic, first_halving(): return (pick(keep, 1 - i) + pick(got, 1 - i), pick(keep, i) + pick(got, i))  10 us
  transfers between devices with their start and end apart: 19, of which 3 were waited for; matrix products, arithmetic and copies ran while one was open for 7% of the time, Pallas kernels for 40%

profile of v9, /device:TPU:1, one launch (start us, length us, event | category | flops | bytes accessed | tf_op | source)
XLA Modules:
  0.0 444.2 jit_solution(12886731401041737470)
XLA Ops:
  3.4 5.5 %fusion.4 = (f32[2,1024,128]{2,1,0:T(8,128)}, f32[2,1024,128]{2,1,0:T(8,128)}) fusion(f32[128]{0:T(128)S(1)} %get-tuple-element.185, f32[128]{0:T(128)S(1)} %get-tuple-element.186, f32[2,1024]{1,0:T(2,128)S(1)} %fusion.6), kind=kLoop, calls=%fused_computation.18 | loop fusion | flops 524288 | bytes 2106368 | tf_op jit(solution)/shard_map/mul | solution.py:39
  8.9 109.6 %shard_map.288 = (bf16[4,512,1024]{2,1,0:T(8,128)(2,1)}, f32[4,8,128]{2,1,0:T(8,128)}, bf16[4,2,2,2,32,1024]{5,4,3,2,1,0:T(8,128)(2,1)}, bf16[4,2,2,2,128,1024]{...) custom-call(bf16[512,1024]{1,0:T(8,128)(2,1)} %bitcast.118, f32[8,128]{1,0:T(8,128)} %bitcast.149, ...), custom_call_target="tpu_custom_call" | custom-call | tf_op jit(solution)/shard_map/pallas_call | solution.py:515
  118.5 16.1 %shard_map.290 = (bf16[1,1024,256]{2,1,0:T(8,128)(2,1)}, bf16[1,4,1024,128]{3,2,1,0:T(8,128)(2,1)}, bf16[1,4,1024,128]{3,2,1,0:T(8,128)(2,1)}, bf16[1,4,1024,128]{3,2,1,0:T(8,128)(2,1)}, f32[1,4,1024]{2,1,0:T(4,128)}) custom-call(s32[2,4]{1,0:T(2,128)} %get-tuple-element.188.lo_ref, s32[2,4]{1,0:T(2,128)} %get-tuple-element.187.hi_ref, ...), custom_call_target="tpu_custom_call" | custom-call | flops 2684354560 | bytes 5767168 | tf_op jit(solution)/shard_map/pallas_call | solution.py:159
  134.6 1.8 constant_dynamic-slice_fusion
  137.9 17.5 %shard_map.289 = (bf16[1,1024,256]{2,1,0:T(8,128)(2,1)}, bf16[1,4,1024,128]{3,2,1,0:T(8,128)(2,1)}, bf16[1,4,1024,128]{3,2,1,0:T(8,128)(2,1)}, bf16[1,4,1024,128]{3,2,1,0:T(8,128)(2,1)}, f32[1,4,1024]{2,1,0:T(4,128)}) custom-call(s32[2,4]{1,0:T(2,128)} %get-tuple-element.188.lo_ref, s32[2,4]{1,0:T(2,128)} %get-tuple-element.187.hi_ref, ...), custom_call_target="tpu_custom_call" | custom-call | flops 2684354560 | bytes 5767168 | tf_op jit(solution)/shard_map/pallas_call | solution.py:159
  155.3 1.8 constant_dynamic-slice_fusion.4
  157.1 2.6 collective-permute-start.2
  161.7 5.6 %collective-permute-done.1.refs_2_ = bf16[1,256,256]{2,1,0:T(8,128)(2,1)S(1)} collective-permute-done((bf16[1,256,256]{2,1,0:T(8,128)(2,1)S(1)}, bf16[1,256,256]{2,1,0:T(8,128)(2,1)S(1)}, u32[]{:S(2)}, u32[]{:S(2)}) %collective-permute-start.1) | collective-permute-done | bytes 131104 | tf_op jit(solution)/shard_map/ppermute | solution.py:1203
  167.9 30.2 %shard_map.291 = (bf16[4,1024,512]{2,1,0:T(8,128)(2,1)}, bf16[4,512,1024]{2,1,0:T(8,128)(2,1)}, bf16[512,1024]{1,0:T(8,128)(2,1)}, bf16[512,1024]{1,0:T(8,128)(2...) custom-call(s32[1]{0:T(128)} %bitcast.z_ref, ...), custom_call_target="tpu_custom_call" | custom-call | tf_op jit(solution)/shard_map/pallas_call | solution.py:1022
  198.2 25.8 %shard_map.292 = (bf16[4,512,1024]{2,1,0:T(8,128)(2,1)}, bf16[4,512,1024]{2,1,0:T(8,128)(2,1)}, bf16[4,512,1024]{2,1,0:T(8,128)(2,1)}, bf16[4,512,1024]{2,1,0:T(...) custom-call(s32[1]{0:T(128)} %bitcast.22.core_ref, bf16[512,1024]{1,0:T(8,128)(2,1)} %get-tuple-element.86.second_ref, ...), custom_call_target="tpu_custom_call" | custom-call | tf_op jit(solution)/shard_map/pallas_call | solution.py:1083
  224.0 7.7 %collective-permute-start.6 = (bf16[4,512,1024]{2,1,0:T(8,128)(2,1)}, bf16[4,512,1024]{2,1,0:T(8,128)(2,1)}, u32[]{:S(2)}, u32[]{:S(2)}) collective-permute-start(bf16[4,512,1024]{2,1,0:T(8,128)(2,1)} %get-tuple-element.91), channel_id=1, source_target_pairs={{0,4},{4,0},{1,5},{5,1},{2,6},{6,2},{3,7},{7,3},{8,12},{12,8},{9,1... | collective-permute-start | bytes 12582920 | tf_op jit(solution)/shard_map/ppermute | solution.py:1222
  232.7 3.2 multiply_reduce_fusion
  241.1 1.5 collective-permute-start.11
  242.6 5.0 %fusion = (bf16[4,2,128,1024]{3,2,1,0:T(8,128)(2,1)}, bf16[4,2,128,1024]{3,2,1,0:T(8,128)(2,1)}) fusion(bf16[4,2,2,128,1024]{4,3,2,1,0:T(8,128)(2,1)} %bitcast.24, s32[]{:T(128)S(6)} %select_n.120, bf16[4,2,2,128,1024]{4,3,2,1,0:T(8,128)(2,1)S(1)} %bitcast.117, s32[]{:T(128)S(6)} %select_n.117), kind=kLoop, calls=%fused_computation.1 | loop fusion | flops 2097152 | bytes 12582920 | tf_op jit(solution)/shard_map/add | solution.py:1118
  247.6 5.0 %fusion.1 = (bf16[4,2,128,1024]{3,2,1,0:T(8,128)(2,1)}, bf16[4,2,128,1024]{3,2,1,0:T(8,128)(2,1)}) fusion(bf16[4,2,2,128,1024]{4,3,2,1,0:T(8,128)(2,1)} %bitcast.27, s32[]{:T(128)S(6)} %select_n.119, bf16[4,2,2,128,1024]{4,3,2,1,0:T(8,128)(2,1)S(1)} %bitcast.116, s32[]{:T(128)S(6)} %select_n.118), kind=kLoop, calls=%fused_computation.3 | loop fusion | flops 2097152 | bytes 12582920 | tf_op jit(solution)/shard_map/add | solution.py:1118
  258.7 2.6 convolution_convert_fusion
  261.3 23.1 %shard_map.293 = (bf16[1,4,256,1024]{3,2,1,0:T(8,128)(2,1)}, f32[3,1024,256]{2,1,0:T(8,128)}, f32[8,256]{1,0:T(8,128)}) custom-call(s32[2,4]{1,0:T(2,128)} %get-tuple-element.188.lo_ref, s32[2,4]{1,0:T(2,128)} %get-tuple-element.187.hi_ref, s32[1]{0:T(128)} %bitcast.z_ref, bf16[1,4,1024,128]{3,2,1,0:T(8,128)(2,1)} %get-tuple-element.102.q_ref, ...), custom_call_target="tpu_custom_call" | custom-call | flops 10737418240 | bytes 12582912 | tf_op jit(solution)/shard_map/pallas_call | solution.py:313
  284.4 2.5 slice_bitcast_fusion
  286.9 1.8 collective-permute-start.18
  289.4 21.3 %shard_map.294 = (bf16[1,4,256,1024]{3,2,1,0:T(8,128)(2,1)}, bf16[3,1024,256]{2,1,0:T(8,128)(2,1)}, f32[8,256]{1,0:T(8,128)}) custom-call(s32[2,4]{1,0:T(2,128)} %get-tuple-element.188.lo_ref, s32[2,4]{1,0:T(2,128)} %get-tuple-element.187.hi_ref, s32[1]{0:T(128)} %bitcast.z_ref, bf16[1,4,1024,128]{3,2,1,0:T(8,128)(2,1)} %get-tuple-element.94.q_ref, ...), custom_call_target="tpu_custom_call" | custom-call | tf_op jit(solution)/shard_map/pallas_call | solution.py:313
  312.2 114.2 %shard_map.295 = (bf16[2,2,2,128,1024]{4,3,2,1,0:T(8,128)(2,1)}, bf16[2,2,2,128,1024]{4,3,2,1,0:T(8,128)(2,1)}, bf16[2,2,2,32,1024]{4,3,2,1,0:T(8,128)(2,1)}, bf...) custom-call(bf16[4,2,128,1024]{3,2,1,0:T(8,128)(2,1)} %get-tuple-ele, ...), custom_call_target="tpu_custom_call" | custom-call | tf_op jit(solution)/shard_map/pallas_call | solution.py:907
  429.1 1.5 fusion.15
  430.7 2.2 convert_bitcast_fusion
  434.0 10.0 %shard_map.296 = (f32[1024,1024]{1,0:T(8,128)}, f32[1024,1024]{1,0:T(8,128)}, f32[256,1024]{1,0:T(8,128)}, f32[3,1024,256]{2,1,0:T(8,128)}, f32[512,1024]{1,0:T(8,128)}) custom-call(bf16[1024,1024]{1,0:T(8,128)(2,1)} %bitcast.129, bf16[1024,1024]{1,0:T(8,128)(2,1)} %bitcast.130, bf16[256,1024]{1,0:T(8,128)(2,1)} %bitcast.137, ...), custom_call_target="tpu_custom_call" | custom-call | tf_op jit(solution)/shard_map/pallas_call | solution.py:1152
  (117 shorter events, 24.9 us)
Async XLA Ops:
  136.4 23.9 %collective-permute-start.5 = (bf16[1,256,256]{2,1,0:T(8,128)(2,1)S(1)}, bf16[1,256,256]{2,1,0:T(8,128)(2,1)S(1)}, u32[]{:S(2)}, u32[]{:S(2)}) collective-permute-start(bf16[1,256,256]{2,1,0:T(8,128)(2,1)S(1)} %get-tuple-element.169), channel_id=1, source_target_pairs={{0,3},{1,0},{2,1},{3,2},{4,7},{5,4},{6,5},{7,6},{8,11},{9,8},{10,9... | collective-permute-start | bytes 393224 | tf_op jit(solution)/shard_map/ppermute | solution.py:1203
  137.2 23.7 %collective-permute-start.4 = (bf16[1,256,256]{2,1,0:T(8,128)(2,1)S(1)}, bf16[1,256,256]{2,1,0:T(8,128)(2,1)S(1)}, u32[]{:S(2)}, u32[]{:S(2)}) collective-permute-start(bf16[1,256,256]{2,1,0:T(8,128)(2,1)S(1)} %get-tuple-element.170), channel_id=1, source_target_pairs={{0,2},{1,3},{2,0},{3,1},{4,6},{5,7},{6,4},{7,5},{8,10},{9,11},{10,... | collective-permute-start | bytes 393224 | tf_op jit(solution)/shard_map/ppermute | solution.py:1203
  137.2 23.7 %collective-permute-start.3 = (bf16[1,256,256]{2,1,0:T(8,128)(2,1)S(1)}, bf16[1,256,256]{2,1,0:T(8,128)(2,1)S(1)}, u32[]{:S(2)}, u32[]{:S(2)}) collective-permute-start(bf16[1,256,256]{2,1,0:T(8,128)(2,1)S(1)} %get-tuple-element.171), channel_id=1, source_target_pairs={{0,1},{1,2},{2,3},{3,0},{4,5},{5,6},{6,7},{7,4},{8,9},{9,10},{10,1... | collective-permute-start | bytes 393224 | tf_op jit(solution)/shard_map/ppermute | solution.py:1203
  157.1 4.6 %collective-permute-start.2 = (bf16[1,256,256]{2,1,0:T(8,128)(2,1)S(1)}, bf16[1,256,256]{2,1,0:T(8,128)(2,1)S(1)}, u32[]{:S(2)}, u32[]{:S(2)}) collective-permute-start(bf16[1,256,256]{2,1,0:T(8,128)(2,1)S(1)} %get-tuple-element.173), channel_id=1, source_target_pairs={{0,3},{1,0},{2,1},{3,2},{4,7},{5,4},{6,5},{7,6},{8,11},{9,8},{10,9... | collective-permute-start | bytes 393224 | tf_op jit(solution)/shard_map/ppermute | solution.py:1203
  159.7 7.5 %collective-permute-start.1 = (bf16[1,256,256]{2,1,0:T(8,128)(2,1)S(1)}, bf16[1,256,256]{2,1,0:T(8,128)(2,1)S(1)}, u32[]{:S(2)}, u32[]{:S(2)}) collective-permute-start(bf16[1,256,256]{2,1,0:T(8,128)(2,1)S(1)} %get-tuple-element.174), channel_id=1, source_target_pairs={{0,2},{1,3},{2,0},{3,1},{4,6},{5,7},{6,4},{7,5},{8,10},{9,11},{10,... | collective-permute-start | bytes 393224 | tf_op jit(solution)/shard_map/ppermute | solution.py:1203
  160.3 7.0 %collective-permute-start = (bf16[1,256,256]{2,1,0:T(8,128)(2,1)S(1)}, bf16[1,256,256]{2,1,0:T(8,128)(2,1)S(1)}, u32[]{:S(2)}, u32[]{:S(2)}) collective-permute-start(bf16[1,256,256]{2,1,0:T(8,128)(2,1)S(1)} %get-tuple-element.175), channel_id=1, source_target_pairs={{0,1},{1,2},{2,3},{3,0},{4,5},{5,6},{6,7},{7,4},{8,9},{9,10},{10,1... | collective-permute-start | bytes 393224 | tf_op jit(solution)/shard_map/ppermute | solution.py:1203
  198.1 33.6 %copy-start.9 = (f32[512,1]{1,0:T(8,128)S(1)}, f32[512,1]{1,0:T(8,128)}, u32[]{:S(2)}) copy-start(f32[512,1]{1,0:T(8,128)} %get-tuple-element.98) | copy-start | bytes 6148
  198.1 34.6 %copy-start.1 = (f32[512,1024]{1,0:T(8,128)S(1)}, f32[512,1024]{1,0:T(8,128)}, u32[]{:S(2)}) copy-start(f32[512,1024]{1,0:T(8,128)} %get-tuple-element.101) | copy-start | bytes 6291460
  198.1 34.6 %copy-start.19 = (f32[1024]{0:T(1024)S(1)}, f32[1024]{0:T(1024)}, u32[]{:S(2)}) copy-start(f32[1024]{0:T(1024)} %param.23) | copy-start | bytes 12292
  224.0 18.5 %collective-permute-start.6 = (bf16[4,512,1024]{2,1,0:T(8,128)(2,1)}, bf16[4,512,1024]{2,1,0:T(8,128)(2,1)}, u32[]{:S(2)}, u32[]{:S(2)}) collective-permute-start(bf16[4,512,1024]{2,1,0:T(8,128)(2,1)} %get-tuple-element.91), channel_id=1, source_target_pairs={{0,4},{4,0},{1,5},{5,1},{2,6},{6,2},{3,7},{7,3},{8,12},{12,8},{9,1... | collective-permute-start | bytes 12582920 | tf_op jit(solution)/shard_map/ppermute | solution.py:1222
  231.7 15.9 %collective-permute-start.7 = (bf16[4,512,1024]{2,1,0:T(8,128)(2,1)}, bf16[4,512,1024]{2,1,0:T(8,128)(2,1)}, u32[]{:S(2)}, u32[]{:S(2)}) collective-permute-start(bf16[4,512,1024]{2,1,0:T(8,128)(2,1)} %get-tuple-element.93), channel_id=1, source_target_pairs={{0,4},{4,0},{1,5},{5,1},{2,6},{6,2},{3,7},{7,3},{8,12},{12,8},{9,1... | collective-permute-start | bytes 12582920 | tf_op jit(solution)/shard_map/ppermute | solution.py:1221
  236.5 22.2 %copy-start = (f32[512,1024]{1,0:T(8,128)}, f32[512,1024]{1,0:T(8,128)S(1)}, u32[]{:S(2)}) copy-start(f32[512,1024]{1,0:T(8,128)S(1)} %get-tuple-element.149.first_ref) | copy-start | bytes 6291460
  239.9 12.7 %collective-permute-start.13 = (bf16[1,256,256]{2,1,0:T(8,128)(2,1)S(1)}, bf16[1,256,256]{2,1,0:T(8,128)(2,1)S(1)}, u32[]{:S(2)}, u32[]{:S(2)}) collective-permute-start(bf16[1,256,256]{2,1,0:T(8,128)(2,1)S(1)} %get-tuple-element.161), channel_id=1, source_target_pairs={{0,3},{1,0},{2,1},{3,2},{4,7},{5,4},{6,5},{7,6},{8,11},{9,8},{10,9... | collective-permute-start | bytes 393224 | tf_op jit(solution)/shard_map/ppermute | solution.py:1203
  240.6 12.4 %collective-permute-start.12 = (bf16[1,256,256]{2,1,0:T(8,128)(2,1)S(1)}, bf16[1,256,256]{2,1,0:T(8,128)(2,1)S(1)}, u32[]{:S(2)}, u32[]{:S(2)}) collective-permute-start(bf16[1,256,256]{2,1,0:T(8,128)(2,1)S(1)} %get-tuple-element.162), channel_id=1, source_target_pairs={{0,2},{1,3},{2,0},{3,1},{4,6},{5,7},{6,4},{7,5},{8,10},{9,11},{10,... | collective-permute-start | bytes 393224 | tf_op jit(solution)/shard_map/ppermute | solution.py:1203
  241.1 11.9 %collective-permute-start.11 = (bf16[1,256,256]{2,1,0:T(8,128)(2,1)S(1)}, bf16[1,256,256]{2,1,0:T(8,128)(2,1)S(1)}, u32[]{:S(2)}, u32[]{:S(2)}) collective-permute-start(bf16[1,256,256]{2,1,0:T(8,128)(2,1)S(1)} %get-tuple-element.163), channel_id=1, source_target_pairs={{0,1},{1,2},{2,3},{3,0},{4,5},{5,6},{6,7},{7,4},{8,9},{9,10},{10,1... | collective-permute-start | bytes 393224 | tf_op jit(solution)/shard_map/ppermute | solution.py:1203
  253.0 58.4 %collective-permute-start.14 = (bf16[4,2,128,1024]{3,2,1,0:T(8,128)(2,1)}, bf16[4,2,128,1024]{3,2,1,0:T(8,128)(2,1)}, u32[]{:S(2)}, u32[]{:S(2)}) collective-permute-start(bf16[4,2,128,1024]{3,2,1,0:T(8,128)(2,1)} %get-tuple-element.112), channel_id=1, source_target_pairs={{0,8},{8,0},{1,9},{9,1},{2,10},{10,2},{3,11},{11,3},{4,12},{12,4},... | collective-permute-start | bytes 6291464 | tf_op jit(solution)/shard_map/ppermute | solution.py:1234
  253.1 58.3 %collective-permute-start.15 = (bf16[4,2,128,1024]{3,2,1,0:T(8,128)(2,1)}, bf16[4,2,128,1024]{3,2,1,0:T(8,128)(2,1)}, u32[]{:S(2)}, u32[]{:S(2)}) collective-permute-start(bf16[4,2,128,1024]{3,2,1,0:T(8,128)(2,1)} %get-tuple-element.113), channel_id=1, source_target_pairs={{0,16},{16,0},{1,17},{17,1},{2,18},{18,2},{3,19},{19,3},{4,20},{20... | collective-permute-start | bytes 6291464 | tf_op jit(solution)/shard_map/ppermute | solution.py:1235
  254.9 32.0 %collective-permute-start.10 = (bf16[1,256,256]{2,1,0:T(8,128)(2,1)S(1)}, bf16[1,256,256]{2,1,0:T(8,128)(2,1)S(1)}, u32[]{:S(2)}, u32[]{:S(2)}) collective-permute-start(bf16[1,256,256]{2,1,0:T(8,128)(2,1)S(1)} %get-tuple-element.165), channel_id=1, source_target_pairs={{0,3},{1,0},{2,1},{3,2},{4,7},{5,4},{6,5},{7,6},{8,11},{9,8},{10,9... | collective-permute-start | bytes 393224 | tf_op jit(solution)/shard_map/ppermute | solution.py:1203
  256.3 32.4 %collective-permute-start.9 = (bf16[1,256,256]{2,1,0:T(8,128)(2,1)S(1)}, bf16[1,256,256]{2,1,0:T(8,128)(2,1)S(1)}, u32[]{:S(2)}, u32[]{:S(2)}) collective-permute-start(bf16[1,256,256]{2,1,0:T(8,128)(2,1)S(1)} %get-tuple-element.166), channel_id=1, source_target_pairs={{0,2},{1,3},{2,0},{3,1},{4,6},{5,7},{6,4},{7,5},{8,10},{9,11},{10,... | collective-permute-start | bytes 393224 | tf_op jit(solution)/shard_map/ppermute | solution.py:1203
  257.2 31.6 %collective-permute-start.8 = (bf16[1,256,256]{2,1,0:T(8,128)(2,1)S(1)}, bf16[1,256,256]{2,1,0:T(8,128)(2,1)S(1)}, u32[]{:S(2)}, u32[]{:S(2)}) collective-permute-start(bf16[1,256,256]{2,1,0:T(8,128)(2,1)S(1)} %get-tuple-element.167), channel_id=1, source_target_pairs={{0,1},{1,2},{2,3},{3,0},{4,5},{5,6},{6,7},{7,4},{8,9},{9,10},{10,1... | collective-permute-start | bytes 393224 | tf_op jit(solution)/shard_map/ppermute | solution.py:1203
  286.9 145.9 %collective-permute-start.18 = (bf16[256,1024]{1,0:T(8,128)(2,1)S(1)}, bf16[256,1024]{1,0:T(8,128)(2,1)S(1)}, u32[]{:S(2)}, u32[]{:S(2)}) collective-permute-start(bf16[256,1024]{1,0:T(8,128)(2,1)S(1)} %get-tuple-element.155), channel_id=1, source_target_pairs={{0,3},{1,0},{2,1},{3,2},{4,7},{5,4},{6,5},{7,6},{8,11},{9,8},{10,9... | collective-permute-start | bytes 1572872 | tf_op jit(solution)/shard_map/ppermute | solution.py:1244
  288.7 144.1 %collective-permute-start.17 = (bf16[256,1024]{1,0:T(8,128)(2,1)S(1)}, bf16[256,1024]{1,0:T(8,128)(2,1)S(1)}, u32[]{:S(2)}, u32[]{:S(2)}) collective-permute-start(bf16[256,1024]{1,0:T(8,128)(2,1)S(1)} %get-tuple-element.156), channel_id=1, source_target_pairs={{0,2},{1,3},{2,0},{3,1},{4,6},{5,7},{6,4},{7,5},{8,10},{9,11},{10,... | collective-permute-start | bytes 1572872 | tf_op jit(solution)/shard_map/ppermute | solution.py:1244
  288.7 144.1 %collective-permute-start.16 = (bf16[256,1024]{1,0:T(8,128)(2,1)S(1)}, bf16[256,1024]{1,0:T(8,128)(2,1)S(1)}, u32[]{:S(2)}, u32[]{:S(2)}) collective-permute-start(bf16[256,1024]{1,0:T(8,128)(2,1)S(1)} %get-tuple-element.157), channel_id=1, source_target_pairs={{0,1},{1,2},{2,3},{3,0},{4,5},{5,6},{6,7},{7,4},{8,9},{9,10},{10,1... | collective-permute-start | bytes 1572872 | tf_op jit(solution)/shard_map/ppermute | solution.py:1244
  289.4 22.1 %copy-start.20 = (f32[8,1024]{1,0:T(8,128)S(1)}, f32[8,1024]{1,0:T(8,128)}, u32[]{:S(2)}) copy-start(f32[8,1024]{1,0:T(8,128)} %get-tuple-element.122) | copy-start | bytes 98308
  (21 other events, 105.4 us)

commit v10 on v9

--- a/solution.py
+++ b/solution.py
@@ -532,7 +532,7 @@
 
 def add_rows(dst, src):
     rows = dst.shape[0]
-    step = math.gcd(rows, 32)
+    step = math.gcd(rows, 64)
 
     def body(i, carry):
         at = pl.ds(pl.multiple_of(i * step, step), step)

time: 448 us -> 453 us (1.011)
  starting transfers between devices: 22.7 us -> 17.5 us
  Pallas kernels: 368 us -> 373 us
    ppermute x1, starting transfers between devices: 7.68 us -> 2.32 us  [per_device(): got_up = lax.ppermute(give_up, 'core', PAIR)]
where the time goes in v10:
time: 453 us; the launch traced here: 448 us
  Pallas kernels  373 us (82%)
  other arithmetic  26.2 us (6%)
  starting transfers between devices  17.5 us (4%)
  local copies, waits for them, and re-layouts  15.7 us (3%)
  waiting for transfers between devices  10.8 us (2%)
    pallas_call x1, Pallas kernels, reduce_end(): pl.pallas_call(functools.partial(reduce_kernel, zsize, orders, w), out_sh...  116 us
    pallas_call x1, Pallas kernels, gather_start(): pl.pallas_call(functools.partial(gather_kernel, zsize, orders), out_shape...  110 us
    pallas_call x2, Pallas kernels, attend_backward(): pl.pallas_call(functools.partial(attend_back_kernel, group, last), grid_s...  45.9 us
    pallas_call x2, Pallas kernels, attend_forward(): pl.pallas_call(functools.partial(attend_kernel, group), grid_spec=pltpu.P...  35 us
    pallas_call x1, Pallas kernels, ffn_forward(): pl.pallas_call(functools.partial(ffn_kernel, zsize, groups), grid_spec=pl...  30.2 us
    pallas_call x1, Pallas kernels, ffn_backward(): pl.pallas_call(ffn_back_kernel, grid_spec=pltpu.PrefetchScalarGridSpec(nu...  25.8 us
    ppermute x12, starting transfers between devices, exchange(): parts.append(lax.ppermute(part, 'z', ring(step)) if step else part)  11.4 us
    ppermute x12, waiting for transfers between devices, exchange(): parts.append(lax.ppermute(part, 'z', ring(step)) if step else part)  10.8 us
  transfers between devices with their start and end apart: 19, of which 3 were waited for; matrix products, arithmetic and copies ran while one was open for 7% of the time, Pallas kernels for 40%

profile of v10, /device:TPU:1, one launch (start us, length us, event | category | flops | bytes accessed | tf_op | source)
XLA Modules:
  0.0 448.3 jit_solution(15341720157984535621)
XLA Ops:
  3.4 5.5 %fusion.4 = (f32[2,1024,128]{2,1,0:T(8,128)}, f32[2,1024,128]{2,1,0:T(8,128)}) fusion(f32[128]{0:T(128)S(1)} %get-tuple-element.185, f32[128]{0:T(128)S(1)} %get-tuple-element.186, f32[2,1024]{1,0:T(2,128)S(1)} %fusion.6), kind=kLoop, calls=%fused_computation.18 | loop fusion | flops 524288 | bytes 2106368 | tf_op jit(solution)/shard_map/mul | solution.py:39
  8.9 109.6 %shard_map.288 = (bf16[4,512,1024]{2,1,0:T(8,128)(2,1)}, f32[4,8,128]{2,1,0:T(8,128)}, bf16[4,2,2,2,32,1024]{5,4,3,2,1,0:T(8,128)(2,1)}, bf16[4,2,2,2,128,1024]{...) custom-call(bf16[512,1024]{1,0:T(8,128)(2,1)} %bitcast.118, f32[8,128]{1,0:T(8,128)} %bitcast.149, ...), custom_call_target="tpu_custom_call" | custom-call | tf_op jit(solution)/shard_map/pallas_call | solution.py:515
  118.5 17.5 %shard_map.290 = (bf16[1,1024,256]{2,1,0:T(8,128)(2,1)}, bf16[1,4,1024,128]{3,2,1,0:T(8,128)(2,1)}, bf16[1,4,1024,128]{3,2,1,0:T(8,128)(2,1)}, bf16[1,4,1024,128]{3,2,1,0:T(8,128)(2,1)}, f32[1,4,1024]{2,1,0:T(4,128)}) custom-call(s32[2,4]{1,0:T(2,128)} %get-tuple-element.188.lo_ref, s32[2,4]{1,0:T(2,128)} %get-tuple-element.187.hi_ref, ...), custom_call_target="tpu_custom_call" | custom-call | flops 2684354560 | bytes 5767168 | tf_op jit(solution)/shard_map/pallas_call | solution.py:159
  136.0 1.8 constant_dynamic-slice_fusion
  139.3 17.5 %shard_map.289 = (bf16[1,1024,256]{2,1,0:T(8,128)(2,1)}, bf16[1,4,1024,128]{3,2,1,0:T(8,128)(2,1)}, bf16[1,4,1024,128]{3,2,1,0:T(8,128)(2,1)}, bf16[1,4,1024,128]{3,2,1,0:T(8,128)(2,1)}, f32[1,4,1024]{2,1,0:T(4,128)}) custom-call(s32[2,4]{1,0:T(2,128)} %get-tuple-element.188.lo_ref, s32[2,4]{1,0:T(2,128)} %get-tuple-element.187.hi_ref, ...), custom_call_target="tpu_custom_call" | custom-call | flops 2684354560 | bytes 5767168 | tf_op jit(solution)/shard_map/pallas_call | solution.py:159
  156.7 1.8 constant_dynamic-slice_fusion.4
  158.5 2.6 collective-permute-start.2
  163.0 9.7 %collective-permute-done.1.refs_2_ = bf16[1,256,256]{2,1,0:T(8,128)(2,1)S(1)} collective-permute-done((bf16[1,256,256]{2,1,0:T(8,128)(2,1)S(1)}, bf16[1,256,256]{2,1,0:T(8,128)(2,1)S(1)}, u32[]{:S(2)}, u32[]{:S(2)}) %collective-permute-start.1) | collective-permute-done | bytes 131104 | tf_op jit(solution)/shard_map/ppermute | solution.py:1203
  173.4 30.2 %shard_map.291 = (bf16[4,1024,512]{2,1,0:T(8,128)(2,1)}, bf16[4,512,1024]{2,1,0:T(8,128)(2,1)}, bf16[512,1024]{1,0:T(8,128)(2,1)}, bf16[512,1024]{1,0:T(8,128)(2...) custom-call(s32[1]{0:T(128)} %bitcast.z_ref, ...), custom_call_target="tpu_custom_call" | custom-call | tf_op jit(solution)/shard_map/pallas_call | solution.py:1022
  203.6 25.8 %shard_map.292 = (bf16[4,512,1024]{2,1,0:T(8,128)(2,1)}, bf16[4,512,1024]{2,1,0:T(8,128)(2,1)}, bf16[4,512,1024]{2,1,0:T(8,128)(2,1)}, bf16[4,512,1024]{2,1,0:T(...) custom-call(s32[1]{0:T(128)} %bitcast.22.core_ref, bf16[512,1024]{1,0:T(8,128)(2,1)} %get-tuple-element.86.second_ref, ...), custom_call_target="tpu_custom_call" | custom-call | tf_op jit(solution)/shard_map/pallas_call | solution.py:1083
  229.5 2.3 collective-permute-start.6
  232.9 3.2 multiply_reduce_fusion
  241.4 1.5 collective-permute-start.11
  242.9 5.0 %fusion = (bf16[4,2,128,1024]{3,2,1,0:T(8,128)(2,1)}, bf16[4,2,128,1024]{3,2,1,0:T(8,128)(2,1)}) fusion(bf16[4,2,2,128,1024]{4,3,2,1,0:T(8,128)(2,1)} %bitcast.24, s32[]{:T(128)S(6)} %select_n.120, bf16[4,2,2,128,1024]{4,3,2,1,0:T(8,128)(2,1)S(1)} %bitcast.117, s32[]{:T(128)S(6)} %select_n.117), kind=kLoop, calls=%fused_computation.1 | loop fusion | flops 2097152 | bytes 12582920 | tf_op jit(solution)/shard_map/add | solution.py:1118
  247.9 5.0 %fusion.1 = (bf16[4,2,128,1024]{3,2,1,0:T(8,128)(2,1)}, bf16[4,2,128,1024]{3,2,1,0:T(8,128)(2,1)}) fusion(bf16[4,2,2,128,1024]{4,3,2,1,0:T(8,128)(2,1)} %bitcast.27, s32[]{:T(128)S(6)} %select_n.119, bf16[4,2,2,128,1024]{4,3,2,1,0:T(8,128)(2,1)S(1)} %bitcast.116, s32[]{:T(128)S(6)} %select_n.118), kind=kLoop, calls=%fused_computation.3 | loop fusion | flops 2097152 | bytes 12582920 | tf_op jit(solution)/shard_map/add | solution.py:1118
  258.9 2.6 convolution_convert_fusion
  261.6 23.1 %shard_map.293 = (bf16[1,4,256,1024]{3,2,1,0:T(8,128)(2,1)}, f32[3,1024,256]{2,1,0:T(8,128)}, f32[8,256]{1,0:T(8,128)}) custom-call(s32[2,4]{1,0:T(2,128)} %get-tuple-element.188.lo_ref, s32[2,4]{1,0:T(2,128)} %get-tuple-element.187.hi_ref, s32[1]{0:T(128)} %bitcast.z_ref, bf16[1,4,1024,128]{3,2,1,0:T(8,128)(2,1)} %get-tuple-element.102.q_ref, ...), custom_call_target="tpu_custom_call" | custom-call | flops 10737418240 | bytes 12582912 | tf_op jit(solution)/shard_map/pallas_call | solution.py:313
  284.7 2.5 slice_bitcast_fusion
  287.2 1.8 collective-permute-start.18
  289.8 22.8 %shard_map.294 = (bf16[1,4,256,1024]{3,2,1,0:T(8,128)(2,1)}, bf16[3,1024,256]{2,1,0:T(8,128)(2,1)}, f32[8,256]{1,0:T(8,128)}) custom-call(s32[2,4]{1,0:T(2,128)} %get-tuple-element.188.lo_ref, s32[2,4]{1,0:T(2,128)} %get-tuple-element.187.hi_ref, s32[1]{0:T(128)} %bitcast.z_ref, bf16[1,4,1024,128]{3,2,1,0:T(8,128)(2,1)} %get-tuple-element.94.q_ref, ...), custom_call_target="tpu_custom_call" | custom-call | tf_op jit(solution)/shard_map/pallas_call | solution.py:313
  314.1 116.5 %shard_map.295 = (bf16[2,2,2,128,1024]{4,3,2,1,0:T(8,128)(2,1)}, bf16[2,2,2,128,1024]{4,3,2,1,0:T(8,128)(2,1)}, bf16[2,2,2,32,1024]{4,3,2,1,0:T(8,128)(2,1)}, bf...) custom-call(bf16[4,2,128,1024]{3,2,1,0:T(8,128)(2,1)} %get-tuple-ele, ...), custom_call_target="tpu_custom_call" | custom-call | tf_op jit(solution)/shard_map/pallas_call | solution.py:907
  433.3 1.5 fusion.15
  434.8 2.2 convert_bitcast_fusion
  438.2 10.0 %shard_map.296 = (f32[1024,1024]{1,0:T(8,128)}, f32[1024,1024]{1,0:T(8,128)}, f32[256,1024]{1,0:T(8,128)}, f32[3,1024,256]{2,1,0:T(8,128)}, f32[512,1024]{1,0:T(8,128)}) custom-call(bf16[1024,1024]{1,0:T(8,128)(2,1)} %bitcast.129, bf16[1024,1024]{1,0:T(8,128)(2,1)} %bitcast.130, bf16[256,1024]{1,0:T(8,128)(2,1)} %bitcast.137, ...), custom_call_target="tpu_custom_call" | custom-call | tf_op jit(solution)/shard_map/pallas_call | solution.py:1152
  (117 shorter events, 25.1 us)
Async XLA Ops:
  137.8 23.9 %collective-permute-start.5 = (bf16[1,256,256]{2,1,0:T(8,128)(2,1)S(1)}, bf16[1,256,256]{2,1,0:T(8,128)(2,1)S(1)}, u32[]{:S(2)}, u32[]{:S(2)}) collective-permute-start(bf16[1,256,256]{2,1,0:T(8,128)(2,1)S(1)} %get-tuple-element.169), channel_id=1, source_target_pairs={{0,3},{1,0},{2,1},{3,2},{4,7},{5,4},{6,5},{7,6},{8,11},{9,8},{10,9... | collective-permute-start | bytes 393224 | tf_op jit(solution)/shard_map/ppermute | solution.py:1203
  138.6 23.7 %collective-permute-start.4 = (bf16[1,256,256]{2,1,0:T(8,128)(2,1)S(1)}, bf16[1,256,256]{2,1,0:T(8,128)(2,1)S(1)}, u32[]{:S(2)}, u32[]{:S(2)}) collective-permute-start(bf16[1,256,256]{2,1,0:T(8,128)(2,1)S(1)} %get-tuple-element.170), channel_id=1, source_target_pairs={{0,2},{1,3},{2,0},{3,1},{4,6},{5,7},{6,4},{7,5},{8,10},{9,11},{10,... | collective-permute-start | bytes 393224 | tf_op jit(solution)/shard_map/ppermute | solution.py:1203
  138.6 23.7 %collective-permute-start.3 = (bf16[1,256,256]{2,1,0:T(8,128)(2,1)S(1)}, bf16[1,256,256]{2,1,0:T(8,128)(2,1)S(1)}, u32[]{:S(2)}, u32[]{:S(2)}) collective-permute-start(bf16[1,256,256]{2,1,0:T(8,128)(2,1)S(1)} %get-tuple-element.171), channel_id=1, source_target_pairs={{0,1},{1,2},{2,3},{3,0},{4,5},{5,6},{6,7},{7,4},{8,9},{9,10},{10,1... | collective-permute-start | bytes 393224 | tf_op jit(solution)/shard_map/ppermute | solution.py:1203
  158.5 4.5 %collective-permute-start.2 = (bf16[1,256,256]{2,1,0:T(8,128)(2,1)S(1)}, bf16[1,256,256]{2,1,0:T(8,128)(2,1)S(1)}, u32[]{:S(2)}, u32[]{:S(2)}) collective-permute-start(bf16[1,256,256]{2,1,0:T(8,128)(2,1)S(1)} %get-tuple-element.173), channel_id=1, source_target_pairs={{0,3},{1,0},{2,1},{3,2},{4,7},{5,4},{6,5},{7,6},{8,11},{9,8},{10,9... | collective-permute-start | bytes 393224 | tf_op jit(solution)/shard_map/ppermute | solution.py:1203
  161.1 11.6 %collective-permute-start.1 = (bf16[1,256,256]{2,1,0:T(8,128)(2,1)S(1)}, bf16[1,256,256]{2,1,0:T(8,128)(2,1)S(1)}, u32[]{:S(2)}, u32[]{:S(2)}) collective-permute-start(bf16[1,256,256]{2,1,0:T(8,128)(2,1)S(1)} %get-tuple-element.174), channel_id=1, source_target_pairs={{0,2},{1,3},{2,0},{3,1},{4,6},{5,7},{6,4},{7,5},{8,10},{9,11},{10,... | collective-permute-start | bytes 393224 | tf_op jit(solution)/shard_map/ppermute | solution.py:1203
  161.7 11.0 %collective-permute-start = (bf16[1,256,256]{2,1,0:T(8,128)(2,1)S(1)}, bf16[1,256,256]{2,1,0:T(8,128)(2,1)S(1)}, u32[]{:S(2)}, u32[]{:S(2)}) collective-permute-start(bf16[1,256,256]{2,1,0:T(8,128)(2,1)S(1)} %get-tuple-element.175), channel_id=1, source_target_pairs={{0,1},{1,2},{2,3},{3,0},{4,5},{5,6},{6,7},{7,4},{8,9},{9,10},{10,1... | collective-permute-start | bytes 393224 | tf_op jit(solution)/shard_map/ppermute | solution.py:1203
  203.6 28.3 %copy-start.9 = (f32[512,1]{1,0:T(8,128)S(1)}, f32[512,1]{1,0:T(8,128)}, u32[]{:S(2)}) copy-start(f32[512,1]{1,0:T(8,128)} %get-tuple-element.98) | copy-start | bytes 6148
  203.6 29.2 %copy-start.1 = (f32[512,1024]{1,0:T(8,128)S(1)}, f32[512,1024]{1,0:T(8,128)}, u32[]{:S(2)}) copy-start(f32[512,1024]{1,0:T(8,128)} %get-tuple-element.101) | copy-start | bytes 6291460
  203.6 29.2 %copy-start.19 = (f32[1024]{0:T(1024)S(1)}, f32[1024]{0:T(1024)}, u32[]{:S(2)}) copy-start(f32[1024]{0:T(1024)} %param.23) | copy-start | bytes 12292
  229.5 13.4 %collective-permute-start.6 = (bf16[4,512,1024]{2,1,0:T(8,128)(2,1)}, bf16[4,512,1024]{2,1,0:T(8,128)(2,1)}, u32[]{:S(2)}, u32[]{:S(2)}) collective-permute-start(bf16[4,512,1024]{2,1,0:T(8,128)(2,1)} %get-tuple-element.91), channel_id=1, source_target_pairs={{0,4},{4,0},{1,5},{5,1},{2,6},{6,2},{3,7},{7,3},{8,12},{12,8},{9,1... | collective-permute-start | bytes 12582920 | tf_op jit(solution)/shard_map/ppermute | solution.py:1222
  231.8 16.1 %collective-permute-start.7 = (bf16[4,512,1024]{2,1,0:T(8,128)(2,1)}, bf16[4,512,1024]{2,1,0:T(8,128)(2,1)}, u32[]{:S(2)}, u32[]{:S(2)}) collective-permute-start(bf16[4,512,1024]{2,1,0:T(8,128)(2,1)} %get-tuple-element.93), channel_id=1, source_target_pairs={{0,4},{4,0},{1,5},{5,1},{2,6},{6,2},{3,7},{7,3},{8,12},{12,8},{9,1... | collective-permute-start | bytes 12582920 | tf_op jit(solution)/shard_map/ppermute | solution.py:1221
  240.1 12.9 %collective-permute-start.13 = (bf16[1,256,256]{2,1,0:T(8,128)(2,1)S(1)}, bf16[1,256,256]{2,1,0:T(8,128)(2,1)S(1)}, u32[]{:S(2)}, u32[]{:S(2)}) collective-permute-start(bf16[1,256,256]{2,1,0:T(8,128)(2,1)S(1)} %get-tuple-element.161), channel_id=1, source_target_pairs={{0,3},{1,0},{2,1},{3,2},{4,7},{5,4},{6,5},{7,6},{8,11},{9,8},{10,9... | collective-permute-start | bytes 393224 | tf_op jit(solution)/shard_map/ppermute | solution.py:1203
  240.7 12.6 %collective-permute-start.12 = (bf16[1,256,256]{2,1,0:T(8,128)(2,1)S(1)}, bf16[1,256,256]{2,1,0:T(8,128)(2,1)S(1)}, u32[]{:S(2)}, u32[]{:S(2)}) collective-permute-start(bf16[1,256,256]{2,1,0:T(8,128)(2,1)S(1)} %get-tuple-element.162), channel_id=1, source_target_pairs={{0,2},{1,3},{2,0},{3,1},{4,6},{5,7},{6,4},{7,5},{8,10},{9,11},{10,... | collective-permute-start | bytes 393224 | tf_op jit(solution)/shard_map/ppermute | solution.py:1203
  241.4 11.9 %collective-permute-start.11 = (bf16[1,256,256]{2,1,0:T(8,128)(2,1)S(1)}, bf16[1,256,256]{2,1,0:T(8,128)(2,1)S(1)}, u32[]{:S(2)}, u32[]{:S(2)}) collective-permute-start(bf16[1,256,256]{2,1,0:T(8,128)(2,1)S(1)} %get-tuple-element.163), channel_id=1, source_target_pairs={{0,1},{1,2},{2,3},{3,0},{4,5},{5,6},{6,7},{7,4},{8,9},{9,10},{10,1... | collective-permute-start | bytes 393224 | tf_op jit(solution)/shard_map/ppermute | solution.py:1203
  253.3 60.0 %collective-permute-start.14 = (bf16[4,2,128,1024]{3,2,1,0:T(8,128)(2,1)}, bf16[4,2,128,1024]{3,2,1,0:T(8,128)(2,1)}, u32[]{:S(2)}, u32[]{:S(2)}) collective-permute-start(bf16[4,2,128,1024]{3,2,1,0:T(8,128)(2,1)} %get-tuple-element.112), channel_id=1, source_target_pairs={{0,8},{8,0},{1,9},{9,1},{2,10},{10,2},{3,11},{11,3},{4,12},{12,4},... | collective-permute-start | bytes 6291464 | tf_op jit(solution)/shard_map/ppermute | solution.py:1234
  253.4 59.9 %collective-permute-start.15 = (bf16[4,2,128,1024]{3,2,1,0:T(8,128)(2,1)}, bf16[4,2,128,1024]{3,2,1,0:T(8,128)(2,1)}, u32[]{:S(2)}, u32[]{:S(2)}) collective-permute-start(bf16[4,2,128,1024]{3,2,1,0:T(8,128)(2,1)} %get-tuple-element.113), channel_id=1, source_target_pairs={{0,16},{16,0},{1,17},{17,1},{2,18},{18,2},{3,19},{19,3},{4,20},{20... | collective-permute-start | bytes 6291464 | tf_op jit(solution)/shard_map/ppermute | solution.py:1235
  255.6 31.6 %collective-permute-start.10 = (bf16[1,256,256]{2,1,0:T(8,128)(2,1)S(1)}, bf16[1,256,256]{2,1,0:T(8,128)(2,1)S(1)}, u32[]{:S(2)}, u32[]{:S(2)}) collective-permute-start(bf16[1,256,256]{2,1,0:T(8,128)(2,1)S(1)} %get-tuple-element.165), channel_id=1, source_target_pairs={{0,3},{1,0},{2,1},{3,2},{4,7},{5,4},{6,5},{7,6},{8,11},{9,8},{10,9... | collective-permute-start | bytes 393224 | tf_op jit(solution)/shard_map/ppermute | solution.py:1203
  257.0 32.0 %collective-permute-start.9 = (bf16[1,256,256]{2,1,0:T(8,128)(2,1)S(1)}, bf16[1,256,256]{2,1,0:T(8,128)(2,1)S(1)}, u32[]{:S(2)}, u32[]{:S(2)}) collective-permute-start(bf16[1,256,256]{2,1,0:T(8,128)(2,1)S(1)} %get-tuple-element.166), channel_id=1, source_target_pairs={{0,2},{1,3},{2,0},{3,1},{4,6},{5,7},{6,4},{7,5},{8,10},{9,11},{10,... | collective-permute-start | bytes 393224 | tf_op jit(solution)/shard_map/ppermute | solution.py:1203
  257.4 31.7 %collective-permute-start.8 = (bf16[1,256,256]{2,1,0:T(8,128)(2,1)S(1)}, bf16[1,256,256]{2,1,0:T(8,128)(2,1)S(1)}, u32[]{:S(2)}, u32[]{:S(2)}) collective-permute-start(bf16[1,256,256]{2,1,0:T(8,128)(2,1)S(1)} %get-tuple-element.167), channel_id=1, source_target_pairs={{0,1},{1,2},{2,3},{3,0},{4,5},{5,6},{6,7},{7,4},{8,9},{9,10},{10,1... | collective-permute-start | bytes 393224 | tf_op jit(solution)/shard_map/ppermute | solution.py:1203
  287.2 149.8 %collective-permute-start.18 = (bf16[256,1024]{1,0:T(8,128)(2,1)S(1)}, bf16[256,1024]{1,0:T(8,128)(2,1)S(1)}, u32[]{:S(2)}, u32[]{:S(2)}) collective-permute-start(bf16[256,1024]{1,0:T(8,128)(2,1)S(1)} %get-tuple-element.155), channel_id=1, source_target_pairs={{0,3},{1,0},{2,1},{3,2},{4,7},{5,4},{6,5},{7,6},{8,11},{9,8},{10,9... | collective-permute-start | bytes 1572872 | tf_op jit(solution)/shard_map/ppermute | solution.py:1244
  289.0 148.0 %collective-permute-start.17 = (bf16[256,1024]{1,0:T(8,128)(2,1)S(1)}, bf16[256,1024]{1,0:T(8,128)(2,1)S(1)}, u32[]{:S(2)}, u32[]{:S(2)}) collective-permute-start(bf16[256,1024]{1,0:T(8,128)(2,1)S(1)} %get-tuple-element.156), channel_id=1, source_target_pairs={{0,2},{1,3},{2,0},{3,1},{4,6},{5,7},{6,4},{7,5},{8,10},{9,11},{10,... | collective-permute-start | bytes 1572872 | tf_op jit(solution)/shard_map/ppermute | solution.py:1244
  289.1 147.9 %collective-permute-start.16 = (bf16[256,1024]{1,0:T(8,128)(2,1)S(1)}, bf16[256,1024]{1,0:T(8,128)(2,1)S(1)}, u32[]{:S(2)}, u32[]{:S(2)}) collective-permute-start(bf16[256,1024]{1,0:T(8,128)(2,1)S(1)} %get-tuple-element.157), channel_id=1, source_target_pairs={{0,1},{1,2},{2,3},{3,0},{4,5},{5,6},{6,7},{7,4},{8,9},{9,10},{10,1... | collective-permute-start | bytes 1572872 | tf_op jit(solution)/shard_map/ppermute | solution.py:1244
  289.8 22.8 %copy-start.21 = (f32[8,256]{1,0:T(8,128)S(1)}, f32[8,256]{1,0:T(8,128)}, u32[]{:S(2)}) copy-start(f32[8,256]{1,0:T(8,128)} %get-tuple-element.114) | copy-start | bytes 24580
  289.8 23.7 %copy-start.20 = (f32[8,1024]{1,0:T(8,128)S(1)}, f32[8,1024]{1,0:T(8,128)}, u32[]{:S(2)}) copy-start(f32[8,1024]{1,0:T(8,128)} %get-tuple-element.122) | copy-start | bytes 98308
  (21 other events, 122.7 us)
